TPU v7x, 32 devices: a whole 2x2x4 slice. The times are simulated.
32 devices in a mesh: fsdp: 8 (over y, x, core), tp: 4 (over z).
Axes of the slice: x: 2, y: 2, z: 4, core: 2. Of those that a mesh axis runs over, the one named last changes fastest.
Arguments:
- tokens: bfloat16 [32, 1024, 768], P('fsdp', 'tp'), may hold values from -6 to 6
- segment_ids: int32 [32, 1024], P('fsdp'), may hold values from 0 to 17, as said below
- live_mask: int32 [32, 1024], P('fsdp'), may hold values from 0 to 1, as said below
- query_weight: bfloat16 [768, 768], P('fsdp', 'tp'), may hold values from -0.3125 to 0.3125
- query_bias: bfloat16 [768], P('tp'), may hold values from -3 to 3
- key_weight: bfloat16 [768, 768], P('fsdp', 'tp'), may hold values from -0.3125 to 0.3125
- value_weight: bfloat16 [768, 768], P('fsdp', 'tp'), may hold values from -0.21875 to 0.21875
- value_bias: bfloat16 [768], P('tp'), may hold values from -3 to 3
- output_weight: bfloat16 [768, 768], P('tp', 'fsdp'), may hold values from -0.875 to 0.875
- output_bias: bfloat16 [768], replicated, may hold values from -3 to 3
- first_gain: bfloat16 [768], replicated, may hold values from 0.5 to 1.5
- first_shift: bfloat16 [768], replicated, may hold values from -3 to 3
- inner_weight: bfloat16 [768, 3072], P('fsdp', 'tp'), may hold values from -0.21875 to 0.21875
- inner_bias: bfloat16 [3072], P('tp'), may hold values from -3 to 3
- outer_weight: bfloat16 [3072, 768], P('tp', 'fsdp'), may hold values from -0.15625 to 0.15625
- outer_bias: bfloat16 [768], replicated, may hold values from -3 to 3
- second_gain: bfloat16 [768], replicated, may hold values from 0.5 to 1.5
- second_shift: bfloat16 [768], replicated, may hold values from -3 to 3
- out_grad: bfloat16 [32, 1024, 768], P('fsdp', 'tp'), may hold values from -6 to 6
Outputs:
- layer_out: bfloat16 [32, 1024, 768], P('fsdp', 'tp')
- tokens_grad: float32 [32, 1024, 768], P('fsdp', 'tp')
- query_weight_grad: float32 [768, 768], P('fsdp', 'tp')
- query_bias_grad: float32 [768], P('tp')
- key_weight_grad: float32 [768, 768], P('fsdp', 'tp')
- value_weight_grad: float32 [768, 768], P('fsdp', 'tp')
- value_bias_grad: float32 [768], P('tp')
- output_weight_grad: float32 [768, 768], P('tp', 'fsdp')
- output_bias_grad: float32 [768], replicated
- first_gain_grad: float32 [768], replicated
- first_shift_grad: float32 [768], replicated
- inner_weight_grad: float32 [768, 3072], P('fsdp', 'tp')
- inner_bias_grad: float32 [3072], P('tp')
- outer_weight_grad: float32 [3072, 768], P('tp', 'fsdp')
- outer_bias_grad: float32 [768], replicated
- second_gain_grad: float32 [768], replicated
- second_shift_grad: float32 [768], replicated
Inputs may be any that keep to these rules, and one draw needn't show every extreme that they name: `segment_ids`: in each sequence the ids start at 0 and rise by one from document to document; every document but the last one of a sequence spans 60 to 800 positions. `live_mask`: in each sequence the ones come first: documents that end within the sequence are live, the positions of a last document cut off by the sequence's end are 0.
All inputs are finite; a program needn't handle non-finite values.
Results may differ from a plain program's by a relative error of at most 0.018.
The roundings to bfloat16 on the way count: a program that leaves them out, or rounds other values in their place, can miss the bound.
Values may be sent and summed in bfloat16 or wider, within the bound.
No kernel may reach another device: no remote copies, remote signals or barrier semaphores. Data moves between devices by JAX's collectives and lax.ppermute only.
A program may use at most 192 MiB of HBM per device.

v0:
```python
import jax
import jax.numpy as jnp
from jax import lax
from jax.sharding import PartitionSpec as P

HDIM = 64
FF = 3072


EPSILON = 1e-12
MASKED = -1000000000.0


def normalize(token_rows, gain_row, shift_row):
    centred = token_rows - jnp.mean(token_rows, axis=-1, keepdims=True)
    scaling = lax.rsqrt(jnp.mean(centred * centred, axis=-1, keepdims=True) + EPSILON)
    normed = centred * scaling
    return (normed * gain_row + shift_row, normed, scaling)


def normalize_back(grad_rows, normed, scaling, gain_row):
    grad_normed = grad_rows * gain_row
    adjusted = grad_normed - jnp.mean(grad_normed, axis=-1, keepdims=True)
    adjusted = adjusted - normed * jnp.mean(grad_normed * normed, axis=-1, keepdims=True)
    return (
        scaling * adjusted,
        jnp.sum(grad_rows * normed, axis=(0, 1)),
        jnp.sum(grad_rows, axis=(0, 1)),
    )


def visible(segment, live_row):
    length = segment.shape[0]
    places = lax.broadcasted_iota(jnp.int32, (length, length), 0)
    others = lax.broadcasted_iota(jnp.int32, (length, length), 1)
    same_doc = segment[:, None] == segment[None, :]
    return same_doc & ((live_row[None, :] == 1) | (places == others))


def masked_scores(queries, keys_all, segment, live_row, scaling):
    scores = (
        jnp.einsum("qhe,khe->hqk", queries, keys_all, preferred_element_type=jnp.float32) * scaling
    )
    return jnp.where(visible(segment, live_row)[None], scores, MASKED)


def attend(bundle, scaling):
    queries, keys_all, values, segment, live_row = bundle
    scores = masked_scores(queries, keys_all, segment, live_row, scaling)
    highest = jnp.max(scores, axis=-1, keepdims=True)
    weights = jnp.exp(scores - highest)
    totals = jnp.sum(weights, axis=-1, keepdims=True)
    probs = (weights / totals).astype(jnp.bfloat16)
    context = jnp.einsum("hqk,khe->qhe", probs, values, preferred_element_type=jnp.float32)
    return (context.astype(jnp.bfloat16), (highest + jnp.log(totals))[..., 0])


def attend_back(bundle, scaling):
    queries, keys_all, values, segment, live_row, logsum, grad_context = bundle
    scores = masked_scores(queries, keys_all, segment, live_row, scaling)
    probs = jnp.exp(scores - logsum[..., None])
    grad_probs = jnp.einsum(
        "qhe,khe->hqk", grad_context, values, preferred_element_type=jnp.float32
    )
    value_rows_gradient = jnp.einsum(
        "hqk,qhe->khe", probs.astype(jnp.bfloat16), grad_context, preferred_element_type=jnp.float32
    )
    grad_scores = probs * (grad_probs - jnp.sum(grad_probs * probs, axis=-1, keepdims=True))
    grad_scores = grad_scores.astype(jnp.bfloat16)
    query_rows_gradient = (
        jnp.einsum("hqk,khe->qhe", grad_scores, keys_all, preferred_element_type=jnp.float32)
        * scaling
    )
    key_rows_gradient = (
        jnp.einsum("hqk,qhe->khe", grad_scores, queries, preferred_element_type=jnp.float32)
        * scaling
    )
    return (
        query_rows_gradient.astype(jnp.bfloat16),
        key_rows_gradient.astype(jnp.bfloat16),
        value_rows_gradient.astype(jnp.bfloat16),
    )


def gelu_slope(preactivation):
    cumulative = 0.5 * (1.0 + lax.erf(preactivation * 0.7071067811865476))
    density = jnp.exp(-0.5 * preactivation * preactivation) * 0.3989422804014327
    return cumulative + preactivation * density


def placed(vector, total, rank_index):
    return lax.dynamic_update_slice(
        jnp.zeros((total,), jnp.float32), vector, (rank_index * vector.shape[0],)
    )


def on_device(
    tokens,
    segment_ids,
    live_mask,
    query_weight,
    query_bias,
    key_weight,
    value_weight,
    value_bias,
    output_weight,
    output_bias,
    first_gain,
    first_shift,
    inner_weight,
    inner_bias,
    outer_weight,
    outer_bias,
    second_gain,
    second_shift,
    out_grad,
):
    sequences = tokens.shape[0]
    feature_width = tokens.shape[2]
    local_heads = query_weight.shape[1] // HDIM
    scaling = HDIM ** (-0.5)
    tp_rank = lax.axis_index("tp")

    def attention_weights():
        return (
            lax.all_gather(query_weight, "fsdp", axis=0, tiled=True),
            lax.all_gather(key_weight, "fsdp", axis=0, tiled=True),
            lax.all_gather(value_weight, "fsdp", axis=0, tiled=True),
            lax.all_gather(output_weight, "fsdp", axis=1, tiled=True),
        )

    def inner_weights():
        return (
            lax.all_gather(inner_weight, "fsdp", axis=0, tiled=True),
            lax.all_gather(outer_weight, "fsdp", axis=1, tiled=True),
        )

    collected_rows = lax.all_gather(tokens, "tp", axis=1, tiled=True)
    length = collected_rows.shape[1]
    head_shape = (sequences, length, local_heads, HDIM)
    query_full, key_full, value_full, complete_output = attention_weights()

    def project(weight_matrix):
        return jnp.einsum(
            "mqp,pi->mqi", collected_rows, weight_matrix, preferred_element_type=jnp.float32
        )

    queries = (
        (project(query_full) + query_bias.astype(jnp.float32))
        .astype(jnp.bfloat16)
        .reshape(head_shape)
    )
    keys_all = project(key_full).astype(jnp.bfloat16).reshape(head_shape)
    values = (
        (project(value_full) + value_bias.astype(jnp.float32))
        .astype(jnp.bfloat16)
        .reshape(head_shape)
    )
    context, logsum = lax.map(
        lambda bundle: attend(bundle, scaling), (queries, keys_all, values, segment_ids, live_mask)
    )
    flattened_context = context.reshape(sequences, length, local_heads * HDIM)
    attn_terms = jnp.einsum(
        "nox,xq->noq", flattened_context, complete_output, preferred_element_type=jnp.float32
    )
    mixed = lax.psum_scatter(
        attn_terms, "tp", scatter_dimension=1, tiled=True
    ) + output_bias.astype(jnp.float32)
    first_rows, first_normed, first_scaling = normalize(
        tokens.astype(jnp.float32) + mixed,
        first_gain.astype(jnp.float32),
        first_shift.astype(jnp.float32),
    )
    first_low = first_rows.astype(jnp.bfloat16)
    complete_inner, complete_outer = inner_weights()
    scattered_rows = lax.all_gather(first_low, "tp", axis=1, tiled=True)
    preactivation = jnp.einsum(
        "xmo,oq->xmq", scattered_rows, complete_inner, preferred_element_type=jnp.float32
    )
    preactivation = preactivation + inner_bias.astype(jnp.float32)
    activation_rows = jax.nn.gelu(preactivation, approximate=False).astype(jnp.bfloat16)
    outer_products = jnp.einsum(
        "bra,aw->brw", activation_rows, complete_outer, preferred_element_type=jnp.float32
    )
    branch = lax.psum_scatter(
        outer_products.astype(jnp.bfloat16), "tp", scatter_dimension=1, tiled=True
    ).astype(jnp.float32)
    second_rows, second_normed, second_scaling = normalize(
        first_rows + branch + outer_bias.astype(jnp.float32),
        second_gain.astype(jnp.float32),
        second_shift.astype(jnp.float32),
    )
    layer_out = second_rows.astype(jnp.bfloat16)
    grad_second, second_gain_grad, second_shift_grad = normalize_back(
        out_grad.astype(jnp.float32), second_normed, second_scaling, second_gain.astype(jnp.float32)
    )
    outer_bias_grad = jnp.sum(grad_second, axis=(0, 1))
    grad_branch = grad_second.astype(jnp.bfloat16)
    inner_recomputed, outer_recomputed = inner_weights()
    scattered_gradient = lax.all_gather(grad_branch, "tp", axis=1, tiled=True)
    outer_grad_turned = jnp.einsum(
        "ngb,ngx->bx", scattered_gradient, activation_rows, preferred_element_type=jnp.float32
    )
    grad_activ = jnp.einsum(
        "uyr,qr->uyq", scattered_gradient, outer_recomputed, preferred_element_type=jnp.float32
    )
    preactivation_gradient = (grad_activ * gelu_slope(preactivation)).astype(jnp.bfloat16)
    inner_bias_grad = jnp.sum(preactivation_gradient.astype(jnp.float32), axis=(0, 1))
    inner_gradient = jnp.einsum(
        "ngb,ngx->bx", scattered_rows, preactivation_gradient, preferred_element_type=jnp.float32
    )
    hidden_terms = jnp.einsum(
        "owr,xr->owx", preactivation_gradient, inner_recomputed, preferred_element_type=jnp.float32
    )
    grad_hidden = lax.psum_scatter(hidden_terms, "tp", scatter_dimension=1, tiled=True)
    grad_first = grad_second + grad_hidden
    grad_mixed, first_gain_grad, first_shift_grad = normalize_back(
        grad_first, first_normed, first_scaling, first_gain.astype(jnp.float32)
    )
    output_bias_grad = jnp.sum(grad_mixed, axis=(0, 1))
    query_recomputed, key_recomputed, value_recomputed, output_recomputed = attention_weights()
    collected_gradient = lax.all_gather(grad_mixed.astype(jnp.bfloat16), "tp", axis=1, tiled=True)
    output_grad_turned = jnp.einsum(
        "int,inf->tf", collected_gradient, flattened_context, preferred_element_type=jnp.float32
    )
    grad_context = jnp.einsum(
        "zjg,kg->zjk", collected_gradient, output_recomputed, preferred_element_type=jnp.float32
    )
    grad_context = grad_context.astype(jnp.bfloat16).reshape(head_shape)
    query_rows_gradient, key_rows_gradient, value_rows_gradient = lax.map(
        lambda bundle: attend_back(bundle, scaling),
        (queries, keys_all, values, segment_ids, live_mask, logsum, grad_context),
    )
    flat_shape = (sequences, length, local_heads * HDIM)
    query_rows_gradient = query_rows_gradient.reshape(flat_shape)
    key_rows_gradient = key_rows_gradient.reshape(flat_shape)
    value_rows_gradient = value_rows_gradient.reshape(flat_shape)
    query_bias_grad = jnp.sum(query_rows_gradient.astype(jnp.float32), axis=(0, 1))
    value_bias_grad = jnp.sum(value_rows_gradient.astype(jnp.float32), axis=(0, 1))
    query_grad = jnp.einsum(
        "int,inf->tf", collected_rows, query_rows_gradient, preferred_element_type=jnp.float32
    )
    key_gradient = jnp.einsum(
        "int,inf->tf", collected_rows, key_rows_gradient, preferred_element_type=jnp.float32
    )
    value_grad = jnp.einsum(
        "int,inf->tf", collected_rows, value_rows_gradient, preferred_element_type=jnp.float32
    )
    token_terms = jnp.einsum(
        "gfj,aj->gfa", query_rows_gradient, query_recomputed, preferred_element_type=jnp.float32
    )
    token_terms = token_terms + jnp.einsum(
        "gfj,aj->gfa", key_rows_gradient, key_recomputed, preferred_element_type=jnp.float32
    )
    token_terms = token_terms + jnp.einsum(
        "gfj,aj->gfa", value_rows_gradient, value_recomputed, preferred_element_type=jnp.float32
    )
    tokens_grad = grad_mixed + lax.psum_scatter(
        token_terms.astype(jnp.bfloat16), "tp", scatter_dimension=1, tiled=True
    ).astype(jnp.float32)
    query_share, key_share, value_share, output_share, inner_share, outer_share = (
        lax.psum_scatter(query_grad, "fsdp", scatter_dimension=0, tiled=True),
        lax.psum_scatter(key_gradient, "fsdp", scatter_dimension=0, tiled=True),
        lax.psum_scatter(value_grad, "fsdp", scatter_dimension=0, tiled=True),
        lax.psum_scatter(output_grad_turned, "fsdp", scatter_dimension=0, tiled=True),
        lax.psum_scatter(inner_gradient, "fsdp", scatter_dimension=0, tiled=True),
        lax.psum_scatter(outer_grad_turned, "fsdp", scatter_dimension=0, tiled=True),
    )
    totals = lax.psum(
        (
            placed(query_bias_grad, feature_width, tp_rank),
            placed(value_bias_grad, feature_width, tp_rank),
            placed(inner_bias_grad, FF, tp_rank),
            output_bias_grad,
            outer_bias_grad,
            first_gain_grad,
            first_shift_grad,
            second_gain_grad,
            second_shift_grad,
        ),
        ("fsdp", "tp"),
    )
    head_cols = query_bias.shape[0]
    unit_cols = inner_bias.shape[0]
    query_bias_total = lax.dynamic_slice_in_dim(totals[0], tp_rank * head_cols, head_cols)
    value_bias_total = lax.dynamic_slice_in_dim(totals[1], tp_rank * head_cols, head_cols)
    inner_bias_total = lax.dynamic_slice_in_dim(totals[2], tp_rank * unit_cols, unit_cols)
    return (
        layer_out,
        tokens_grad,
        query_share,
        query_bias_total,
        key_share,
        value_share,
        value_bias_total,
        output_share.T,
        totals[3],
        totals[5],
        totals[6],
        inner_share,
        inner_bias_total,
        outer_share.T,
        totals[4],
        totals[7],
        totals[8],
    )


def solution(mesh):
    return jax.shard_map(
        on_device,
        mesh=mesh,
        in_specs=(
            P("fsdp", "tp", None),
            P("fsdp", None),
            P("fsdp", None),
            P("fsdp", "tp"),
            P("tp"),
            P("fsdp", "tp"),
            P("fsdp", "tp"),
            P("tp"),
            P("tp", "fsdp"),
            P(),
            P(),
            P(),
            P("fsdp", "tp"),
            P("tp"),
            P("tp", "fsdp"),
            P(),
            P(),
            P(),
            P("fsdp", "tp", None),
        ),
        out_specs=(
            P("fsdp", "tp", None),
            P("fsdp", "tp", None),
            P("fsdp", "tp"),
            P("tp"),
            P("fsdp", "tp"),
            P("fsdp", "tp"),
            P("tp"),
            P("tp", "fsdp"),
            P(),
            P(),
            P(),
            P("fsdp", "tp"),
            P("tp"),
            P("tp", "fsdp"),
            P(),
            P(),
            P(),
        ),
        check_vma=False,
    )
```

profile of v0, /device:TPU:0, one launch (start us, length us, event | category | flops | bytes accessed | tf_op | source)
XLA Modules:
  0.0 1705.5 jit_solution(15262781231712489662)
XLA Ops:
  11.0 11.1 all_gather.40
  22.1 9.5 all_gather.38
  31.6 8.8 all_gather.39
  40.5 9.3 all_gather.37
  49.7 78.7 %all-gather.7.cloned.1.call-done = bf16[4,1024,768]{2,1,0:T(8,128)(2,1)} async-done(((bf16[4,256,768]{2,1,0:T(8,128)(2,1)}), bf16[4,1024,768]{2,1,0:T(8,128)(2,1)}) %all-gather.7.cloned.1.call-update) | async-done | bytes 6291472 | tf_op jit(solution)/shard_map/all_gather | solution.py:138
  128.5 6.3 convolution_convert_fusion.2
  143.0 70.0 %while.26 = (s32[]{:T(128)}, bf16[4,1024,3,64]{1,3,2,0:T(8,128)(2,1)}, f32[4,3,1024]{2,1,0:T(4,128)}, bf16[4,1024,3,64]{1,3,2,0:T(8,128)(2,1)}, s32[4,1024]{1,0:...) while((s32[]{:T(128)}, ...), condition=%wide.region_3.4_spmd, body=%wide.region_0.3_spmd.sunk | while | flops 847443968 | bytes 47833228 | solution.py:159
  146.3 4.2 fusion.158
  150.5 3.9 fusion.159
  154.4 5.7 fusion.160
  163.7 4.2 fusion.158
  168.0 3.9 fusion.159
  171.8 5.7 fusion.160
  181.1 4.2 fusion.158
  185.4 3.9 fusion.159
  189.3 5.7 fusion.160
  198.5 4.2 fusion.158
  202.8 3.9 fusion.159
  206.7 5.7 fusion.160
  213.0 7.9 fusion.95
  221.6 209.5 %reduce-scatter.17.cloned.1.call-done = f32[4,256,768]{2,1,0:T(8,128)} async-done(((f32[4,1024,768]{2,1,0:T(8,128)}), f32[4,256,768]{2,1,0:T(8,128)}) %reduce-scatter.17.cloned.1.call-update) | async-done | bytes 3145744 | tf_op jit(solution)/shard_map/reduce_scatter | solution.py:166
  438.1 114.4 %all-gather.9.cloned.1.call-done = bf16[4,1024,768]{2,1,0:T(8,128)(2,1)} async-done(((bf16[4,256,768]{2,1,0:T(8,128)(2,1)}), bf16[4,1024,768]{2,1,0:T(8,128)(2,1)}) %all-gather.9.cloned.1.call-update) | async-done | bytes 6291472 | tf_op jit(solution)/shard_map/all_gather | solution.py:176
  552.5 11.7 fusion.86
  564.2 4.6 copy-done.8
  568.8 29.9 %fusion.65 = bf16[4,1024,768]{2,1,0:T(8,128)(2,1)} fusion(f32[4,1024,768]{2,1,0:T(8,128)S(1)} %get-tuple-element.233, f32[768]{0:T(1024)S(1)} %copy-done.23, u8[1024,768]{1,0:T(8,128)(4,1)S(1)} %get-tuple-element.159, u8[1024,768]{1,0:T(8,128)(4,1)S(1)} %get-tuple-element.158), kind=kLoop, calls=%fused_computation.76 | loop fusion | flops 223346688 | bytes 20450304 | tf_op jit(solution)/shard_map/convert_element_type | solution.py:181
  598.7 9.2 convolution_convert_fusion
  610.5 106.4 %reduce-scatter.19.cloned.1.call-done = bf16[4,256,768]{2,1,0:T(8,128)(2,1)} async-done(((bf16[4,1024,768]{2,1,0:T(8,128)(2,1)}), bf16[4,256,768]{2,1,0:T(8,128)(2,1)}) %reduce-scatter.19.cloned.1.call-update) | async-done | bytes 1572880 | tf_op jit(solution)/shard_map/reduce_scatter | solution.py:185
  723.7 115.8 %all-gather.15.cloned.1.call-done = bf16[4,1024,768]{2,1,0:T(8,128)(2,1)} async-done(((bf16[4,256,768]{2,1,0:T(8,128)(2,1)}), bf16[4,1024,768]{2,1,0:T(8,128)(2,1)}) %all-gather.15.cloned.1.call-update) | async-done | bytes 6291472 | tf_op jit(solution)/shard_map/all_gather | solution.py:200
  839.5 13.1 convert_reduce_fusion
  855.2 8.3 fusion.90
  864.9 208.9 %reduce-scatter.21.cloned.1.call-done = f32[4,256,768]{2,1,0:T(8,128)} async-done(((f32[4,1024,768]{2,1,0:T(8,128)}), f32[4,256,768]{2,1,0:T(8,128)}) %reduce-scatter.21.cloned.1.call-update) | async-done | bytes 3145744 | tf_op jit(solution)/shard_map/reduce_scatter | solution.py:215
  1073.8 7.0 fusion.84
  1085.4 116.3 %all-gather.17.cloned.1.call-done = bf16[4,1024,768]{2,1,0:T(8,128)(2,1)} async-done(((bf16[4,256,768]{2,1,0:T(8,128)(2,1)}), bf16[4,1024,768]{2,1,0:T(8,128)(2,1)}) %all-gather.17.cloned.1.call-update) | async-done | bytes 6291472 | tf_op jit(solution)/shard_map/all_gather | solution.py:222
  1201.7 6.1 convolution_convert_fusion.1
  1210.7 125.1 %while.27 = (s32[]{:T(128)}, bf16[4,1024,3,64]{1,3,2,0:T(8,128)(2,1)S(1)}, bf16[4,1024,3,64]{1,3,2,0:T(8,128)(2,1)}, bf16[4,1024,3,64]{1,3,2,0:T(8,128)(2,1)}, b...) while((s32[]{:T(128)}, ...), condition=%wide.region_17.18_spmd, body=%wide.region_15.17_spmd.sunk | while | flops 2065627136 | bytes 108907688 | solution.py:230
  1217.6 4.4 fusion.173
  1222.0 8.2 multiply_reduce_fusion.7
  1230.2 6.9 multiply_convert_fusion.2
  1248.8 4.4 fusion.173
  1253.3 8.2 multiply_reduce_fusion.7
  1261.4 6.9 multiply_convert_fusion.2
  1280.0 4.4 fusion.173
  1284.5 8.2 multiply_reduce_fusion.7
  1292.6 6.9 multiply_convert_fusion.2
  1311.2 4.4 fusion.173
  1315.6 8.2 multiply_reduce_fusion.7
  1323.8 6.9 multiply_convert_fusion.2
  1330.8 3.8 fusion.172
  1335.8 6.5 convolution_bitcast_fusion.2
  1342.9 6.5 fusion.100
  1349.3 6.4 fusion.97
  1355.7 12.3 add_convert_fusion
  1368.0 10.2 convolution_bitcast_fusion.1
  1378.3 10.1 convolution_bitcast_fusion
  1388.4 5.0 convolution_bitcast_fusion.3
  1395.7 4.2 convolution_bitcast_fusion.5
  1401.5 5.7 convolution_bitcast_fusion.4
  1413.8 48.2 %all-reduce = (f32[768]{0:T(1024)S(1)}, f32[768]{0:T(1024)S(1)}, f32[768]{0:T(1024)}, f32[768]{0:T(1024)}, f32[768]{0:T(1024)}, /*index=5*/f32[3072]{0:T(1024)S(1)}, f32[768]{0:T(1024)}, f32[768]{0:T(1024)}, f32[768]{0:T(1024)}) all-reduce(f32[768]{0:T(1024)S(1)} %dynamic_update_slice.26, ...), channel_id=1, replica_groups=mesh['fsdp'=8,'tp'=4] {'fsdp','tp'}, use_global_device_ids=true, to_apply=%region_21.22 | all-reduce | flops 9216 | bytes 73728 | tf_op jit(solution)/shard_map/psum | solution.py:269
  1465.6 24.0 %reduce-scatter.23.cloned.1.call-done = bf16[4,256,768]{2,1,0:T(8,128)(2,1)} async-done(((bf16[4,1024,768]{2,1,0:T(8,128)(2,1)}), bf16[4,256,768]{2,1,0:T(8,128)(2,1)}) %reduce-scatter.23.cloned.1.call-update) | async-done | bytes 1572880 | tf_op jit(solution)/shard_map/reduce_scatter | solution.py:258
  1493.0 43.0 %reduce-scatter.27.cloned.1.call-done = f32[96,768]{1,0:T(8,128)} async-done(((f32[768,768]{1,0:T(8,128)}), f32[96,768]{1,0:T(8,128)}) %reduce-scatter.27.cloned.1.call-update) | async-done | bytes 294928 | tf_op jit(solution)/shard_map/reduce_scatter | solution.py:266
  1536.0 46.2 %reduce-scatter.29.cloned.1.call-done = f32[96,768]{1,0:T(8,128)} async-done(((f32[768,768]{1,0:T(8,128)}), f32[96,768]{1,0:T(8,128)}) %reduce-scatter.29.cloned.1.call-update) | async-done | bytes 294928 | tf_op jit(solution)/shard_map/reduce_scatter | solution.py:267
  1582.2 38.6 %reduce-scatter.35.cloned.1.call-done = f32[96,192]{1,0:T(8,128)} async-done(((f32[768,192]{1,0:T(8,128)}), f32[96,192]{1,0:T(8,128)}) %reduce-scatter.35.cloned.1.call-update) | async-done | bytes 73744
  1620.8 38.7 %reduce-scatter.31.cloned.1.call-done = f32[96,192]{1,0:T(8,128)} async-done(((f32[768,192]{1,0:T(8,128)}), f32[96,192]{1,0:T(8,128)}) %reduce-scatter.31.cloned.1.call-update) | async-done | bytes 73744
  1659.4 38.5 %reduce-scatter.33.cloned.1.call-done = f32[96,192]{1,0:T(8,128)} async-done(((f32[768,192]{1,0:T(8,128)}), f32[96,192]{1,0:T(8,128)}) %reduce-scatter.33.cloned.1.call-update) | async-done | bytes 73744
  (210 shorter events, 114.5 us)
Async XLA Ops:
  8.0 120.5 %all-gather.7.cloned.1.call-start = ((), (), s32[]{:S(2)}) async-start(), calls=%async_computation.10 | async-start | bytes 7864320 | tf_op jit(solution)/shard_map/all_gather | solution.py:138
  8.8 422.4 %reduce-scatter.17.cloned.1.call-start = ((), (), s32[]{:S(2)}) async-start(), calls=%async_computation.11 | async-start | bytes 15728640 | tf_op jit(solution)/shard_map/reduce_scatter | solution.py:166
  31.6 106.6 %copy-start.16 = (bf16[768,192]{1,0:T(8,128)(2,1)}, bf16[768,192]{1,0:T(8,128)(2,1)S(1)}, u32[]{:S(2)}) copy-start(bf16[768,192]{1,0:T(8,128)(2,1)S(1)} %all_gather.38) | copy-start | bytes 884740
  40.5 97.8 %copy-start.12 = (bf16[768,192]{1,0:T(8,128)(2,1)}, bf16[768,192]{1,0:T(8,128)(2,1)S(1)}, u32[]{:S(2)}) copy-start(bf16[768,192]{1,0:T(8,128)(2,1)S(1)} %all_gather.39) | copy-start | bytes 884740
  49.7 88.5 %copy-start.14 = (bf16[768,192]{1,0:T(8,128)(2,1)}, bf16[768,192]{1,0:T(8,128)(2,1)S(1)}, u32[]{:S(2)}) copy-start(bf16[768,192]{1,0:T(8,128)(2,1)S(1)} %all_gather.37) | copy-start | bytes 884740
  128.5 6.3 copy-start.11
  146.3 4.3 copy-start
  163.7 4.3 copy-start
  181.1 4.3 copy-start
  198.5 4.3 copy-start
  220.9 0.7 copy-start.30
  220.9 0.7 copy-start.31
  220.9 0.7 copy-start.32
  220.9 217.2 %all-gather.11.cloned.1.call-start = ((), (), s32[]{:S(2)}) async-start(), calls=%async_computation.13 | async-start | bytes 1327104 | tf_op jit(solution)/shard_map/all_gather | solution.py:134
  221.5 331.0 %all-gather.9.cloned.1.call-start = ((), (), s32[]{:S(2)}) async-start(), calls=%async_computation.12 | async-start | bytes 7864320 | tf_op jit(solution)/shard_map/all_gather | solution.py:176
  436.2 162.5 %all-gather.13.cloned.1.call-start = ((), (), s32[]{:S(2)}) async-start(), calls=%async_computation.14 | async-start | bytes 1327104 | tf_op jit(solution)/shard_map/all_gather | solution.py:135
  436.8 280.2 %reduce-scatter.19.cloned.1.call-start = ((), (), s32[]{:S(2)}) async-start(), calls=%async_computation.15 | async-start | bytes 7864320 | tf_op jit(solution)/shard_map/reduce_scatter | solution.py:185
  552.5 16.3 copy-start.23
  564.2 4.6 copy-start.8
  607.9 231.6 %all-gather.15.cloned.1.call-start = ((), (), s32[]{:S(2)}) async-start(), calls=%async_computation.16 | async-start | bytes 7864320 | tf_op jit(solution)/shard_map/all_gather | solution.py:200
  716.9 3.1 copy-start.7
  716.9 3.1 copy-start.18
  719.6 1.7 copy-start.1
  720.1 1.2 copy-start.19
  721.2 0.6 copy-start.20
  721.2 0.6 copy-start.21
  723.7 350.1 %reduce-scatter.21.cloned.1.call-start = ((), (), s32[]{:S(2)}) async-start(), calls=%async_computation.17 | async-start | bytes 15728640 | tf_op jit(solution)/shard_map/reduce_scatter | solution.py:215
  839.5 15.7 copy-start.33
  852.6 2.6 copy-start.34
  863.5 338.1 %all-gather.17.cloned.1.call-start = ((), (), s32[]{:S(2)}) async-start(), calls=%async_computation.18 | async-start | bytes 7864320 | tf_op jit(solution)/shard_map/all_gather | solution.py:222
  1082.4 1.7 copy-start.2
  1085.4 378.6 %reduce-scatter.25.cloned.1.call-start = ((), (), s32[]{:S(2)}) async-start(), calls=%async_computation.20 | async-start | bytes 884736 | tf_op jit(solution)/shard_map/reduce_scatter | solution.py:265
  1085.4 125.3 %copy-start.5 = (bf16[4,1024,3,64]{1,3,2,0:T(8,128)(2,1)S(1)}, bf16[4,1024,3,64]{1,3,2,0:T(8,128)(2,1)}, u32[]{:S(2)}) copy-start(bf16[4,1024,3,64]{1,3,2,0:T(8,128)(2,1)} %get-tuple-element.445) | copy-start | bytes 4718596
  1214.6 3.0 copy-start.10
  1245.9 3.0 copy-start.10
  1277.1 3.0 copy-start.10
  1308.3 3.0 copy-start.10
  1335.8 59.9 %copy-start.4 = (bf16[4,1024,3,64]{1,3,2,0:T(8,128)(2,1)}, bf16[4,1024,3,64]{1,3,2,0:T(8,128)(2,1)S(1)}, u32[]{:S(2)}) copy-start(bf16[4,1024,3,64]{1,3,2,0:T(8,128)(2,1)S(1)} %get-tuple-element.121) | copy-start | bytes 4718596
  1335.8 7.0 copy-start.17
  1342.4 147.2 %reduce-scatter.23.cloned.1.call-start = ((), (), s32[]{:S(2)}) async-start(), calls=%async_computation.19 | async-start | bytes 7864320 | tf_op jit(solution)/shard_map/reduce_scatter | solution.py:258
  1342.8 6.5 copy-start.9
  1342.8 6.5 copy-start.13
  1349.3 6.4 copy-start.6
  1349.3 6.4 copy-start.15
  1368.0 168.0 %reduce-scatter.27.cloned.1.call-start = ((), (), s32[]{:S(2)}) async-start(), calls=%async_computation.21 | async-start | bytes 2654208 | tf_op jit(solution)/shard_map/reduce_scatter | solution.py:266
  1378.2 204.0 %reduce-scatter.29.cloned.1.call-start = ((), (), s32[]{:S(2)}) async-start(), calls=%async_computation.22 | async-start | bytes 2654208 | tf_op jit(solution)/shard_map/reduce_scatter | solution.py:267
  1388.4 232.4 %reduce-scatter.35.cloned.1.call-start = ((), (), s32[]{:S(2)}) async-start(), calls=%async_computation.25 | async-start | bytes 884736
  1395.7 263.8 %reduce-scatter.31.cloned.1.call-start = ((), (), s32[]{:S(2)}) async-start(), calls=%async_computation.23 | async-start | bytes 884736
  1400.0 9.5 copy-start.29
  1401.2 12.6 copy-start.22
  1401.2 12.5 copy-start.24
  1401.2 12.5 copy-start.25
  1401.2 12.5 copy-start.26
  1401.2 12.5 copy-start.27
  1401.2 12.5 copy-start.28
  1401.2 88.3 %copy-start.3 = (f32[4,256,768]{2,1,0:T(8,128)S(1)}, f32[4,256,768]{2,1,0:T(8,128)}, u32[]{:S(2)}) copy-start(f32[4,256,768]{2,1,0:T(8,128)} %copy-done.2) | copy-start | bytes 9437188
  1401.3 296.7 %reduce-scatter.33.cloned.1.call-start = ((), (), s32[]{:S(2)}) async-start(), calls=%async_computation.24 | async-start | bytes 884736
Sparse Core Ops, SparseCore 0:
  10.4 118.0 all-gather.6
  221.0 210.0 reduce-scatter.16
  863.7 210.0 reduce-scatter.20
Sparse Core Ops, SparseCore 1:
  223.3 22.0 all-gather.10
  436.3 116.2 all-gather.8
  554.3 22.0 all-gather.12
  608.0 108.9 reduce-scatter.18
  723.8 115.7 all-gather.14
  1085.4 116.2 all-gather.16
  1342.5 33.1 reduce-scatter.24
  1377.7 111.8 reduce-scatter.22
  1493.3 42.6 reduce-scatter.26
  1540.0 42.2 reduce-scatter.28
  1585.8 34.9 reduce-scatter.34
  1624.5 34.9 reduce-scatter.30
  1663.0 34.9 reduce-scatter.32
where the time goes:
time: 1710 us
  waiting for transfers between devices  1180 us (69%)
  matrix products  258 us (15%)
  other arithmetic  128 us (7%)
  blocking collectives  86.9 us (5%)
  local copies, waits for them, and re-layouts  33.5 us (2%)
    reduce_scatter x1, waiting for transfers between devices, on_device(): lax.psum_scatter(attn_terms, 'tp', scatter_dimension=1, tiled=True)  210 us
    reduce_scatter x1, waiting for transfers between devices, on_device(): lax.psum_scatter(hidden_terms, 'tp', scatter_dimension=1, tiled=True)  209 us
    unnamed x19, waiting for transfers between devices  118 us
    all_gather x1, waiting for transfers between devices, on_device(): lax.all_gather(grad_mixed.astype(jnp.bfloat16), 'tp', axis=1, tiled=True)  116 us
    all_gather x1, waiting for transfers between devices, on_device(): scattered_gradient = lax.all_gather(grad_branch, 'tp', axis=1, tiled=True)  116 us
    all_gather x1, waiting for transfers between devices, on_device(): scattered_rows = lax.all_gather(first_low, 'tp', axis=1, tiled=True)  114 us
    reduce_scatter x1, waiting for transfers between devices, on_device(): lax.psum_scatter(outer_products.astype(jnp.bfloat16), 'tp', scatter_dimen...  106 us
    all_gather x1, waiting for transfers between devices, on_device(): collected_rows = lax.all_gather(tokens, 'tp', axis=1, tiled=True)  78.7 us
  transfers between devices with their start and end apart: 16, of which 13 were waited for; matrix products, arithmetic and copies ran while one was open for 8% of the time, Pallas kernels for 0%

commit v1 on v0

v1 whole, which is shorter than its diff:
```python
import functools

import jax
import jax.numpy as jnp
from jax import lax
from jax.experimental import pallas as pl
from jax.sharding import PartitionSpec as P

HDIM = 64
EPSILON = 1e-12
MASKED = -1000000000.0
PAIR = 2 * HDIM
BLOCK = 256
LOW = jnp.bfloat16
WIDE = jnp.float32
BY_LAST = (((1,), (1,)), ((), ()))
BY_ROWS = (((1,), (0,)), ((), ()))
BY_FIRST = (((0,), (0,)), ((), ()))


def dot(left, right, dims):
    return lax.dot_general(left, right, dims, preferred_element_type=WIDE)


def halves(pair):
    lane = lax.broadcasted_iota(jnp.int32, (1, PAIR), 1)
    zero = jnp.zeros((), pair.dtype)
    return jnp.where(lane < HDIM, pair, zero), jnp.where(lane < HDIM, zero, pair)


def attend_kernel(q_ref, k_ref, v_ref, row_ref, col_ref, context_ref, logsum_ref, *, scaling):
    keys_all = k_ref[0]
    turned = [half.T for half in halves(v_ref[0])]
    key_ids = col_ref[0]
    for start in range(0, q_ref.shape[1], BLOCK):
        part = slice(start, start + BLOCK)
        seen = key_ids == row_ref[0, :, part]
        total = None
        for head, queries in enumerate(halves(q_ref[0, part, :] * scaling)):
            scores = jnp.where(seen, dot(keys_all, queries, BY_LAST), MASKED)
            highest = jnp.max(scores, axis=0, keepdims=True)
            weights = jnp.exp(scores - highest)
            sums = jnp.sum(weights, axis=0, keepdims=True)
            probs = (weights * (1.0 / sums)).astype(LOW)
            logsum_ref[0, 0, head : head + 1, part] = highest + jnp.log(sums)
            piece = dot(turned[head], probs, BY_ROWS)
            total = piece if total is None else total + piece
        context_ref[0, part, :] = total.T.astype(LOW)


def attend_back_kernel(
    q_ref, k_ref, v_ref, g_ref, logsum_ref, row_ref, col_ref, dq_ref, dk_ref, dv_ref, *, scaling
):
    keys_all = k_ref[0]
    values = v_ref[0]
    turned = [half.T for half in halves(keys_all)]
    key_ids = col_ref[0]
    length = q_ref.shape[1]
    key_grad = jnp.zeros((length, PAIR), WIDE)
    value_grad = jnp.zeros((length, PAIR), WIDE)
    for start in range(0, length, BLOCK):
        part = slice(start, start + BLOCK)
        seen = key_ids == row_ref[0, :, part]
        total = None
        queries_of = halves(q_ref[0, part, :] * scaling)
        grads_of = halves(g_ref[0, part, :])
        for head in range(2):
            queries, grads = queries_of[head], grads_of[head]
            scores = jnp.where(seen, dot(keys_all, queries, BY_LAST), MASKED)
            probs = jnp.exp(scores - logsum_ref[0, 0, head : head + 1, part])
            grad_probs = dot(values, grads, BY_LAST)
            value_grad = value_grad + dot(probs.astype(LOW), grads, BY_ROWS)
            level = jnp.sum(probs * grad_probs, axis=0, keepdims=True)
            grad_scores = (probs * (grad_probs - level)).astype(LOW)
            key_grad = key_grad + dot(grad_scores, queries, BY_ROWS)
            piece = dot(turned[head], grad_scores, BY_ROWS)
            total = piece if total is None else total + piece
        dq_ref[0, part, :] = (total.T * HDIM ** (-0.5)).astype(LOW)
    dk_ref[0] = key_grad.astype(LOW)
    dv_ref[0] = value_grad.astype(LOW)


def attention_specs(length):
    return (
        pl.BlockSpec((1, length, PAIR), lambda s, p: (s, 0, p)),
        pl.BlockSpec((1, 1, length), lambda s, p: (s, 0, 0)),
        pl.BlockSpec((1, length, 1), lambda s, p: (s, 0, 0)),
        pl.BlockSpec((1, 1, 2, length), lambda s, p: (s, p, 0, 0)),
    )


def attend(queries, keys_all, values, ids):
    count, length, width = queries.shape
    rows, as_row, as_col, sums = attention_specs(length)
    scaling = HDIM ** (-0.5)
    return pl.pallas_call(
        functools.partial(attend_kernel, scaling=scaling),
        grid=(count, width // PAIR),
        in_specs=[rows, rows, rows, as_row, as_col],
        out_specs=[rows, sums],
        out_shape=[
            jax.ShapeDtypeStruct(queries.shape, LOW),
            jax.ShapeDtypeStruct((count, width // PAIR, 2, length), WIDE),
        ],
        name="attend",
    )(queries, keys_all, values, ids[:, None, :], ids[:, :, None])


def attend_back(queries, keys_all, values, grad_context, logsum, ids):
    count, length, width = queries.shape
    rows, as_row, as_col, sums = attention_specs(length)
    scaling = HDIM ** (-0.5)
    return pl.pallas_call(
        functools.partial(attend_back_kernel, scaling=scaling),
        grid=(count, width // PAIR),
        in_specs=[rows, rows, rows, rows, sums, as_row, as_col],
        out_specs=[rows, rows, rows],
        out_shape=[jax.ShapeDtypeStruct(queries.shape, LOW)] * 3,
        name="attend_back",
    )(queries, keys_all, values, grad_context, logsum, ids[:, None, :], ids[:, :, None])


def swap_over(axis, blocks):
    members = blocks.shape[0]
    rank = lax.axis_index(axis)
    result = lax.dynamic_update_slice_in_dim(
        jnp.zeros_like(blocks), lax.dynamic_slice_in_dim(blocks, rank, 1, 0), rank, 0
    )
    for step in range(1, members):
        moved = lax.ppermute(
            lax.dynamic_slice_in_dim(blocks, (rank + step) % members, 1, 0),
            axis,
            [(i, (i + step) % members) for i in range(members)],
        )
        result = lax.dynamic_update_slice_in_dim(result, moved, (rank - step) % members, 0)
    return result


def gather_over(axis, members, block):
    rank = lax.axis_index(axis)
    result = lax.dynamic_update_slice_in_dim(
        jnp.zeros((members,) + block.shape, block.dtype), block[None], rank, 0
    )
    for step in range(1, members):
        moved = lax.ppermute(block, axis, [(i, (i + step) % members) for i in range(members)])
        result = lax.dynamic_update_slice_in_dim(result, moved[None], (rank - step) % members, 0)
    return result


def flip(axis, members, bit, block):
    return lax.ppermute(block, axis, [(i, i ^ bit) for i in range(members)])


def paths(members):
    far = [1 << i for i in range(1, members.bit_length() - 1)]
    return (far + [1], far[::-1] + [1])


def gather_rows(axis, members, block):
    if members != 8:
        return lax.all_gather(block, axis, axis=0, tiled=True)
    rank = lax.axis_index(axis)
    rows, cols = block.shape
    half = cols // 2
    sides = []
    for order, piece in zip(paths(members), (block[:, :half], block[:, half:])):
        held = {0: piece}
        for bit in order:
            for mask in list(held):
                held[mask | bit] = flip(axis, members, bit, held[mask])
        side = jnp.zeros((members, rows, half), block.dtype)
        for mask in sorted(held):
            side = lax.dynamic_update_slice_in_dim(side, held[mask][None], rank ^ mask, 0)
        sides.append(side.reshape(members * rows, half))
    return jnp.concatenate(sides, axis=1)


def scatter_rows(axis, members, grad):
    if members != 8:
        return lax.psum_scatter(grad, axis, scatter_dimension=0, tiled=True)
    rank = lax.axis_index(axis)
    total_rows, cols = grad.shape
    rows = total_rows // members
    half = cols // 2
    sides = []
    for order, first in zip(paths(members), (0, half)):
        blocks = grad[:, first : first + half].reshape(members, rows, half)
        held = {mask: None for mask in range(members)}

        def own(mask):
            if held[mask] is None:
                return lax.dynamic_slice_in_dim(blocks, rank ^ mask, 1, 0)[0]
            return held[mask]

        for bit in order[::-1]:
            for mask in [m for m in held if not m & bit]:
                moved = flip(axis, members, bit, own(mask | bit))
                held[mask] = (own(mask).astype(WIDE) + moved.astype(WIDE)).astype(LOW)
            held = {m: v for m, v in held.items() if not m & bit}
        sides.append(held[0])
    return jnp.concatenate(sides, axis=1)


def total_over_all(vector, fsdp, tp):
    pieces = gather_over("tp", tp, vector)
    result = pieces[0]
    for i in range(1, tp):
        result = result + pieces[i]
    bit = 1
    if fsdp & (fsdp - 1):
        return lax.psum(result, "fsdp")
    while bit < fsdp:
        result = result + flip("fsdp", fsdp, bit, result)
        bit *= 2
    return result


def normalize(token_rows):
    centred = token_rows - jnp.mean(token_rows, axis=-1, keepdims=True)
    scaling = lax.rsqrt(jnp.mean(centred * centred, axis=-1, keepdims=True) + EPSILON)
    return centred * scaling, scaling


def normalize_back(grad_rows, normed, scaling, gain_row):
    grad_normed = grad_rows * gain_row
    adjusted = grad_normed - jnp.mean(grad_normed, axis=-1, keepdims=True)
    adjusted = adjusted - normed * jnp.mean(grad_normed * normed, axis=-1, keepdims=True)
    return scaling * adjusted, jnp.sum(grad_rows * normed, axis=0), jnp.sum(grad_rows, axis=0)


def on_device(
    fsdp,
    tp,
    tokens,
    segment_ids,
    live_mask,
    query_weight,
    query_bias,
    key_weight,
    value_weight,
    value_bias,
    output_weight,
    output_bias,
    first_gain,
    first_shift,
    inner_weight,
    inner_bias,
    outer_weight,
    outer_bias,
    second_gain,
    second_shift,
    out_grad,
):
    sequences, places, width = tokens.shape
    count = sequences // tp
    length = places * tp
    rank = lax.axis_index("tp")
    head_cols = query_weight.shape[1]
    unit_cols = inner_weight.shape[1]

    def whole_rows(array):
        blocks = swap_over("tp", array.reshape(tp, count, places, width))
        return blocks.transpose(1, 0, 2, 3).reshape(count * length, width)

    def own_places(array):
        blocks = array.reshape(count, tp, places, width).transpose(1, 0, 2, 3)
        return swap_over("tp", blocks).reshape(sequences, places, width)

    def whole_weight(block):
        return gather_rows("fsdp", fsdp, columns(gather_over("tp", tp, block)))

    def columns(blocks):
        members, rows, cols = blocks.shape
        return blocks.transpose(1, 0, 2).reshape(rows, members * cols)

    def own_share(grad):
        share = scatter_rows("fsdp", fsdp, grad.astype(LOW))
        rows, cols = share.shape
        blocks = share.reshape(rows, tp, cols // tp).transpose(1, 0, 2)
        return jnp.sum(swap_over("tp", blocks).astype(WIDE), axis=0)

    query_full = whole_weight(query_weight)
    key_full = whole_weight(key_weight)
    value_full = whole_weight(value_weight)
    rows = whole_rows(tokens)
    output_turned = whole_weight(output_weight.T)
    inner_full = whole_weight(inner_weight)
    outer_turned = whole_weight(outer_weight.T)
    biases = gather_over(
        "tp", tp, jnp.concatenate([query_bias, value_bias, inner_bias])
    ).astype(WIDE)
    query_bias_full = biases[:, :head_cols].reshape(-1)
    value_bias_full = biases[:, head_cols : 2 * head_cols].reshape(-1)
    inner_bias_full = biases[:, 2 * head_cols :].reshape(-1)

    first = rank * count
    segment = lax.dynamic_slice_in_dim(segment_ids, first, count, 0)
    live = lax.dynamic_slice_in_dim(live_mask, first, count, 0)
    spots = lax.broadcasted_iota(jnp.int32, segment.shape, 1)
    ids = jnp.where(live == 1, segment, length + spots)

    shape = (count, length, width)
    queries = (dot(rows, query_full, BY_ROWS) + query_bias_full).astype(LOW).reshape(shape)
    keys_all = dot(rows, key_full, BY_ROWS).astype(LOW).reshape(shape)
    values = (dot(rows, value_full, BY_ROWS) + value_bias_full).astype(LOW).reshape(shape)
    context, logsum = attend(queries, keys_all, values, ids)
    context = context.reshape(count * length, width)
    mixed = dot(context, output_turned, BY_LAST) + output_bias.astype(WIDE)
    first_normed, first_scaling = normalize(rows.astype(WIDE) + mixed)
    first_rows = first_normed * first_gain.astype(WIDE) + first_shift.astype(WIDE)
    first_low = first_rows.astype(LOW)
    preactivation = dot(first_low, inner_full, BY_ROWS) + inner_bias_full
    cumulative = 0.5 * (1.0 + lax.erf(preactivation * 0.7071067811865476))
    activation_rows = (preactivation * cumulative).astype(LOW)
    density = jnp.exp(-0.5 * preactivation * preactivation) * 0.3989422804014327
    slope = cumulative + preactivation * density
    branch = dot(activation_rows, outer_turned, BY_LAST)
    second_normed, second_scaling = normalize(first_rows + branch + outer_bias.astype(WIDE))
    second_rows = second_normed * second_gain.astype(WIDE) + second_shift.astype(WIDE)
    layer_out = own_places(second_rows.astype(LOW))

    grad_out = whole_rows(out_grad).astype(WIDE)
    grad_second, second_gain_grad, second_shift_grad = normalize_back(
        grad_out, second_normed, second_scaling, second_gain.astype(WIDE)
    )
    outer_bias_grad = jnp.sum(grad_second, axis=0)
    grad_branch = grad_second.astype(LOW)
    outer_share = own_share(dot(grad_branch, activation_rows, BY_FIRST))
    grad_activ = dot(grad_branch, outer_turned, BY_ROWS)
    grad_pre = (grad_activ * slope).astype(LOW)
    inner_bias_grad = jnp.sum(grad_pre.astype(WIDE), axis=0)
    inner_share = own_share(dot(first_low, grad_pre, BY_FIRST))
    grad_first = grad_second + dot(grad_pre, inner_full, BY_LAST)
    grad_mixed, first_gain_grad, first_shift_grad = normalize_back(
        grad_first, first_normed, first_scaling, first_gain.astype(WIDE)
    )
    output_bias_grad = jnp.sum(grad_mixed, axis=0)
    grad_mixed_low = grad_mixed.astype(LOW)
    output_share = own_share(dot(grad_mixed_low, context, BY_FIRST))
    grad_context = dot(grad_mixed_low, output_turned, BY_ROWS).astype(LOW).reshape(shape)
    query_rows_grad, key_rows_grad, value_rows_grad = (
        array.reshape(count * length, width)
        for array in attend_back(queries, keys_all, values, grad_context, logsum, ids)
    )
    query_bias_grad = jnp.sum(query_rows_grad.astype(WIDE), axis=0)
    value_bias_grad = jnp.sum(value_rows_grad.astype(WIDE), axis=0)
    tokens_grad = (
        grad_mixed
        + dot(query_rows_grad, query_full, BY_LAST)
        + dot(key_rows_grad, key_full, BY_LAST)
        + dot(value_rows_grad, value_full, BY_LAST)
    )
    tokens_grad = own_places(tokens_grad.astype(LOW)).astype(WIDE)
    query_share = own_share(dot(rows, query_rows_grad, BY_FIRST))
    key_share = own_share(dot(rows, key_rows_grad, BY_FIRST))
    value_share = own_share(dot(rows, value_rows_grad, BY_FIRST))

    early = total_over_all(
        jnp.concatenate(
            [
                output_bias_grad,
                first_gain_grad,
                first_shift_grad,
                outer_bias_grad,
                second_gain_grad,
                second_shift_grad,
                inner_bias_grad,
            ]
        ),
        fsdp,
        tp,
    )
    late = total_over_all(jnp.concatenate([query_bias_grad, value_bias_grad]), fsdp, tp)
    rowwise = [early[i * width : (i + 1) * width] for i in range(6)]
    inner_bias_total = lax.dynamic_slice_in_dim(early, 6 * width + rank * unit_cols, unit_cols)
    query_bias_total = lax.dynamic_slice_in_dim(late, rank * head_cols, head_cols)
    value_bias_total = lax.dynamic_slice_in_dim(late, width + rank * head_cols, head_cols)
    return (
        layer_out,
        tokens_grad,
        query_share,
        query_bias_total,
        key_share,
        value_share,
        value_bias_total,
        output_share.T,
        rowwise[0],
        rowwise[1],
        rowwise[2],
        inner_share,
        inner_bias_total,
        outer_share.T,
        rowwise[3],
        rowwise[4],
        rowwise[5],
    )


def solution(mesh):
    split = P("fsdp", "tp", None)
    across, turned = P("fsdp", "tp"), P("tp", "fsdp")
    seqs, units, copied = P("fsdp", None), P("tp"), P()
    return jax.shard_map(
        functools.partial(on_device, mesh.shape["fsdp"], mesh.shape["tp"]),
        mesh=mesh,
        in_specs=(
            split,
            seqs,
            seqs,
            across,
            units,
            across,
            across,
            units,
            turned,
            copied,
            copied,
            copied,
            across,
            units,
            turned,
            copied,
            copied,
            copied,
            split,
        ),
        out_specs=(
            split,
            split,
            across,
            units,
            across,
            across,
            units,
            turned,
            copied,
            copied,
            copied,
            across,
            units,
            turned,
            copied,
            copied,
            copied,
        ),
        check_vma=False,
    )
```

time: 1710 us -> 959 us (0.56)
  waiting for transfers between devices: 1180 us -> 205 us
  local copies, waits for them, and re-layouts: 33.5 us -> 303 us
  starting transfers between devices: 1.26 us -> 213 us
  matrix products: 258 us -> 90.7 us
  blocking collectives: 86.9 us -> 0 us
  other arithmetic: 128 us -> 53.6 us
  Pallas kernels: 0 us -> 74.2 us
    reduce_scatter x7 -> x0, waiting for transfers between devices: 638 us -> none  [the longest x1 210 us: on_device(): lax.psum_scatter(attn_terms, 'tp', scatter_dimension=1, tiled=True)]
    all_gather x6 -> x0, waiting for transfers between devices: 425 us -> none  [the longest x1 116 us: on_device(): lax.all_gather(grad_mixed.astype(jnp.bfloat16), 'tp', axis=1, tiled=True)]
    ppermute x0 -> x231, starting transfers between devices: none -> 213 us  [the longest x174 124 us: flip(): return lax.ppermute(block, axis, [(i, i ^ bit) for i in range(members)])]
    ppermute x0 -> x231, waiting for transfers between devices: none -> 205 us  [the longest x174 156 us: flip(): return lax.ppermute(block, axis, [(i, i ^ bit) for i in range(members)])]
    dynamic_update_slice x3 -> x172, local copies, waits for them, and re-layouts: 0.69 us -> 194 us  [the longest x27 67.7 us: gather_over(): lax.dynamic_update_slice_in_dim(result, moved[None], (rank - step) % memb...]
    dot_general x46 -> x18, matrix products: 258 us -> 90.7 us  [dot(): return lax.dot_general(left, right, dims, preferred_element_type=WIDE)]
    unnamed x19 -> x0, waiting for transfers between devices: 118 us -> none
    pallas_call x0 -> x2, Pallas kernels: none -> 74.2 us  [the longest x1 44.1 us: attend_back(): pl.pallas_call(functools.partial(attend_back_kernel, scaling=scaling), gr...]
  transfers between devices with their start and end apart: 16 -> 231, of which waited for: 13 -> 98; matrix products, arithmetic and copies ran while one was open for 8% -> 39% of each run, Pallas kernels for 0% -> 8%
where the time goes in v1:
time: 959 us; the launch traced here: 944 us
  local copies, waits for them, and re-layouts  303 us (32%)
  starting transfers between devices  213 us (22%)
  waiting for transfers between devices  205 us (21%)
  matrix products  90.7 us (9%)
  Pallas kernels  74.2 us (8%)
  other arithmetic  53.6 us (6%)
    ppermute x174, waiting for transfers between devices, flip(): return lax.ppermute(block, axis, [(i, i ^ bit) for i in range(members)])  156 us
    ppermute x174, starting transfers between devices, flip(): return lax.ppermute(block, axis, [(i, i ^ bit) for i in range(members)])  124 us
    dot_general x18, matrix products, dot(): return lax.dot_general(left, right, dims, preferred_element_type=WIDE)  90.7 us
    dynamic_update_slice x27, local copies, waits for them, and re-layouts, gather_over(): lax.dynamic_update_slice_in_dim(result, moved[None], (rank - step) % memb...  67.7 us
    dynamic_update_slice x30, local copies, waits for them, and re-layouts, swap_over(): lax.dynamic_update_slice_in_dim(result, moved, (rank - step) % members, 0)  50.2 us
    ppermute x30, waiting for transfers between devices, swap_over(): lax.ppermute(lax.dynamic_slice_in_dim(blocks, (rank + step) % members, 1,...  48.9 us
    ppermute x30, starting transfers between devices, swap_over(): lax.ppermute(lax.dynamic_slice_in_dim(blocks, (rank + step) % members, 1,...  46.9 us
    dynamic_update_slice x96, local copies, waits for them, and re-layouts, gather_rows(): lax.dynamic_update_slice_in_dim(side, held[mask][None], rank ^ mask, 0)  44.4 us
  transfers between devices with their start and end apart: 231, of which 98 were waited for; matrix products, arithmetic and copies ran while one was open for 39% of the time, Pallas kernels for 8%

profile of v1, /device:TPU:0, one launch (start us, length us, event | category | flops | bytes accessed | tf_op | source)
XLA Modules:
  0.0 943.8 jit_solution(14350406401096269768)
XLA Ops:
  0.7 3.1 collective-permute-start.3
  33.1 3.1 dynamic_update_slice.592
  36.4 4.1 dynamic_update_slice.612
  40.6 4.1 dynamic_update_slice.632
  86.1 3.1 dynamic_update_slice.553
  89.2 3.1 dynamic_update_slice.554
  92.3 3.1 dynamic_update_slice.555
  106.4 3.1 dynamic_update_slice.593
  109.6 3.1 dynamic_update_slice.594
  112.7 3.1 dynamic_update_slice.595
  167.3 3.1 collective-permute-start.93
  177.4 5.8 dynamic_update_slice.613
  183.2 5.9 dynamic_update_slice.614
  189.1 5.9 dynamic_update_slice.615
  199.9 2.9 collective-permute-start.2
  206.7 4.0 dynamic_update_slice.633
  210.7 4.1 dynamic_update_slice.634
  214.8 5.9 dynamic_update_slice.635
  227.5 2.9 collective-permute-done.9
  244.6 2.9 collective-permute-done.11
  325.9 2.9 collective-permute-start.113
  333.7 4.4 fusion.44.k_ref
  338.1 3.6 fusion.46.q_ref
  344.4 30.1 %attend.1 = (bf16[1,1024,768]{2,1,0:T(8,128)(2,1)}, f32[1,6,2,1024]{3,2,1,0:T(2,128)}) custom-call(bf16[1,1024,768]{2,1,0:T(8,128)(2,1)} %fusion.46.q_ref, bf16[1,1024,768]{2,1,0:T(8,128)(2,1)} %fusion.44.k_ref, bf16[1,1024,768]{2,1,0:T(8,128)(2,1)} %fusion.47.v_ref, s32[1,1,1024]{2,1,0:T(1,128)} %fusion.147.row_ref, s32[1,1024,1]{2,1,0:T(8,128)} %copy.276.col_ref), custom_call_target="tpu_custom_call" | custom-call | tf_op jit(solution)/shard_map/attend/pallas_call | solution.py:96
  374.5 3.3 fusion.134
  393.0 5.1 collective-permute-done.95
  401.8 4.9 collective-permute-done.102
  432.9 12.7 %multiply_convert_fusion = (bf16[1024,3072]{1,0:T(8,128)(2,1)}, f32[1024,3072]{1,0:T(8,128)}) fusion(f32[3072]{0:T(1024)S(1)} %copy-done.110, bf16[768,1536]{1,0:T(8,128)(2,1)S(1)} %bitcast.708, bf16[768,1536]{1,0:T(8,128)(2,1)} %bitcast.117, f32[1024,768]{1,0:T(8,128)S(1)} %get-tuple-element.235, f32[768]{0:T(1024)S(1)} %convert_element_type.1024, ...), kind=kOutput, calls=%fused_computation.8 | convolution fusion | flops 4864081920 | bytes 26765312 | tf_op jit(solution)/shard_map/dot_general | solution.py:22
  446.3 8.9 fusion.135
  459.4 7.1 convolution_convert_fusion
  466.5 12.6 %convert_reduce_fusion = (f32[3072]{0:T(1024)S(1)}, bf16[1024,3072]{1,0:T(8,128)(2,1)S(1)}) fusion(f32[1024,3072]{1,0:T(8,128)} %get-tuple-element.237, f32[3072]{0:T(1024)S(1)} %copy-done.110, bf16[768,1536]{1,0:T(8,128)(2,1)S(1)} %bitcast.711, bf16[768,1536]{1,0:T(8,128)(2,1)} %bitcast.141, f32[1024,768]{1,0:T(8,128)S(1)} %get-tuple-element.87), kind=kOutput, calls=%fused_computation.7 | convolution fusion | flops 4882953216 | bytes 26763264 | tf_op jit(solution)/shard_map/dot_general | solution.py:22
  479.1 7.9 convolution_convert_fusion.1
  487.0 7.7 multiply_reduce_fusion
  506.6 3.9 fusion.45.g_ref
  513.0 44.1 %attend_back.1 = (bf16[1,1024,768]{2,1,0:T(8,128)(2,1)}, bf16[1,1024,768]{2,1,0:T(8,128)(2,1)}, bf16[1,1024,768]{2,1,0:T(8,128)(2,1)}) custom-call(bf16[1,1024,768]{2,1,0:T(8,128)(2,1)} %fusion.46.q_ref, bf16[1,1024,768]{2,1,0:T(8,128)(2,1)} %fusion.44.k_ref, bf16[1,1024,768]{2,1,0:T(8,128)(2,1)} %fusion.47.v_ref, bf16[1,1024,768]{2,1,0:T(8,128)(2,1)} %fusion.45.g_ref, ...), custom_call_target="tpu_custom_call" | custom-call | tf_op jit(solution)/shard_map/attend_back/pallas_call | solution.py:113
  557.1 3.5 fusion.41
  562.6 3.0 collective-permute-start.134
  572.4 2.8 fusion.23
  662.1 2.8 collective-permute-done.186
  715.2 3.3 collective-permute-start.190
  728.3 2.9 collective-permute-start.173
  737.4 3.0 collective-permute-start.156
  747.7 2.8 collective-permute-start.133
  773.7 12.0 %collective-permute-done.114 = bf16[1,1,256,768]{3,2,1,0:T(8,128)(2,1)S(1)} collective-permute-done((bf16[1,1,256,768]{3,2,1,0:T(8,128)(2,1)S(1)}, bf16[1,1,256,768]{3,2,1,0:T(8,128)(2,1)S(1)}, u32[]{:S(2)}, u32[]{:S(2)}) %collective-permute-start.114) | collective-permute-done | bytes 393248 | tf_op jit(solution)/shard_map/ppermute | solution.py:130
  785.7 15.9 %collective-permute-done.115 = bf16[1,1,256,768]{3,2,1,0:T(8,128)(2,1)S(1)} collective-permute-done((bf16[1,1,256,768]{3,2,1,0:T(8,128)(2,1)S(1)}, bf16[1,1,256,768]{3,2,1,0:T(8,128)(2,1)S(1)}, u32[]{:S(2)}, u32[]{:S(2)}) %collective-permute-start.115) | collective-permute-done | bytes 393248 | tf_op jit(solution)/shard_map/ppermute | solution.py:130
  801.6 6.0 collective-permute-start.108
  807.7 3.4 collective-permute-start.109
  811.1 9.3 collective-permute-done.108
  824.0 11.6 %collective-permute-done.109 = bf16[1,1,256,768]{3,2,1,0:T(8,128)(2,1)S(1)} collective-permute-done((bf16[1,1,256,768]{3,2,1,0:T(8,128)(2,1)S(1)}, bf16[1,1,256,768]{3,2,1,0:T(8,128)(2,1)S(1)}, u32[]{:S(2)}, u32[]{:S(2)}) %collective-permute-start.109) | collective-permute-done | bytes 393248 | tf_op jit(solution)/shard_map/ppermute | solution.py:130
  839.7 6.1 collective-permute-done.226
  847.9 6.1 collective-permute-done.202
  857.7 3.6 collective-permute-done.209
  864.8 4.7 collective-permute-done.220
  876.4 4.5 collective-permute-start.203
  895.2 3.5 collective-permute-start.230
  902.9 4.1 dynamic_update_slice.692
  907.1 4.1 dynamic_update_slice.688
  911.2 3.2 collective-permute-start.213
  914.7 4.1 dynamic_update_slice.693
  919.0 4.1 dynamic_update_slice.694
  923.3 4.1 dynamic_update_slice.695
  927.7 4.1 dynamic_update_slice.689
  932.0 4.1 dynamic_update_slice.690
  937.8 4.1 dynamic_update_slice.691
  (1093 shorter events, 557.0 us)
Async XLA Ops:
  0.7 50.5 %collective-permute-start.3 = (bf16[96,192]{1,0:T(8,128)(2,1)}, bf16[96,192]{1,0:T(8,128)(2,1)}, u32[]{:S(2)}, u32[]{:S(2)}) collective-permute-start(bf16[96,192]{1,0:T(8,128)(2,1)} %param.22), channel_id=1, source_target_pairs={{0,1},{1,2},{2,3},{3,0},{4,5},{5,6},{6,7},{7,4},{8,9},{9,10},{10,1... | collective-permute-start | bytes 110600 | tf_op jit(solution)/shard_map/ppermute | solution.py:145
  3.8 49.2 %collective-permute-start.4 = (bf16[96,192]{1,0:T(8,128)(2,1)}, bf16[96,192]{1,0:T(8,128)(2,1)}, u32[]{:S(2)}, u32[]{:S(2)}) collective-permute-start(bf16[96,192]{1,0:T(8,128)(2,1)} %param.22), channel_id=1, source_target_pairs={{0,2},{1,3},{2,0},{3,1},{4,6},{5,7},{6,4},{7,5},{8,10},{9,11},{10,... | collective-permute-start | bytes 110600 | tf_op jit(solution)/shard_map/ppermute | solution.py:145
  8.5 36.3 %collective-permute-start.20 = (bf16[1152]{0:T(1024)(128)(2,1)S(1)}, bf16[1152]{0:T(1024)(128)(2,1)S(1)}, u32[]{:S(2)}, u32[]{:S(2)}) collective-permute-start(bf16[1152]{0:T(1024)(128)(2,1)S(1)} %concatenate.46), channel_id=1, source_target_pairs={{0,1},{1,2},{2,3},{3,0},{4,5},{5,6},{6,7},{7,4},{8,9},{9,10},{10,1... | collective-permute-start | bytes 6920 | tf_op jit(solution)/shard_map/ppermute | solution.py:145
  8.5 37.0 %collective-permute-start.21 = (bf16[1152]{0:T(1024)(128)(2,1)S(1)}, bf16[1152]{0:T(1024)(128)(2,1)S(1)}, u32[]{:S(2)}, u32[]{:S(2)}) collective-permute-start(bf16[1152]{0:T(1024)(128)(2,1)S(1)} %concatenate.46), channel_id=1, source_target_pairs={{0,2},{1,3},{2,0},{3,1},{4,6},{5,7},{6,4},{7,5},{8,10},{9,11},{10,... | collective-permute-start | bytes 6920 | tf_op jit(solution)/shard_map/ppermute | solution.py:145
  10.4 36.6 %collective-permute-start.22 = (bf16[1152]{0:T(1024)(128)(2,1)S(1)}, bf16[1152]{0:T(1024)(128)(2,1)S(1)}, u32[]{:S(2)}, u32[]{:S(2)}) collective-permute-start(bf16[1152]{0:T(1024)(128)(2,1)S(1)} %concatenate.46), channel_id=1, source_target_pairs={{0,3},{1,0},{2,1},{3,2},{4,7},{5,4},{6,5},{7,6},{8,11},{9,8},{10,9... | collective-permute-start | bytes 6920 | tf_op jit(solution)/shard_map/ppermute | solution.py:145
  47.0 19.8 %collective-permute-start.41 = (bf16[96,192]{1,0:T(8,128)(2,1)}, bf16[96,192]{1,0:T(8,128)(2,1)}, u32[]{:S(2)}, u32[]{:S(2)}) collective-permute-start(bf16[96,192]{1,0:T(8,128)(2,1)} %param.25), channel_id=1, source_target_pairs={{0,2},{1,3},{2,0},{3,1},{4,6},{5,7},{6,4},{7,5},{8,10},{9,11},{10,... | collective-permute-start | bytes 110600 | tf_op jit(solution)/shard_map/ppermute | solution.py:145
  53.0 24.8 %collective-permute-start.23 = (bf16[96,192]{1,0:T(8,128)(2,1)}, bf16[96,192]{1,0:T(8,128)(2,1)}, u32[]{:S(2)}, u32[]{:S(2)}) collective-permute-start(bf16[96,192]{1,0:T(8,128)(2,1)} %param.24), channel_id=1, source_target_pairs={{0,1},{1,2},{2,3},{3,0},{4,5},{5,6},{6,7},{7,4},{8,9},{9,10},{10,1... | collective-permute-start | bytes 110600 | tf_op jit(solution)/shard_map/ppermute | solution.py:145
  55.1 26.4 %collective-permute-start.24 = (bf16[96,192]{1,0:T(8,128)(2,1)}, bf16[96,192]{1,0:T(8,128)(2,1)S(1)}, u32[]{:S(2)}, u32[]{:S(2)}) collective-permute-start(bf16[96,192]{1,0:T(8,128)(2,1)} %param.24), channel_id=1, source_target_pairs={{0,2},{1,3},{2,0},{3,1},{4,6},{5,7},{6,4},{7,5},{8,10},{9,11},{10,... | collective-permute-start | bytes 110600 | tf_op jit(solution)/shard_map/ppermute | solution.py:145
  63.5 19.5 %collective-permute-start.25 = (bf16[96,192]{1,0:T(8,128)(2,1)}, bf16[96,192]{1,0:T(8,128)(2,1)}, u32[]{:S(2)}, u32[]{:S(2)}) collective-permute-start(bf16[96,192]{1,0:T(8,128)(2,1)} %param.24), channel_id=1, source_target_pairs={{0,3},{1,0},{2,1},{3,2},{4,7},{5,4},{6,5},{7,6},{8,11},{9,8},{10,9... | collective-permute-start | bytes 110600 | tf_op jit(solution)/shard_map/ppermute | solution.py:145
  66.9 33.4 %collective-permute-start.57 = (bf16[96,192]{0,1:T(8,128)(2,1)}, bf16[96,192]{0,1:T(8,128)(2,1)}, u32[]{:S(2)}, u32[]{:S(2)}) collective-permute-start(bf16[96,192]{0,1:T(8,128)(2,1)} %bitcast.80), channel_id=1, source_target_pairs={{0,1},{1,2},{2,3},{3,0},{4,5},{5,6},{6,7},{7,4},{8,9},{9,10},{10,1... | collective-permute-start | bytes 110600 | tf_op jit(solution)/shard_map/ppermute | solution.py:145
  67.8 36.0 %collective-permute-start.58 = (bf16[96,192]{0,1:T(8,128)(2,1)}, bf16[96,192]{0,1:T(8,128)(2,1)}, u32[]{:S(2)}, u32[]{:S(2)}) collective-permute-start(bf16[96,192]{0,1:T(8,128)(2,1)} %bitcast.80), channel_id=1, source_target_pairs={{0,2},{1,3},{2,0},{3,1},{4,6},{5,7},{6,4},{7,5},{8,10},{9,11},{10,... | collective-permute-start | bytes 110600 | tf_op jit(solution)/shard_map/ppermute | solution.py:145
  77.8 27.0 %collective-permute-start.59 = (bf16[96,192]{0,1:T(8,128)(2,1)}, bf16[96,192]{0,1:T(8,128)(2,1)}, u32[]{:S(2)}, u32[]{:S(2)}) collective-permute-start(bf16[96,192]{0,1:T(8,128)(2,1)} %bitcast.80), channel_id=1, source_target_pairs={{0,3},{1,0},{2,1},{3,2},{4,7},{5,4},{6,5},{7,6},{8,11},{9,8},{10,9... | collective-permute-start | bytes 110600 | tf_op jit(solution)/shard_map/ppermute | solution.py:145
  81.5 85.8 %collective-permute-start.74 = (bf16[96,768]{1,0:T(8,128)(2,1)}, bf16[96,768]{1,0:T(8,128)(2,1)}, u32[]{:S(2)}, u32[]{:S(2)}) collective-permute-start(bf16[96,768]{1,0:T(8,128)(2,1)} %param.31), channel_id=1, source_target_pairs={{0,1},{1,2},{2,3},{3,0},{4,5},{5,6},{6,7},{7,4},{8,9},{9,10},{10,1... | collective-permute-start | bytes 442376 | tf_op jit(solution)/shard_map/ppermute | solution.py:145
  83.0 89.3 %collective-permute-start.75 = (bf16[96,768]{1,0:T(8,128)(2,1)}, bf16[96,768]{1,0:T(8,128)(2,1)}, u32[]{:S(2)}, u32[]{:S(2)}) collective-permute-start(bf16[96,768]{1,0:T(8,128)(2,1)} %param.31), channel_id=1, source_target_pairs={{0,2},{1,3},{2,0},{3,1},{4,6},{5,7},{6,4},{7,5},{8,10},{9,11},{10,... | collective-permute-start | bytes 442376 | tf_op jit(solution)/shard_map/ppermute | solution.py:145
  100.3 73.8 %collective-permute-start.76 = (bf16[96,768]{1,0:T(8,128)(2,1)}, bf16[96,768]{1,0:T(8,128)(2,1)}, u32[]{:S(2)}, u32[]{:S(2)}) collective-permute-start(bf16[96,768]{1,0:T(8,128)(2,1)} %param.31), channel_id=1, source_target_pairs={{0,3},{1,0},{2,1},{3,2},{4,7},{5,4},{6,5},{7,6},{8,11},{9,8},{10,9... | collective-permute-start | bytes 442376 | tf_op jit(solution)/shard_map/ppermute | solution.py:145
  103.8 96.1 %collective-permute-start.91 = (bf16[96,768]{1,0:T(8,128)(2,1)}, bf16[96,768]{1,0:T(8,128)(2,1)}, u32[]{:S(2)}, u32[]{:S(2)}) collective-permute-start(bf16[96,768]{1,0:T(8,128)(2,1)} %bitcast.127), channel_id=1, source_target_pairs={{0,1},{1,2},{2,3},{3,0},{4,5},{5,6},{6,7},{7,4},{8,9},{9,10},{10,1... | collective-permute-start | bytes 442376 | tf_op jit(solution)/shard_map/ppermute | solution.py:145
  165.3 38.7 %collective-permute-start.92 = (bf16[96,768]{1,0:T(8,128)(2,1)}, bf16[96,768]{1,0:T(8,128)(2,1)S(1)}, u32[]{:S(2)}, u32[]{:S(2)}) collective-permute-start(bf16[96,768]{1,0:T(8,128)(2,1)} %bitcast.127), channel_id=1, source_target_pairs={{0,2},{1,3},{2,0},{3,1},{4,6},{5,7},{6,4},{7,5},{8,10},{9,11},{10,... | collective-permute-start | bytes 442376 | tf_op jit(solution)/shard_map/ppermute | solution.py:145
  167.3 37.5 %collective-permute-start.93 = (bf16[96,768]{1,0:T(8,128)(2,1)}, bf16[96,768]{1,0:T(8,128)(2,1)}, u32[]{:S(2)}, u32[]{:S(2)}) collective-permute-start(bf16[96,768]{1,0:T(8,128)(2,1)} %bitcast.127), channel_id=1, source_target_pairs={{0,3},{1,0},{2,1},{3,2},{4,7},{5,4},{6,5},{7,6},{8,11},{9,8},{10,9... | collective-permute-start | bytes 442376 | tf_op jit(solution)/shard_map/ppermute | solution.py:145
  172.3 153.7 %collective-permute-start = (bf16[1,1,256,768]{3,2,0,1:T(8,128)(2,1)}, bf16[1,1,256,768]{3,2,0,1:T(8,128)(2,1)}, u32[]{:S(2)}, u32[]{:S(2)}) collective-permute-start(bf16[1,1,256,768]{3,2,0,1:T(8,128)(2,1)} %get-tuple-element.129), channel_id=1, source_target_pairs={{0,1},{1,2},{2,3},{3,0},{4,5},{5,6},{6,7},{7,4},{8,9},{9,10},{10,1... | collective-permute-start | bytes 1179656 | tf_op jit(solution)/shard_map/ppermute | solution.py:130
  174.1 155.7 %collective-permute-start.1 = (bf16[1,1,256,768]{3,2,0,1:T(8,128)(2,1)}, bf16[1,1,256,768]{3,2,0,1:T(8,128)(2,1)}, u32[]{:S(2)}, u32[]{:S(2)}) collective-permute-start(bf16[1,1,256,768]{3,2,0,1:T(8,128)(2,1)} %get-tuple-element.130), channel_id=1, source_target_pairs={{0,2},{1,3},{2,0},{3,1},{4,6},{5,7},{6,4},{7,5},{8,10},{9,11},{10,... | collective-permute-start | bytes 1179656 | tf_op jit(solution)/shard_map/ppermute | solution.py:130
  199.9 131.0 %collective-permute-start.2 = (bf16[1,1,256,768]{3,2,0,1:T(8,128)(2,1)}, bf16[1,1,256,768]{3,2,0,1:T(8,128)(2,1)}, u32[]{:S(2)}, u32[]{:S(2)}) collective-permute-start(bf16[1,1,256,768]{3,2,0,1:T(8,128)(2,1)} %get-tuple-element.128), channel_id=1, source_target_pairs={{0,3},{1,0},{2,1},{3,2},{4,7},{5,4},{6,5},{7,6},{8,11},{9,8},{10,9... | collective-permute-start | bytes 1179656 | tf_op jit(solution)/shard_map/ppermute | solution.py:130
  204.0 173.8 %collective-permute-start.111 = (bf16[1,1,256,768]{3,2,0,1:T(8,128)(2,1)}, bf16[1,1,256,768]{3,2,0,1:T(8,128)(2,1)}, u32[]{:S(2)}, u32[]{:S(2)}) collective-permute-start(bf16[1,1,256,768]{3,2,0,1:T(8,128)(2,1)} %get-tuple-element.123), channel_id=1, source_target_pairs={{0,1},{1,2},{2,3},{3,0},{4,5},{5,6},{6,7},{7,4},{8,9},{9,10},{10,1... | collective-permute-start | bytes 1179656 | tf_op jit(solution)/shard_map/ppermute | solution.py:130
  204.8 19.6 %collective-permute-start.8 = (bf16[96,384]{1,0:T(8,128)(2,1)}, bf16[96,384]{1,0:T(8,128)(2,1)S(1)}, u32[]{:S(2)}, u32[]{:S(2)}) collective-permute-start(bf16[96,384]{1,0:T(8,128)(2,1)} %collective-permute-done.7), channel_id=1, source_target_pairs={{0,4},{4,0},{8,12},{12,8},{16,20},{20,16},{24,28},{28,24},{1,5},{5... | collective-permute-start | bytes 221192 | tf_op jit(solution)/shard_map/ppermute | solution.py:151
  323.8 56.6 %collective-permute-start.112 = (bf16[1,1,256,768]{3,2,0,1:T(8,128)(2,1)}, bf16[1,1,256,768]{3,2,0,1:T(8,128)(2,1)}, u32[]{:S(2)}, u32[]{:S(2)}) collective-permute-start(bf16[1,1,256,768]{3,2,0,1:T(8,128)(2,1)} %get-tuple-element.124), channel_id=1, source_target_pairs={{0,2},{1,3},{2,0},{3,1},{4,6},{5,7},{6,4},{7,5},{8,10},{9,11},{10,... | collective-permute-start | bytes 1179656 | tf_op jit(solution)/shard_map/ppermute | solution.py:130
  325.9 56.2 %collective-permute-start.113 = (bf16[1,1,256,768]{3,2,0,1:T(8,128)(2,1)}, bf16[1,1,256,768]{3,2,0,1:T(8,128)(2,1)}, u32[]{:S(2)}, u32[]{:S(2)}) collective-permute-start(bf16[1,1,256,768]{3,2,0,1:T(8,128)(2,1)} %get-tuple-element.122), channel_id=1, source_target_pairs={{0,3},{1,0},{2,1},{3,2},{4,7},{5,4},{6,5},{7,6},{8,11},{9,8},{10,9... | collective-permute-start | bytes 1179656 | tf_op jit(solution)/shard_map/ppermute | solution.py:130
  329.9 54.9 %collective-permute-start.77 = (bf16[96,1536]{1,0:T(8,128)(2,1)}, bf16[96,1536]{1,0:T(8,128)(2,1)}, u32[]{:S(2)}, u32[]{:S(2)}) collective-permute-start(bf16[96,1536]{1,0:T(8,128)(2,1)} %get-tuple-element.197), channel_id=1, source_target_pairs={{0,4},{4,0},{8,12},{12,8},{16,20},{20,16},{24,28},{28,24},{1,5},{5... | collective-permute-start | bytes 884744 | tf_op jit(solution)/shard_map/ppermute | solution.py:151
  331.0 56.0 %collective-permute-start.78 = (bf16[96,1536]{1,0:T(8,128)(2,1)}, bf16[96,1536]{1,0:T(8,128)(2,1)}, u32[]{:S(2)}, u32[]{:S(2)}) collective-permute-start(bf16[96,1536]{1,0:T(8,128)(2,1)} %get-tuple-element.197), channel_id=1, source_target_pairs={{0,8},{4,12},{8,0},{12,4},{16,24},{20,28},{24,16},{28,20},{1,9},{5... | collective-permute-start | bytes 884744 | tf_op jit(solution)/shard_map/ppermute | solution.py:151
  377.8 28.8 %collective-permute-start.80 = (bf16[96,1536]{1,0:T(8,128)(2,1)}, bf16[96,1536]{1,0:T(8,128)(2,1)S(1)}, u32[]{:S(2)}, u32[]{:S(2)}) collective-permute-start(bf16[96,1536]{1,0:T(8,128)(2,1)} %get-tuple-element.197), channel_id=1, source_target_pairs={{0,16},{4,20},{8,24},{12,28},{16,0},{20,4},{24,8},{28,12},{1,17},{... | collective-permute-start | bytes 884744 | tf_op jit(solution)/shard_map/ppermute | solution.py:151
  384.7 26.9 %collective-permute-start.87 = (bf16[96,1536]{1,0:T(8,128)(2,1)S(1)}, bf16[96,1536]{1,0:T(8,128)(2,1)S(1)}, u32[]{:S(2)}, u32[]{:S(2)}) collective-permute-start(bf16[96,1536]{1,0:T(8,128)(2,1)S(1)} %copy-done.61), channel_id=1, source_target_pairs={{0,16},{4,20},{8,24},{12,28},{16,0},{20,4},{24,8},{28,12},{1,17},{... | collective-permute-start | bytes 884744 | tf_op jit(solution)/shard_map/ppermute | solution.py:151
  391.6 22.6 %collective-permute-start.97 = (bf16[96,1536]{1,0:T(8,128)(2,1)S(1)}, bf16[96,1536]{1,0:T(8,128)(2,1)S(1)}, u32[]{:S(2)}, u32[]{:S(2)}) collective-permute-start(bf16[96,1536]{1,0:T(8,128)(2,1)S(1)} %copy-done.62), channel_id=1, source_target_pairs={{0,16},{4,20},{8,24},{12,28},{16,0},{20,4},{24,8},{28,12},{1,17},{... | collective-permute-start | bytes 884744 | tf_op jit(solution)/shard_map/ppermute | solution.py:151
  400.2 21.6 %collective-permute-start.104 = (bf16[96,1536]{1,0:T(8,128)(2,1)S(1)}, bf16[96,1536]{1,0:T(8,128)(2,1)S(1)}, u32[]{:S(2)}, u32[]{:S(2)}) collective-permute-start(bf16[96,1536]{1,0:T(8,128)(2,1)S(1)} %copy-done.60), channel_id=1, source_target_pairs={{0,16},{4,20},{8,24},{12,28},{16,0},{20,4},{24,8},{28,12},{1,17},{... | collective-permute-start | bytes 884744 | tf_op jit(solution)/shard_map/ppermute | solution.py:151
  504.9 113.4 %collective-permute-start.191 = (f32[7680]{0:T(1024)}, f32[7680]{0:T(1024)}, u32[]{:S(2)}, u32[]{:S(2)}) collective-permute-start(f32[7680]{0:T(1024)} %constant_dynamic-update-slice_fusion.6), channel_id=1, source_target_pairs={{0,1},{1,2},{2,3},{3,0},{4,5},{5,6},{6,7},{7,4},{8,9},{9,10},{10,1... | collective-permute-start | bytes 92168 | tf_op jit(solution)/shard_map/ppermute | solution.py:145
  505.1 116.8 %collective-permute-start.192 = (f32[7680]{0:T(1024)}, f32[7680]{0:T(1024)}, u32[]{:S(2)}, u32[]{:S(2)}) collective-permute-start(f32[7680]{0:T(1024)} %constant_dynamic-update-slice_fusion.6), channel_id=1, source_target_pairs={{0,2},{1,3},{2,0},{3,1},{4,6},{5,7},{6,4},{7,5},{8,10},{9,11},{10,... | collective-permute-start | bytes 92168 | tf_op jit(solution)/shard_map/ppermute | solution.py:145
  562.6 35.0 %collective-permute-start.134 = (f32[1536]{0:T(1024)S(1)}, f32[1536]{0:T(1024)}, u32[]{:S(2)}, u32[]{:S(2)}) collective-permute-start(f32[1536]{0:T(1024)S(1)} %pad_maximum_fusion.28), channel_id=1, source_target_pairs={{0,1},{1,2},{2,3},{3,0},{4,5},{5,6},{6,7},{7,4},{8,9},{9,10},{10,1... | collective-permute-start | bytes 18440 | tf_op jit(solution)/shard_map/ppermute | solution.py:145
  565.6 36.4 %collective-permute-start.135 = (f32[1536]{0:T(1024)S(1)}, f32[1536]{0:T(1024)}, u32[]{:S(2)}, u32[]{:S(2)}) collective-permute-start(f32[1536]{0:T(1024)S(1)} %pad_maximum_fusion.28), channel_id=1, source_target_pairs={{0,2},{1,3},{2,0},{3,1},{4,6},{5,7},{6,4},{7,5},{8,10},{9,11},{10,... | collective-permute-start | bytes 18440 | tf_op jit(solution)/shard_map/ppermute | solution.py:145
  566.0 38.0 %collective-permute-start.136 = (f32[1536]{0:T(1024)S(1)}, f32[1536]{0:T(1024)}, u32[]{:S(2)}, u32[]{:S(2)}) collective-permute-start(f32[1536]{0:T(1024)S(1)} %pad_maximum_fusion.28), channel_id=1, source_target_pairs={{0,3},{1,0},{2,1},{3,2},{4,7},{5,4},{6,5},{7,6},{8,11},{9,8},{10,9... | collective-permute-start | bytes 18440 | tf_op jit(solution)/shard_map/ppermute | solution.py:145
  597.5 27.4 %collective-permute-start.193 = (f32[7680]{0:T(1024)}, f32[7680]{0:T(1024)}, u32[]{:S(2)}, u32[]{:S(2)}) collective-permute-start(f32[7680]{0:T(1024)} %constant_dynamic-update-slice_fusion.6), channel_id=1, source_target_pairs={{0,3},{1,0},{2,1},{3,2},{4,7},{5,4},{6,5},{7,6},{8,11},{9,8},{10,9... | collective-permute-start | bytes 92168 | tf_op jit(solution)/shard_map/ppermute | solution.py:145
  602.0 29.3 %collective-permute-start.158 = (bf16[96,384]{1,0:T(8,128)(2,1)}, bf16[96,384]{1,0:T(8,128)(2,1)}, u32[]{:S(2)}, u32[]{:S(2)}) collective-permute-start(bf16[96,384]{1,0:T(8,128)(2,1)} %get-tuple-element.162), channel_id=1, source_target_pairs={{0,4},{4,0},{8,12},{12,8},{16,20},{20,16},{24,28},{28,24},{1,5},{5... | collective-permute-start | bytes 221192 | tf_op jit(solution)/shard_map/ppermute | solution.py:151
  618.3 31.4 %collective-permute-start.160 = (bf16[96,384]{1,0:T(8,128)(2,1)}, bf16[96,384]{1,0:T(8,128)(2,1)}, u32[]{:S(2)}, u32[]{:S(2)}) collective-permute-start(bf16[96,384]{1,0:T(8,128)(2,1)} %get-tuple-element.161), channel_id=1, source_target_pairs={{0,4},{4,0},{8,12},{12,8},{16,20},{20,16},{24,28},{28,24},{1,5},{5... | collective-permute-start | bytes 221192 | tf_op jit(solution)/shard_map/ppermute | solution.py:151
  621.9 62.7 %collective-permute-start.157 = (bf16[96,384]{1,0:T(8,128)(2,1)}, bf16[96,384]{1,0:T(8,128)(2,1)}, u32[]{:S(2)}, u32[]{:S(2)}) collective-permute-start(bf16[96,384]{1,0:T(8,128)(2,1)} %get-tuple-element.159), channel_id=1, source_target_pairs={{0,4},{4,0},{8,12},{12,8},{16,20},{20,16},{24,28},{28,24},{1,5},{5... | collective-permute-start | bytes 221192 | tf_op jit(solution)/shard_map/ppermute | solution.py:151
  642.9 46.5 %collective-permute-start.164 = (bf16[96,384]{1,0:T(8,128)(2,1)S(1)}, bf16[96,384]{1,0:T(8,128)(2,1)S(1)}, u32[]{:S(2)}, u32[]{:S(2)}) collective-permute-start(bf16[96,384]{1,0:T(8,128)(2,1)S(1)} %copy-done.67), channel_id=1, source_target_pairs={{0,4},{4,0},{8,12},{12,8},{16,20},{20,16},{24,28},{28,24},{1,5},{5... | collective-permute-start | bytes 221192 | tf_op jit(solution)/shard_map/ppermute | solution.py:151
  654.2 39.5 %collective-permute-start.174 = (bf16[96,384]{1,0:T(8,128)(2,1)S(1)}, bf16[96,384]{1,0:T(8,128)(2,1)S(1)}, u32[]{:S(2)}, u32[]{:S(2)}) collective-permute-start(bf16[96,384]{1,0:T(8,128)(2,1)S(1)} %copy-done.66), channel_id=1, source_target_pairs={{0,4},{4,0},{8,12},{12,8},{16,20},{20,16},{24,28},{28,24},{1,5},{5... | collective-permute-start | bytes 221192 | tf_op jit(solution)/shard_map/ppermute | solution.py:151
  714.8 18.7 %collective-permute-start.189 = (bf16[1,96,192]{2,1,0:T(8,128)(2,1)S(1)}, bf16[1,96,192]{2,1,0:T(8,128)(2,1)S(1)}, u32[]{:S(2)}, u32[]{:S(2)}) collective-permute-start(bf16[1,96,192]{2,1,0:T(8,128)(2,1)S(1)} %bitcast.780), channel_id=1, source_target_pairs={{0,2},{1,3},{2,0},{3,1},{4,6},{5,7},{6,4},{7,5},{8,10},{9,11},{10,... | collective-permute-start | bytes 110600 | tf_op jit(solution)/shard_map/ppermute | solution.py:130
  715.2 19.7 %collective-permute-start.190 = (bf16[1,96,192]{2,1,0:T(8,128)(2,1)S(1)}, bf16[1,96,192]{2,1,0:T(8,128)(2,1)S(1)}, u32[]{:S(2)}, u32[]{:S(2)}) collective-permute-start(bf16[1,96,192]{2,1,0:T(8,128)(2,1)S(1)} %bitcast.779), channel_id=1, source_target_pairs={{0,3},{1,0},{2,1},{3,2},{4,7},{5,4},{6,5},{7,6},{8,11},{9,8},{10,9... | collective-permute-start | bytes 110600 | tf_op jit(solution)/shard_map/ppermute | solution.py:130
  718.5 18.8 %collective-permute-start.171 = (bf16[1,96,192]{2,1,0:T(8,128)(2,1)S(1)}, bf16[1,96,192]{2,1,0:T(8,128)(2,1)S(1)}, u32[]{:S(2)}, u32[]{:S(2)}) collective-permute-start(bf16[1,96,192]{2,1,0:T(8,128)(2,1)S(1)} %bitcast.777), channel_id=1, source_target_pairs={{0,1},{1,2},{2,3},{3,0},{4,5},{5,6},{6,7},{7,4},{8,9},{9,10},{10,1... | collective-permute-start | bytes 110600 | tf_op jit(solution)/shard_map/ppermute | solution.py:130
  719.3 22.7 %collective-permute-start.172 = (bf16[1,96,192]{2,1,0:T(8,128)(2,1)S(1)}, bf16[1,96,192]{2,1,0:T(8,128)(2,1)S(1)}, u32[]{:S(2)}, u32[]{:S(2)}) collective-permute-start(bf16[1,96,192]{2,1,0:T(8,128)(2,1)S(1)} %bitcast.775), channel_id=1, source_target_pairs={{0,2},{1,3},{2,0},{3,1},{4,6},{5,7},{6,4},{7,5},{8,10},{9,11},{10,... | collective-permute-start | bytes 110600 | tf_op jit(solution)/shard_map/ppermute | solution.py:130
  742.1 21.3 %collective-permute-start.215 = (bf16[96,1536]{1,0:T(8,128)(2,1)S(1)}, bf16[96,1536]{1,0:T(8,128)(2,1)S(1)}, u32[]{:S(2)}, u32[]{:S(2)}) collective-permute-start(bf16[96,1536]{1,0:T(8,128)(2,1)S(1)} %copy-done.59), channel_id=1, source_target_pairs={{0,4},{4,0},{8,12},{12,8},{16,20},{20,16},{24,28},{28,24},{1,5},{5... | collective-permute-start | bytes 884744 | tf_op jit(solution)/shard_map/ppermute | solution.py:151
  743.6 20.3 %collective-permute-start.218 = (bf16[96,1536]{1,0:T(8,128)(2,1)S(1)}, bf16[96,1536]{1,0:T(8,128)(2,1)S(1)}, u32[]{:S(2)}, u32[]{:S(2)}) collective-permute-start(bf16[96,1536]{1,0:T(8,128)(2,1)S(1)} %copy-done.58), channel_id=1, source_target_pairs={{0,4},{4,0},{8,12},{12,8},{16,20},{20,16},{24,28},{28,24},{1,5},{5... | collective-permute-start | bytes 884744 | tf_op jit(solution)/shard_map/ppermute | solution.py:151
  756.5 79.8 %collective-permute-start.217 = (bf16[96,1536]{1,0:T(8,128)(2,1)S(1)}, bf16[96,1536]{1,0:T(8,128)(2,1)}, u32[]{:S(2)}, u32[]{:S(2)}) collective-permute-start(bf16[96,1536]{1,0:T(8,128)(2,1)S(1)} %copy-done.56), channel_id=1, source_target_pairs={{0,4},{4,0},{8,12},{12,8},{16,20},{20,16},{24,28},{28,24},{1,5},{5... | collective-permute-start | bytes 884744 | tf_op jit(solution)/shard_map/ppermute | solution.py:151
  758.1 105.6 %collective-permute-start.214 = (bf16[96,1536]{1,0:T(8,128)(2,1)S(1)}, bf16[96,1536]{1,0:T(8,128)(2,1)}, u32[]{:S(2)}, u32[]{:S(2)}) collective-permute-start(bf16[96,1536]{1,0:T(8,128)(2,1)S(1)} %copy-done.52), channel_id=1, source_target_pairs={{0,4},{4,0},{8,12},{12,8},{16,20},{20,16},{24,28},{28,24},{1,5},{5... | collective-permute-start | bytes 884744 | tf_op jit(solution)/shard_map/ppermute | solution.py:151
  764.9 74.8 %collective-permute-start.224 = (bf16[96,1536]{1,0:T(8,128)(2,1)S(1)}, bf16[96,1536]{1,0:T(8,128)(2,1)S(1)}, u32[]{:S(2)}, u32[]{:S(2)}) collective-permute-start(bf16[96,1536]{1,0:T(8,128)(2,1)S(1)} %copy-done.55), channel_id=1, source_target_pairs={{0,4},{4,0},{8,12},{12,8},{16,20},{20,16},{24,28},{28,24},{1,5},{5... | collective-permute-start | bytes 884744 | tf_op jit(solution)/shard_map/ppermute | solution.py:151
  771.8 29.8 %collective-permute-start.115 = (bf16[1,1,256,768]{3,2,1,0:T(8,128)(2,1)S(1)}, bf16[1,1,256,768]{3,2,1,0:T(8,128)(2,1)S(1)}, u32[]{:S(2)}, u32[]{:S(2)}) collective-permute-start(bf16[1,1,256,768]{3,2,1,0:T(8,128)(2,1)S(1)} %copy-done.49), channel_id=1, source_target_pairs={{0,2},{1,3},{2,0},{3,1},{4,6},{5,7},{6,4},{7,5},{8,10},{9,11},{10,... | collective-permute-start | bytes 1179656 | tf_op jit(solution)/shard_map/ppermute | solution.py:130
  785.7 21.9 %collective-permute-start.116 = (bf16[1,1,256,768]{3,2,1,0:T(8,128)(2,1)S(1)}, bf16[1,1,256,768]{3,2,1,0:T(8,128)(2,1)S(1)}, u32[]{:S(2)}, u32[]{:S(2)}) collective-permute-start(bf16[1,1,256,768]{3,2,1,0:T(8,128)(2,1)S(1)} %copy-done.48), channel_id=1, source_target_pairs={{0,3},{1,0},{2,1},{3,2},{4,7},{5,4},{6,5},{7,6},{8,11},{9,8},{10,9... | collective-permute-start | bytes 1179656 | tf_op jit(solution)/shard_map/ppermute | solution.py:130
  801.6 18.8 %collective-permute-start.108 = (bf16[1,1,256,768]{3,2,1,0:T(8,128)(2,1)S(1)}, bf16[1,1,256,768]{3,2,1,0:T(8,128)(2,1)S(1)}, u32[]{:S(2)}, u32[]{:S(2)}) collective-permute-start(bf16[1,1,256,768]{3,2,1,0:T(8,128)(2,1)S(1)} %copy-done.47), channel_id=1, source_target_pairs={{0,1},{1,2},{2,3},{3,0},{4,5},{5,6},{6,7},{7,4},{8,9},{9,10},{10,1... | collective-permute-start | bytes 1179656 | tf_op jit(solution)/shard_map/ppermute | solution.py:130
  807.7 27.9 %collective-permute-start.109 = (bf16[1,1,256,768]{3,2,1,0:T(8,128)(2,1)S(1)}, bf16[1,1,256,768]{3,2,1,0:T(8,128)(2,1)S(1)}, u32[]{:S(2)}, u32[]{:S(2)}) collective-permute-start(bf16[1,1,256,768]{3,2,1,0:T(8,128)(2,1)S(1)} %copy-done.46), channel_id=1, source_target_pairs={{0,2},{1,3},{2,0},{3,1},{4,6},{5,7},{6,4},{7,5},{8,10},{9,11},{10,... | collective-permute-start | bytes 1179656 | tf_op jit(solution)/shard_map/ppermute | solution.py:130
  835.6 36.1 %collective-permute-start.221 = (bf16[96,1536]{1,0:T(8,128)(2,1)S(1)}, bf16[96,1536]{1,0:T(8,128)(2,1)S(1)}, u32[]{:S(2)}, u32[]{:S(2)}) collective-permute-start(bf16[96,1536]{1,0:T(8,128)(2,1)S(1)} %copy-done.51), channel_id=1, source_target_pairs={{0,4},{4,0},{8,12},{12,8},{16,20},{20,16},{24,28},{28,24},{1,5},{5... | collective-permute-start | bytes 884744 | tf_op jit(solution)/shard_map/ppermute | solution.py:151
  839.7 42.8 %collective-permute-start.197 = (bf16[96,1536]{1,0:T(8,128)(2,1)}, bf16[96,1536]{1,0:T(8,128)(2,1)}, u32[]{:S(2)}, u32[]{:S(2)}) collective-permute-start(bf16[96,1536]{1,0:T(8,128)(2,1)} %get-tuple-element.107), channel_id=1, source_target_pairs={{0,4},{4,0},{8,12},{12,8},{16,20},{20,16},{24,28},{28,24},{1,5},{5... | collective-permute-start | bytes 884744 | tf_op jit(solution)/shard_map/ppermute | solution.py:151
  863.7 23.6 %collective-permute-start.204 = (bf16[96,1536]{1,0:T(8,128)(2,1)}, bf16[96,1536]{1,0:T(8,128)(2,1)}, u32[]{:S(2)}, u32[]{:S(2)}) collective-permute-start(bf16[96,1536]{1,0:T(8,128)(2,1)} %get-tuple-element.113), channel_id=1, source_target_pairs={{0,4},{4,0},{8,12},{12,8},{16,20},{20,16},{24,28},{28,24},{1,5},{5... | collective-permute-start | bytes 884744 | tf_op jit(solution)/shard_map/ppermute | solution.py:151
  871.6 27.7 %collective-permute-start.110 = (bf16[1,1,256,768]{3,2,1,0:T(8,128)(2,1)}, bf16[1,1,256,768]{3,2,1,0:T(8,128)(2,1)}, u32[]{:S(2)}, u32[]{:S(2)}) collective-permute-start(bf16[1,1,256,768]{3,2,1,0:T(8,128)(2,1)} %get-tuple-element.125), channel_id=1, source_target_pairs={{0,3},{1,0},{2,1},{3,2},{4,7},{5,4},{6,5},{7,6},{8,11},{9,8},{10,9... | collective-permute-start | bytes 1179656 | tf_op jit(solution)/shard_map/ppermute | solution.py:130
  894.7 24.0 %collective-permute-start.229 = (bf16[1,96,768]{2,1,0:T(8,128)(2,1)S(1)}, bf16[1,96,768]{2,1,0:T(8,128)(2,1)S(1)}, u32[]{:S(2)}, u32[]{:S(2)}) collective-permute-start(bf16[1,96,768]{2,1,0:T(8,128)(2,1)S(1)} %bitcast.770), channel_id=1, source_target_pairs={{0,2},{1,3},{2,0},{3,1},{4,6},{5,7},{6,4},{7,5},{8,10},{9,11},{10,... | collective-permute-start | bytes 442376 | tf_op jit(solution)/shard_map/ppermute | solution.py:130
  895.2 27.9 %collective-permute-start.230 = (bf16[1,96,768]{2,1,0:T(8,128)(2,1)S(1)}, bf16[1,96,768]{2,1,0:T(8,128)(2,1)S(1)}, u32[]{:S(2)}, u32[]{:S(2)}) collective-permute-start(bf16[1,96,768]{2,1,0:T(8,128)(2,1)S(1)} %bitcast.769), channel_id=1, source_target_pairs={{0,3},{1,0},{2,1},{3,2},{4,7},{5,4},{6,5},{7,6},{8,11},{9,8},{10,9... | collective-permute-start | bytes 442376 | tf_op jit(solution)/shard_map/ppermute | solution.py:130
  898.7 28.7 %collective-permute-start.211 = (bf16[1,96,768]{2,1,0:T(8,128)(2,1)S(1)}, bf16[1,96,768]{2,1,0:T(8,128)(2,1)S(1)}, u32[]{:S(2)}, u32[]{:S(2)}) collective-permute-start(bf16[1,96,768]{2,1,0:T(8,128)(2,1)S(1)} %bitcast.768), channel_id=1, source_target_pairs={{0,1},{1,2},{2,3},{3,0},{4,5},{5,6},{6,7},{7,4},{8,9},{9,10},{10,1... | collective-permute-start | bytes 442376 | tf_op jit(solution)/shard_map/ppermute | solution.py:130
  899.4 32.4 %collective-permute-start.212 = (bf16[1,96,768]{2,1,0:T(8,128)(2,1)S(1)}, bf16[1,96,768]{2,1,0:T(8,128)(2,1)S(1)}, u32[]{:S(2)}, u32[]{:S(2)}) collective-permute-start(bf16[1,96,768]{2,1,0:T(8,128)(2,1)S(1)} %bitcast.766), channel_id=1, source_target_pairs={{0,2},{1,3},{2,0},{3,1},{4,6},{5,7},{6,4},{7,5},{8,10},{9,11},{10,... | collective-permute-start | bytes 442376 | tf_op jit(solution)/shard_map/ppermute | solution.py:130
  911.2 26.4 %collective-permute-start.213 = (bf16[1,96,768]{2,1,0:T(8,128)(2,1)S(1)}, bf16[1,96,768]{2,1,0:T(8,128)(2,1)S(1)}, u32[]{:S(2)}, u32[]{:S(2)}) collective-permute-start(bf16[1,96,768]{2,1,0:T(8,128)(2,1)S(1)} %bitcast.767), channel_id=1, source_target_pairs={{0,3},{1,0},{2,1},{3,2},{4,7},{5,4},{6,5},{7,6},{8,11},{9,8},{10,9... | collective-permute-start | bytes 442376 | tf_op jit(solution)/shard_map/ppermute | solution.py:130
  (294 other events, 3162.7 us)

commit v2 on v1

--- a/solution.py
+++ b/solution.py
@@ -120,30 +120,26 @@
     )(queries, keys_all, values, grad_context, logsum, ids[:, None, :], ids[:, :, None])
 
 
-def swap_over(axis, blocks):
-    members = blocks.shape[0]
+def dealt(axis, members, blocks):
     rank = lax.axis_index(axis)
-    result = lax.dynamic_update_slice_in_dim(
-        jnp.zeros_like(blocks), lax.dynamic_slice_in_dim(blocks, rank, 1, 0), rank, 0
-    )
-    for step in range(1, members):
-        moved = lax.ppermute(
-            lax.dynamic_slice_in_dim(blocks, (rank + step) % members, 1, 0),
-            axis,
-            [(i, (i + step) % members) for i in range(members)],
-        )
-        result = lax.dynamic_update_slice_in_dim(result, moved, (rank - step) % members, 0)
-    return result
-
-
-def gather_over(axis, members, block):
+    parts = []
+    for step in range(members):
+        block = lax.dynamic_slice_in_dim(blocks, (rank + step) % members, 1, 0)[0]
+        pairs = [(i, (i + step) % members) for i in range(members)]
+        parts.append(lax.ppermute(block, axis, pairs) if step else block)
+    return parts
+
+
+def returned(axis, members, parts):
     rank = lax.axis_index(axis)
-    result = lax.dynamic_update_slice_in_dim(
-        jnp.zeros((members,) + block.shape, block.dtype), block[None], rank, 0
-    )
-    for step in range(1, members):
-        moved = lax.ppermute(block, axis, [(i, (i + step) % members) for i in range(members)])
-        result = lax.dynamic_update_slice_in_dim(result, moved[None], (rank - step) % members, 0)
+    result = None
+    for step in range(members):
+        pairs = [(i, (i - step) % members) for i in range(members)]
+        block = (lax.ppermute(parts[step], axis, pairs) if step else parts[step])[None]
+        if result is None:
+            result = jnp.broadcast_to(block, (members,) + block.shape[1:])
+        else:
+            result = lax.dynamic_update_slice_in_dim(result, block, (rank + step) % members, 0)
     return result
 
 
@@ -151,68 +147,69 @@
     return lax.ppermute(block, axis, [(i, i ^ bit) for i in range(members)])
 
 
-def paths(members):
-    far = [1 << i for i in range(1, members.bit_length() - 1)]
-    return (far + [1], far[::-1] + [1])
-
-
-def gather_rows(axis, members, block):
+def joined(axis, members, bit, block, place):
+    mine = lax.axis_index(axis) // bit % 2
+    other = flip(axis, members, bit, block)
+    shape = block.shape[:place] + (2,) + block.shape[place:]
+    spot = lax.broadcasted_iota(jnp.int32, shape, place)
+    return jnp.where(spot == mine, jnp.expand_dims(block, place), jnp.expand_dims(other, place))
+
+
+def halved(axis, members, bit, array, place):
+    mine = lax.axis_index(axis) // bit % 2
+    theirs = lax.squeeze(lax.dynamic_slice_in_dim(array, 1 - mine, 1, place), (place,))
+    kept = lax.squeeze(lax.dynamic_slice_in_dim(array, mine, 1, place), (place,))
+    return kept.astype(WIDE) + flip(axis, members, bit, theirs).astype(WIDE)
+
+
+def gather_tp(members, block):
+    if members != 4:
+        return lax.all_gather(block, "tp", axis=0)
+    shape = block.shape
+    block = joined("tp", members, 1, block, 0)
+    block = joined("tp", members, 2, block, 0)
+    return block.reshape((members,) + shape)
+
+
+def gather_rows(members, block):
     if members != 8:
-        return lax.all_gather(block, axis, axis=0, tiled=True)
-    rank = lax.axis_index(axis)
+        return lax.all_gather(block, "fsdp", axis=0, tiled=True)
     rows, cols = block.shape
-    half = cols // 2
-    sides = []
-    for order, piece in zip(paths(members), (block[:, :half], block[:, half:])):
-        held = {0: piece}
-        for bit in order:
-            for mask in list(held):
-                held[mask | bit] = flip(axis, members, bit, held[mask])
-        side = jnp.zeros((members, rows, half), block.dtype)
-        for mask in sorted(held):
-            side = lax.dynamic_update_slice_in_dim(side, held[mask][None], rank ^ mask, 0)
-        sides.append(side.reshape(members * rows, half))
-    return jnp.concatenate(sides, axis=1)
-
-
-def scatter_rows(axis, members, grad):
+    first = joined("fsdp", members, 2, block[:, : cols // 2], 0)
+    second = joined("fsdp", members, 4, block[:, cols // 2 :], 0)
+    first = joined("fsdp", members, 4, first, 0)
+    second = joined("fsdp", members, 2, second, 1)
+    both = jnp.concatenate([first, second], axis=3)
+    return joined("fsdp", members, 1, both, 2).reshape(members * rows, cols)
+
+
+def scatter_rows(members, grad):
     if members != 8:
-        return lax.psum_scatter(grad, axis, scatter_dimension=0, tiled=True)
-    rank = lax.axis_index(axis)
+        return lax.psum_scatter(grad, "fsdp", scatter_dimension=0, tiled=True).astype(WIDE)
     total_rows, cols = grad.shape
     rows = total_rows // members
-    half = cols // 2
-    sides = []
-    for order, first in zip(paths(members), (0, half)):
-        blocks = grad[:, first : first + half].reshape(members, rows, half)
-        held = {mask: None for mask in range(members)}
-
-        def own(mask):
-            if held[mask] is None:
-                return lax.dynamic_slice_in_dim(blocks, rank ^ mask, 1, 0)[0]
-            return held[mask]
-
-        for bit in order[::-1]:
-            for mask in [m for m in held if not m & bit]:
-                moved = flip(axis, members, bit, own(mask | bit))
-                held[mask] = (own(mask).astype(WIDE) + moved.astype(WIDE)).astype(LOW)
-            held = {m: v for m, v in held.items() if not m & bit}
-        sides.append(held[0])
-    return jnp.concatenate(sides, axis=1)
-
-
-def total_over_all(vector, fsdp, tp):
-    pieces = gather_over("tp", tp, vector)
-    result = pieces[0]
-    for i in range(1, tp):
-        result = result + pieces[i]
-    bit = 1
-    if fsdp & (fsdp - 1):
-        return lax.psum(result, "fsdp")
-    while bit < fsdp:
-        result = result + flip("fsdp", fsdp, bit, result)
-        bit *= 2
-    return result
+    grad = halved("fsdp", members, 1, grad.reshape(2, 2, 2, rows, cols), 2).astype(LOW)
+    first = halved("fsdp", members, 4, grad[..., : cols // 2], 0).astype(LOW)
+    second = halved("fsdp", members, 2, grad[..., cols // 2 :], 1).astype(LOW)
+    first = halved("fsdp", members, 2, first, 0)
+    second = halved("fsdp", members, 4, second, 0)
+    return jnp.concatenate([first, second], axis=1)
+
+
+def scatter_tp(members, blocks):
+    if members != 4:
+        return lax.psum_scatter(blocks.astype(LOW), "tp", scatter_dimension=0).astype(WIDE)
+    blocks = blocks.astype(LOW).reshape((2, 2) + blocks.shape[1:])
+    return halved("tp", members, 1, halved("tp", members, 2, blocks, 0).astype(LOW), 0)
+
+
+def total_over_all(fsdp, tp, vector):
+    for axis, members in (("fsdp", fsdp), ("tp", tp)):
+        bit = 1
+        while bit < members:
+            vector = vector + flip(axis, members, bit, vector)
+            bit *= 2
+    return vector
 
 
 def normalize(token_rows):
@@ -257,47 +254,60 @@
     rank = lax.axis_index("tp")
     head_cols = query_weight.shape[1]
     unit_cols = inner_weight.shape[1]
+    shard_rows = query_weight.shape[0]
 
     def whole_rows(array):
-        blocks = swap_over("tp", array.reshape(tp, count, places, width))
-        return blocks.transpose(1, 0, 2, 3).reshape(count * length, width)
+        parts = dealt("tp", tp, array.reshape(tp, count, places, width))
+        return jnp.concatenate(parts, axis=1).reshape(count * length, width)
 
     def own_places(array):
-        blocks = array.reshape(count, tp, places, width).transpose(1, 0, 2, 3)
-        return swap_over("tp", blocks).reshape(sequences, places, width)
-
-    def whole_weight(block):
-        return gather_rows("fsdp", fsdp, columns(gather_over("tp", tp, block)))
+        parts = array.reshape(count, tp, places, width)
+        parts = returned("tp", tp, [parts[:, step] for step in range(tp)])
+        return parts.reshape(sequences, places, width)
 
     def columns(blocks):
         members, rows, cols = blocks.shape
         return blocks.transpose(1, 0, 2).reshape(rows, members * cols)
 
-    def own_share(grad):
-        share = scatter_rows("fsdp", fsdp, grad.astype(LOW))
-        rows, cols = share.shape
-        blocks = share.reshape(rows, tp, cols // tp).transpose(1, 0, 2)
-        return jnp.sum(swap_over("tp", blocks).astype(WIDE), axis=0)
-
-    query_full = whole_weight(query_weight)
-    key_full = whole_weight(key_weight)
-    value_full = whole_weight(value_weight)
-    rows = whole_rows(tokens)
-    output_turned = whole_weight(output_weight.T)
-    inner_full = whole_weight(inner_weight)
-    outer_turned = whole_weight(outer_weight.T)
-    biases = gather_over(
-        "tp", tp, jnp.concatenate([query_bias, value_bias, inner_bias])
-    ).astype(WIDE)
+    def own_share(grad, widths):
+        share = scatter_rows(fsdp, grad)
+        rows, first, blocks = share.shape[0], 0, []
+        for cols in widths:
+            piece = share[:, first : first + cols].reshape(rows, tp, cols // tp)
+            blocks.append(piece.transpose(1, 0, 2))
+            first += cols
+        share, first, pieces = scatter_tp(tp, jnp.concatenate(blocks, axis=2)), 0, []
+        for cols in widths:
+            pieces.append(share[:, first : first + cols // tp])
+            first += cols // tp
+        return pieces
+
+    biases = jnp.concatenate([query_bias, value_bias, inner_bias]).reshape(-1, 3 * head_cols)
+    heads = jnp.concatenate(
+        [jnp.concatenate([query_weight, key_weight, value_weight], axis=1), biases], axis=0
+    )
+    heads = gather_tp(tp, heads)
+    biases = heads[:, shard_rows:].reshape(tp, -1).astype(WIDE)
     query_bias_full = biases[:, :head_cols].reshape(-1)
     value_bias_full = biases[:, head_cols : 2 * head_cols].reshape(-1)
     inner_bias_full = biases[:, 2 * head_cols :].reshape(-1)
+    heads = heads[:, :shard_rows].reshape(tp, shard_rows, 3, head_cols).transpose(1, 2, 0, 3)
+    heads = gather_rows(fsdp, heads.reshape(shard_rows, 3 * width))
+    query_full, key_full, value_full = (heads[:, i * width : (i + 1) * width] for i in range(3))
+    rows = whole_rows(tokens)
+    rest = jnp.concatenate([inner_weight, outer_weight.T, output_weight.T], axis=1)
+    rest = lax.all_gather(rest, ("tp", "fsdp"), axis=0, tiled=True).reshape(tp, width, -1)
+    inner_full = columns(rest[:, :, :unit_cols])
+    outer_turned = columns(rest[:, :, unit_cols : 2 * unit_cols])
+    output_turned = columns(rest[:, :, 2 * unit_cols :])
 
     first = rank * count
     segment = lax.dynamic_slice_in_dim(segment_ids, first, count, 0)
     live = lax.dynamic_slice_in_dim(live_mask, first, count, 0)
     spots = lax.broadcasted_iota(jnp.int32, segment.shape, 1)
-    ids = jnp.where(live == 1, segment, length + spots)
+    ids = jnp.where(live == 1, segment, length + spots).reshape(count, tp, places)
+    ids = [lax.dynamic_slice_in_dim(ids, (rank - step) % tp, 1, 1) for step in range(tp)]
+    ids = jnp.concatenate(ids, axis=1).reshape(count, length)
 
     shape = (count, length, width)
     queries = (dot(rows, query_full, BY_ROWS) + query_bias_full).astype(LOW).reshape(shape)
@@ -325,18 +335,21 @@
     )
     outer_bias_grad = jnp.sum(grad_second, axis=0)
     grad_branch = grad_second.astype(LOW)
-    outer_share = own_share(dot(grad_branch, activation_rows, BY_FIRST))
+    (outer_share,) = own_share(dot(grad_branch, activation_rows, BY_FIRST).astype(LOW), (outer_turned.shape[1],))
     grad_activ = dot(grad_branch, outer_turned, BY_ROWS)
     grad_pre = (grad_activ * slope).astype(LOW)
     inner_bias_grad = jnp.sum(grad_pre.astype(WIDE), axis=0)
-    inner_share = own_share(dot(first_low, grad_pre, BY_FIRST))
+    inner_grad = dot(first_low, grad_pre, BY_FIRST).astype(LOW)
     grad_first = grad_second + dot(grad_pre, inner_full, BY_LAST)
     grad_mixed, first_gain_grad, first_shift_grad = normalize_back(
         grad_first, first_normed, first_scaling, first_gain.astype(WIDE)
     )
     output_bias_grad = jnp.sum(grad_mixed, axis=0)
     grad_mixed_low = grad_mixed.astype(LOW)
-    output_share = own_share(dot(grad_mixed_low, context, BY_FIRST))
+    output_grad = dot(grad_mixed_low, context, BY_FIRST).astype(LOW)
+    inner_share, output_share = own_share(
+        jnp.concatenate([inner_grad, output_grad], axis=1), (inner_grad.shape[1], width)
+    )
     grad_context = dot(grad_mixed_low, output_turned, BY_ROWS).astype(LOW).reshape(shape)
     query_rows_grad, key_rows_grad, value_rows_grad = (
         array.reshape(count * length, width)
@@ -351,11 +364,16 @@
         + dot(value_rows_grad, value_full, BY_LAST)
     )
     tokens_grad = own_places(tokens_grad.astype(LOW)).astype(WIDE)
-    query_share = own_share(dot(rows, query_rows_grad, BY_FIRST))
-    key_share = own_share(dot(rows, key_rows_grad, BY_FIRST))
-    value_share = own_share(dot(rows, value_rows_grad, BY_FIRST))
-
-    early = total_over_all(
+    head_grads = [
+        dot(rows, grad, BY_FIRST).astype(LOW)
+        for grad in (query_rows_grad, key_rows_grad, value_rows_grad)
+    ]
+    query_share, key_share, value_share = own_share(
+        jnp.concatenate(head_grads, axis=1), (width, width, width)
+    )
+    totals = total_over_all(
+        fsdp,
+        tp,
         jnp.concatenate(
             [
                 output_bias_grad,
@@ -364,17 +382,16 @@
                 outer_bias_grad,
                 second_gain_grad,
                 second_shift_grad,
+                query_bias_grad,
+                value_bias_grad,
                 inner_bias_grad,
             ]
         ),
-        fsdp,
-        tp,
-    )
-    late = total_over_all(jnp.concatenate([query_bias_grad, value_bias_grad]), fsdp, tp)
-    rowwise = [early[i * width : (i + 1) * width] for i in range(6)]
-    inner_bias_total = lax.dynamic_slice_in_dim(early, 6 * width + rank * unit_cols, unit_cols)
-    query_bias_total = lax.dynamic_slice_in_dim(late, rank * head_cols, head_cols)
-    value_bias_total = lax.dynamic_slice_in_dim(late, width + rank * head_cols, head_cols)
+    )
+    rowwise = [totals[i * width : (i + 1) * width] for i in range(6)]
+    query_bias_total = lax.dynamic_slice_in_dim(totals, 6 * width + rank * head_cols, head_cols)
+    value_bias_total = lax.dynamic_slice_in_dim(totals, 7 * width + rank * head_cols, head_cols)
+    inner_bias_total = lax.dynamic_slice_in_dim(totals, 8 * width + rank * unit_cols, unit_cols)
     return (
         layer_out,
         tokens_grad,

time: 959 us -> 614 us (0.64)
  local copies, waits for them, and re-layouts: 303 us -> 71.6 us
  starting transfers between devices: 213 us -> 73.1 us
  waiting for transfers between devices: 205 us -> 236 us
  other arithmetic: 53.6 us -> 39.2 us
  between operations: 4.51 us -> 15.5 us
    dynamic_update_slice x172 -> x6, local copies, waits for them, and re-layouts: 194 us -> 0.19 us  [returned(): lax.dynamic_update_slice_in_dim(result, block, (rank + step) % members, 0)]
    ppermute x174 -> x33, starting transfers between devices: 124 us -> 48.3 us  [flip(): return lax.ppermute(block, axis, [(i, i ^ bit) for i in range(members)])]
    ppermute x57 -> x12, starting transfers between devices: 89 us -> 24.7 us  [the longest x6 19.6 us: dealt(): parts.append(lax.ppermute(block, axis, pairs) if step else block)]
    ppermute x57 -> x12, waiting for transfers between devices: 48.9 us -> 90.2 us  [the longest x6 66.4 us: dealt(): parts.append(lax.ppermute(block, axis, pairs) if step else block)]
    broadcast_in_dim x40 -> x4, local copies, waits for them, and re-layouts: 36.5 us -> 1.31 us  [joined(): jnp.where(spot == mine, jnp.expand_dims(block, place), jnp.expand_dims(ot...]
    transpose x0 -> x10, local copies, waits for them, and re-layouts: none -> 25.2 us  [the longest x5 24.3 us: columns(): return blocks.transpose(1, 0, 2).reshape(rows, members * cols)]
    convert_element_type x36 -> x13, other arithmetic: 29.4 us -> 7.38 us  [the longest x3 5.45 us: scatter_rows(): halved('fsdp', members, 1, grad.reshape(2, 2, 2, rows, cols), 2).astype(LOW)]
    another operation x29 -> x2, local copies, waits for them, and re-layouts: 14.2 us -> 1.78 us  [the longest x1 1.18 us: attend(): ids[:, :, None]]
  transfers between devices with their start and end apart: 231 -> 46, of which waited for: 98 -> 27; matrix products, arithmetic and copies ran while one was open for 39% -> 14% of each run, Pallas kernels for 8% -> 5%
where the time goes in v2:
time: 614 us; the launch traced here: 605 us
  waiting for transfers between devices  236 us (38%)
  matrix products  94.6 us (15%)
  Pallas kernels  74.6 us (12%)
  starting transfers between devices  73.1 us (12%)
  local copies, waits for them, and re-layouts  71.6 us (12%)
  other arithmetic  39.2 us (6%)
  between operations  15.5 us (3%)
    ppermute x33, waiting for transfers between devices, flip(): return lax.ppermute(block, axis, [(i, i ^ bit) for i in range(members)])  146 us
    dot_general x18, matrix products, dot(): return lax.dot_general(left, right, dims, preferred_element_type=WIDE)  94.6 us
    ppermute x6, waiting for transfers between devices, dealt(): parts.append(lax.ppermute(block, axis, pairs) if step else block)  66.4 us
    ppermute x33, starting transfers between devices, flip(): return lax.ppermute(block, axis, [(i, i ^ bit) for i in range(members)])  48.3 us
    pallas_call x1, Pallas kernels, attend_back(): pl.pallas_call(functools.partial(attend_back_kernel, scaling=scaling), gr...  44.6 us
    pallas_call x1, Pallas kernels, attend(): pl.pallas_call(functools.partial(attend_kernel, scaling=scaling), grid=(c...  30.1 us
    transpose x5, local copies, waits for them, and re-layouts, columns(): return blocks.transpose(1, 0, 2).reshape(rows, members * cols)  24.3 us
    ppermute x6, waiting for transfers between devices, returned(): lax.ppermute(parts[step], axis, pairs)  23.9 us
  transfers between devices with their start and end apart: 46, of which 27 were waited for; matrix products, arithmetic and copies ran while one was open for 14% of the time, Pallas kernels for 5%

profile of v2, /device:TPU:0, one launch (start us, length us, event | category | flops | bytes accessed | tf_op | source)
XLA Modules:
  0.0 604.6 jit_solution(4946366648900050916)
XLA Ops:
  9.9 2.1 concatenate.67
  13.0 3.1 collective-permute-start.3
  16.2 3.5 collective-permute-done.3
  20.1 2.8 collective-permute-start.4
  23.7 17.3 %collective-permute-done.4 = bf16[2,98,576]{2,0,1:T(2,128)(2,1)S(1)} collective-permute-done((bf16[2,98,576]{2,0,1:T(2,128)(2,1)S(1)}, bf16[2,98,576]{2,0,1:T(2,128)(2,1)S(1)}, u32[]{:S(2)}, u32[]{:S(2)}) %collective-permute-start.4) | collective-permute-done | bytes 225824 | tf_op jit(solution)/shard_map/ppermute | solution.py:147
  47.8 8.2 %collective-permute-done.5 = bf16[96,1152]{1,0:T(8,128)(2,1)S(1)} collective-permute-done((bf16[96,1152]{1,0:T(8,128)(2,1)S(1)}, bf16[96,1152]{1,0:T(8,128)(2,1)S(1)}, u32[]{:S(2)}, u32[]{:S(2)}) %collective-permute-start.5) | collective-permute-done | bytes 221216 | tf_op jit(solution)/shard_map/ppermute | solution.py:147
  60.0 5.4 collective-permute-done.6
  65.6 4.5 collective-permute-done.8
  70.6 2.4 constant_dynamic-slice_fusion.3
  74.9 3.4 collective-permute-start.14
  78.3 2.5 constant_dynamic-slice_fusion.13
  86.0 8.9 %collective-permute-done.13 = bf16[1,256,768]{2,1,0:T(8,128)(2,1)S(1)} collective-permute-done((bf16[1,256,768]{2,1,0:T(8,128)(2,1)}, bf16[1,256,768]{2,1,0:T(8,128)(2,1)S(1)}, u32[]{:S(2)}, u32[]{:S(2)}) %collective-permute-start.13) | collective-permute-done | bytes 393248 | tf_op jit(solution)/shard_map/ppermute | solution.py:129
  94.9 10.5 %collective-permute-start.2 = (bf16[1,256,768]{2,1,0:T(8,128)(2,1)}, bf16[1,256,768]{2,1,0:T(8,128)(2,1)}, u32[]{:S(2)}, u32[]{:S(2)}) collective-permute-start(bf16[1,256,768]{2,1,0:T(8,128)(2,1)} %get-tuple-element.129), channel_id=1, source_target_pairs={{0,3},{1,0},{2,1},{3,2},{4,7},{5,4},{6,5},{7,6},{8,11},{9,8},{10,9... | collective-permute-start | bytes 1179656 | tf_op jit(solution)/shard_map/ppermute | solution.py:129
  105.4 39.2 %collective-permute-done.14 = bf16[1,256,768]{2,1,0:T(8,128)(2,1)S(1)} collective-permute-done((bf16[1,256,768]{2,1,0:T(8,128)(2,1)S(1)}, bf16[1,256,768]{2,1,0:T(8,128)(2,1)S(1)}, u32[]{:S(2)}, u32[]{:S(2)}) %collective-permute-start.14) | collective-permute-done | bytes 393248 | tf_op jit(solution)/shard_map/ppermute | solution.py:129
  144.6 3.3 collective-permute-start.15
  149.6 18.2 %collective-permute-done.15 = bf16[1,256,768]{2,1,0:T(8,128)(2,1)S(1)} collective-permute-done((bf16[1,256,768]{2,1,0:T(8,128)(2,1)}, bf16[1,256,768]{2,1,0:T(8,128)(2,1)S(1)}, u32[]{:S(2)}, u32[]{:S(2)}) %collective-permute-start.15) | collective-permute-done | bytes 393248 | tf_op jit(solution)/shard_map/ppermute | solution.py:129
  170.7 4.7 fusion.45.k_ref
  175.3 3.8 fusion.48.v_ref
  179.1 3.8 fusion.47.q_ref
  182.9 30.1 %attend.1 = (bf16[1,1024,768]{2,1,0:T(8,128)(2,1)}, f32[1,6,2,1024]{3,2,1,0:T(2,128)}) custom-call(bf16[1,1024,768]{2,1,0:T(8,128)(2,1)} %fusion.47.q_ref, bf16[1,1024,768]{2,1,0:T(8,128)(2,1)} %fusion.45.k_ref, bf16[1,1024,768]{2,1,0:T(8,128)(2,1)} %fusion.48.v_ref, s32[1,1,1024]{2,1,0:T(1,128)} %broadcast_in_dim_reshape.4.row_ref, ...), custom_call_target="tpu_custom_call" | custom-call | tf_op jit(solution)/shard_map/attend/pallas_call | solution.py:96
  214.5 8.0 %slice_bitcast_fusion = (bf16[768,4,768]{2,0,1:T(8,128)(2,1)}, bf16[768,4,768]{2,0,1:T(8,128)(2,1)}) fusion(bf16[4,768,1728]{2,1,0:T(8,128)(2,1)} %bitcast.266), kind=kLoop, calls=%fused_computation.15 | loop fusion | bytes 18874368 | tf_op jit(solution)/shard_map/transpose | solution.py:270
  224.0 3.7 fusion.95
  228.8 6.6 %copy.85 = bf16[768,4,768]{0,2,1:T(8,128)(2,1)} copy(bf16[768,4,768]{2,0,1:T(8,128)(2,1)} %get-tuple-element.107) | data formatting | bytes 9437184 | tf_op jit(solution)/shard_map/transpose | solution.py:270
  235.4 6.7 %copy.86 = bf16[768,4,768]{0,2,1:T(8,128)(2,1)} copy(bf16[768,4,768]{2,0,1:T(8,128)(2,1)} %get-tuple-element.106) | data formatting | bytes 9437184 | tf_op jit(solution)/shard_map/transpose | solution.py:270
  242.1 12.0 %multiply_convert_fusion = (bf16[1024,3072]{1,0:T(8,128)(2,1)S(1)}, f32[1024,3072]{1,0:T(8,128)}) fusion(f32[3072]{0:T(1024)} %add.449, bf16[768,3072]{0,1:T(8,128)(2,1)} %bitcast.275, f32[1024,768]{1,0:T(8,128)S(1)} %get-tuple-element.155, f32[768]{0:T(1024)} %convert_element_type.342, f32[768]{0:T(1024)S(1)} %convert_element_type.341, ...), kind=kOutput, calls=%fused_computation.8 | convolution fusion | flops 4854644736 | bytes 26765312 | tf_op jit(solution)/shard_map/dot_general | solution.py:22
  254.2 5.4 fusion.96
  260.9 3.9 fusion.17
  264.8 3.2 fusion.83
  268.0 6.9 %convolution_convert_fusion = bf16[768,3072]{1,0:T(8,128)(2,1)} fusion(bf16[1024,3072]{1,0:T(8,128)(2,1)S(1)} %get-tuple-element.156, f32[1024,768]{1,0:T(8,128)S(1)} %get-tuple-element.103), kind=kOutput, calls=%fused_computation.13 | convolution fusion | flops 4834983936 | bytes 14155776 | tf_op jit(solution)/shard_map/dot_general | solution.py:22
  274.9 12.3 %convert_reduce_fusion = (f32[3072]{0:T(1024)}, bf16[1024,3072]{1,0:T(8,128)(2,1)S(1)}) fusion(f32[1024,3072]{1,0:T(8,128)} %get-tuple-element.157, f32[3072]{0:T(1024)S(1)} %copy-done.29, bf16[768,3072]{0,1:T(8,128)(2,1)S(1)} %bitcast.280, f32[1024,768]{1,0:T(8,128)S(1)} %get-tuple-element.103), kind=kOutput, calls=%fused_computation.7 | convolution fusion | flops 4873516032 | bytes 26763264 | tf_op jit(solution)/shard_map/dot_general | solution.py:22
  287.2 8.1 %convolution_convert_fusion.1 = bf16[768,3072]{1,0:T(8,128)(2,1)} fusion(bf16[1024,3072]{1,0:T(8,128)(2,1)S(1)} %get-tuple-element.162, f32[1024,768]{1,0:T(8,128)S(1)} %get-tuple-element.155, f32[768]{0:T(1024)S(1)} %copy-done.31, f32[768]{0:T(1024)S(1)} %copy-done.24, f32[1024]{0:T(1024)S(1)} %copy-done.27, f32[1024]{0:T(1024)S(1)} %broadcast_multiply_fusion.5), kind=kOutput, calls=%fused_computation.14 | convolution fusion | flops 4838129664 | bytes 14170112 | tf_op jit(solution)/shard_map/dot_general | solution.py:22
  295.4 6.5 %multiply_reduce_fusion = (f32[768]{0:T(1024)}, f32[1024]{0:T(1024)S(1)}, f32[1024]{0:T(1024)S(1)}, f32[768]{0:T(1024)}, f32[1024,768]{1,0:T(8,128)S(1)}) fusion(f32[1024,768]{1,0:T(8,128)S(1)} %get-tuple-element.155, f32[1024]{0:T(1024)S(1)} %copy-done.27, f32[1024]{0:T(1024)S(1)} %broadcast_multiply_fusion.5, f32[768]{0:T(1024)S(1)} %copy-done.24, ...), kind=kOutput, calls=%fused_computation.36 | convolution fusion | flops 4839698432 | bytes 20472832 | tf_op jit(solution)/shard_map/dot_general | solution.py:22
  303.6 2.6 fusion.33
  306.2 2.6 fusion.46.g_ref
  308.8 44.6 %attend_back.1 = (bf16[1,1024,768]{2,1,0:T(8,128)(2,1)}, bf16[1,1024,768]{2,1,0:T(8,128)(2,1)}, bf16[1,1024,768]{2,1,0:T(8,128)(2,1)}) custom-call(bf16[1,1024,768]{2,1,0:T(8,128)(2,1)} %fusion.47.q_ref, bf16[1,1024,768]{2,1,0:T(8,128)(2,1)} %fusion.45.k_ref, bf16[1,1024,768]{2,1,0:T(8,128)(2,1)} %fusion.48.v_ref, bf16[1,1024,768]{2,1,0:T(8,128)(2,1)} %fusion.46.g_ref, ...), custom_call_target="tpu_custom_call" | custom-call | tf_op jit(solution)/shard_map/attend_back/pallas_call | solution.py:113
  355.1 4.6 fusion.28
  371.1 3.1 fusion.24
  374.2 2.7 fusion.36
  376.9 2.7 fusion.39
  379.6 2.7 fusion.42
  382.3 2.1 pad_maximum_fusion.1
  384.3 4.3 copy.88
  391.2 6.5 %add_convert_fusion = bf16[1024,768]{1,0:T(8,128)(2,1)} fusion(f32[1024,768]{1,0:T(8,128)} %fusion.24, f32[1024,768]{1,0:T(8,128)S(1)} %copy-done.2, f32[1024,768]{1,0:T(8,128)} %fusion.28, bf16[1,1024,768]{2,1,0:T(8,128)(2,1)} %get-tuple-element.26, bf16[768,2304]{1,0:T(8,128)(2,1)} %copy-done.4), kind=kOutput, calls=%fused_computation.37 | convolution fusion | flops 1211105280 | bytes 13762560 | tf_op jit(solution)/shard_map/dot_general | solution.py:22
  397.6 2.7 pad_maximum_fusion
  409.2 9.1 %collective-permute-start.29 = (f32[9216]{0:T(1024)S(1)}, f32[9216]{0:T(1024)S(1)}, u32[]{:S(2)}, u32[]{:S(2)}) collective-permute-start(f32[9216]{0:T(1024)S(1)} %add.484), channel_id=1, source_target_pairs={{0,1},{1,0},{2,3},{3,2},{4,5},{5,4},{6,7},{7,6},{8,9},{9,8},{10,11... | collective-permute-start | bytes 110600 | tf_op jit(solution)/shard_map/ppermute | solution.py:147
  420.6 2.9 collective-permute-start.30
  423.6 31.1 %collective-permute-done.30 = f32[9216]{0:T(1024)S(1)} collective-permute-done((f32[9216]{0:T(1024)S(1)}, f32[9216]{0:T(1024)S(1)}, u32[]{:S(2)}, u32[]{:S(2)}) %collective-permute-start.30) | collective-permute-done | bytes 36896 | tf_op jit(solution)/shard_map/ppermute | solution.py:147
  454.7 2.6 collective-permute-start.10
  461.5 5.4 collective-permute-done.10
  471.6 18.5 %collective-permute-done.11 = bf16[1,256,768]{2,1,0:T(8,128)(2,1)S(1)} collective-permute-done((bf16[1,256,768]{2,1,0:T(8,128)(2,1)S(1)}, bf16[1,256,768]{2,1,0:T(8,128)(2,1)S(1)}, u32[]{:S(2)}, u32[]{:S(2)}) %collective-permute-start.11) | collective-permute-done | bytes 393248 | tf_op jit(solution)/shard_map/ppermute | solution.py:138
  492.5 10.8 %collective-permute-done.20 = bf16[2,96,1152]{2,1,0:T(8,128)(2,1)S(1)} collective-permute-done((bf16[2,96,1152]{2,1,0:T(8,128)(2,1)S(1)}, bf16[2,96,1152]{2,1,0:T(8,128)(2,1)S(1)}, u32[]{:S(2)}, u32[]{:S(2)}) %collective-permute-start.20) | collective-permute-done | bytes 442400 | tf_op jit(solution)/shard_map/ppermute | solution.py:147
  507.0 2.5 collective-permute-done.21
  512.0 4.3 collective-permute-start.24
  518.4 6.7 %collective-permute-done.24 = bf16[2,96,576]{2,1,0:T(8,128)(2,1)S(1)} collective-permute-done((bf16[2,96,576]{2,1,0:T(8,128)(2,1)S(1)}, bf16[2,96,576]{2,1,0:T(8,128)(2,1)S(1)}, u32[]{:S(2)}, u32[]{:S(2)}) %collective-permute-start.24) | collective-permute-done | bytes 221216 | tf_op jit(solution)/shard_map/ppermute | solution.py:147
  526.3 3.9 collective-permute-done.25
  531.4 10.3 %collective-permute-done.41 = bf16[2,96,1536]{2,1,0:T(8,128)(2,1)S(1)} collective-permute-done((bf16[2,96,1536]{2,1,0:T(8,128)(2,1)S(1)}, bf16[2,96,1536]{2,1,0:T(8,128)(2,1)S(1)}, u32[]{:S(2)}, u32[]{:S(2)}) %collective-permute-start.41) | collective-permute-done | bytes 589856 | tf_op jit(solution)/shard_map/ppermute | solution.py:147
  542.6 2.5 fusion.6
  547.9 3.9 collective-permute-done.42
  553.9 8.4 %collective-permute-done.34 = bf16[2,96,1920]{2,1,0:T(8,128)(2,1)S(1)} collective-permute-done((bf16[2,96,1920]{2,1,0:T(8,128)(2,1)S(1)}, bf16[2,96,1920]{2,1,0:T(8,128)(2,1)S(1)}, u32[]{:S(2)}, u32[]{:S(2)}) %collective-permute-start.34) | collective-permute-done | bytes 737312 | tf_op jit(solution)/shard_map/ppermute | solution.py:147
  563.3 3.3 collective-permute-done.32
  568.4 3.3 collective-permute-done.35
  571.9 2.5 collective-permute-done.33
  577.3 12.8 %collective-permute-done.36 = bf16[2,96,960]{2,1,0:T(8,128)(2,1)S(1)} collective-permute-done((bf16[2,96,960]{2,1,0:T(8,128)(2,1)S(1)}, bf16[2,96,960]{2,1,0:T(8,128)(2,1)S(1)}, u32[]{:S(2)}, u32[]{:S(2)}) %collective-permute-start.36) | collective-permute-done | bytes 368672 | tf_op jit(solution)/shard_map/ppermute | solution.py:147
  591.2 4.9 collective-permute-done.37
  (320 shorter events, 97.2 us)
Async XLA Ops:
  7.2 205.8 %all-gather.2.cloned.1.call-start = ((), (), s32[]{:S(2)}) async-start(), calls=%async_computation | async-start | bytes 11354112 | tf_op jit(solution)/shard_map/all_gather | solution.py:299
  13.0 6.7 %collective-permute-start.3 = (bf16[98,576]{1,0:T(8,128)(2,1)S(1)}, bf16[98,576]{1,0:T(8,128)(2,1)S(1)}, u32[]{:S(2)}, u32[]{:S(2)}) collective-permute-start(bf16[98,576]{1,0:T(8,128)(2,1)S(1)} %pad_maximum_fusion.9), channel_id=1, source_target_pairs={{0,1},{1,0},{2,3},{3,2},{4,5},{5,4},{6,7},{7,6},{8,9},{9,8},{10,11... | collective-permute-start | bytes 338696 | tf_op jit(solution)/shard_map/ppermute | solution.py:147
  20.1 20.9 %collective-permute-start.4 = (bf16[2,98,576]{2,0,1:T(2,128)(2,1)S(1)}, bf16[2,98,576]{2,0,1:T(2,128)(2,1)S(1)}, u32[]{:S(2)}, u32[]{:S(2)}) collective-permute-start(bf16[2,98,576]{2,0,1:T(2,128)(2,1)S(1)} %broadcast_select_fusion.3), channel_id=1, source_target_pairs={{0,2},{1,3},{2,0},{3,1},{4,6},{5,7},{6,4},{7,5},{8,10},{9,11},{10,... | collective-permute-start | bytes 677384 | tf_op jit(solution)/shard_map/ppermute | solution.py:147
  44.8 11.3 %collective-permute-start.5 = (bf16[96,1152]{1,0:T(8,128)(2,1)S(1)}, bf16[96,1152]{1,0:T(8,128)(2,1)S(1)}, u32[]{:S(2)}, u32[]{:S(2)}) collective-permute-start(bf16[96,1152]{1,0:T(8,128)(2,1)S(1)} %get-tuple-element.131), channel_id=1, source_target_pairs={{0,8},{4,12},{8,0},{12,4},{16,24},{20,28},{24,16},{28,20},{1,9},{5... | collective-permute-start | bytes 663560 | tf_op jit(solution)/shard_map/ppermute | solution.py:147
  46.2 12.1 %collective-permute-start.7 = (bf16[96,1152]{1,0:T(8,128)(2,1)S(1)}, bf16[96,1152]{1,0:T(8,128)(2,1)S(1)}, u32[]{:S(2)}, u32[]{:S(2)}) collective-permute-start(bf16[96,1152]{1,0:T(8,128)(2,1)S(1)} %get-tuple-element.132), channel_id=1, source_target_pairs={{0,16},{4,20},{8,24},{12,28},{16,0},{20,4},{24,8},{28,12},{1,17},{... | collective-permute-start | bytes 663560 | tf_op jit(solution)/shard_map/ppermute | solution.py:147
  56.2 9.2 %collective-permute-start.6 = (bf16[2,96,1152]{2,1,0:T(8,128)(2,1)S(1)}, bf16[2,96,1152]{2,1,0:T(8,128)(2,1)S(1)}, u32[]{:S(2)}, u32[]{:S(2)}) collective-permute-start(bf16[2,96,1152]{2,1,0:T(8,128)(2,1)S(1)} %broadcast_select_fusion.5), channel_id=1, source_target_pairs={{0,16},{4,20},{8,24},{12,28},{16,0},{20,4},{24,8},{28,12},{1,17},{... | collective-permute-start | bytes 1327112 | tf_op jit(solution)/shard_map/ppermute | solution.py:147
  58.5 11.6 %collective-permute-start.8 = (bf16[2,96,1152]{2,1,0:T(8,128)(2,1)S(1)}, bf16[2,96,1152]{2,1,0:T(8,128)(2,1)S(1)}, u32[]{:S(2)}, u32[]{:S(2)}) collective-permute-start(bf16[2,96,1152]{2,1,0:T(8,128)(2,1)S(1)} %broadcast_select_fusion.4), channel_id=1, source_target_pairs={{0,8},{4,12},{8,0},{12,4},{16,24},{20,28},{24,16},{28,20},{1,9},{5... | collective-permute-start | bytes 1327112 | tf_op jit(solution)/shard_map/ppermute | solution.py:147
  70.4 98.3 %collective-permute-start.9 = (bf16[2,2,96,2304]{3,2,1,0:T(8,128)(2,1)S(1)}, bf16[2,2,96,2304]{3,2,1,0:T(8,128)(2,1)}, u32[]{:S(2)}, u32[]{:S(2)}) collective-permute-start(bf16[2,2,96,2304]{3,2,1,0:T(8,128)(2,1)S(1)} %pad_maximum_fusion.2), channel_id=1, source_target_pairs={{0,4},{4,0},{8,12},{12,8},{16,20},{20,16},{24,28},{28,24},{1,5},{5... | collective-permute-start | bytes 5308424 | tf_op jit(solution)/shard_map/ppermute | solution.py:147
  70.6 14.7 %copy-start.39 = (bf16[768]{0:T(1024)(128)(2,1)S(1)}, bf16[768]{0:T(1024)(128)(2,1)}, u32[]{:S(2)}) copy-start(bf16[768]{0:T(1024)(128)(2,1)} %param.34) | copy-start | bytes 4612
  70.6 15.3 %copy-start.40 = (bf16[768]{0:T(1024)(128)(2,1)S(1)}, bf16[768]{0:T(1024)(128)(2,1)}, u32[]{:S(2)}) copy-start(bf16[768]{0:T(1024)(128)(2,1)} %param.35) | copy-start | bytes 4612
  70.6 15.3 %copy-start.41 = (bf16[768]{0:T(1024)(128)(2,1)S(1)}, bf16[768]{0:T(1024)(128)(2,1)}, u32[]{:S(2)}) copy-start(bf16[768]{0:T(1024)(128)(2,1)} %param.36) | copy-start | bytes 4612
  73.0 21.9 %collective-permute-start.13 = (bf16[1,256,768]{2,1,0:T(8,128)(2,1)}, bf16[1,256,768]{2,1,0:T(8,128)(2,1)S(1)}, u32[]{:S(2)}, u32[]{:S(2)}) collective-permute-start(bf16[1,256,768]{2,1,0:T(8,128)(2,1)} %get-tuple-element.120), channel_id=1, source_target_pairs={{0,1},{1,2},{2,3},{3,0},{4,5},{5,6},{6,7},{7,4},{8,9},{9,10},{10,1... | collective-permute-start | bytes 1179656 | tf_op jit(solution)/shard_map/ppermute | solution.py:129
  74.9 69.7 %collective-permute-start.14 = (bf16[1,256,768]{2,1,0:T(8,128)(2,1)S(1)}, bf16[1,256,768]{2,1,0:T(8,128)(2,1)S(1)}, u32[]{:S(2)}, u32[]{:S(2)}) collective-permute-start(bf16[1,256,768]{2,1,0:T(8,128)(2,1)S(1)} %get-tuple-element.122), channel_id=1, source_target_pairs={{0,2},{1,3},{2,0},{3,1},{4,6},{5,7},{6,4},{7,5},{8,10},{9,11},{10,... | collective-permute-start | bytes 1179656 | tf_op jit(solution)/shard_map/ppermute | solution.py:129
  80.8 89.8 %collective-permute-start = (bf16[1,256,768]{2,1,0:T(8,128)(2,1)}, bf16[1,256,768]{2,1,0:T(8,128)(2,1)}, u32[]{:S(2)}, u32[]{:S(2)}) collective-permute-start(bf16[1,256,768]{2,1,0:T(8,128)(2,1)} %get-tuple-element.128), channel_id=1, source_target_pairs={{0,1},{1,2},{2,3},{3,0},{4,5},{5,6},{6,7},{7,4},{8,9},{9,10},{10,1... | collective-permute-start | bytes 1179656 | tf_op jit(solution)/shard_map/ppermute | solution.py:129
  81.3 89.3 %collective-permute-start.1 = (bf16[1,256,768]{2,1,0:T(8,128)(2,1)}, bf16[1,256,768]{2,1,0:T(8,128)(2,1)}, u32[]{:S(2)}, u32[]{:S(2)}) collective-permute-start(bf16[1,256,768]{2,1,0:T(8,128)(2,1)} %get-tuple-element.130), channel_id=1, source_target_pairs={{0,2},{1,3},{2,0},{3,1},{4,6},{5,7},{6,4},{7,5},{8,10},{9,11},{10,... | collective-permute-start | bytes 1179656 | tf_op jit(solution)/shard_map/ppermute | solution.py:129
  84.7 169.5 %copy-start.23 = (f32[768]{0:T(1024)}, f32[768]{0:T(1024)S(1)}, u32[]{:S(2)}) copy-start(f32[768]{0:T(1024)S(1)} %convert_element_type.341) | copy-start | bytes 9220
  94.9 75.7 %copy-start.10 = (bf16[1,256,768]{2,1,0:T(8,128)(2,1)}, bf16[1,256,768]{2,1,0:T(8,128)(2,1)S(1)}, u32[]{:S(2)}) copy-start(bf16[1,256,768]{2,1,0:T(8,128)(2,1)S(1)} %collective-permute-done.13) | copy-start | bytes 1179652
  94.9 75.7 %collective-permute-start.2 = (bf16[1,256,768]{2,1,0:T(8,128)(2,1)}, bf16[1,256,768]{2,1,0:T(8,128)(2,1)}, u32[]{:S(2)}, u32[]{:S(2)}) collective-permute-start(bf16[1,256,768]{2,1,0:T(8,128)(2,1)} %get-tuple-element.129), channel_id=1, source_target_pairs={{0,3},{1,0},{2,1},{3,2},{4,7},{5,4},{6,5},{7,6},{8,11},{9,8},{10,9... | collective-permute-start | bytes 1179656 | tf_op jit(solution)/shard_map/ppermute | solution.py:129
  144.6 26.0 %copy-start.12 = (bf16[1,256,768]{2,1,0:T(8,128)(2,1)}, bf16[1,256,768]{2,1,0:T(8,128)(2,1)S(1)}, u32[]{:S(2)}) copy-start(bf16[1,256,768]{2,1,0:T(8,128)(2,1)S(1)} %collective-permute-done.14) | copy-start | bytes 1179652
  144.6 23.2 %collective-permute-start.15 = (bf16[1,256,768]{2,1,0:T(8,128)(2,1)}, bf16[1,256,768]{2,1,0:T(8,128)(2,1)S(1)}, u32[]{:S(2)}, u32[]{:S(2)}) collective-permute-start(bf16[1,256,768]{2,1,0:T(8,128)(2,1)} %get-tuple-element.121), channel_id=1, source_target_pairs={{0,3},{1,0},{2,1},{3,2},{4,7},{5,4},{6,5},{7,6},{8,11},{9,8},{10,9... | collective-permute-start | bytes 1179656 | tf_op jit(solution)/shard_map/ppermute | solution.py:129
  268.0 27.3 %slice-start.4 = ((s8[4718592]{0:T(1024)(128)(4,1)}), s8[4194304]{0:T(1024)(128)(4,1)S(1)}, s32[]{:S(2)}) async-start(s8[4718592]{0:T(1024)(128)(4,1)} %bitcast.276), calls=%async_computation.5 | async-start | bytes 8388608
  274.9 20.4 %slice-start.5 = ((s8[4718592]{0:T(1024)(128)(4,1)}), s8[524288]{0:T(1024)(128)(4,1)S(1)}, s32[]{:S(2)}) async-start(s8[4718592]{0:T(1024)(128)(4,1)} %bitcast.276), calls=%async_computation.6 | async-start | bytes 1048576
  308.8 46.3 %copy-start.5 = (bf16[768,2304]{1,0:T(8,128)(2,1)S(1)}, bf16[768,2304]{1,0:T(8,128)(2,1)}, u32[]{:S(2)}) copy-start(bf16[768,2304]{1,0:T(8,128)(2,1)} %copy-done.4) | copy-start | bytes 10616836
  355.1 15.3 %copy-start.30 = (f32[3072]{0:T(1024)S(1)}, f32[3072]{0:T(1024)}, u32[]{:S(2)}) copy-start(f32[3072]{0:T(1024)} %get-tuple-element.161) | copy-start | bytes 36868
  355.1 15.9 %copy-start.43 = (bf16[1,1024,768]{2,1,0:T(8,128)(2,1)S(1)}, bf16[1,1024,768]{2,1,0:T(8,128)(2,1)}, u32[]{:S(2)}) copy-start(bf16[1,1024,768]{2,1,0:T(8,128)(2,1)} %get-tuple-element.25) | copy-start | bytes 4718596
  371.0 29.4 %collective-permute-start.26 = (f32[9216]{0:T(1024)}, f32[9216]{0:T(1024)}, u32[]{:S(2)}, u32[]{:S(2)}) collective-permute-start(f32[9216]{0:T(1024)} %constant_dynamic-update-slice_fusion.6), channel_id=1, source_target_pairs={{0,4},{4,0},{8,12},{12,8},{16,20},{20,16},{24,28},{28,24},{1,5},{5... | collective-permute-start | bytes 110600 | tf_op jit(solution)/shard_map/ppermute | solution.py:147
  390.0 77.4 %collective-permute-start.19 = (bf16[2,2,96,2304]{3,2,1,0:T(8,128)(2,1)}, bf16[2,2,96,2304]{3,2,1,0:T(8,128)(2,1)}, u32[]{:S(2)}, u32[]{:S(2)}) collective-permute-start(bf16[2,2,96,2304]{3,2,1,0:T(8,128)(2,1)} %dynamic-slice_bitcast_fusion.2), channel_id=1, source_target_pairs={{0,4},{4,0},{8,12},{12,8},{16,20},{20,16},{24,28},{28,24},{1,5},{5... | collective-permute-start | bytes 5308424 | tf_op jit(solution)/shard_map/ppermute | solution.py:147
  401.3 4.0 collective-permute-start.27
  405.2 4.0 collective-permute-start.28
  406.8 16.7 %copy-start.3 = (bf16[1024,768]{1,0:T(8,128)(2,1)S(1)}, bf16[1024,768]{1,0:T(8,128)(2,1)}, u32[]{:S(2)}) copy-start(bf16[1024,768]{1,0:T(8,128)(2,1)} %get-tuple-element.108) | copy-start | bytes 4718596
  409.2 11.4 %collective-permute-start.29 = (f32[9216]{0:T(1024)S(1)}, f32[9216]{0:T(1024)S(1)}, u32[]{:S(2)}, u32[]{:S(2)}) collective-permute-start(f32[9216]{0:T(1024)S(1)} %add.484), channel_id=1, source_target_pairs={{0,1},{1,0},{2,3},{3,2},{4,5},{5,4},{6,7},{7,6},{8,9},{9,8},{10,11... | collective-permute-start | bytes 110600 | tf_op jit(solution)/shard_map/ppermute | solution.py:147
  418.4 40.3 %collective-permute-start.16 = (bf16[1,256,768]{2,1,0:T(8,128)(2,1)S(1)}, bf16[1,256,768]{2,1,0:T(8,128)(2,1)S(1)}, u32[]{:S(2)}, u32[]{:S(2)}) collective-permute-start(bf16[1,256,768]{2,1,0:T(8,128)(2,1)S(1)} %get-tuple-element.117), channel_id=1, source_target_pairs={{0,3},{1,0},{2,1},{3,2},{4,7},{5,4},{6,5},{7,6},{8,11},{9,8},{10,9... | collective-permute-start | bytes 1179656 | tf_op jit(solution)/shard_map/ppermute | solution.py:138
  419.0 39.9 %collective-permute-start.17 = (bf16[1,256,768]{2,1,0:T(8,128)(2,1)S(1)}, bf16[1,256,768]{2,1,0:T(8,128)(2,1)S(1)}, u32[]{:S(2)}, u32[]{:S(2)}) collective-permute-start(bf16[1,256,768]{2,1,0:T(8,128)(2,1)S(1)} %get-tuple-element.116), channel_id=1, source_target_pairs={{0,2},{1,3},{2,0},{3,1},{4,6},{5,7},{6,4},{7,5},{8,10},{9,11},{10,... | collective-permute-start | bytes 1179656 | tf_op jit(solution)/shard_map/ppermute | solution.py:138
  419.9 39.5 %collective-permute-start.18 = (bf16[1,256,768]{2,1,0:T(8,128)(2,1)S(1)}, bf16[1,256,768]{2,1,0:T(8,128)(2,1)S(1)}, u32[]{:S(2)}, u32[]{:S(2)}) collective-permute-start(bf16[1,256,768]{2,1,0:T(8,128)(2,1)S(1)} %get-tuple-element.115), channel_id=1, source_target_pairs={{0,1},{1,2},{2,3},{3,0},{4,5},{5,6},{6,7},{7,4},{8,9},{9,10},{10,1... | collective-permute-start | bytes 1179656 | tf_op jit(solution)/shard_map/ppermute | solution.py:138
  420.6 34.1 %collective-permute-start.30 = (f32[9216]{0:T(1024)S(1)}, f32[9216]{0:T(1024)S(1)}, u32[]{:S(2)}, u32[]{:S(2)}) collective-permute-start(f32[9216]{0:T(1024)S(1)} %add.485), channel_id=1, source_target_pairs={{0,2},{1,3},{2,0},{3,1},{4,6},{5,7},{6,4},{7,5},{8,10},{9,11},{10,... | collective-permute-start | bytes 110600 | tf_op jit(solution)/shard_map/ppermute | solution.py:147
  454.7 12.2 %collective-permute-start.10 = (bf16[1,256,768]{2,1,0:T(8,128)(2,1)S(1)}, bf16[1,256,768]{2,1,0:T(8,128)(2,1)S(1)}, u32[]{:S(2)}, u32[]{:S(2)}) collective-permute-start(bf16[1,256,768]{2,1,0:T(8,128)(2,1)S(1)} %get-tuple-element.125), channel_id=1, source_target_pairs={{0,3},{1,0},{2,1},{3,2},{4,7},{5,4},{6,5},{7,6},{8,11},{9,8},{10,9... | collective-permute-start | bytes 1179656 | tf_op jit(solution)/shard_map/ppermute | solution.py:138
  458.7 46.0 %collective-permute-start.38 = (bf16[2,2,96,3072]{3,2,1,0:T(8,128)(2,1)S(1)}, bf16[2,2,96,3072]{3,2,1,0:T(8,128)(2,1)S(1)}, u32[]{:S(2)}, u32[]{:S(2)}) collective-permute-start(bf16[2,2,96,3072]{3,2,1,0:T(8,128)(2,1)S(1)} %dynamic-slice_bitcast_fusion.1), channel_id=1, source_target_pairs={{0,4},{4,0},{8,12},{12,8},{16,20},{20,16},{24,28},{28,24},{1,5},{5... | collective-permute-start | bytes 7077896 | tf_op jit(solution)/shard_map/ppermute | solution.py:147
  458.9 83.8 %collective-permute-start.31 = (bf16[2,2,96,3840]{3,2,1,0:T(8,128)(2,1)}, bf16[2,2,96,3840]{3,2,1,0:T(8,128)(2,1)}, u32[]{:S(2)}, u32[]{:S(2)}) collective-permute-start(bf16[2,2,96,3840]{3,2,1,0:T(8,128)(2,1)} %dynamic-slice_bitcast_fusion), channel_id=1, source_target_pairs={{0,4},{4,0},{8,12},{12,8},{16,20},{20,16},{24,28},{28,24},{1,5},{5... | collective-permute-start | bytes 8847368 | tf_op jit(solution)/shard_map/ppermute | solution.py:147
  459.5 30.6 %collective-permute-start.11 = (bf16[1,256,768]{2,1,0:T(8,128)(2,1)S(1)}, bf16[1,256,768]{2,1,0:T(8,128)(2,1)S(1)}, u32[]{:S(2)}, u32[]{:S(2)}) collective-permute-start(bf16[1,256,768]{2,1,0:T(8,128)(2,1)S(1)} %get-tuple-element.124), channel_id=1, source_target_pairs={{0,2},{1,3},{2,0},{3,1},{4,6},{5,7},{6,4},{7,5},{8,10},{9,11},{10,... | collective-permute-start | bytes 1179656 | tf_op jit(solution)/shard_map/ppermute | solution.py:138
  466.9 23.1 %collective-permute-start.12 = (bf16[1,256,768]{2,1,0:T(8,128)(2,1)S(1)}, bf16[1,256,768]{2,1,0:T(8,128)(2,1)S(1)}, u32[]{:S(2)}, u32[]{:S(2)}) collective-permute-start(bf16[1,256,768]{2,1,0:T(8,128)(2,1)S(1)} %get-tuple-element.123), channel_id=1, source_target_pairs={{0,1},{1,2},{2,3},{3,0},{4,5},{5,6},{6,7},{7,4},{8,9},{9,10},{10,1... | collective-permute-start | bytes 1179656 | tf_op jit(solution)/shard_map/ppermute | solution.py:138
  467.4 37.3 %slice-start.2 = ((s8[4718592]{0:T(1024)(128)(4,1)}), s8[4194304]{0:T(1024)(128)(4,1)S(1)}, s32[]{:S(2)}) async-start(s8[4718592]{0:T(1024)(128)(4,1)} %bitcast.272), calls=%async_computation.3 | async-start | bytes 8388608
  469.4 35.3 %slice-start.3 = ((s8[4718592]{0:T(1024)(128)(4,1)}), s8[524288]{0:T(1024)(128)(4,1)S(1)}, s32[]{:S(2)}) async-start(s8[4718592]{0:T(1024)(128)(4,1)} %bitcast.272), calls=%async_computation.4 | async-start | bytes 1048576
  469.7 21.6 %collective-permute-start.22 = (bf16[2,96,1152]{2,1,0:T(8,128)(2,1)S(1)}, bf16[2,96,1152]{2,1,0:T(8,128)(2,1)S(1)}, u32[]{:S(2)}, u32[]{:S(2)}) collective-permute-start(bf16[2,96,1152]{2,1,0:T(8,128)(2,1)S(1)} %dynamic-slice_bitcast_fusion.7), channel_id=1, source_target_pairs={{0,8},{4,12},{8,0},{12,4},{16,24},{20,28},{24,16},{28,20},{1,9},{5... | collective-permute-start | bytes 1327112 | tf_op jit(solution)/shard_map/ppermute | solution.py:147
  490.1 14.6 %copy-start.18 = (bf16[4,256,768]{2,1,0:T(8,128)(2,1)}, bf16[4,256,768]{2,1,0:T(8,128)(2,1)S(1)}, u32[]{:S(2)}) copy-start(bf16[4,256,768]{2,1,0:T(8,128)(2,1)S(1)} %constant_dynamic-update-slice_fusion.3) | copy-start | bytes 4718596
  490.2 13.1 %collective-permute-start.20 = (bf16[2,96,1152]{2,1,0:T(8,128)(2,1)S(1)}, bf16[2,96,1152]{2,1,0:T(8,128)(2,1)S(1)}, u32[]{:S(2)}, u32[]{:S(2)}) collective-permute-start(bf16[2,96,1152]{2,1,0:T(8,128)(2,1)S(1)} %dynamic-slice_bitcast_fusion.8), channel_id=1, source_target_pairs={{0,16},{4,20},{8,24},{12,28},{16,0},{20,4},{24,8},{28,12},{1,17},{... | collective-permute-start | bytes 1327112 | tf_op jit(solution)/shard_map/ppermute | solution.py:147
  491.4 15.5 %collective-permute-start.23 = (bf16[96,1152]{1,0:T(8,128)(2,1)S(1)}, bf16[96,1152]{1,0:T(8,128)(2,1)S(1)}, u32[]{:S(2)}, u32[]{:S(2)}) collective-permute-start(bf16[96,1152]{1,0:T(8,128)(2,1)S(1)} %dynamic-slice_bitcast_fusion.15), channel_id=1, source_target_pairs={{0,16},{4,20},{8,24},{12,28},{16,0},{20,4},{24,8},{28,12},{1,17},{... | collective-permute-start | bytes 663560 | tf_op jit(solution)/shard_map/ppermute | solution.py:147
  503.5 6.0 collective-permute-start.21
  506.9 35.7 %slice-start = ((s8[5898240]{0:T(1024)(128)(4,1)}), s8[1703936]{0:T(1024)(128)(4,1)S(1)}, s32[]{:S(2)}) async-start(s8[5898240]{0:T(1024)(128)(4,1)} %bitcast.260), calls=%async_computation.1 | async-start | bytes 3407872
  511.8 18.4 %copy-start.9 = (bf16[2,2,96,1536]{3,2,1,0:T(8,128)(2,1)S(1)}, bf16[2,2,96,1536]{3,2,1,0:T(8,128)(2,1)}, u32[]{:S(2)}) copy-start(bf16[2,2,96,1536]{3,2,1,0:T(8,128)(2,1)} %get-tuple-element.111) | copy-start | bytes 3538948
  512.0 13.1 %collective-permute-start.24 = (bf16[2,96,576]{2,1,0:T(8,128)(2,1)S(1)}, bf16[2,96,576]{2,1,0:T(8,128)(2,1)S(1)}, u32[]{:S(2)}, u32[]{:S(2)}) collective-permute-start(bf16[2,96,576]{2,1,0:T(8,128)(2,1)S(1)} %dynamic-slice_bitcast_fusion.14), channel_id=1, source_target_pairs={{0,2},{1,3},{2,0},{3,1},{4,6},{5,7},{6,4},{7,5},{8,10},{9,11},{10,... | collective-permute-start | bytes 663560 | tf_op jit(solution)/shard_map/ppermute | solution.py:147
  516.4 26.2 %slice-start.1 = ((s8[5898240]{0:T(1024)(128)(4,1)}), s8[4194304]{0:T(1024)(128)(4,1)S(1)}, s32[]{:S(2)}) async-start(s8[5898240]{0:T(1024)(128)(4,1)} %bitcast.260), calls=%async_computation.2 | async-start | bytes 8388608
  517.6 12.6 %collective-permute-start.39 = (bf16[2,96,1536]{2,1,0:T(8,128)(2,1)S(1)}, bf16[2,96,1536]{2,1,0:T(8,128)(2,1)S(1)}, u32[]{:S(2)}, u32[]{:S(2)}) collective-permute-start(bf16[2,96,1536]{2,1,0:T(8,128)(2,1)S(1)} %dynamic-slice_bitcast_fusion.6), channel_id=1, source_target_pairs={{0,16},{4,20},{8,24},{12,28},{16,0},{20,4},{24,8},{28,12},{1,17},{... | collective-permute-start | bytes 1769480 | tf_op jit(solution)/shard_map/ppermute | solution.py:147
  525.2 4.9 collective-permute-start.25
  525.4 16.3 %collective-permute-start.41 = (bf16[2,96,1536]{2,1,0:T(8,128)(2,1)S(1)}, bf16[2,96,1536]{2,1,0:T(8,128)(2,1)S(1)}, u32[]{:S(2)}, u32[]{:S(2)}) collective-permute-start(bf16[2,96,1536]{2,1,0:T(8,128)(2,1)S(1)} %dynamic-slice_bitcast_fusion.5), channel_id=1, source_target_pairs={{0,8},{4,12},{8,0},{12,4},{16,24},{20,28},{24,16},{28,20},{1,9},{5... | collective-permute-start | bytes 1769480 | tf_op jit(solution)/shard_map/ppermute | solution.py:147
  530.4 17.4 %collective-permute-start.40 = (bf16[96,1536]{1,0:T(8,128)(2,1)S(1)}, bf16[96,1536]{1,0:T(8,128)(2,1)S(1)}, u32[]{:S(2)}, u32[]{:S(2)}) collective-permute-start(bf16[96,1536]{1,0:T(8,128)(2,1)S(1)} %dynamic-slice_bitcast_fusion.13), channel_id=1, source_target_pairs={{0,8},{4,12},{8,0},{12,4},{16,24},{20,28},{24,16},{28,20},{1,9},{5... | collective-permute-start | bytes 884744 | tf_op jit(solution)/shard_map/ppermute | solution.py:147
  541.8 9.9 %collective-permute-start.42 = (bf16[96,1536]{1,0:T(8,128)(2,1)S(1)}, bf16[96,1536]{1,0:T(8,128)(2,1)S(1)}, u32[]{:S(2)}, u32[]{:S(2)}) collective-permute-start(bf16[96,1536]{1,0:T(8,128)(2,1)S(1)} %dynamic-slice_bitcast_fusion.12), channel_id=1, source_target_pairs={{0,16},{4,20},{8,24},{12,28},{16,0},{20,4},{24,8},{28,12},{1,17},{... | collective-permute-start | bytes 884744 | tf_op jit(solution)/shard_map/ppermute | solution.py:147
  545.5 21.1 %collective-permute-start.32 = (bf16[2,96,1920]{2,1,0:T(8,128)(2,1)S(1)}, bf16[2,96,1920]{2,1,0:T(8,128)(2,1)S(1)}, u32[]{:S(2)}, u32[]{:S(2)}) collective-permute-start(bf16[2,96,1920]{2,1,0:T(8,128)(2,1)S(1)} %dynamic-slice_bitcast_fusion.4), channel_id=1, source_target_pairs={{0,16},{4,20},{8,24},{12,28},{16,0},{20,4},{24,8},{28,12},{1,17},{... | collective-permute-start | bytes 2211848 | tf_op jit(solution)/shard_map/ppermute | solution.py:147
  546.9 15.3 %collective-permute-start.34 = (bf16[2,96,1920]{2,1,0:T(8,128)(2,1)S(1)}, bf16[2,96,1920]{2,1,0:T(8,128)(2,1)S(1)}, u32[]{:S(2)}, u32[]{:S(2)}) collective-permute-start(bf16[2,96,1920]{2,1,0:T(8,128)(2,1)S(1)} %dynamic-slice_bitcast_fusion.3), channel_id=1, source_target_pairs={{0,8},{4,12},{8,0},{12,4},{16,24},{20,28},{24,16},{28,20},{1,9},{5... | collective-permute-start | bytes 2211848 | tf_op jit(solution)/shard_map/ppermute | solution.py:147
  552.7 23.0 %collective-permute-start.43 = (bf16[2,96,768]{2,1,0:T(8,128)(2,1)}, bf16[2,96,768]{2,1,0:T(8,128)(2,1)S(1)}, u32[]{:S(2)}, u32[]{:S(2)}) collective-permute-start(bf16[2,96,768]{2,1,0:T(8,128)(2,1)} %dynamic-slice_bitcast_fusion.11), channel_id=1, source_target_pairs={{0,2},{1,3},{2,0},{3,1},{4,6},{5,7},{6,4},{7,5},{8,10},{9,11},{10,... | collective-permute-start | bytes 884744 | tf_op jit(solution)/shard_map/ppermute | solution.py:147
  562.5 9.3 %collective-permute-start.35 = (bf16[96,1920]{1,0:T(8,128)(2,1)S(1)}, bf16[96,1920]{1,0:T(8,128)(2,1)S(1)}, u32[]{:S(2)}, u32[]{:S(2)}) collective-permute-start(bf16[96,1920]{1,0:T(8,128)(2,1)S(1)} %dynamic-slice_bitcast_fusion.9), channel_id=1, source_target_pairs={{0,16},{4,20},{8,24},{12,28},{16,0},{20,4},{24,8},{28,12},{1,17},{... | collective-permute-start | bytes 1105928 | tf_op jit(solution)/shard_map/ppermute | solution.py:147
  566.8 7.6 %collective-permute-start.33 = (bf16[96,1920]{1,0:T(8,128)(2,1)S(1)}, bf16[96,1920]{1,0:T(8,128)(2,1)S(1)}, u32[]{:S(2)}, u32[]{:S(2)}) collective-permute-start(bf16[96,1920]{1,0:T(8,128)(2,1)S(1)} %dynamic-slice_bitcast_fusion.10), channel_id=1, source_target_pairs={{0,8},{4,12},{8,0},{12,4},{16,24},{20,28},{24,16},{28,20},{1,9},{5... | collective-permute-start | bytes 1105928 | tf_op jit(solution)/shard_map/ppermute | solution.py:147
  574.9 15.3 %collective-permute-start.36 = (bf16[2,96,960]{2,1,0:T(8,128)(2,1)S(1)}, bf16[2,96,960]{2,1,0:T(8,128)(2,1)S(1)}, u32[]{:S(2)}, u32[]{:S(2)}) collective-permute-start(bf16[2,96,960]{2,1,0:T(8,128)(2,1)S(1)} %fusion.75), channel_id=1, source_target_pairs={{0,2},{1,3},{2,0},{3,1},{4,6},{5,7},{6,4},{7,5},{8,10},{9,11},{10,... | collective-permute-start | bytes 1105928 | tf_op jit(solution)/shard_map/ppermute | solution.py:147
  575.8 14.6 %collective-permute-start.44 = (bf16[96,768]{1,0:T(8,128)(2,1)S(1)}, bf16[96,768]{1,0:T(8,128)(2,1)S(1)}, u32[]{:S(2)}, u32[]{:S(2)}) collective-permute-start(bf16[96,768]{1,0:T(8,128)(2,1)S(1)} %dynamic-slice_bitcast_fusion.18), channel_id=1, source_target_pairs={{0,1},{1,0},{2,3},{3,2},{4,5},{5,4},{6,7},{7,6},{8,9},{9,8},{10,11... | collective-permute-start | bytes 442376 | tf_op jit(solution)/shard_map/ppermute | solution.py:147
  590.3 5.7 collective-permute-start.37
  (32 other events, 226.8 us)
Sparse Core Ops, SparseCore 0:
  10.9 148.7 all-gather.1

commit v3 on v2

--- a/solution.py
+++ b/solution.py
@@ -102,6 +102,11 @@
             jax.ShapeDtypeStruct(queries.shape, LOW),
             jax.ShapeDtypeStruct((count, width // PAIR, 2, length), WIDE),
         ],
+        cost_estimate=pl.CostEstimate(
+            flops=28 * count * width * length * length,
+            transcendentals=count * width * length * length // HDIM,
+            bytes_accessed=8 * count * width * length,
+        ),
         name="attend",
     )(queries, keys_all, values, ids[:, None, :], ids[:, :, None])
 
@@ -116,6 +121,11 @@
         in_specs=[rows, rows, rows, rows, sums, as_row, as_col],
         out_specs=[rows, rows, rows],
         out_shape=[jax.ShapeDtypeStruct(queries.shape, LOW)] * 3,
+        cost_estimate=pl.CostEstimate(
+            flops=48 * count * width * length * length,
+            transcendentals=count * width * length * length // HDIM,
+            bytes_accessed=14 * count * width * length,
+        ),
         name="attend_back",
     )(queries, keys_all, values, grad_context, logsum, ids[:, None, :], ids[:, :, None])
 
@@ -130,16 +140,21 @@
     return parts
 
 
-def returned(axis, members, parts):
+def sent_back(axis, members, parts):
+    moved = [parts[0]]
+    for step in range(1, members):
+        pairs = [(i, (i - step) % members) for i in range(members)]
+        moved.append(lax.ppermute(parts[step], axis, pairs))
+    return moved
+
+
+def by_source(axis, members, moved):
     rank = lax.axis_index(axis)
-    result = None
-    for step in range(members):
-        pairs = [(i, (i - step) % members) for i in range(members)]
-        block = (lax.ppermute(parts[step], axis, pairs) if step else parts[step])[None]
-        if result is None:
-            result = jnp.broadcast_to(block, (members,) + block.shape[1:])
-        else:
-            result = lax.dynamic_update_slice_in_dim(result, block, (rank + step) % members, 0)
+    result = jnp.broadcast_to(moved[0][None], (members,) + moved[0].shape)
+    for step in range(1, members):
+        result = lax.dynamic_update_slice_in_dim(
+            result, moved[step][None], (rank + step) % members, 0
+        )
     return result
 
 
@@ -171,16 +186,16 @@
     return block.reshape((members,) + shape)
 
 
-def gather_rows(members, block):
+def gather_rows(members, block, before):
     if members != 8:
-        return lax.all_gather(block, "fsdp", axis=0, tiled=True)
+        return lax.all_gather(block, "fsdp", axis=0, tiled=True), before
     rows, cols = block.shape
     first = joined("fsdp", members, 2, block[:, : cols // 2], 0)
     second = joined("fsdp", members, 4, block[:, cols // 2 :], 0)
     first = joined("fsdp", members, 4, first, 0)
     second = joined("fsdp", members, 2, second, 1)
-    both = jnp.concatenate([first, second], axis=3)
-    return joined("fsdp", members, 1, both, 2).reshape(members * rows, cols)
+    both, before = lax.optimization_barrier((jnp.concatenate([first, second], axis=3), before))
+    return joined("fsdp", members, 1, both, 2).reshape(members * rows, cols), before
 
 
 def scatter_rows(members, grad):
@@ -196,11 +211,19 @@
     return jnp.concatenate([first, second], axis=1)
 
 
-def scatter_tp(members, blocks):
+def scatter_long(members, grad):
+    return lax.psum_scatter(grad, "fsdp", scatter_dimension=0, tiled=True).astype(WIDE)
+
+
+def scatter_tp_first(members, blocks):
+    blocks = blocks.astype(LOW)
     if members != 4:
-        return lax.psum_scatter(blocks.astype(LOW), "tp", scatter_dimension=0).astype(WIDE)
-    blocks = blocks.astype(LOW).reshape((2, 2) + blocks.shape[1:])
-    return halved("tp", members, 1, halved("tp", members, 2, blocks, 0).astype(LOW), 0)
+        return lax.psum_scatter(blocks, "tp", scatter_dimension=0)
+    return halved("tp", members, 2, blocks.reshape((2, 2) + blocks.shape[1:]), 0).astype(LOW)
+
+
+def scatter_tp_last(members, blocks):
+    return halved("tp", members, 1, blocks, 0) if members == 4 else blocks.astype(WIDE)
 
 
 def total_over_all(fsdp, tp, vector):
@@ -260,23 +283,28 @@
         parts = dealt("tp", tp, array.reshape(tp, count, places, width))
         return jnp.concatenate(parts, axis=1).reshape(count * length, width)
 
-    def own_places(array):
+    def to_owners(array):
         parts = array.reshape(count, tp, places, width)
-        parts = returned("tp", tp, [parts[:, step] for step in range(tp)])
-        return parts.reshape(sequences, places, width)
+        return sent_back("tp", tp, [parts[:, step] for step in range(tp)])
+
+    def own_places(parts):
+        return by_source("tp", tp, parts).reshape(sequences, places, width)
 
     def columns(blocks):
         members, rows, cols = blocks.shape
         return blocks.transpose(1, 0, 2).reshape(rows, members * cols)
 
-    def own_share(grad, widths):
-        share = scatter_rows(fsdp, grad)
+    def blocks_of(share, widths):
         rows, first, blocks = share.shape[0], 0, []
         for cols in widths:
             piece = share[:, first : first + cols].reshape(rows, tp, cols // tp)
             blocks.append(piece.transpose(1, 0, 2))
             first += cols
-        share, first, pieces = scatter_tp(tp, jnp.concatenate(blocks, axis=2)), 0, []
+        return jnp.concatenate(blocks, axis=2)
+
+    def own_share(share, widths):
+        share = scatter_tp_last(tp, scatter_tp_first(tp, blocks_of(share, widths)))
+        first, pieces = 0, []
         for cols in widths:
             pieces.append(share[:, first : first + cols // tp])
             first += cols // tp
@@ -292,14 +320,16 @@
     value_bias_full = biases[:, head_cols : 2 * head_cols].reshape(-1)
     inner_bias_full = biases[:, 2 * head_cols :].reshape(-1)
     heads = heads[:, :shard_rows].reshape(tp, shard_rows, 3, head_cols).transpose(1, 2, 0, 3)
-    heads = gather_rows(fsdp, heads.reshape(shard_rows, 3 * width))
+    rows = whole_rows(tokens)
+    heads, rows = gather_rows(fsdp, heads.reshape(shard_rows, 3 * width), rows)
     query_full, key_full, value_full = (heads[:, i * width : (i + 1) * width] for i in range(3))
-    rows = whole_rows(tokens)
-    rest = jnp.concatenate([inner_weight, outer_weight.T, output_weight.T], axis=1)
-    rest = lax.all_gather(rest, ("tp", "fsdp"), axis=0, tiled=True).reshape(tp, width, -1)
-    inner_full = columns(rest[:, :, :unit_cols])
-    outer_turned = columns(rest[:, :, unit_cols : 2 * unit_cols])
-    output_turned = columns(rest[:, :, 2 * unit_cols :])
+    wide = jnp.concatenate([inner_weight, output_weight.T], axis=1)
+    wide = gather_tp(tp, wide)
+    wide = jnp.concatenate([columns(wide[:, :, :unit_cols]), columns(wide[:, :, unit_cols:])], axis=1)
+    wide = lax.all_gather(wide, "fsdp", axis=0, tiled=True)
+    inner_full, output_turned = wide[:, : tp * unit_cols], wide[:, tp * unit_cols :]
+    outer_turned = columns(gather_tp(tp, outer_weight.T))
+    outer_turned = lax.all_gather(outer_turned, "fsdp", axis=0, tiled=True)
 
     first = rank * count
     segment = lax.dynamic_slice_in_dim(segment_ids, first, count, 0)
@@ -327,7 +357,7 @@
     branch = dot(activation_rows, outer_turned, BY_LAST)
     second_normed, second_scaling = normalize(first_rows + branch + outer_bias.astype(WIDE))
     second_rows = second_normed * second_gain.astype(WIDE) + second_shift.astype(WIDE)
-    layer_out = own_places(second_rows.astype(LOW))
+    layer_out = to_owners(second_rows.astype(LOW))
 
     grad_out = whole_rows(out_grad).astype(WIDE)
     grad_second, second_gain_grad, second_shift_grad = normalize_back(
@@ -335,7 +365,7 @@
     )
     outer_bias_grad = jnp.sum(grad_second, axis=0)
     grad_branch = grad_second.astype(LOW)
-    (outer_share,) = own_share(dot(grad_branch, activation_rows, BY_FIRST).astype(LOW), (outer_turned.shape[1],))
+    outer_share = scatter_rows(fsdp, dot(grad_branch, activation_rows, BY_FIRST).astype(LOW))
     grad_activ = dot(grad_branch, outer_turned, BY_ROWS)
     grad_pre = (grad_activ * slope).astype(LOW)
     inner_bias_grad = jnp.sum(grad_pre.astype(WIDE), axis=0)
@@ -347,14 +377,23 @@
     output_bias_grad = jnp.sum(grad_mixed, axis=0)
     grad_mixed_low = grad_mixed.astype(LOW)
     output_grad = dot(grad_mixed_low, context, BY_FIRST).astype(LOW)
-    inner_share, output_share = own_share(
-        jnp.concatenate([inner_grad, output_grad], axis=1), (inner_grad.shape[1], width)
-    )
     grad_context = dot(grad_mixed_low, output_turned, BY_ROWS).astype(LOW).reshape(shape)
+    grad_context, inner_grad, output_grad, outer_share = lax.optimization_barrier(
+        (grad_context, inner_grad, output_grad, outer_share)
+    )
+    inner_share = scatter_long(fsdp, inner_grad)
+    outer_share = blocks_of(outer_share, (outer_turned.shape[1],))
+    outer_share = scatter_tp_first(tp, outer_share)
     query_rows_grad, key_rows_grad, value_rows_grad = (
         array.reshape(count * length, width)
         for array in attend_back(queries, keys_all, values, grad_context, logsum, ids)
     )
+    query_rows_grad, layer_out, outer_share, inner_share = lax.optimization_barrier(
+        (query_rows_grad, layer_out, outer_share, inner_share)
+    )
+    layer_out = own_places(layer_out)
+    outer_share = scatter_tp_last(tp, outer_share)
+    (inner_share,) = own_share(inner_share, (inner_full.shape[1],))
     query_bias_grad = jnp.sum(query_rows_grad.astype(WIDE), axis=0)
     value_bias_grad = jnp.sum(value_rows_grad.astype(WIDE), axis=0)
     tokens_grad = (
@@ -363,14 +402,15 @@
         + dot(key_rows_grad, key_full, BY_LAST)
         + dot(value_rows_grad, value_full, BY_LAST)
     )
-    tokens_grad = own_places(tokens_grad.astype(LOW)).astype(WIDE)
+    tokens_grad = to_owners(tokens_grad.astype(LOW))
     head_grads = [
         dot(rows, grad, BY_FIRST).astype(LOW)
         for grad in (query_rows_grad, key_rows_grad, value_rows_grad)
     ]
-    query_share, key_share, value_share = own_share(
-        jnp.concatenate(head_grads, axis=1), (width, width, width)
-    )
+    heads_share = scatter_rows(fsdp, jnp.concatenate(head_grads + [output_grad], axis=1))
+    heads_share, tokens_grad = lax.optimization_barrier((heads_share, tokens_grad))
+    query_share, key_share, value_share, output_share = own_share(heads_share, (width,) * 4)
+    tokens_grad = own_places(tokens_grad).astype(WIDE)
     totals = total_over_all(
         fsdp,
         tp,

time: 614 us -> 512 us (0.83)
  waiting for transfers between devices: 236 us -> 170 us
  local copies, waits for them, and re-layouts: 71.6 us -> 49.2 us
  starting transfers between devices: 73.1 us -> 56.5 us
    ppermute x6, waiting for transfers between devices: 66.4 us -> 0.02 us  [dealt(): parts.append(lax.ppermute(block, axis, pairs) if step else block)]
    ppermute x33 -> x32, waiting for transfers between devices: 146 us -> 170 us  [flip(): return lax.ppermute(block, axis, [(i, i ^ bit) for i in range(members)])]
    transpose x5 -> x1, local copies, waits for them, and re-layouts: 24.3 us -> 0.07 us  [columns(): return blocks.transpose(1, 0, 2).reshape(rows, members * cols)]
    ppermute x6, waiting for transfers between devices: 23.9 us -> 0.02 us  [sent_back(): moved.append(lax.ppermute(parts[step], axis, pairs))]
    ppermute x33 -> x32, starting transfers between devices: 48.3 us -> 37 us  [flip(): return lax.ppermute(block, axis, [(i, i ^ bit) for i in range(members)])]
    ppermute x6, starting transfers between devices: 19.6 us -> 10.1 us  [dealt(): parts.append(lax.ppermute(block, axis, pairs) if step else block)]
    unnamed x110 -> x136, local copies, waits for them, and re-layouts: 14.3 us -> 19.8 us
  transfers between devices with their start and end apart: 46 -> 47, of which waited for: 27 -> 20; matrix products, arithmetic and copies ran while one was open for 14% -> 28% of each run, Pallas kernels for 5% -> 15%
where the time goes in v3:
time: 512 us; the launch traced here: 502 us
  waiting for transfers between devices  170 us (33%)
  matrix products  92.1 us (18%)
  Pallas kernels  74.3 us (15%)
  starting transfers between devices  56.5 us (11%)
  local copies, waits for them, and re-layouts  49.2 us (10%)
  other arithmetic  44.4 us (9%)
  between operations  15.4 us (3%)
    ppermute x32, waiting for transfers between devices, flip(): return lax.ppermute(block, axis, [(i, i ^ bit) for i in range(members)])  170 us
    dot_general x18, matrix products, dot(): return lax.dot_general(left, right, dims, preferred_element_type=WIDE)  92.1 us
    pallas_call x1, Pallas kernels, attend_back(): pl.pallas_call(functools.partial(attend_back_kernel, scaling=scaling), gr...  44.4 us
    ppermute x32, starting transfers between devices, flip(): return lax.ppermute(block, axis, [(i, i ^ bit) for i in range(members)])  37 us
    pallas_call x1, Pallas kernels, attend(): pl.pallas_call(functools.partial(attend_kernel, scaling=scaling), grid=(c...  29.9 us
    unnamed x136, local copies, waits for them, and re-layouts  19.8 us
  transfers between devices with their start and end apart: 47, of which 20 were waited for; matrix products, arithmetic and copies ran while one was open for 28% of the time, Pallas kernels for 15%

profile of v3, /device:TPU:0, one launch (start us, length us, event | category | flops | bytes accessed | tf_op | source)
XLA Modules:
  0.0 502.2 jit_solution(11987247514143578308)
XLA Ops:
  9.1 3.1 collective-permute-start.10
  12.2 4.9 collective-permute-done.10
  17.7 2.8 collective-permute-start.11
  21.7 15.7 %collective-permute-done.11 = bf16[2,96,960]{2,0,1:T(2,128)(2,1)S(1)} collective-permute-done((bf16[2,96,960]{2,0,1:T(2,128)(2,1)S(1)}, bf16[2,96,960]{2,0,1:T(2,128)(2,1)S(1)}, u32[]{:S(2)}, u32[]{:S(2)}) %collective-permute-start.11) | collective-permute-done | bytes 368672 | tf_op jit(solution)/shard_map/ppermute | solution.py:162
  43.9 2.0 collective-permute-start.7
  45.9 2.8 collective-permute-start.8
  50.5 24.7 %collective-permute-done.12 = bf16[96,768]{1,0:T(8,128)(2,1)S(1)} collective-permute-done((bf16[96,768]{1,0:T(8,128)(2,1)S(1)}, bf16[96,768]{1,0:T(8,128)(2,1)S(1)}, u32[]{:S(2)}, u32[]{:S(2)}) %collective-permute-start.12) | collective-permute-done | bytes 147488 | tf_op jit(solution)/shard_map/ppermute | solution.py:162
  75.6 2.6 collective-permute-start.13
  78.8 20.1 %collective-permute-done.1 = bf16[2,98,576]{2,0,1:T(2,128)(2,1)S(1)} collective-permute-done((bf16[2,98,576]{2,0,1:T(2,128)(2,1)S(1)}, bf16[2,98,576]{2,0,1:T(2,128)(2,1)S(1)}, u32[]{:S(2)}, u32[]{:S(2)}) %collective-permute-start.1) | collective-permute-done | bytes 225824 | tf_op jit(solution)/shard_map/ppermute | solution.py:162
  105.4 2.5 maximum_bitcast_fusion
  114.8 11.1 %collective-permute-done.3 = bf16[2,96,1152]{2,1,0:T(8,128)(2,1)S(1)} collective-permute-done((bf16[2,96,1152]{2,1,0:T(8,128)(2,1)S(1)}, bf16[2,96,1152]{2,1,0:T(8,128)(2,1)S(1)}, u32[]{:S(2)}, u32[]{:S(2)}) %collective-permute-start.3) | collective-permute-done | bytes 442400 | tf_op jit(solution)/shard_map/ppermute | solution.py:162
  126.0 3.5 collective-permute-done.5
  131.1 2.2 collective-permute-start.15
  133.2 1.6 collective-permute-start.16
  140.5 2.1 bitcast_select_fusion
  142.5 2.6 fusion.44.k_ref
  145.1 2.5 fusion.47.v_ref
  147.7 2.5 fusion.46.q_ref
  150.2 29.9 %attend.1 = (bf16[1,1024,768]{2,1,0:T(8,128)(2,1)}, f32[1,6,2,1024]{3,2,1,0:T(2,128)}) custom-call(bf16[1,1024,768]{2,1,0:T(8,128)(2,1)} %fusion.46.q_ref, bf16[1,1024,768]{2,1,0:T(8,128)(2,1)} %fusion.44.k_ref, bf16[1,1024,768]{2,1,0:T(8,128)(2,1)} %fusion.47.v_ref, s32[1,1,1024]{2,1,0:T(1,128)} %broadcast_in_dim_reshape.4.row_ref, ...), custom_call_target="tpu_custom_call" | custom-call | flops 22548578304 | bytes 6291456 | tf_op jit(solution)/shard_map/attend/pallas_call | solution.py:96
  180.0 3.9 fusion.82
  184.7 9.9 %multiply_convert_fusion = (bf16[1024,3072]{1,0:T(8,128)(2,1)}, f32[1024,3072]{1,0:T(8,128)}) fusion(f32[3072]{0:T(1024)S(1)} %copy-done.36, bf16[768,3840]{1,0:T(8,128)(2,1)S(1)} %bitcast.264, f32[1024,768]{1,0:T(8,128)S(1)} %get-tuple-element.189, f32[768]{0:T(1024)S(1)} %copy-done.38, f32[768]{0:T(1024)S(1)} %convert_element_type.299, ...), kind=kOutput, calls=%fused_computation.8 | convolution fusion | flops 4854644736 | bytes 26767360 | tf_op jit(solution)/shard_map/dot_general | solution.py:22
  194.6 8.9 %fusion.83 = (f32[1024]{0:T(1024)S(1)}, f32[1024,768]{1,0:T(8,128)S(1)}) fusion(f32[768]{0:T(1024)} %convert_element_type.303, bf16[1024,3072]{1,0:T(8,128)(2,1)} %get-tuple-element.190, bf16[768,3072]{1,0:T(8,128)(2,1)} %all-gather.5.cloned.1.call-done, f32[768]{0:T(1024)} %convert_element_type.300, f32[768]{0:T(1024)S(1)} %convert_element_type.299, ...), kind=kOutput, calls=%fused_computation.209 | convolution fusion | flops 4837342208 | bytes 17323008 | tf_op jit(solution)/shard_map/dot_general | solution.py:22
  204.2 5.8 %fusion.20 = (f32[768]{0:T(1024)}, f32[1024]{0:T(1024)S(1)}, f32[1024]{0:T(1024)S(1)}, bf16[1024,768]{1,0:T(8,128)(2,1)}) fusion(f32[1024,768]{1,0:T(8,128)S(1)} %get-tuple-element.193, f32[1024]{0:T(1024)S(1)} %add_rsqrt_fusion, f32[1024]{0:T(1024)S(1)} %broadcast_multiply_fusion.4, bf16[1,256,768]{2,1,0:T(8,128)(2,1)} %collective-permute-done.16, ...), kind=kLoop, calls=%fused_computation.32 | loop fusion | flops 14939392 | bytes 6317056 | tf_op jit(solution)/shard_map/reduce_sum | solution.py:248
  210.1 3.2 fusion.72
  213.3 5.5 %convolution_convert_fusion = bf16[768,3072]{1,0:T(8,128)(2,1)S(1)} fusion(bf16[1024,3072]{1,0:T(8,128)(2,1)S(1)} %bitcast.272, f32[1024,768]{1,0:T(8,128)S(1)} %get-tuple-element.139), kind=kOutput, calls=%fused_computation.10 | convolution fusion | flops 4834983936 | bytes 14155776 | tf_op jit(solution)/shard_map/dot_general | solution.py:22
  218.8 2.1 copy-done.6
  222.5 14.3 %convert_reduce_fusion = (f32[3072]{0:T(1024)}, bf16[1024,3072]{1,0:T(8,128)(2,1)}) fusion(f32[1024,3072]{1,0:T(8,128)} %get-tuple-element.191, f32[3072]{0:T(1024)S(1)} %copy-done.37, bf16[768,3072]{1,0:T(8,128)(2,1)S(1)} %bitcast.268, f32[1024,768]{1,0:T(8,128)S(1)} %get-tuple-element.139), kind=kOutput, calls=%fused_computation.7 | convolution fusion | flops 4873516032 | bytes 26763264 | tf_op jit(solution)/shard_map/dot_general | solution.py:22
  236.8 8.7 %multiply_reduce_fusion = (f32[768]{0:T(1024)}, f32[1024]{0:T(1024)S(1)}, f32[1024]{0:T(1024)S(1)}, f32[768]{0:T(1024)}, f32[1024,768]{1,0:T(8,128)S(1)}) fusion(f32[1024,768]{1,0:T(8,128)S(1)} %get-tuple-element.189, f32[1024]{0:T(1024)S(1)} %copy-done.32, f32[1024]{0:T(1024)S(1)} %broadcast_multiply_fusion.5, f32[768]{0:T(1024)S(1)} %convert_element_type.299, ...), kind=kOutput, calls=%fused_computation.35 | convolution fusion | flops 4839698432 | bytes 20473856 | tf_op jit(solution)/shard_map/dot_general | solution.py:22
  246.6 1.7 copy-done
  248.3 2.5 fusion.35
  250.8 8.2 %convolution_convert_fusion.1 = bf16[768,3072]{1,0:T(8,128)(2,1)} fusion(bf16[1024,3072]{1,0:T(8,128)(2,1)S(1)} %bitcast.270, f32[1024,768]{1,0:T(8,128)S(1)} %get-tuple-element.189, f32[768]{0:T(1024)S(1)} %copy-done.39, f32[768]{0:T(1024)S(1)} %convert_element_type.299, f32[1024]{0:T(1024)S(1)} %copy-done.32, f32[1024]{0:T(1024)S(1)} %broadcast_multiply_fusion.5), kind=kOutput, calls=%fused_computation.11 | convolution fusion | flops 4838129664 | bytes 14170112 | tf_op jit(solution)/shard_map/dot_general | solution.py:22
  259.0 3.3 fusion.7
  262.6 1.6 collective-permute-start.18
  264.2 3.8 fusion.45.g_ref
  268.7 9.3 %collective-permute-done.18 = bf16[2,96,1536]{2,1,0:T(8,128)(2,1)S(1)} collective-permute-done((bf16[2,96,1536]{2,1,0:T(8,128)(2,1)S(1)}, bf16[2,96,1536]{2,1,0:T(8,128)(2,1)S(1)}, u32[]{:S(2)}, u32[]{:S(2)}) %collective-permute-start.18) | collective-permute-done | bytes 589856 | tf_op jit(solution)/shard_map/ppermute | solution.py:162
  278.9 5.5 %collective-permute-done.20 = bf16[2,96,1536]{2,1,0:T(8,128)(2,1)S(1)} collective-permute-done((bf16[2,96,1536]{2,1,0:T(8,128)(2,1)S(1)}, bf16[2,96,1536]{2,1,0:T(8,128)(2,1)S(1)}, u32[]{:S(2)}, u32[]{:S(2)}) %collective-permute-start.20) | collective-permute-done | bytes 589856 | tf_op jit(solution)/shard_map/ppermute | solution.py:162
  284.5 1.6 collective-permute-start.21
  286.1 3.7 collective-permute-done.19
  289.8 2.0 collective-permute-done.21
  294.5 2.6 slice_bitcast_fusion.4
  299.2 1.9 collective-permute-start.24
  310.9 44.4 %attend_back.1 = (bf16[1,1024,768]{2,1,0:T(8,128)(2,1)}, bf16[1,1024,768]{2,1,0:T(8,128)(2,1)}, bf16[1,1024,768]{2,1,0:T(8,128)(2,1)}) custom-call(bf16[1,1024,768]{2,1,0:T(8,128)(2,1)} %fusion.46.q_ref, bf16[1,1024,768]{2,1,0:T(8,128)(2,1)} %fusion.44.k_ref, bf16[1,1024,768]{2,1,0:T(8,128)(2,1)} %fusion.47.v_ref, bf16[1,1024,768]{2,1,0:T(8,128)(2,1)} %fusion.45.g_ref, ...), custom_call_target="tpu_custom_call" | custom-call | flops 38654705664 | bytes 11010048 | tf_op jit(solution)/shard_map/attend_back/pallas_call | solution.py:118
  355.3 4.5 fusion.38
  359.9 2.5 fusion.41
  362.4 4.4 fusion.28
  368.2 1.7 convert_reduce_fusion.3
  369.9 4.4 convolution_convert_fusion.4
  376.6 2.5 convert_element_type.376
  380.8 3.3 pad_maximum_fusion
  387.7 1.6 add_convert_fusion
  390.1 2.5 collective-permute-start.31
  397.4 2.0 collective-permute-start.39
  401.7 2.0 collective-permute-start.32
  404.7 1.7 fusion.68
  406.4 16.2 %collective-permute-done.40 = f32[9216]{0:T(1024)S(1)} collective-permute-done((f32[9216]{0:T(1024)S(1)}, f32[9216]{0:T(1024)S(1)}, u32[]{:S(2)}, u32[]{:S(2)}) %collective-permute-start.40) | collective-permute-done | bytes 36896 | tf_op jit(solution)/shard_map/ppermute | solution.py:162
  427.0 12.8 %collective-permute-done.27 = bf16[2,96,1536]{2,1,0:T(8,128)(2,1)S(1)} collective-permute-done((bf16[2,96,1536]{2,1,0:T(8,128)(2,1)S(1)}, bf16[2,96,1536]{2,1,0:T(8,128)(2,1)S(1)}, u32[]{:S(2)}, u32[]{:S(2)}) %collective-permute-start.27) | collective-permute-done | bytes 589856 | tf_op jit(solution)/shard_map/ppermute | solution.py:162
  441.6 12.1 %collective-permute-done.29 = bf16[2,96,1536]{2,1,0:T(8,128)(2,1)S(1)} collective-permute-done((bf16[2,96,1536]{2,1,0:T(8,128)(2,1)S(1)}, bf16[2,96,1536]{2,1,0:T(8,128)(2,1)S(1)}, u32[]{:S(2)}, u32[]{:S(2)}) %collective-permute-start.29) | collective-permute-done | bytes 589856 | tf_op jit(solution)/shard_map/ppermute | solution.py:162
  453.7 1.7 collective-permute-start.28
  455.6 4.9 collective-permute-done.28
  462.1 5.2 %collective-permute-done.30 = bf16[96,1536]{1,0:T(8,128)(2,1)S(1)} collective-permute-done((bf16[96,1536]{1,0:T(8,128)(2,1)S(1)}, bf16[96,1536]{1,0:T(8,128)(2,1)S(1)}, u32[]{:S(2)}, u32[]{:S(2)}) %collective-permute-start.30) | collective-permute-done | bytes 294944 | tf_op jit(solution)/shard_map/ppermute | solution.py:162
  469.4 3.7 collective-permute-start.34
  474.0 12.1 %collective-permute-done.34 = bf16[2,96,768]{1,2,0:T(8,128)(2,1)S(1)} collective-permute-done((bf16[2,96,768]{1,2,0:T(8,128)(2,1)S(1)}, bf16[2,96,768]{1,2,0:T(8,128)(2,1)S(1)}, u32[]{:S(2)}, u32[]{:S(2)}) %collective-permute-start.34) | collective-permute-done | bytes 294944 | tf_op jit(solution)/shard_map/ppermute | solution.py:162
  487.5 2.1 convert_element_type.364
  489.6 3.0 collective-permute-done.35
  (345 shorter events, 86.4 us)
Async XLA Ops:
  7.2 172.8 %all-gather.3.cloned.1.call-start = ((), (), s32[]{:S(2)}) async-start(), calls=%async_computation.1 | async-start | bytes 6635520 | tf_op jit(solution)/shard_map/all_gather | solution.py:329
  9.1 8.0 %collective-permute-start.10 = (bf16[96,960]{1,0:T(8,128)(2,1)S(1)}, bf16[96,960]{1,0:T(8,128)(2,1)S(1)}, u32[]{:S(2)}, u32[]{:S(2)}) collective-permute-start(bf16[96,960]{1,0:T(8,128)(2,1)S(1)} %pad_maximum_fusion.7), channel_id=1, source_target_pairs={{0,1},{1,0},{2,3},{3,2},{4,5},{5,4},{6,7},{7,6},{8,9},{9,8},{10,11... | collective-permute-start | bytes 552968 | tf_op jit(solution)/shard_map/ppermute | solution.py:162
  17.7 19.7 %collective-permute-start.11 = (bf16[2,96,960]{2,0,1:T(2,128)(2,1)S(1)}, bf16[2,96,960]{2,0,1:T(2,128)(2,1)S(1)}, u32[]{:S(2)}, u32[]{:S(2)}) collective-permute-start(bf16[2,96,960]{2,0,1:T(2,128)(2,1)S(1)} %broadcast_select_fusion.3), channel_id=1, source_target_pairs={{0,2},{1,3},{2,0},{3,1},{4,6},{5,7},{6,4},{7,5},{8,10},{9,11},{10,... | collective-permute-start | bytes 1105928 | tf_op jit(solution)/shard_map/ppermute | solution.py:162
  39.3 9.5 %copy-start.26 = (bf16[768,96]{0,1:T(8,128)(2,1)S(1)}, bf16[768,96]{0,1:T(8,128)(2,1)}, u32[]{:S(2)}) copy-start(bf16[768,96]{0,1:T(8,128)(2,1)} %param.33) | copy-start | bytes 442372
  40.4 154.1 %all-gather.5.cloned.1.call-start = ((), (), s32[]{:S(2)}) async-start(), calls=%async_computation.2 | async-start | bytes 5308416 | tf_op jit(solution)/shard_map/all_gather | solution.py:332
  40.8 8.0 %collective-permute-start = (bf16[98,576]{1,0:T(8,128)(2,1)S(1)}, bf16[98,576]{1,0:T(8,128)(2,1)S(1)}, u32[]{:S(2)}, u32[]{:S(2)}) collective-permute-start(bf16[98,576]{1,0:T(8,128)(2,1)S(1)} %pad_maximum_fusion.8), channel_id=1, source_target_pairs={{0,1},{1,0},{2,3},{3,2},{4,5},{5,4},{6,7},{7,6},{8,9},{9,8},{10,11... | collective-permute-start | bytes 338696 | tf_op jit(solution)/shard_map/ppermute | solution.py:162
  42.5 61.4 %collective-permute-start.6 = (bf16[1,256,768]{2,1,0:T(8,128)(2,1)}, bf16[1,256,768]{2,1,0:T(8,128)(2,1)}, u32[]{:S(2)}, u32[]{:S(2)}) collective-permute-start(bf16[1,256,768]{2,1,0:T(8,128)(2,1)} %get-tuple-element.160), channel_id=1, source_target_pairs={{0,1},{1,2},{2,3},{3,0},{4,5},{5,6},{6,7},{7,4},{8,9},{9,10},{10,1... | collective-permute-start | bytes 1179656 | tf_op jit(solution)/shard_map/ppermute | solution.py:139
  43.9 61.5 %collective-permute-start.7 = (bf16[1,256,768]{2,1,0:T(8,128)(2,1)}, bf16[1,256,768]{2,1,0:T(8,128)(2,1)}, u32[]{:S(2)}, u32[]{:S(2)}) collective-permute-start(bf16[1,256,768]{2,1,0:T(8,128)(2,1)} %get-tuple-element.162), channel_id=1, source_target_pairs={{0,2},{1,3},{2,0},{3,1},{4,6},{5,7},{6,4},{7,5},{8,10},{9,11},{10,... | collective-permute-start | bytes 1179656 | tf_op jit(solution)/shard_map/ppermute | solution.py:139
  45.9 59.5 %collective-permute-start.8 = (bf16[1,256,768]{2,1,0:T(8,128)(2,1)}, bf16[1,256,768]{2,1,0:T(8,128)(2,1)}, u32[]{:S(2)}, u32[]{:S(2)}) collective-permute-start(bf16[1,256,768]{2,1,0:T(8,128)(2,1)} %get-tuple-element.161), channel_id=1, source_target_pairs={{0,3},{1,0},{2,1},{3,2},{4,7},{5,4},{6,5},{7,6},{8,11},{9,8},{10,9... | collective-permute-start | bytes 1179656 | tf_op jit(solution)/shard_map/ppermute | solution.py:139
  48.8 26.4 %collective-permute-start.12 = (bf16[96,768]{1,0:T(8,128)(2,1)S(1)}, bf16[96,768]{1,0:T(8,128)(2,1)S(1)}, u32[]{:S(2)}, u32[]{:S(2)}) collective-permute-start(bf16[96,768]{1,0:T(8,128)(2,1)S(1)} %bitcast.261), channel_id=1, source_target_pairs={{0,1},{1,0},{2,3},{3,2},{4,5},{5,4},{6,7},{7,6},{8,9},{9,8},{10,11... | collective-permute-start | bytes 442376 | tf_op jit(solution)/shard_map/ppermute | solution.py:162
  49.2 49.6 %collective-permute-start.1 = (bf16[2,98,576]{2,0,1:T(2,128)(2,1)S(1)}, bf16[2,98,576]{2,0,1:T(2,128)(2,1)S(1)}, u32[]{:S(2)}, u32[]{:S(2)}) collective-permute-start(bf16[2,98,576]{2,0,1:T(2,128)(2,1)S(1)} %broadcast_select_fusion.7), channel_id=1, source_target_pairs={{0,2},{1,3},{2,0},{3,1},{4,6},{5,7},{6,4},{7,5},{8,10},{9,11},{10,... | collective-permute-start | bytes 677384 | tf_op jit(solution)/shard_map/ppermute | solution.py:162
  75.6 32.3 %collective-permute-start.13 = (bf16[2,96,768]{2,0,1:T(2,128)(2,1)S(1)}, bf16[2,96,768]{2,0,1:T(2,128)(2,1)}, u32[]{:S(2)}, u32[]{:S(2)}) collective-permute-start(bf16[2,96,768]{2,0,1:T(2,128)(2,1)S(1)} %broadcast_select_fusion.5), channel_id=1, source_target_pairs={{0,2},{1,3},{2,0},{3,1},{4,6},{5,7},{6,4},{7,5},{8,10},{9,11},{10,... | collective-permute-start | bytes 884744 | tf_op jit(solution)/shard_map/ppermute | solution.py:162
  102.5 8.8 %collective-permute-start.2 = (bf16[96,1152]{1,0:T(8,128)(2,1)}, bf16[96,1152]{1,0:T(8,128)(2,1)}, u32[]{:S(2)}, u32[]{:S(2)}) collective-permute-start(bf16[96,1152]{1,0:T(8,128)(2,1)} %get-tuple-element.167), channel_id=1, source_target_pairs={{0,8},{4,12},{8,0},{12,4},{16,24},{20,28},{24,16},{28,20},{1,9},{5... | collective-permute-start | bytes 663560 | tf_op jit(solution)/shard_map/ppermute | solution.py:162
  103.9 9.1 %collective-permute-start.4 = (bf16[96,1152]{1,0:T(8,128)(2,1)S(1)}, bf16[96,1152]{1,0:T(8,128)(2,1)}, u32[]{:S(2)}, u32[]{:S(2)}) collective-permute-start(bf16[96,1152]{1,0:T(8,128)(2,1)S(1)} %get-tuple-element.168), channel_id=1, source_target_pairs={{0,16},{4,20},{8,24},{12,28},{16,0},{20,4},{24,8},{28,12},{1,17},{... | collective-permute-start | bytes 663560 | tf_op jit(solution)/shard_map/ppermute | solution.py:162
  110.8 257.4 %reduce-scatter.2.cloned.1.call-start = ((), (), s32[]{:S(2)}) async-start(), calls=%async_computation.3 | async-start | bytes 5308416 | tf_op jit(solution)/shard_map/reduce_scatter | solution.py:215
  112.4 13.4 %collective-permute-start.3 = (bf16[2,96,1152]{2,1,0:T(8,128)(2,1)S(1)}, bf16[2,96,1152]{2,1,0:T(8,128)(2,1)S(1)}, u32[]{:S(2)}, u32[]{:S(2)}) collective-permute-start(bf16[2,96,1152]{2,1,0:T(8,128)(2,1)S(1)} %broadcast_select_fusion.9), channel_id=1, source_target_pairs={{0,16},{4,20},{8,24},{12,28},{16,0},{20,4},{24,8},{28,12},{1,17},{... | collective-permute-start | bytes 1327112 | tf_op jit(solution)/shard_map/ppermute | solution.py:162
  114.1 15.9 %copy-start.15 = (bf16[4,256,768]{2,1,0:T(8,128)(2,1)S(1)}, bf16[4,256,768]{2,1,0:T(8,128)(2,1)}, u32[]{:S(2)}) copy-start(bf16[4,256,768]{2,1,0:T(8,128)(2,1)} %param.37) | copy-start | bytes 4718596
  114.1 15.4 %collective-permute-start.5 = (bf16[2,96,1152]{2,1,0:T(8,128)(2,1)S(1)}, bf16[2,96,1152]{2,1,0:T(8,128)(2,1)S(1)}, u32[]{:S(2)}, u32[]{:S(2)}) collective-permute-start(bf16[2,96,1152]{2,1,0:T(8,128)(2,1)S(1)} %broadcast_select_fusion.8), channel_id=1, source_target_pairs={{0,8},{4,12},{8,0},{12,4},{16,24},{20,28},{24,16},{28,20},{1,9},{5... | collective-permute-start | bytes 1327112 | tf_op jit(solution)/shard_map/ppermute | solution.py:162
  129.7 9.2 %copy-start.45 = (bf16[768]{0:T(1024)(128)(2,1)S(1)}, bf16[768]{0:T(1024)(128)(2,1)}, u32[]{:S(2)}) copy-start(bf16[768]{0:T(1024)(128)(2,1)} %param.35) | copy-start | bytes 4612
  129.7 9.2 %copy-start.46 = (bf16[768]{0:T(1024)(128)(2,1)S(1)}, bf16[768]{0:T(1024)(128)(2,1)}, u32[]{:S(2)}) copy-start(bf16[768]{0:T(1024)(128)(2,1)} %param.36) | copy-start | bytes 4612
  129.9 10.6 %collective-permute-start.9 = (bf16[2,2,96,2304]{3,2,1,0:T(8,128)(2,1)S(1)}, bf16[2,2,96,2304]{3,2,1,0:T(8,128)(2,1)}, u32[]{:S(2)}, u32[]{:S(2)}) collective-permute-start(bf16[2,2,96,2304]{3,2,1,0:T(8,128)(2,1)S(1)} %pad_maximum_fusion.1), channel_id=1, source_target_pairs={{0,4},{4,0},{8,12},{12,8},{16,20},{20,16},{24,28},{28,24},{1,5},{5... | collective-permute-start | bytes 5308424 | tf_op jit(solution)/shard_map/ppermute | solution.py:162
  131.1 73.1 %collective-permute-start.14 = (bf16[1,256,768]{2,1,0:T(8,128)(2,1)}, bf16[1,256,768]{2,1,0:T(8,128)(2,1)}, u32[]{:S(2)}, u32[]{:S(2)}) collective-permute-start(bf16[1,256,768]{2,1,0:T(8,128)(2,1)} %get-tuple-element.156), channel_id=1, source_target_pairs={{0,1},{1,2},{2,3},{3,0},{4,5},{5,6},{6,7},{7,4},{8,9},{9,10},{10,1... | collective-permute-start | bytes 1179656 | tf_op jit(solution)/shard_map/ppermute | solution.py:139
  131.1 73.1 %collective-permute-start.15 = (bf16[1,256,768]{2,1,0:T(8,128)(2,1)}, bf16[1,256,768]{2,1,0:T(8,128)(2,1)}, u32[]{:S(2)}, u32[]{:S(2)}) collective-permute-start(bf16[1,256,768]{2,1,0:T(8,128)(2,1)} %get-tuple-element.158), channel_id=1, source_target_pairs={{0,2},{1,3},{2,0},{3,1},{4,6},{5,7},{6,4},{7,5},{8,10},{9,11},{10,... | collective-permute-start | bytes 1179656 | tf_op jit(solution)/shard_map/ppermute | solution.py:139
  133.2 70.9 %collective-permute-start.16 = (bf16[1,256,768]{2,1,0:T(8,128)(2,1)}, bf16[1,256,768]{2,1,0:T(8,128)(2,1)}, u32[]{:S(2)}, u32[]{:S(2)}) collective-permute-start(bf16[1,256,768]{2,1,0:T(8,128)(2,1)} %get-tuple-element.157), channel_id=1, source_target_pairs={{0,3},{1,0},{2,1},{3,2},{4,7},{5,4},{6,5},{7,6},{8,11},{9,8},{10,9... | collective-permute-start | bytes 1179656 | tf_op jit(solution)/shard_map/ppermute | solution.py:139
  184.7 9.9 %copy-start.31 = (f32[1024]{0:T(1024)}, f32[1024]{0:T(1024)S(1)}, u32[]{:S(2)}) copy-start(f32[1024]{0:T(1024)S(1)} %add_rsqrt_fusion.1) | copy-start | bytes 12292
  203.6 9.7 %slice-start.8 = ((s8[6291456]{0:T(1024)(128)(4,1)}), s8[4194304]{0:T(1024)(128)(4,1)S(1)}, s32[]{:S(2)}) async-start(s8[6291456]{0:T(1024)(128)(4,1)} %bitcast.271), calls=%async_computation.12 | async-start | bytes 8388608
  204.2 9.0 %slice-start.9 = ((s8[6291456]{0:T(1024)(128)(4,1)}), s8[2097152]{0:T(1024)(128)(4,1)S(1)}, s32[]{:S(2)}) async-start(s8[6291456]{0:T(1024)(128)(4,1)} %bitcast.271), calls=%async_computation.13 | async-start | bytes 4194304
  210.1 12.4 %slice-start.4 = ((s8[4718592]{0:T(1024)(128)(4,1)}), s8[4194304]{0:T(1024)(128)(4,1)S(1)}, s32[]{:S(2)}) async-start(s8[4718592]{0:T(1024)(128)(4,1)} %bitcast.267), calls=%async_computation.8 | async-start | bytes 8388608
  213.3 9.2 %slice-start.5 = ((s8[4718592]{0:T(1024)(128)(4,1)}), s8[524288]{0:T(1024)(128)(4,1)S(1)}, s32[]{:S(2)}) async-start(s8[4718592]{0:T(1024)(128)(4,1)} %bitcast.267), calls=%async_computation.9 | async-start | bytes 1048576
  220.9 15.9 %slice-start.2 = ((s8[5898240]{0:T(1024)(128)(4,1)}), s8[4194304]{0:T(1024)(128)(4,1)S(1)}, s32[]{:S(2)}) async-start(s8[5898240]{0:T(1024)(128)(4,1)} %bitcast.265), calls=%async_computation.6 | async-start | bytes 8388608
  222.5 36.5 %collective-permute-start.17 = (bf16[2,2,96,3072]{3,2,1,0:T(8,128)(2,1)}, bf16[2,2,96,3072]{3,2,1,0:T(8,128)(2,1)}, u32[]{:S(2)}, u32[]{:S(2)}) collective-permute-start(bf16[2,2,96,3072]{3,2,1,0:T(8,128)(2,1)} %dynamic-slice_bitcast_fusion.1), channel_id=1, source_target_pairs={{0,4},{4,0},{8,12},{12,8},{16,20},{20,16},{24,28},{28,24},{1,5},{5... | collective-permute-start | bytes 7077896 | tf_op jit(solution)/shard_map/ppermute | solution.py:162
  222.5 14.3 %copy-start.32 = (f32[1024]{0:T(1024)S(1)}, f32[1024]{0:T(1024)}, u32[]{:S(2)}) copy-start(f32[1024]{0:T(1024)} %copy-done.31) | copy-start | bytes 12292
  222.5 14.3 %slice-start.3 = ((s8[5898240]{0:T(1024)(128)(4,1)}), s8[1703936]{0:T(1024)(128)(4,1)S(1)}, s32[]{:S(2)}) async-start(s8[5898240]{0:T(1024)(128)(4,1)} %bitcast.265), calls=%async_computation.7 | async-start | bytes 3407872
  262.6 15.4 %collective-permute-start.18 = (bf16[2,96,1536]{2,1,0:T(8,128)(2,1)S(1)}, bf16[2,96,1536]{2,1,0:T(8,128)(2,1)S(1)}, u32[]{:S(2)}, u32[]{:S(2)}) collective-permute-start(bf16[2,96,1536]{2,1,0:T(8,128)(2,1)S(1)} %dynamic-slice_bitcast_fusion.5), channel_id=1, source_target_pairs={{0,16},{4,20},{8,24},{12,28},{16,0},{20,4},{24,8},{28,12},{1,17},{... | collective-permute-start | bytes 1769480 | tf_op jit(solution)/shard_map/ppermute | solution.py:162
  268.0 16.3 %collective-permute-start.20 = (bf16[2,96,1536]{2,1,0:T(8,128)(2,1)S(1)}, bf16[2,96,1536]{2,1,0:T(8,128)(2,1)S(1)}, u32[]{:S(2)}, u32[]{:S(2)}) collective-permute-start(bf16[2,96,1536]{2,1,0:T(8,128)(2,1)S(1)} %dynamic-slice_bitcast_fusion.4), channel_id=1, source_target_pairs={{0,8},{4,12},{8,0},{12,4},{16,24},{20,28},{24,16},{28,20},{1,9},{5... | collective-permute-start | bytes 1769480 | tf_op jit(solution)/shard_map/ppermute | solution.py:162
  278.2 11.6 %collective-permute-start.19 = (bf16[96,1536]{1,0:T(8,128)(2,1)S(1)}, bf16[96,1536]{1,0:T(8,128)(2,1)S(1)}, u32[]{:S(2)}, u32[]{:S(2)}) collective-permute-start(bf16[96,1536]{1,0:T(8,128)(2,1)S(1)} %dynamic-slice_bitcast_fusion.12), channel_id=1, source_target_pairs={{0,8},{4,12},{8,0},{12,4},{16,24},{20,28},{24,16},{28,20},{1,9},{5... | collective-permute-start | bytes 884744 | tf_op jit(solution)/shard_map/ppermute | solution.py:162
  284.5 7.4 %collective-permute-start.21 = (bf16[96,1536]{1,0:T(8,128)(2,1)S(1)}, bf16[96,1536]{1,0:T(8,128)(2,1)S(1)}, u32[]{:S(2)}, u32[]{:S(2)}) collective-permute-start(bf16[96,1536]{1,0:T(8,128)(2,1)S(1)} %dynamic-slice_bitcast_fusion.11), channel_id=1, source_target_pairs={{0,16},{4,20},{8,24},{12,28},{16,0},{20,4},{24,8},{28,12},{1,17},{... | collective-permute-start | bytes 884744 | tf_op jit(solution)/shard_map/ppermute | solution.py:162
  292.8 13.5 %copy-start.33 = (f32[768]{0:T(1024)S(1)}, f32[768]{0:T(1024)}, u32[]{:S(2)}) copy-start(f32[768]{0:T(1024)} %get-tuple-element.133) | copy-start | bytes 9220
  292.9 16.1 %copy-start.8 = (bf16[96,3072]{1,0:T(8,128)(2,1)S(1)}, bf16[96,3072]{1,0:T(8,128)(2,1)}, u32[]{:S(2)}) copy-start(bf16[96,3072]{1,0:T(8,128)(2,1)} %pad_maximum_fusion.3) | copy-start | bytes 1769476
  297.1 71.1 %collective-permute-start.22 = (bf16[1,256,768]{2,1,0:T(8,128)(2,1)}, bf16[1,256,768]{2,1,0:T(8,128)(2,1)}, u32[]{:S(2)}, u32[]{:S(2)}) collective-permute-start(bf16[1,256,768]{2,1,0:T(8,128)(2,1)} %get-tuple-element.153), channel_id=1, source_target_pairs={{0,3},{1,0},{2,1},{3,2},{4,7},{5,4},{6,5},{7,6},{8,11},{9,8},{10,9... | collective-permute-start | bytes 1179656 | tf_op jit(solution)/shard_map/ppermute | solution.py:147
  297.6 70.5 %collective-permute-start.23 = (bf16[1,256,768]{2,1,0:T(8,128)(2,1)}, bf16[1,256,768]{2,1,0:T(8,128)(2,1)}, u32[]{:S(2)}, u32[]{:S(2)}) collective-permute-start(bf16[1,256,768]{2,1,0:T(8,128)(2,1)} %get-tuple-element.152), channel_id=1, source_target_pairs={{0,2},{1,3},{2,0},{3,1},{4,6},{5,7},{6,4},{7,5},{8,10},{9,11},{10,... | collective-permute-start | bytes 1179656 | tf_op jit(solution)/shard_map/ppermute | solution.py:147
  299.2 69.0 %collective-permute-start.24 = (bf16[1,256,768]{2,1,0:T(8,128)(2,1)}, bf16[1,256,768]{2,1,0:T(8,128)(2,1)}, u32[]{:S(2)}, u32[]{:S(2)}) collective-permute-start(bf16[1,256,768]{2,1,0:T(8,128)(2,1)} %get-tuple-element.151), channel_id=1, source_target_pairs={{0,1},{1,2},{2,3},{3,0},{4,5},{5,6},{6,7},{7,4},{8,9},{9,10},{10,1... | collective-permute-start | bytes 1179656 | tf_op jit(solution)/shard_map/ppermute | solution.py:147
  309.9 57.1 %collective-permute-start.25 = (bf16[2,96,768]{2,1,0:T(8,128)(2,1)S(1)}, bf16[2,96,768]{2,1,0:T(8,128)(2,1)}, u32[]{:S(2)}, u32[]{:S(2)}) collective-permute-start(bf16[2,96,768]{2,1,0:T(8,128)(2,1)S(1)} %dynamic-slice_bitcast_fusion.10), channel_id=1, source_target_pairs={{0,2},{1,3},{2,0},{3,1},{4,6},{5,7},{6,4},{7,5},{8,10},{9,11},{10,... | collective-permute-start | bytes 884744 | tf_op jit(solution)/shard_map/ppermute | solution.py:162
  375.0 28.7 %collective-permute-start.43 = (bf16[96,768]{1,0:T(8,128)(2,1)}, bf16[96,768]{1,0:T(8,128)(2,1)}, u32[]{:S(2)}, u32[]{:S(2)}) collective-permute-start(bf16[96,768]{1,0:T(8,128)(2,1)} %dynamic-slice_bitcast_fusion.14), channel_id=1, source_target_pairs={{0,1},{1,0},{2,3},{3,2},{4,5},{5,4},{6,7},{7,6},{8,9},{9,8},{10,11... | collective-permute-start | bytes 442376 | tf_op jit(solution)/shard_map/ppermute | solution.py:162
  380.2 46.5 %collective-permute-start.41 = (bf16[2,96,768]{2,1,0:T(8,128)(2,1)S(1)}, bf16[2,96,768]{2,1,0:T(8,128)(2,1)S(1)}, u32[]{:S(2)}, u32[]{:S(2)}) collective-permute-start(bf16[2,96,768]{2,1,0:T(8,128)(2,1)S(1)} %dynamic-slice_bitcast_fusion.7), channel_id=1, source_target_pairs={{0,2},{1,3},{2,0},{3,1},{4,6},{5,7},{6,4},{7,5},{8,10},{9,11},{10,... | collective-permute-start | bytes 884744 | tf_op jit(solution)/shard_map/ppermute | solution.py:162
  384.3 39.8 %collective-permute-start.26 = (bf16[2,2,96,3072]{3,2,1,0:T(8,128)(2,1)S(1)}, bf16[2,2,96,3072]{3,2,1,0:T(8,128)(2,1)S(1)}, u32[]{:S(2)}, u32[]{:S(2)}) collective-permute-start(bf16[2,2,96,3072]{3,2,1,0:T(8,128)(2,1)S(1)} %dynamic-slice_bitcast_fusion), channel_id=1, source_target_pairs={{0,4},{4,0},{8,12},{12,8},{16,20},{20,16},{24,28},{28,24},{1,5},{5... | collective-permute-start | bytes 7077896 | tf_op jit(solution)/shard_map/ppermute | solution.py:162
  384.9 4.5 collective-permute-start.36
  389.4 4.0 collective-permute-start.37
  389.9 14.8 %copy-start.19 = (bf16[2,96,768]{2,1,0:T(8,128)(2,1)S(1)}, bf16[2,96,768]{2,1,0:T(8,128)(2,1)}, u32[]{:S(2)}) copy-start(bf16[2,96,768]{2,1,0:T(8,128)(2,1)} %copy-done.18) | copy-start | bytes 884740
  390.1 77.4 %collective-permute-start.31 = (bf16[1,256,768]{2,1,0:T(8,128)(2,1)S(1)}, bf16[1,256,768]{2,1,0:T(8,128)(2,1)S(1)}, u32[]{:S(2)}, u32[]{:S(2)}) collective-permute-start(bf16[1,256,768]{2,1,0:T(8,128)(2,1)S(1)} %get-tuple-element.149), channel_id=1, source_target_pairs={{0,3},{1,0},{2,1},{3,2},{4,7},{5,4},{6,5},{7,6},{8,11},{9,8},{10,9... | collective-permute-start | bytes 1179656 | tf_op jit(solution)/shard_map/ppermute | solution.py:147
  393.4 4.0 collective-permute-start.38
  397.4 4.3 collective-permute-start.39
  401.7 65.8 %collective-permute-start.32 = (bf16[1,256,768]{2,1,0:T(8,128)(2,1)S(1)}, bf16[1,256,768]{2,1,0:T(8,128)(2,1)S(1)}, u32[]{:S(2)}, u32[]{:S(2)}) collective-permute-start(bf16[1,256,768]{2,1,0:T(8,128)(2,1)S(1)} %get-tuple-element.148), channel_id=1, source_target_pairs={{0,2},{1,3},{2,0},{3,1},{4,6},{5,7},{6,4},{7,5},{8,10},{9,11},{10,... | collective-permute-start | bytes 1179656 | tf_op jit(solution)/shard_map/ppermute | solution.py:147
  403.8 18.8 %collective-permute-start.40 = (f32[9216]{0:T(1024)S(1)}, f32[9216]{0:T(1024)S(1)}, u32[]{:S(2)}, u32[]{:S(2)}) collective-permute-start(f32[9216]{0:T(1024)S(1)} %add.467), channel_id=1, source_target_pairs={{0,2},{1,3},{2,0},{3,1},{4,6},{5,7},{6,4},{7,5},{8,10},{9,11},{10,... | collective-permute-start | bytes 110600 | tf_op jit(solution)/shard_map/ppermute | solution.py:162
  422.5 44.9 %collective-permute-start.33 = (bf16[1,256,768]{2,1,0:T(8,128)(2,1)S(1)}, bf16[1,256,768]{2,1,0:T(8,128)(2,1)S(1)}, u32[]{:S(2)}, u32[]{:S(2)}) collective-permute-start(bf16[1,256,768]{2,1,0:T(8,128)(2,1)S(1)} %get-tuple-element.147), channel_id=1, source_target_pairs={{0,1},{1,2},{2,3},{3,0},{4,5},{5,6},{6,7},{7,4},{8,9},{9,10},{10,1... | collective-permute-start | bytes 1179656 | tf_op jit(solution)/shard_map/ppermute | solution.py:147
  425.2 14.6 %collective-permute-start.27 = (bf16[2,96,1536]{2,1,0:T(8,128)(2,1)S(1)}, bf16[2,96,1536]{2,1,0:T(8,128)(2,1)S(1)}, u32[]{:S(2)}, u32[]{:S(2)}) collective-permute-start(bf16[2,96,1536]{2,1,0:T(8,128)(2,1)S(1)} %dynamic-slice_bitcast_fusion.3), channel_id=1, source_target_pairs={{0,16},{4,20},{8,24},{12,28},{16,0},{20,4},{24,8},{28,12},{1,17},{... | collective-permute-start | bytes 1769480 | tf_op jit(solution)/shard_map/ppermute | solution.py:162
  426.8 46.3 %collective-permute-start.42 = (bf16[96,768]{1,0:T(8,128)(2,1)S(1)}, bf16[96,768]{1,0:T(8,128)(2,1)S(1)}, u32[]{:S(2)}, u32[]{:S(2)}) collective-permute-start(bf16[96,768]{1,0:T(8,128)(2,1)S(1)} %dynamic-slice_bitcast_fusion.15), channel_id=1, source_target_pairs={{0,1},{1,0},{2,3},{3,2},{4,5},{5,4},{6,7},{7,6},{8,9},{9,8},{10,11... | collective-permute-start | bytes 442376 | tf_op jit(solution)/shard_map/ppermute | solution.py:162
  439.8 13.9 %collective-permute-start.29 = (bf16[2,96,1536]{2,1,0:T(8,128)(2,1)S(1)}, bf16[2,96,1536]{2,1,0:T(8,128)(2,1)S(1)}, u32[]{:S(2)}, u32[]{:S(2)}) collective-permute-start(bf16[2,96,1536]{2,1,0:T(8,128)(2,1)S(1)} %dynamic-slice_bitcast_fusion.2), channel_id=1, source_target_pairs={{0,8},{4,12},{8,0},{12,4},{16,24},{20,28},{24,16},{28,20},{1,9},{5... | collective-permute-start | bytes 1769480 | tf_op jit(solution)/shard_map/ppermute | solution.py:162
  453.7 6.9 %collective-permute-start.28 = (bf16[96,1536]{1,0:T(8,128)(2,1)S(1)}, bf16[96,1536]{1,0:T(8,128)(2,1)S(1)}, u32[]{:S(2)}, u32[]{:S(2)}) collective-permute-start(bf16[96,1536]{1,0:T(8,128)(2,1)S(1)} %dynamic-slice_bitcast_fusion.9), channel_id=1, source_target_pairs={{0,8},{4,12},{8,0},{12,4},{16,24},{20,28},{24,16},{28,20},{1,9},{5... | collective-permute-start | bytes 884744 | tf_op jit(solution)/shard_map/ppermute | solution.py:162
  460.6 6.7 %collective-permute-start.30 = (bf16[96,1536]{1,0:T(8,128)(2,1)S(1)}, bf16[96,1536]{1,0:T(8,128)(2,1)S(1)}, u32[]{:S(2)}, u32[]{:S(2)}) collective-permute-start(bf16[96,1536]{1,0:T(8,128)(2,1)S(1)} %dynamic-slice_bitcast_fusion.8), channel_id=1, source_target_pairs={{0,16},{4,20},{8,24},{12,28},{16,0},{20,4},{24,8},{28,12},{1,17},{... | collective-permute-start | bytes 884744 | tf_op jit(solution)/shard_map/ppermute | solution.py:162
  469.3 17.1 %copy-start.23 = (bf16[1,256,768]{2,1,0:T(8,128)(2,1)S(1)}, bf16[1,256,768]{2,1,0:T(8,128)(2,1)}, u32[]{:S(2)}) copy-start(bf16[1,256,768]{2,1,0:T(8,128)(2,1)} %copy-done.22) | copy-start | bytes 1179652
  469.3 17.1 %copy-start.25 = (bf16[1,256,768]{2,1,0:T(8,128)(2,1)S(1)}, bf16[1,256,768]{2,1,0:T(8,128)(2,1)}, u32[]{:S(2)}) copy-start(bf16[1,256,768]{2,1,0:T(8,128)(2,1)} %copy-done.24) | copy-start | bytes 1179652
  469.4 16.8 %collective-permute-start.34 = (bf16[2,96,768]{1,2,0:T(8,128)(2,1)S(1)}, bf16[2,96,768]{1,2,0:T(8,128)(2,1)S(1)}, u32[]{:S(2)}, u32[]{:S(2)}) collective-permute-start(bf16[2,96,768]{1,2,0:T(8,128)(2,1)S(1)} %dynamic-slice_bitcast_fusion.6), channel_id=1, source_target_pairs={{0,2},{1,3},{2,0},{3,1},{4,6},{5,7},{6,4},{7,5},{8,10},{9,11},{10,... | collective-permute-start | bytes 884744 | tf_op jit(solution)/shard_map/ppermute | solution.py:162
  486.3 6.3 %collective-permute-start.35 = (bf16[96,768]{0,1:T(8,128)(2,1)S(1)}, bf16[96,768]{0,1:T(8,128)(2,1)S(1)}, u32[]{:S(2)}, u32[]{:S(2)}) collective-permute-start(bf16[96,768]{0,1:T(8,128)(2,1)S(1)} %dynamic-slice_bitcast_fusion.13), channel_id=1, source_target_pairs={{0,1},{1,0},{2,3},{3,2},{4,5},{5,4},{6,7},{7,6},{8,9},{9,8},{10,11... | collective-permute-start | bytes 442376 | tf_op jit(solution)/shard_map/ppermute | solution.py:162
  (44 other events, 141.7 us)
Sparse Core Ops, SparseCore 0:
  40.6 44.7 all-gather.2
  110.9 39.6 all-gather.4
  293.0 52.5 reduce-scatter.1

commit v4 on v2

v4 whole, which is shorter than its diff:
```python
import functools

import jax
import jax.numpy as jnp
from jax import lax
from jax.experimental import pallas as pl
from jax.sharding import PartitionSpec as P

HDIM = 64
EPSILON = 1e-12
MASKED = -1000000000.0
PAIR = 2 * HDIM
BLOCK = 256
LOW = jnp.bfloat16
WIDE = jnp.float32
BY_LAST = (((1,), (1,)), ((), ()))
BY_ROWS = (((1,), (0,)), ((), ()))
BY_FIRST = (((0,), (0,)), ((), ()))


def dot(left, right, dims):
    return lax.dot_general(left, right, dims, preferred_element_type=WIDE)


def halves(pair):
    lane = lax.broadcasted_iota(jnp.int32, (1, PAIR), 1)
    zero = jnp.zeros((), pair.dtype)
    return jnp.where(lane < HDIM, pair, zero), jnp.where(lane < HDIM, zero, pair)


def attend_kernel(q_ref, k_ref, v_ref, row_ref, col_ref, context_ref, logsum_ref, *, scaling):
    keys_all = k_ref[0]
    turned = [half.T for half in halves(v_ref[0])]
    key_ids = col_ref[0]
    for start in range(0, q_ref.shape[1], BLOCK):
        part = slice(start, start + BLOCK)
        seen = key_ids == row_ref[0, :, part]
        total = None
        for head, queries in enumerate(halves(q_ref[0, part, :] * scaling)):
            scores = jnp.where(seen, dot(keys_all, queries, BY_LAST), MASKED)
            highest = jnp.max(scores, axis=0, keepdims=True)
            weights = jnp.exp(scores - highest)
            sums = jnp.sum(weights, axis=0, keepdims=True)
            probs = (weights * (1.0 / sums)).astype(LOW)
            logsum_ref[0, 0, head : head + 1, part] = highest + jnp.log(sums)
            piece = dot(turned[head], probs, BY_ROWS)
            total = piece if total is None else total + piece
        context_ref[0, part, :] = total.T.astype(LOW)


def attend_back_kernel(
    q_ref, k_ref, v_ref, g_ref, logsum_ref, row_ref, col_ref, dq_ref, dk_ref, dv_ref, *, scaling
):
    keys_all = k_ref[0]
    values = v_ref[0]
    turned = [half.T for half in halves(keys_all)]
    key_ids = col_ref[0]
    length = q_ref.shape[1]
    key_grad = jnp.zeros((length, PAIR), WIDE)
    value_grad = jnp.zeros((length, PAIR), WIDE)
    for start in range(0, length, BLOCK):
        part = slice(start, start + BLOCK)
        seen = key_ids == row_ref[0, :, part]
        total = None
        queries_of = halves(q_ref[0, part, :] * scaling)
        grads_of = halves(g_ref[0, part, :])
        for head in range(2):
            queries, grads = queries_of[head], grads_of[head]
            scores = jnp.where(seen, dot(keys_all, queries, BY_LAST), MASKED)
            probs = jnp.exp(scores - logsum_ref[0, 0, head : head + 1, part])
            grad_probs = dot(values, grads, BY_LAST)
            value_grad = value_grad + dot(probs.astype(LOW), grads, BY_ROWS)
            level = jnp.sum(probs * grad_probs, axis=0, keepdims=True)
            grad_scores = (probs * (grad_probs - level)).astype(LOW)
            key_grad = key_grad + dot(grad_scores, queries, BY_ROWS)
            piece = dot(turned[head], grad_scores, BY_ROWS)
            total = piece if total is None else total + piece
        dq_ref[0, part, :] = (total.T * HDIM ** (-0.5)).astype(LOW)
    dk_ref[0] = key_grad.astype(LOW)
    dv_ref[0] = value_grad.astype(LOW)


def attention_specs(length, first=0):
    return (
        pl.BlockSpec((1, length, PAIR), lambda s, p: (s, 0, p + first)),
        pl.BlockSpec((1, 1, length), lambda s, p: (s, 0, 0)),
        pl.BlockSpec((1, length, 1), lambda s, p: (s, 0, 0)),
        pl.BlockSpec((1, 1, 2, length), lambda s, p: (s, p + first, 0, 0)),
    )


def attend(queries, keys_all, values, ids):
    count, length, width = queries.shape
    rows, as_row, as_col, sums = attention_specs(length)
    scaling = HDIM ** (-0.5)
    return pl.pallas_call(
        functools.partial(attend_kernel, scaling=scaling),
        grid=(count, width // PAIR),
        in_specs=[rows, rows, rows, as_row, as_col],
        out_specs=[rows, sums],
        out_shape=[
            jax.ShapeDtypeStruct(queries.shape, LOW),
            jax.ShapeDtypeStruct((count, width // PAIR, 2, length), WIDE),
        ],
        cost_estimate=pl.CostEstimate(
            flops=28 * count * width * length * length,
            transcendentals=count * width * length * length // HDIM,
            bytes_accessed=8 * count * width * length,
        ),
        name="attend",
    )(queries, keys_all, values, ids[:, None, :], ids[:, :, None])


def attend_back(queries, keys_all, values, grad_context, logsum, ids, earlier, part):
    count, length, width = queries.shape
    pairs = width // PAIR
    first = pairs // 2 * part
    rows, as_row, as_col, sums = attention_specs(length, first)
    body = functools.partial(attend_back_kernel, scaling=HDIM ** (-0.5))
    operands = [queries, keys_all, values, grad_context, logsum, ids[:, None, :], ids[:, :, None]]
    in_specs = [rows, rows, rows, rows, sums, as_row, as_col]
    aliases = {}
    if earlier is not None:

        def body(*refs):
            attend_back_kernel(*refs[:7], *refs[10:], scaling=HDIM ** (-0.5))

        aliases = {7 + i: i for i in range(3)}
        operands += list(earlier)
        in_specs += [pl.BlockSpec(memory_space=pl.ANY)] * 3
    return pl.pallas_call(
        body,
        grid=(count, (pairs - first) if part else pairs // 2),
        in_specs=in_specs,
        out_specs=[rows, rows, rows],
        out_shape=[jax.ShapeDtypeStruct(queries.shape, LOW)] * 3,
        input_output_aliases=aliases,
        cost_estimate=pl.CostEstimate(
            flops=24 * count * width * length * length,
            transcendentals=count * width * length * length // HDIM // 2,
            bytes_accessed=7 * count * width * length,
        ),
        name="attend_back",
    )(*operands)


def meet(value, parts, picks):
    picked = [step for step in picks if step < len(parts)]
    value, held = lax.optimization_barrier((value, [parts[step] for step in picked]))
    parts = list(parts)
    for step, part in zip(picked, held):
        parts[step] = part
    return value, parts


def spread(block):
    members = lax.axis_size("tp")
    rank_pairs = [[(i, (i + step) % members) for i in range(members)] for step in range(1, members)]
    return [block] + [lax.ppermute(block, "tp", pairs) for pairs in rank_pairs]


def dealt(blocks):
    members, rank = lax.axis_size("tp"), lax.axis_index("tp")
    parts = []
    for step in range(members):
        block = lax.dynamic_slice_in_dim(blocks, (rank + step) % members, 1, 0)[0]
        pairs = [(i, (i + step) % members) for i in range(members)]
        parts.append(lax.ppermute(block, "tp", pairs) if step else block)
    return parts


def sent_back(parts):
    members = lax.axis_size("tp")
    moved = [parts[0]]
    for step in range(1, members):
        pairs = [(i, (i - step) % members) for i in range(members)]
        moved.append(lax.ppermute(parts[step], "tp", pairs))
    return moved


def by_source(moved):
    members, rank = len(moved), lax.axis_index("tp")
    shape = (members,) + moved[0].shape
    above = (lax.broadcasted_iota(jnp.int32, shape, 0) - rank) % members
    result = jnp.broadcast_to(moved[0][None], shape)
    for step in range(1, members):
        result = jnp.where(above == step, moved[step][None], result)
    return result


def flip(axis, members, bit, block):
    return lax.ppermute(block, axis, [(i, i ^ bit) for i in range(members)])


def beside(bit, block, other, place):
    mine = lax.axis_index("fsdp") // bit % 2
    shape = block.shape[:place] + (2,) + block.shape[place:]
    spot = lax.broadcasted_iota(jnp.int32, shape, place)
    return jnp.where(spot == mine, jnp.expand_dims(block, place), jnp.expand_dims(other, place))


def entries(bit, array, place):
    mine = lax.axis_index("fsdp") // bit % 2
    return [
        lax.squeeze(lax.dynamic_slice_in_dim(array, spot, 1, place), (place,)) for spot in (mine, 1 - mine)
    ]


def gather_rows(members, block, before, beyond):
    if members != 8:
        return lax.all_gather(block, "fsdp", axis=0, tiled=True), before, beyond
    rows, cols = block.shape
    first, second = block[:, : cols // 2], block[:, cols // 2 :]
    (over_x, over_y), beyond = meet(
        (flip("fsdp", members, 2, first), flip("fsdp", members, 4, second)), beyond, (2, 3)
    )
    first, second = beside(2, first, over_x, 0), beside(4, second, over_y, 0)
    (over_y, over_x), before = meet(
        (flip("fsdp", members, 4, first), flip("fsdp", members, 2, second)), before, (1, 2)
    )
    both = jnp.concatenate([beside(4, first, over_y, 0), beside(2, second, over_x, 1)], axis=3)
    other, before = meet(flip("fsdp", members, 1, both), before, (3,))
    return beside(1, both, other, 2).reshape(members * rows, cols), before, beyond


def add_low(kept, moved):
    return (kept.astype(WIDE) + moved.astype(WIDE)).astype(LOW)


def scatter_core(grad):
    if lax.axis_size("fsdp") != 8:
        return lax.psum_scatter(grad, "fsdp", scatter_dimension=0, tiled=True)
    total_rows, cols = grad.shape
    kept, theirs = entries(1, grad.reshape(2, 2, 2, total_rows // 8, cols), 2)
    return add_low(kept, flip("fsdp", 8, 1, theirs))


def scatter_near(grad):
    if lax.axis_size("fsdp") != 8:
        return grad
    half = grad.shape[-1] // 2
    first, first_out = entries(4, grad[..., :half], 0)
    second, second_out = entries(2, grad[..., half:], 1)
    over_y, over_x = lax.optimization_barrier(
        (flip("fsdp", 8, 4, first_out), flip("fsdp", 8, 2, second_out))
    )
    return add_low(first, over_y), add_low(second, over_x)


def scatter_far(grad):
    if lax.axis_size("fsdp") != 8:
        return grad
    first, first_out = entries(2, grad[0], 0)
    second, second_out = entries(4, grad[1], 0)
    over_x, over_y = lax.optimization_barrier(
        (flip("fsdp", 8, 2, first_out), flip("fsdp", 8, 4, second_out))
    )
    return jnp.concatenate([add_low(first, over_x), add_low(second, over_y)], axis=1)


def total_over_tp(vector):
    bit = 1
    while bit < lax.axis_size("tp"):
        vector = vector + flip("tp", lax.axis_size("tp"), bit, vector)
        bit *= 2
    return vector


def total_over_fsdp(vector):
    bit = 1
    while bit < lax.axis_size("fsdp"):
        vector = vector + flip("fsdp", lax.axis_size("fsdp"), bit, vector)
        bit *= 2
    return vector


def normalize(token_rows):
    centred = token_rows - jnp.mean(token_rows, axis=-1, keepdims=True)
    scaling = lax.rsqrt(jnp.mean(centred * centred, axis=-1, keepdims=True) + EPSILON)
    return centred * scaling, scaling


def normalize_back(grad_rows, normed, scaling, gain_row):
    grad_normed = grad_rows * gain_row
    adjusted = grad_normed - jnp.mean(grad_normed, axis=-1, keepdims=True)
    adjusted = adjusted - normed * jnp.mean(grad_normed * normed, axis=-1, keepdims=True)
    return scaling * adjusted, jnp.sum(grad_rows * normed, axis=0), jnp.sum(grad_rows, axis=0)


def on_device(
    fsdp,
    tp,
    tokens,
    segment_ids,
    live_mask,
    query_weight,
    query_bias,
    key_weight,
    value_weight,
    value_bias,
    output_weight,
    output_bias,
    first_gain,
    first_shift,
    inner_weight,
    inner_bias,
    outer_weight,
    outer_bias,
    second_gain,
    second_shift,
    out_grad,
):
    sequences, places, width = tokens.shape
    count = sequences // tp
    length = places * tp
    rank = lax.axis_index("tp")
    head_cols = query_weight.shape[1]
    unit_cols = inner_weight.shape[1]
    shard_rows = query_weight.shape[0]

    def whole_rows(parts):
        return jnp.concatenate(parts, axis=1).reshape(count * length, width)

    def by_member(array):
        return array.reshape(tp, count, places, width)

    def to_owners(array):
        parts = array.reshape(count, tp, places, width)
        return sent_back([parts[:, step] for step in range(tp)])

    def own_places(parts):
        return by_source(parts).reshape(sequences, places, width)

    def columns(parts, widths):
        pieces, first = [], 0
        for cols in widths:
            pieces += [part[:shard_rows, first : first + cols] for part in parts]
            first += cols
        return jnp.concatenate(pieces, axis=1)

    def own_columns(share, widths):
        parts = []
        for step in range(tp):
            pieces, first = [], 0
            for cols in widths:
                pieces.append(share[:, first + step * cols : first + (step + 1) * cols])
                first += tp * cols
            parts.append(jnp.concatenate(pieces, axis=1))
        return sent_back(parts)

    def summed(parts, widths):
        total, first, pieces = sum(part.astype(WIDE) for part in parts), 0, []
        for cols in widths:
            pieces.append(total[:, first : first + cols])
            first += cols
        return pieces

    def by_rank(vector):
        parts = vector.reshape(tp, -1)
        parts = [lax.dynamic_slice_in_dim(parts, (rank - spot) % tp, 1, 0) for spot in range(tp)]
        return jnp.concatenate(parts, axis=0).reshape(-1)

    biases = jnp.concatenate([query_bias, value_bias, inner_bias]).reshape(-1, 4 * head_cols // 2)
    biases = jnp.pad(biases, ((0, 0), (0, 4 * head_cols - biases.shape[1])))
    heads = jnp.concatenate([query_weight, key_weight, value_weight, output_weight.T], axis=1)
    heads = spread(jnp.concatenate([heads, biases], axis=0))
    rest = jnp.concatenate([inner_weight, outer_weight.T], axis=1)
    rest, heads = meet(rest, heads, (1, 2, 3))
    rest = spread(rest)
    tokens, rest = meet(tokens, rest, (1,))
    rows = dealt(by_member(tokens))
    biases = [part[shard_rows:, : 2 * head_cols].reshape(-1).astype(WIDE) for part in heads]
    query_bias_full = jnp.concatenate([part[:head_cols] for part in biases])
    value_bias_full = jnp.concatenate([part[head_cols : 2 * head_cols] for part in biases])
    inner_bias_full = jnp.concatenate([part[2 * head_cols :] for part in biases])
    heads, rows, rest = gather_rows(fsdp, columns(heads, (head_cols,) * 4), rows, rest)
    query_full, key_full, value_full, output_turned = (
        heads[:, i * width : (i + 1) * width] for i in range(4)
    )
    rows = whole_rows(rows)
    rows, out_grad = lax.optimization_barrier((rows, out_grad))
    rest = lax.all_gather(columns(rest, (unit_cols, unit_cols)), "fsdp", axis=0, tiled=True)
    inner_full, outer_turned = rest[:, : tp * unit_cols], rest[:, tp * unit_cols :]

    first = rank * count
    segment = lax.dynamic_slice_in_dim(segment_ids, first, count, 0)
    live = lax.dynamic_slice_in_dim(live_mask, first, count, 0)
    spots = lax.broadcasted_iota(jnp.int32, segment.shape, 1)
    ids = jnp.where(live == 1, segment, length + spots).reshape(count, tp, places)
    ids = [lax.dynamic_slice_in_dim(ids, (rank - step) % tp, 1, 1) for step in range(tp)]
    ids = jnp.concatenate(ids, axis=1).reshape(count, length)

    shape = (count, length, width)
    queries = (dot(rows, query_full, BY_ROWS) + query_bias_full).astype(LOW).reshape(shape)
    keys_all = dot(rows, key_full, BY_ROWS).astype(LOW).reshape(shape)
    values = (dot(rows, value_full, BY_ROWS) + value_bias_full).astype(LOW).reshape(shape)
    context, logsum = attend(queries, keys_all, values, ids)
    context, grad_out = meet(context, dealt(by_member(out_grad)), (2,))
    context = context.reshape(count * length, width)
    mixed = dot(context, output_turned, BY_LAST) + output_bias.astype(WIDE)
    first_normed, first_scaling = normalize(rows.astype(WIDE) + mixed)
    first_rows = first_normed * first_gain.astype(WIDE) + first_shift.astype(WIDE)
    first_low = first_rows.astype(LOW)
    preactivation = dot(first_low, inner_full, BY_ROWS) + inner_bias_full
    cumulative = 0.5 * (1.0 + lax.erf(preactivation * 0.7071067811865476))
    activation_rows = (preactivation * cumulative).astype(LOW)
    density = jnp.exp(-0.5 * preactivation * preactivation) * 0.3989422804014327
    slope = cumulative + preactivation * density
    activation_rows, grad_out = meet(activation_rows, grad_out, (1, 3))
    branch = dot(activation_rows, outer_turned, BY_LAST)
    second_normed, second_scaling = normalize(first_rows + branch + outer_bias.astype(WIDE))
    second_rows = second_normed * second_gain.astype(WIDE) + second_shift.astype(WIDE)
    layer_out = to_owners(second_rows.astype(LOW))

    grad_out = whole_rows(grad_out).astype(WIDE)
    grad_second, second_gain_grad, second_shift_grad = normalize_back(
        grad_out, second_normed, second_scaling, second_gain.astype(WIDE)
    )
    outer_bias_grad = jnp.sum(grad_second, axis=0)
    grad_branch = grad_second.astype(LOW)
    outer_grad = dot(grad_branch, activation_rows, BY_FIRST).astype(LOW)
    outer_share = lax.psum_scatter(outer_grad, "fsdp", scatter_dimension=0, tiled=True)
    grad_activ = dot(grad_branch, outer_turned, BY_ROWS)
    grad_pre = (grad_activ * slope).astype(LOW)
    grad_pre, layer_out = meet(grad_pre, layer_out, (2,))
    inner_bias_grad = jnp.sum(grad_pre.astype(WIDE), axis=0)
    inner_share = scatter_core(dot(first_low, grad_pre, BY_FIRST).astype(LOW))
    grad_first = grad_second + dot(grad_pre, inner_full, BY_LAST)
    grad_mixed, first_gain_grad, first_shift_grad = normalize_back(
        grad_first, first_normed, first_scaling, first_gain.astype(WIDE)
    )
    output_bias_grad = jnp.sum(grad_mixed, axis=0)
    grad_mixed_low = grad_mixed.astype(LOW)
    output_grad = dot(grad_mixed_low, context, BY_FIRST).astype(LOW)
    grad_context = dot(grad_mixed_low, output_turned, BY_ROWS).astype(LOW).reshape(shape)
    early = total_over_tp(
        jnp.concatenate(
            [
                output_bias_grad,
                first_gain_grad,
                first_shift_grad,
                outer_bias_grad,
                second_gain_grad,
                second_shift_grad,
                by_rank(inner_bias_grad),
            ]
        )
    )
    grad_context, inner_share, output_grad, layer_out, early = lax.optimization_barrier(
        (grad_context, scatter_near(inner_share), output_grad, layer_out, early)
    )
    early = total_over_fsdp(early)
    inner_share = scatter_far(inner_share)
    back = functools.partial(attend_back, queries, keys_all, values, grad_context, logsum, ids)
    halfway = back(None, 0)
    halfway, inner_share, outer_share, early = lax.optimization_barrier(
        (halfway, inner_share, outer_share, early)
    )
    layer_out = own_places(layer_out)
    inner_parts = own_columns(inner_share, (unit_cols,))
    outer_parts = own_columns(outer_share, (unit_cols,))
    rows_grads = back(halfway, 1)
    rows_grads, inner_parts, outer_parts = lax.optimization_barrier(
        (rows_grads, inner_parts, outer_parts)
    )
    (inner_share,) = summed(inner_parts, (unit_cols,))
    (outer_share,) = summed(outer_parts, (unit_cols,))
    query_rows_grad, key_rows_grad, value_rows_grad = (
        array.reshape(count * length, width) for array in rows_grads
    )
    query_bias_grad = jnp.sum(query_rows_grad.astype(WIDE), axis=0)
    value_bias_grad = jnp.sum(value_rows_grad.astype(WIDE), axis=0)
    late = total_over_tp(
        jnp.concatenate([by_rank(query_bias_grad), by_rank(value_bias_grad)])
    )
    head_grads = [
        dot(rows, grad, BY_FIRST).astype(LOW)
        for grad in (query_rows_grad, key_rows_grad, value_rows_grad)
    ]
    heads_share = scatter_core(jnp.concatenate(head_grads + [output_grad], axis=1))
    tokens_grad = (
        grad_mixed
        + dot(query_rows_grad, query_full, BY_LAST)
        + dot(key_rows_grad, key_full, BY_LAST)
        + dot(value_rows_grad, value_full, BY_LAST)
    ).astype(LOW)
    tokens_grad, late = lax.optimization_barrier((tokens_grad, late))
    tokens_grad = to_owners(tokens_grad)
    late = total_over_fsdp(late)
    heads_share, tokens_grad = meet(scatter_near(heads_share), tokens_grad, (2,))
    heads_share, tokens_grad = meet(scatter_far(heads_share), tokens_grad, (1, 3))
    heads_share, late = lax.optimization_barrier((heads_share, late))
    query_share, key_share, value_share, output_share = summed(
        own_columns(heads_share, (head_cols,) * 4), (head_cols,) * 4
    )
    tokens_grad = own_places(tokens_grad).astype(WIDE)
    totals = jnp.concatenate([early[: 6 * width], late, early[6 * width :]])
    rowwise = [totals[i * width : (i + 1) * width] for i in range(6)]
    query_bias_total = lax.dynamic_slice_in_dim(totals, 6 * width + rank * head_cols, head_cols)
    value_bias_total = lax.dynamic_slice_in_dim(totals, 7 * width + rank * head_cols, head_cols)
    inner_bias_total = lax.dynamic_slice_in_dim(totals, 8 * width + rank * unit_cols, unit_cols)
    return (
        layer_out,
        tokens_grad,
        query_share,
        query_bias_total,
        key_share,
        value_share,
        value_bias_total,
        output_share.T,
        rowwise[0],
        rowwise[1],
        rowwise[2],
        inner_share,
        inner_bias_total,
        outer_share.T,
        rowwise[3],
        rowwise[4],
        rowwise[5],
    )


def solution(mesh):
    split = P("fsdp", "tp", None)
    across, turned = P("fsdp", "tp"), P("tp", "fsdp")
    seqs, units, copied = P("fsdp", None), P("tp"), P()
    return jax.shard_map(
        functools.partial(on_device, mesh.shape["fsdp"], mesh.shape["tp"]),
        mesh=mesh,
        in_specs=(
            split,
            seqs,
            seqs,
            across,
            units,
            across,
            across,
            units,
            turned,
            copied,
            copied,
            copied,
            across,
            units,
            turned,
            copied,
            copied,
            copied,
            split,
        ),
        out_specs=(
            split,
            split,
            across,
            units,
            across,
            across,
            units,
            turned,
            copied,
            copied,
            copied,
            across,
            units,
            turned,
            copied,
            copied,
            copied,
        ),
        check_vma=False,
    )
```

time: 614 us -> 465 us (0.76)
  waiting for transfers between devices: 236 us -> 132 us
  local copies, waits for them, and re-layouts: 71.6 us -> 42.3 us
  matrix products: 94.6 us -> 80.1 us
  starting transfers between devices: 73.1 us -> 61.5 us
  other arithmetic: 39.2 us -> 47.5 us
    ppermute x33 -> x25, waiting for transfers between devices: 146 us -> 19.5 us  [flip(): return lax.ppermute(block, axis, [(i, i ^ bit) for i in range(members)])]
    transpose x9 -> x0, local copies, waits for them, and re-layouts: 25.1 us -> none  [the longest x5 24.3 us: columns(): return blocks.transpose(1, 0, 2).reshape(rows, members * cols)]
    ppermute x12 -> x27, waiting for transfers between devices: 90.2 us -> 113 us  [the longest x15 46.6 us: sent_back(): moved.append(lax.ppermute(parts[step], 'tp', pairs))]
    ppermute x33 -> x25, starting transfers between devices: 48.3 us -> 26 us  [flip(): return lax.ppermute(block, axis, [(i, i ^ bit) for i in range(members)])]
    dot_general x18, matrix products: 94.6 us -> 80.1 us  [dot(): return lax.dot_general(left, right, dims, preferred_element_type=WIDE)]
    ppermute x12 -> x27, starting transfers between devices: 24.7 us -> 35.4 us  [the longest x15 21.8 us: sent_back(): moved.append(lax.ppermute(parts[step], 'tp', pairs))]
    convert_element_type x14 -> x13, other arithmetic: 9.31 us -> 12.5 us  [the longest x10 6.93 us: add_low(): return (kept.astype(WIDE) + moved.astype(WIDE)).astype(LOW)]
    pallas_call x1 -> x2, Pallas kernels: 44.6 us -> 46.7 us  [attend_back(): pl.pallas_call(body, grid=(count, pairs - first if part else pairs // 2),...]
  transfers between devices with their start and end apart: 46 -> 54, of which waited for: 27 -> 21; matrix products, arithmetic and copies ran while one was open for 14% -> 27% of each run, Pallas kernels for 5% -> 17%
where the time goes in v4:
time: 465 us; the launch traced here: 457 us
  waiting for transfers between devices  132 us (28%)
  matrix products  80.1 us (17%)
  Pallas kernels  76.7 us (16%)
  starting transfers between devices  61.5 us (13%)
  other arithmetic  47.5 us (10%)
  local copies, waits for them, and re-layouts  42.3 us (9%)
  between operations  16.2 us (3%)
    dot_general x18, matrix products, dot(): return lax.dot_general(left, right, dims, preferred_element_type=WIDE)  80.1 us
    pallas_call x2, Pallas kernels, attend_back(): pl.pallas_call(body, grid=(count, pairs - first if part else pairs // 2),...  46.7 us
    ppermute x15, waiting for transfers between devices, sent_back(): moved.append(lax.ppermute(parts[step], 'tp', pairs))  46.6 us
    ppermute x6, waiting for transfers between devices, spread(): return [block] + [lax.ppermute(block, 'tp', pairs) for pairs in rank_pairs]  34 us
    ppermute x6, waiting for transfers between devices, dealt(): parts.append(lax.ppermute(block, 'tp', pairs) if step else block)  32.2 us
    pallas_call x1, Pallas kernels, attend(): pl.pallas_call(functools.partial(attend_kernel, scaling=scaling), grid=(c...  30 us
    ppermute x25, starting transfers between devices, flip(): return lax.ppermute(block, axis, [(i, i ^ bit) for i in range(members)])  26 us
    ppermute x15, starting transfers between devices, sent_back(): moved.append(lax.ppermute(parts[step], 'tp', pairs))  21.8 us
  transfers between devices with their start and end apart: 54, of which 21 were waited for; matrix products, arithmetic and copies ran while one was open for 27% of the time, Pallas kernels for 17%

profile of v4, /device:TPU:0, one launch (start us, length us, event | category | flops | bytes accessed | tf_op | source)
XLA Modules:
  0.0 456.6 jit_solution(7551474904811607164)
XLA Ops:
  7.2 2.1 concatenate.84
  13.2 5.1 %collective-permute-start.2 = (bf16[99,768]{0,1:T(8,128)(2,1)S(1)}, bf16[99,768]{0,1:T(8,128)(2,1)S(1)}, u32[]{:S(2)}, u32[]{:S(2)}) collective-permute-start(bf16[99,768]{0,1:T(8,128)(2,1)S(1)} %fusion.88), channel_id=1, source_target_pairs={{0,3},{1,0},{2,1},{3,2},{4,7},{5,4},{6,5},{7,6},{8,11},{9,8},{10,9... | collective-permute-start | bytes 456200 | tf_op jit(solution)/shard_map/ppermute | solution.py:159
  20.4 3.3 collective-permute-done.2
  23.7 11.4 %collective-permute-done.1 = bf16[99,768]{0,1:T(8,128)(2,1)S(1)} collective-permute-done((bf16[99,768]{0,1:T(8,128)(2,1)S(1)}, bf16[99,768]{0,1:T(8,128)(2,1)S(1)}, u32[]{:S(2)}, u32[]{:S(2)}) %collective-permute-start.1) | collective-permute-done | bytes 152096 | tf_op jit(solution)/shard_map/ppermute | solution.py:159
  35.4 2.4 collective-permute-start.6
  37.8 2.0 collective-permute-start.3
  40.8 1.6 collective-permute-start.5
  43.9 14.3 %collective-permute-done.3 = bf16[96,1536]{1,0:T(8,128)(2,1)S(1)} collective-permute-done((bf16[96,1536]{1,0:T(8,128)(2,1)S(1)}, bf16[96,1536]{1,0:T(8,128)(2,1)S(1)}, u32[]{:S(2)}, u32[]{:S(2)}) %collective-permute-start.3) | collective-permute-done | bytes 294944 | tf_op jit(solution)/shard_map/ppermute | solution.py:159
  58.2 5.0 %collective-permute-done.6 = bf16[96,1536]{1,0:T(8,128)(2,1)S(1)} collective-permute-done((bf16[96,1536]{1,0:T(8,128)(2,1)S(1)}, bf16[96,1536]{1,0:T(8,128)(2,1)S(1)}, u32[]{:S(2)}, u32[]{:S(2)}) %collective-permute-start.6) | collective-permute-done | bytes 294944 | tf_op jit(solution)/shard_map/ppermute | solution.py:159
  70.8 1.6 collective-permute-start.8
  73.3 25.7 %collective-permute-done.11 = bf16[1,256,768]{2,1,0:T(8,128)(2,1)S(1)} collective-permute-done((bf16[1,256,768]{2,1,0:T(8,128)(2,1)S(1)}, bf16[1,256,768]{2,1,0:T(8,128)(2,1)S(1)}, u32[]{:S(2)}, u32[]{:S(2)}) %collective-permute-start.11) | collective-permute-done | bytes 393248 | tf_op jit(solution)/shard_map/ppermute | solution.py:168
  117.8 6.4 %collective-permute-done.13 = bf16[1,256,768]{2,1,0:T(8,128)(2,1)} collective-permute-done((bf16[1,256,768]{2,1,0:T(8,128)(2,1)}, bf16[1,256,768]{2,1,0:T(8,128)(2,1)}, u32[]{:S(2)}, u32[]{:S(2)}) %collective-permute-start.13) | collective-permute-done | bytes 393248 | tf_op jit(solution)/shard_map/ppermute | solution.py:168
  126.8 2.1 collective-permute-start.16
  129.4 2.2 bitcast_select_fusion
  131.6 2.7 fusion.63.k_ref.refs_1_
  134.3 2.6 fusion.66.v_ref.refs_2_
  136.9 2.5 fusion.65.q_ref.refs_0_
  139.4 30.0 %attend.1 = (bf16[1,1024,768]{2,1,0:T(8,128)(2,1)}, f32[1,6,2,1024]{3,2,1,0:T(2,128)}) custom-call(bf16[1,1024,768]{2,1,0:T(8,128)(2,1)} %fusion.65.q_ref.refs_0_, bf16[1,1024,768]{2,1,0:T(8,128)(2,1)} %fusion.63.k_ref.refs_1_, bf16[1,1024,768]{2,1,0:T(8,128)(2,1)} %fusion.66.v_ref.refs_2_, s32[1,1,1024]{2,1,0:T(1,128)} %broadcast_in_dim_reshape.4.row_ref.refs_5_, ...), custom_call_target="tpu_custom_call" | custom-call | flops 22548578304 | bytes 6291456 | tf_op jit(solution)/shard_map/attend/pallas_call | solution.py:96
  170.2 3.8 fusion.107
  174.6 11.2 %multiply_convert_fusion = (bf16[1024,3072]{1,0:T(8,128)(2,1)S(1)}, f32[1024,3072]{1,0:T(8,128)}) fusion(f32[3072]{0:T(1024)} %pad_maximum_fusion.10, bf16[768,6144]{1,0:T(8,128)(2,1)} %all-gather.2.cloned.1.call-done, f32[1024,768]{1,0:T(8,128)S(1)} %get-tuple-element.331, f32[768]{0:T(1024)} %convert_element_type.284, f32[768]{0:T(1024)S(1)} %convert_element_type.283, ...), kind=kOutput, calls=%fused_computation.8 | convolution fusion | flops 4854644736 | bytes 26766336 | tf_op jit(solution)/shard_map/dot_general | solution.py:22
  185.8 5.4 %fusion.108 = (f32[1024]{0:T(1024)S(1)}, f32[1024,768]{1,0:T(8,128)S(1)}) fusion(f32[768]{0:T(1024)S(1)} %copy-done.49, bf16[1024,3072]{1,0:T(8,128)(2,1)S(1)} %get-tuple-element.114, bf16[768,6144]{1,0:T(8,128)(2,1)S(1)} %copy-done.57, f32[768]{0:T(1024)S(1)} %copy-done.47, f32[768]{0:T(1024)S(1)} %convert_element_type.283, ...), kind=kOutput, calls=%fused_computation.260 | convolution fusion | flops 4837342208 | bytes 17326080 | tf_op jit(solution)/shard_map/dot_general | solution.py:22
  192.2 5.3 %fusion.29 = (f32[768]{0:T(1024)}, f32[1024]{0:T(1024)S(1)}, f32[1024]{0:T(1024)S(1)}, bf16[1024,768]{1,0:T(8,128)(2,1)}) fusion(f32[1024,768]{1,0:T(8,128)S(1)} %get-tuple-element.335, f32[1024]{0:T(1024)S(1)} %add_rsqrt_fusion, f32[1024]{0:T(1024)S(1)} %broadcast_multiply_fusion.4, bf16[1,256,768]{2,1,0:T(8,128)(2,1)} %collective-permute-done.16, ...), kind=kLoop, calls=%fused_computation.44 | loop fusion | flops 14939392 | bytes 6317056 | tf_op jit(solution)/shard_map/reduce_sum | solution.py:287
  197.6 4.1 fusion.93
  201.6 1.7 copy-done.9
  203.3 6.9 %convolution_convert_fusion = bf16[768,3072]{1,0:T(8,128)(2,1)} fusion(bf16[1024,3072]{1,0:T(8,128)(2,1)S(1)} %get-tuple-element.114, f32[1024,768]{1,0:T(8,128)S(1)} %get-tuple-element.230), kind=kOutput, calls=%fused_computation.13 | convolution fusion | flops 4834983936 | bytes 14155776 | tf_op jit(solution)/shard_map/dot_general | solution.py:22
  210.2 2.6 slice_bitcast_fusion.4
  212.8 3.8 collective-permute-start.22
  218.1 12.1 %fusion.5 = bf16[1024,3072]{1,0:T(8,128)(2,1)S(1)} fusion(f32[1024,3072]{1,0:T(8,128)} %get-tuple-element.333, f32[3072]{0:T(1024)} %pad_maximum_fusion.10, bf16[768,6144]{1,0:T(8,128)(2,1)} %all-gather.2.cloned.1.call-done, f32[1024,768]{1,0:T(8,128)S(1)} %copy-done.10), kind=kOutput, calls=%fused_computation.6 | convolution fusion | flops 4867227648 | bytes 26750976 | tf_op jit(solution)/shard_map/dot_general | solution.py:22
  230.2 2.0 convert_reduce_fusion.1
  232.2 18.2 %collective-permute-done.17 = bf16[1,256,768]{2,1,0:T(8,128)(2,1)} collective-permute-done((bf16[1,256,768]{2,1,0:T(8,128)(2,1)S(1)}, bf16[1,256,768]{2,1,0:T(8,128)(2,1)}, u32[]{:S(2)}, u32[]{:S(2)}) %collective-permute-start.17) | collective-permute-done | bytes 393248 | tf_op jit(solution)/shard_map/ppermute | solution.py:177
  250.5 6.9 %convolution_convert_fusion.1 = bf16[768,3072]{1,0:T(8,128)(2,1)S(1)} fusion(bf16[1024,3072]{1,0:T(8,128)(2,1)S(1)} %fusion.5, f32[1024,768]{1,0:T(8,128)S(1)} %get-tuple-element.331, f32[768]{0:T(1024)S(1)} %copy-done.48, f32[768]{0:T(1024)S(1)} %convert_element_type.283, f32[1024]{0:T(1024)S(1)} %add_rsqrt_fusion.1, f32[1024]{0:T(1024)S(1)} %broadcast_multiply_fusion.5), kind=kOutput, calls=%fused_computation.14 | convolution fusion | flops 4838129664 | bytes 14170112 | tf_op jit(solution)/shard_map/dot_general | solution.py:22
  257.4 1.7 constant_dynamic-slice_fusion.13
  259.1 1.6 copy.126
  260.7 7.5 %multiply_reduce_fusion = (f32[768]{0:T(1024)S(1)}, f32[1024]{0:T(1024)S(1)}, f32[1024]{0:T(1024)S(1)}, f32[768]{0:T(1024)S(1)}, f32[1024,768]{1,0:T(8,128)}) fusion(f32[1024,768]{1,0:T(8,128)S(1)} %get-tuple-element.331, f32[1024]{0:T(1024)S(1)} %add_rsqrt_fusion.1, f32[1024]{0:T(1024)S(1)} %broadcast_multiply_fusion.5, ...), kind=kOutput, calls=%fused_computation.48 | convolution fusion | flops 4839698432 | bytes 20473856 | tf_op jit(solution)/shard_map/dot_general | solution.py:22
  269.3 2.6 fusion.95
  272.2 3.5 fusion.7
  277.3 2.5 fusion.51
  279.9 1.9 collective-permute-start.24
  281.8 3.8 fusion.64.g_ref.refs_3_
  285.6 6.2 %collective-permute-done.19 = bf16[2,96,1536]{2,1,0:T(8,128)(2,1)S(1)} collective-permute-done((bf16[2,96,1536]{2,1,0:T(8,128)(2,1)S(1)}, bf16[2,96,1536]{2,1,0:T(8,128)(2,1)S(1)}, u32[]{:S(2)}, u32[]{:S(2)}) %collective-permute-start.19) | collective-permute-done | bytes 589856 | tf_op jit(solution)/shard_map/ppermute | solution.py:192
  294.4 1.6 collective-permute-start.26
  297.6 1.9 collective-permute-start.29
  299.5 23.3 %attend_back.2 = (bf16[1,1024,768]{2,1,0:T(8,128)(2,1)}, bf16[1,1024,768]{2,1,0:T(8,128)(2,1)}, bf16[1,1024,768]{2,1,0:T(8,128)(2,1)}) custom-call(bf16[1,1024,768]{2,1,0:T(8,128)(2,1)} %fusion.65.q_ref.refs_0_, bf16[1,1024,768]{2,1,0:T(8,128)(2,1)} %fusion.63.k_ref.refs_1_, bf16[1,1024,768]{2,1,0:T(8,128)(2,1)} %fusion.66.v_ref.refs_2_, ...), custom_call_target="tpu_custom_call" | custom-call | flops 19327352832 | bytes 5505024 | tf_op jit(solution)/shard_map/attend_back/pallas_call | solution.py:131
  324.0 2.1 collective-permute-start.31
  326.1 1.7 collective-permute-start.30
  331.8 1.6 collective-permute-start.33
  333.4 23.4 %attend_back.3 = (bf16[1,1024,768]{2,1,0:T(8,128)(2,1)}, bf16[1,1024,768]{2,1,0:T(8,128)(2,1)}, bf16[1,1024,768]{2,1,0:T(8,128)(2,1)}) custom-call(bf16[1,1024,768]{2,1,0:T(8,128)(2,1)} %fusion.65.q_ref.refs_0_, bf16[1,1024,768]{2,1,0:T(8,128)(2,1)} %fusion.63.k_ref.refs_1_, ...), custom_call_target="tpu_custom_call", output_to_operand_aliasing={{0}: (7, {}), {1}: (8, {}), {2}: (9, {})} | custom-call | flops 19327352832 | bytes 5505024 | tf_op jit(solution)/shard_map/attend_back/pallas_call | solution.py:131
  357.6 3.0 fusion.57
  364.5 2.2 copy-done
  366.6 1.6 dynamic-slice_bitcast_fusion
  371.1 3.3 fusion.44
  375.9 5.3 %collective-permute-start.40 = (f32[1536]{0:T(1024)S(1)}, f32[1536]{0:T(1024)S(1)}, u32[]{:S(2)}, u32[]{:S(2)}) collective-permute-start(f32[1536]{0:T(1024)S(1)} %add.457), channel_id=1, source_target_pairs={{0,2},{1,3},{2,0},{3,1},{4,6},{5,7},{6,4},{7,5},{8,10},{9,11},{10,... | collective-permute-start | bytes 18440 | tf_op jit(solution)/shard_map/ppermute | solution.py:192
  381.1 2.6 fusion.6
  389.0 10.4 %collective-permute-done.37 = bf16[2,96,1536]{2,1,0:T(8,128)(2,1)S(1)} collective-permute-done((bf16[2,96,1536]{2,1,0:T(8,128)(2,1)S(1)}, bf16[2,96,1536]{2,1,0:T(8,128)(2,1)S(1)}, u32[]{:S(2)}, u32[]{:S(2)}) %collective-permute-start.37) | collective-permute-done | bytes 589856 | tf_op jit(solution)/shard_map/ppermute | solution.py:192
  399.9 8.1 %collective-permute-done.41 = bf16[1,256,768]{2,1,0:T(8,128)(2,1)S(1)} collective-permute-done((bf16[1,256,768]{2,1,0:T(8,128)(2,1)S(1)}, bf16[1,256,768]{2,1,0:T(8,128)(2,1)S(1)}, u32[]{:S(2)}, u32[]{:S(2)}) %collective-permute-start.41) | collective-permute-done | bytes 393248 | tf_op jit(solution)/shard_map/ppermute | solution.py:177
  408.8 1.8 collective-permute-start.42
  411.6 1.7 add_bitcast_fusion
  413.3 3.8 collective-permute-start.44
  417.8 9.3 %collective-permute-done.45 = bf16[1,256,768]{2,1,0:T(8,128)(2,1)S(1)} collective-permute-done((bf16[1,256,768]{2,1,0:T(8,128)(2,1)S(1)}, bf16[1,256,768]{2,1,0:T(8,128)(2,1)S(1)}, u32[]{:S(2)}, u32[]{:S(2)}) %collective-permute-start.45) | collective-permute-done | bytes 393248 | tf_op jit(solution)/shard_map/ppermute | solution.py:177
  427.1 5.2 %collective-permute-done.44 = bf16[1,256,768]{2,1,0:T(8,128)(2,1)S(1)} collective-permute-done((bf16[1,256,768]{2,1,0:T(8,128)(2,1)S(1)}, bf16[1,256,768]{2,1,0:T(8,128)(2,1)S(1)}, u32[]{:S(2)}, u32[]{:S(2)}) %collective-permute-start.44) | collective-permute-done | bytes 393248 | tf_op jit(solution)/shard_map/ppermute | solution.py:177
  432.6 2.1 collective-permute-start.49
  435.3 2.1 collective-permute-start.51
  437.4 4.5 fusion.36
  443.2 4.5 collective-permute-done.50
  (382 shorter events, 75.2 us)
Async XLA Ops:
  7.2 167.3 %all-gather.2.cloned.1.call-start = ((), (), s32[]{:S(2)}) async-start(), calls=%async_computation.1 | async-start | bytes 10616832 | tf_op jit(solution)/shard_map/all_gather | solution.py:382
  13.2 10.5 %collective-permute-start.2 = (bf16[99,768]{0,1:T(8,128)(2,1)S(1)}, bf16[99,768]{0,1:T(8,128)(2,1)S(1)}, u32[]{:S(2)}, u32[]{:S(2)}) collective-permute-start(bf16[99,768]{0,1:T(8,128)(2,1)S(1)} %fusion.88), channel_id=1, source_target_pairs={{0,3},{1,0},{2,1},{3,2},{4,7},{5,4},{6,5},{7,6},{8,11},{9,8},{10,9... | collective-permute-start | bytes 456200 | tf_op jit(solution)/shard_map/ppermute | solution.py:159
  18.3 16.7 %collective-permute-start.1 = (bf16[99,768]{0,1:T(8,128)(2,1)S(1)}, bf16[99,768]{0,1:T(8,128)(2,1)S(1)}, u32[]{:S(2)}, u32[]{:S(2)}) collective-permute-start(bf16[99,768]{0,1:T(8,128)(2,1)S(1)} %fusion.88), channel_id=1, source_target_pairs={{0,2},{1,3},{2,0},{3,1},{4,6},{5,7},{6,4},{7,5},{8,10},{9,11},{10,... | collective-permute-start | bytes 456200 | tf_op jit(solution)/shard_map/ppermute | solution.py:159
  18.3 16.7 %collective-permute-start = (bf16[99,768]{0,1:T(8,128)(2,1)S(1)}, bf16[99,768]{0,1:T(8,128)(2,1)S(1)}, u32[]{:S(2)}, u32[]{:S(2)}) collective-permute-start(bf16[99,768]{0,1:T(8,128)(2,1)S(1)} %fusion.88), channel_id=1, source_target_pairs={{0,1},{1,2},{2,3},{3,0},{4,5},{5,6},{6,7},{7,4},{8,9},{9,10},{10,1... | collective-permute-start | bytes 456200 | tf_op jit(solution)/shard_map/ppermute | solution.py:159
  23.7 39.7 %copy-start.21 = (bf16[99,768]{0,1:T(8,128)(2,1)}, bf16[99,768]{0,1:T(8,128)(2,1)S(1)}, u32[]{:S(2)}) copy-start(bf16[99,768]{0,1:T(8,128)(2,1)S(1)} %collective-permute-done.2) | copy-start | bytes 456196
  35.0 28.4 %copy-start.23 = (bf16[99,768]{0,1:T(8,128)(2,1)}, bf16[99,768]{0,1:T(8,128)(2,1)S(1)}, u32[]{:S(2)}) copy-start(bf16[99,768]{0,1:T(8,128)(2,1)S(1)} %collective-permute-done.1) | copy-start | bytes 456196
  35.0 28.4 %copy-start.24 = (bf16[99,768]{0,1:T(8,128)(2,1)}, bf16[99,768]{0,1:T(8,128)(2,1)S(1)}, u32[]{:S(2)}) copy-start(bf16[99,768]{0,1:T(8,128)(2,1)S(1)} %collective-permute-done) | copy-start | bytes 456196
  35.0 23.2 %collective-permute-start.7 = (bf16[96,1536]{1,0:T(8,128)(2,1)S(1)}, bf16[96,1536]{1,0:T(8,128)(2,1)S(1)}, u32[]{:S(2)}, u32[]{:S(2)}) collective-permute-start(bf16[96,1536]{1,0:T(8,128)(2,1)S(1)} %pad_maximum_fusion.5), channel_id=1, source_target_pairs={{0,3},{1,0},{2,1},{3,2},{4,7},{5,4},{6,5},{7,6},{8,11},{9,8},{10,9... | collective-permute-start | bytes 884744 | tf_op jit(solution)/shard_map/ppermute | solution.py:159
  35.4 27.9 %collective-permute-start.6 = (bf16[96,1536]{1,0:T(8,128)(2,1)S(1)}, bf16[96,1536]{1,0:T(8,128)(2,1)S(1)}, u32[]{:S(2)}, u32[]{:S(2)}) collective-permute-start(bf16[96,1536]{1,0:T(8,128)(2,1)S(1)} %pad_maximum_fusion.5), channel_id=1, source_target_pairs={{0,2},{1,3},{2,0},{3,1},{4,6},{5,7},{6,4},{7,5},{8,10},{9,11},{10,... | collective-permute-start | bytes 884744 | tf_op jit(solution)/shard_map/ppermute | solution.py:159
  37.8 20.4 %collective-permute-start.3 = (bf16[96,1536]{1,0:T(8,128)(2,1)S(1)}, bf16[96,1536]{1,0:T(8,128)(2,1)S(1)}, u32[]{:S(2)}, u32[]{:S(2)}) collective-permute-start(bf16[96,1536]{1,0:T(8,128)(2,1)S(1)} %pad_maximum_fusion.5), channel_id=1, source_target_pairs={{0,1},{1,2},{2,3},{3,0},{4,5},{5,6},{6,7},{7,4},{8,9},{9,10},{10,1... | collective-permute-start | bytes 884744 | tf_op jit(solution)/shard_map/ppermute | solution.py:159
  40.8 22.4 %collective-permute-start.5 = (bf16[96,1536]{0,1:T(8,128)(2,1)S(1)}, bf16[96,1536]{0,1:T(8,128)(2,1)S(1)}, u32[]{:S(2)}, u32[]{:S(2)}) collective-permute-start(bf16[96,1536]{0,1:T(8,128)(2,1)S(1)} %get-tuple-element.284), channel_id=1, source_target_pairs={{0,16},{4,20},{8,24},{12,28},{16,0},{20,4},{24,8},{28,12},{1,17},{... | collective-permute-start | bytes 884744 | tf_op jit(solution)/shard_map/ppermute | solution.py:192
  42.4 20.8 %collective-permute-start.4 = (bf16[96,1536]{0,1:T(8,128)(2,1)S(1)}, bf16[96,1536]{0,1:T(8,128)(2,1)S(1)}, u32[]{:S(2)}, u32[]{:S(2)}) collective-permute-start(bf16[96,1536]{0,1:T(8,128)(2,1)S(1)} %get-tuple-element.285), channel_id=1, source_target_pairs={{0,8},{4,12},{8,0},{12,4},{16,24},{20,28},{24,16},{28,20},{1,9},{5... | collective-permute-start | bytes 884744 | tf_op jit(solution)/shard_map/ppermute | solution.py:192
  65.2 257.9 %reduce-scatter.2.cloned.1.call-start = ((), (), s32[]{:S(2)}) async-start(), calls=%async_computation.2 | async-start | bytes 5308416 | tf_op jit(solution)/shard_map/reduce_scatter | solution.py:422
  69.1 29.9 %collective-permute-start.9 = (bf16[2,96,1536]{2,1,0:T(8,128)(2,1)S(1)}, bf16[2,96,1536]{2,1,0:T(8,128)(2,1)}, u32[]{:S(2)}, u32[]{:S(2)}) collective-permute-start(bf16[2,96,1536]{2,1,0:T(8,128)(2,1)S(1)} %broadcast_select_fusion.2), channel_id=1, source_target_pairs={{0,8},{4,12},{8,0},{12,4},{16,24},{20,28},{24,16},{28,20},{1,9},{5... | collective-permute-start | bytes 1769480 | tf_op jit(solution)/shard_map/ppermute | solution.py:192
  70.8 28.3 %collective-permute-start.8 = (bf16[2,96,1536]{2,1,0:T(8,128)(2,1)S(1)}, bf16[2,96,1536]{2,1,0:T(8,128)(2,1)}, u32[]{:S(2)}, u32[]{:S(2)}) collective-permute-start(bf16[2,96,1536]{2,1,0:T(8,128)(2,1)S(1)} %broadcast_select_fusion.3), channel_id=1, source_target_pairs={{0,16},{4,20},{8,24},{12,28},{16,0},{20,4},{24,8},{28,12},{1,17},{... | collective-permute-start | bytes 1769480 | tf_op jit(solution)/shard_map/ppermute | solution.py:192
  73.2 25.8 %collective-permute-start.11 = (bf16[1,256,768]{2,1,0:T(8,128)(2,1)S(1)}, bf16[1,256,768]{2,1,0:T(8,128)(2,1)S(1)}, u32[]{:S(2)}, u32[]{:S(2)}) collective-permute-start(bf16[1,256,768]{2,1,0:T(8,128)(2,1)S(1)} %get-tuple-element.254), channel_id=1, source_target_pairs={{0,2},{1,3},{2,0},{3,1},{4,6},{5,7},{6,4},{7,5},{8,10},{9,11},{10,... | collective-permute-start | bytes 1179656 | tf_op jit(solution)/shard_map/ppermute | solution.py:168
  73.3 25.8 %collective-permute-start.10 = (bf16[1,256,768]{2,1,0:T(8,128)(2,1)S(1)}, bf16[1,256,768]{2,1,0:T(8,128)(2,1)S(1)}, u32[]{:S(2)}, u32[]{:S(2)}) collective-permute-start(bf16[1,256,768]{2,1,0:T(8,128)(2,1)S(1)} %get-tuple-element.255), channel_id=1, source_target_pairs={{0,1},{1,2},{2,3},{3,0},{4,5},{5,6},{6,7},{7,4},{8,9},{9,10},{10,1... | collective-permute-start | bytes 1179656 | tf_op jit(solution)/shard_map/ppermute | solution.py:168
  102.4 21.8 %collective-permute-start.12 = (bf16[2,2,96,3072]{3,2,1,0:T(8,128)(2,1)S(1)}, bf16[2,2,96,3072]{3,2,1,0:T(8,128)(2,1)}, u32[]{:S(2)}, u32[]{:S(2)}) collective-permute-start(bf16[2,2,96,3072]{3,2,1,0:T(8,128)(2,1)S(1)} %pad_maximum_fusion.1), channel_id=1, source_target_pairs={{0,4},{4,0},{8,12},{12,8},{16,20},{20,16},{24,28},{28,24},{1,5},{5... | collective-permute-start | bytes 7077896 | tf_op jit(solution)/shard_map/ppermute | solution.py:192
  112.5 11.7 %collective-permute-start.13 = (bf16[1,256,768]{2,1,0:T(8,128)(2,1)}, bf16[1,256,768]{2,1,0:T(8,128)(2,1)}, u32[]{:S(2)}, u32[]{:S(2)}) collective-permute-start(bf16[1,256,768]{2,1,0:T(8,128)(2,1)} %get-tuple-element.253), channel_id=1, source_target_pairs={{0,3},{1,0},{2,1},{3,2},{4,7},{5,4},{6,5},{7,6},{8,11},{9,8},{10,9... | collective-permute-start | bytes 1179656 | tf_op jit(solution)/shard_map/ppermute | solution.py:168
  126.8 59.0 %collective-permute-start.16 = (bf16[1,256,768]{2,1,0:T(8,128)(2,1)}, bf16[1,256,768]{2,1,0:T(8,128)(2,1)}, u32[]{:S(2)}, u32[]{:S(2)}) collective-permute-start(bf16[1,256,768]{2,1,0:T(8,128)(2,1)} %get-tuple-element.249), channel_id=1, source_target_pairs={{0,3},{1,0},{2,1},{3,2},{4,7},{5,4},{6,5},{7,6},{8,11},{9,8},{10,9... | collective-permute-start | bytes 1179656 | tf_op jit(solution)/shard_map/ppermute | solution.py:168
  128.8 56.9 %collective-permute-start.15 = (bf16[1,256,768]{2,1,0:T(8,128)(2,1)}, bf16[1,256,768]{2,1,0:T(8,128)(2,1)}, u32[]{:S(2)}, u32[]{:S(2)}) collective-permute-start(bf16[1,256,768]{2,1,0:T(8,128)(2,1)} %get-tuple-element.250), channel_id=1, source_target_pairs={{0,1},{1,2},{2,3},{3,0},{4,5},{5,6},{6,7},{7,4},{8,9},{9,10},{10,1... | collective-permute-start | bytes 1179656 | tf_op jit(solution)/shard_map/ppermute | solution.py:168
  128.8 40.6 %collective-permute-start.14 = (bf16[1,256,768]{2,1,0:T(8,128)(2,1)S(1)}, bf16[1,256,768]{2,1,0:T(8,128)(2,1)S(1)}, u32[]{:S(2)}, u32[]{:S(2)}) collective-permute-start(bf16[1,256,768]{2,1,0:T(8,128)(2,1)S(1)} %get-tuple-element.251), channel_id=1, source_target_pairs={{0,2},{1,3},{2,0},{3,1},{4,6},{5,7},{6,4},{7,5},{8,10},{9,11},{10,... | collective-permute-start | bytes 1179656 | tf_op jit(solution)/shard_map/ppermute | solution.py:168
  139.4 30.8 %copy-start.50 = (f32[768]{0:T(1024)S(1)}, f32[768]{0:T(1024)}, u32[]{:S(2)}) copy-start(f32[768]{0:T(1024)} %convert_element_type.282) | copy-start | bytes 9220
  212.8 79.6 %collective-permute-start.22 = (bf16[1,256,768]{2,1,0:T(8,128)(2,1)}, bf16[1,256,768]{2,1,0:T(8,128)(2,1)}, u32[]{:S(2)}, u32[]{:S(2)}) collective-permute-start(bf16[1,256,768]{2,1,0:T(8,128)(2,1)} %get-tuple-element.244), channel_id=1, source_target_pairs={{0,1},{1,2},{2,3},{3,0},{4,5},{5,6},{6,7},{7,4},{8,9},{9,10},{10,1... | collective-permute-start | bytes 1179656 | tf_op jit(solution)/shard_map/ppermute | solution.py:177
  216.6 75.8 %collective-permute-start.21 = (bf16[1,256,768]{2,1,0:T(8,128)(2,1)}, bf16[1,256,768]{2,1,0:T(8,128)(2,1)}, u32[]{:S(2)}, u32[]{:S(2)}) collective-permute-start(bf16[1,256,768]{2,1,0:T(8,128)(2,1)} %get-tuple-element.245), channel_id=1, source_target_pairs={{0,3},{1,0},{2,1},{3,2},{4,7},{5,4},{6,5},{7,6},{8,11},{9,8},{10,9... | collective-permute-start | bytes 1179656 | tf_op jit(solution)/shard_map/ppermute | solution.py:177
  216.6 33.8 %collective-permute-start.17 = (bf16[1,256,768]{2,1,0:T(8,128)(2,1)S(1)}, bf16[1,256,768]{2,1,0:T(8,128)(2,1)}, u32[]{:S(2)}, u32[]{:S(2)}) collective-permute-start(bf16[1,256,768]{2,1,0:T(8,128)(2,1)S(1)} %get-tuple-element.247), channel_id=1, source_target_pairs={{0,2},{1,3},{2,0},{3,1},{4,6},{5,7},{6,4},{7,5},{8,10},{9,11},{10,... | collective-permute-start | bytes 1179656 | tf_op jit(solution)/shard_map/ppermute | solution.py:177
  218.1 32.4 %copy-start.48 = (f32[768]{0:T(1024)S(1)}, f32[768]{0:T(1024)}, u32[]{:S(2)}) copy-start(f32[768]{0:T(1024)} %convert_element_type.284) | copy-start | bytes 9220
  260.7 11.5 %collective-permute-start.18 = (bf16[2,2,96,3072]{3,2,0,1:T(8,128)(2,1)}, bf16[2,2,96,3072]{3,2,0,1:T(8,128)(2,1)}, u32[]{:S(2)}, u32[]{:S(2)}) collective-permute-start(bf16[2,2,96,3072]{3,2,0,1:T(8,128)(2,1)} %bitcast.165), channel_id=1, source_target_pairs={{0,4},{4,0},{8,12},{12,8},{16,20},{20,16},{24,28},{28,24},{1,5},{5... | collective-permute-start | bytes 7077896 | tf_op jit(solution)/shard_map/ppermute | solution.py:192
  272.1 7.8 %collective-permute-start.23 = (f32[7680]{0:T(1024)S(1)}, f32[7680]{0:T(1024)S(1)}, u32[]{:S(2)}, u32[]{:S(2)}) collective-permute-start(f32[7680]{0:T(1024)S(1)} %constant_dynamic-update-slice_fusion.20), channel_id=1, source_target_pairs={{0,1},{1,0},{2,3},{3,2},{4,5},{5,4},{6,7},{7,6},{8,9},{9,8},{10,11... | collective-permute-start | bytes 92168 | tf_op jit(solution)/shard_map/ppermute | solution.py:192
  276.0 15.8 %collective-permute-start.19 = (bf16[2,96,1536]{2,1,0:T(8,128)(2,1)S(1)}, bf16[2,96,1536]{2,1,0:T(8,128)(2,1)S(1)}, u32[]{:S(2)}, u32[]{:S(2)}) collective-permute-start(bf16[2,96,1536]{2,1,0:T(8,128)(2,1)S(1)} %dynamic-slice_bitcast_fusion.4), channel_id=1, source_target_pairs={{0,16},{4,20},{8,24},{12,28},{16,0},{20,4},{24,8},{28,12},{1,17},{... | collective-permute-start | bytes 1769480 | tf_op jit(solution)/shard_map/ppermute | solution.py:192
  276.5 15.5 %collective-permute-start.20 = (bf16[2,96,1536]{2,1,0:T(8,128)(2,1)S(1)}, bf16[2,96,1536]{2,1,0:T(8,128)(2,1)S(1)}, u32[]{:S(2)}, u32[]{:S(2)}) collective-permute-start(bf16[2,96,1536]{2,1,0:T(8,128)(2,1)S(1)} %dynamic-slice_bitcast_fusion.3), channel_id=1, source_target_pairs={{0,8},{4,12},{8,0},{12,4},{16,24},{20,28},{24,16},{28,20},{1,9},{5... | collective-permute-start | bytes 1769480 | tf_op jit(solution)/shard_map/ppermute | solution.py:192
  279.9 5.7 %collective-permute-start.24 = (f32[7680]{0:T(1024)S(1)}, f32[7680]{0:T(1024)S(1)}, u32[]{:S(2)}, u32[]{:S(2)}) collective-permute-start(f32[7680]{0:T(1024)S(1)} %add.444), channel_id=1, source_target_pairs={{0,2},{1,3},{2,0},{3,1},{4,6},{5,7},{6,4},{7,5},{8,10},{9,11},{10,... | collective-permute-start | bytes 92168 | tf_op jit(solution)/shard_map/ppermute | solution.py:192
  292.4 1.3 collective-permute-start.27
  293.7 3.9 collective-permute-start.28
  294.4 28.4 %collective-permute-start.26 = (bf16[96,1536]{1,0:T(8,128)(2,1)S(1)}, bf16[96,1536]{1,0:T(8,128)(2,1)S(1)}, u32[]{:S(2)}, u32[]{:S(2)}) collective-permute-start(bf16[96,1536]{1,0:T(8,128)(2,1)S(1)} %dynamic-slice_bitcast_fusion.7), channel_id=1, source_target_pairs={{0,16},{4,20},{8,24},{12,28},{16,0},{20,4},{24,8},{28,12},{1,17},{... | collective-permute-start | bytes 884744 | tf_op jit(solution)/shard_map/ppermute | solution.py:192
  296.0 26.8 %collective-permute-start.25 = (bf16[96,1536]{1,0:T(8,128)(2,1)S(1)}, bf16[96,1536]{1,0:T(8,128)(2,1)S(1)}, u32[]{:S(2)}, u32[]{:S(2)}) collective-permute-start(bf16[96,1536]{1,0:T(8,128)(2,1)S(1)} %dynamic-slice_bitcast_fusion.8), channel_id=1, source_target_pairs={{0,8},{4,12},{8,0},{12,4},{16,24},{20,28},{24,16},{28,20},{1,9},{5... | collective-permute-start | bytes 884744 | tf_op jit(solution)/shard_map/ppermute | solution.py:192
  297.6 25.2 %collective-permute-start.29 = (f32[7680]{0:T(1024)S(1)}, f32[7680]{0:T(1024)S(1)}, u32[]{:S(2)}, u32[]{:S(2)}) collective-permute-start(f32[7680]{0:T(1024)S(1)} %add.449), channel_id=1, source_target_pairs={{0,16},{4,20},{8,24},{12,28},{16,0},{20,4},{24,8},{28,12},{1,17},{... | collective-permute-start | bytes 92168 | tf_op jit(solution)/shard_map/ppermute | solution.py:192
  322.8 45.5 %copy-start.30 = (f32[7680]{0:T(1024)}, f32[7680]{0:T(1024)S(1)}, u32[]{:S(2)}) copy-start(f32[7680]{0:T(1024)S(1)} %add.450) | copy-start | bytes 92164
  323.2 8.6 %collective-permute-start.32 = (bf16[96,768]{1,0:T(8,128)(2,1)S(1)}, bf16[96,768]{1,0:T(8,128)(2,1)S(1)}, u32[]{:S(2)}, u32[]{:S(2)}) collective-permute-start(bf16[96,768]{1,0:T(8,128)(2,1)S(1)} %get-tuple-element.276), channel_id=1, source_target_pairs={{0,1},{1,2},{2,3},{3,0},{4,5},{5,6},{6,7},{7,4},{8,9},{9,10},{10,1... | collective-permute-start | bytes 442376 | tf_op jit(solution)/shard_map/ppermute | solution.py:177
  324.0 32.7 %collective-permute-start.31 = (bf16[96,768]{1,0:T(8,128)(2,1)S(1)}, bf16[96,768]{1,0:T(8,128)(2,1)S(1)}, u32[]{:S(2)}, u32[]{:S(2)}) collective-permute-start(bf16[96,768]{1,0:T(8,128)(2,1)S(1)} %get-tuple-element.277), channel_id=1, source_target_pairs={{0,2},{1,3},{2,0},{3,1},{4,6},{5,7},{6,4},{7,5},{8,10},{9,11},{10,... | collective-permute-start | bytes 442376 | tf_op jit(solution)/shard_map/ppermute | solution.py:177
  326.1 30.7 %collective-permute-start.30 = (bf16[96,768]{1,0:T(8,128)(2,1)S(1)}, bf16[96,768]{1,0:T(8,128)(2,1)S(1)}, u32[]{:S(2)}, u32[]{:S(2)}) collective-permute-start(bf16[96,768]{1,0:T(8,128)(2,1)S(1)} %get-tuple-element.278), channel_id=1, source_target_pairs={{0,3},{1,0},{2,1},{3,2},{4,7},{5,4},{6,5},{7,6},{8,11},{9,8},{10,9... | collective-permute-start | bytes 442376 | tf_op jit(solution)/shard_map/ppermute | solution.py:177
  329.0 27.8 %collective-permute-start.35 = (bf16[96,768]{1,0:T(8,128)(2,1)S(1)}, bf16[96,768]{1,0:T(8,128)(2,1)S(1)}, u32[]{:S(2)}, u32[]{:S(2)}) collective-permute-start(bf16[96,768]{1,0:T(8,128)(2,1)S(1)} %get-tuple-element.272), channel_id=1, source_target_pairs={{0,1},{1,2},{2,3},{3,0},{4,5},{5,6},{6,7},{7,4},{8,9},{9,10},{10,1... | collective-permute-start | bytes 442376 | tf_op jit(solution)/shard_map/ppermute | solution.py:177
  329.4 27.5 %collective-permute-start.34 = (bf16[96,768]{1,0:T(8,128)(2,1)S(1)}, bf16[96,768]{1,0:T(8,128)(2,1)}, u32[]{:S(2)}, u32[]{:S(2)}) collective-permute-start(bf16[96,768]{1,0:T(8,128)(2,1)S(1)} %get-tuple-element.273), channel_id=1, source_target_pairs={{0,2},{1,3},{2,0},{3,1},{4,6},{5,7},{6,4},{7,5},{8,10},{9,11},{10,... | collective-permute-start | bytes 442376 | tf_op jit(solution)/shard_map/ppermute | solution.py:177
  331.8 25.0 %copy-start.31 = (bf16[96,768]{1,0:T(8,128)(2,1)}, bf16[96,768]{1,0:T(8,128)(2,1)S(1)}, u32[]{:S(2)}) copy-start(bf16[96,768]{1,0:T(8,128)(2,1)S(1)} %collective-permute-done.32) | copy-start | bytes 442372
  331.8 25.8 %copy-start.13 = (bf16[1024,768]{1,0:T(8,128)(2,1)S(1)}, bf16[1024,768]{1,0:T(8,128)(2,1)}, u32[]{:S(2)}) copy-start(bf16[1024,768]{1,0:T(8,128)(2,1)} %copy-done.12) | copy-start | bytes 4718596
  331.8 25.1 %collective-permute-start.33 = (bf16[96,768]{1,0:T(8,128)(2,1)S(1)}, bf16[96,768]{1,0:T(8,128)(2,1)S(1)}, u32[]{:S(2)}, u32[]{:S(2)}) collective-permute-start(bf16[96,768]{1,0:T(8,128)(2,1)S(1)} %get-tuple-element.274), channel_id=1, source_target_pairs={{0,3},{1,0},{2,1},{3,2},{4,7},{5,4},{6,5},{7,6},{8,11},{9,8},{10,9... | collective-permute-start | bytes 442376 | tf_op jit(solution)/shard_map/ppermute | solution.py:177
  368.3 12.9 %collective-permute-start.36 = (bf16[2,2,96,3072]{3,2,1,0:T(8,128)(2,1)}, bf16[2,2,96,3072]{3,2,1,0:T(8,128)(2,1)}, u32[]{:S(2)}, u32[]{:S(2)}) collective-permute-start(bf16[2,2,96,3072]{3,2,1,0:T(8,128)(2,1)} %dynamic-slice_bitcast_fusion), channel_id=1, source_target_pairs={{0,4},{4,0},{8,12},{12,8},{16,20},{20,16},{24,28},{28,24},{1,5},{5... | collective-permute-start | bytes 7077896 | tf_op jit(solution)/shard_map/ppermute | solution.py:192
  369.9 5.9 %collective-permute-start.39 = (f32[1536]{0:T(1024)S(1)}, f32[1536]{0:T(1024)S(1)}, u32[]{:S(2)}, u32[]{:S(2)}) collective-permute-start(f32[1536]{0:T(1024)S(1)} %constant_dynamic-update-slice_fusion.19), channel_id=1, source_target_pairs={{0,1},{1,0},{2,3},{3,2},{4,5},{5,4},{6,7},{7,6},{8,9},{9,8},{10,11... | collective-permute-start | bytes 18440 | tf_op jit(solution)/shard_map/ppermute | solution.py:192
  375.9 11.3 %collective-permute-start.40 = (f32[1536]{0:T(1024)S(1)}, f32[1536]{0:T(1024)S(1)}, u32[]{:S(2)}, u32[]{:S(2)}) collective-permute-start(f32[1536]{0:T(1024)S(1)} %add.457), channel_id=1, source_target_pairs={{0,2},{1,3},{2,0},{3,1},{4,6},{5,7},{6,4},{7,5},{8,10},{9,11},{10,... | collective-permute-start | bytes 18440 | tf_op jit(solution)/shard_map/ppermute | solution.py:192
  384.1 15.3 %collective-permute-start.37 = (bf16[2,96,1536]{2,1,0:T(8,128)(2,1)S(1)}, bf16[2,96,1536]{2,1,0:T(8,128)(2,1)S(1)}, u32[]{:S(2)}, u32[]{:S(2)}) collective-permute-start(bf16[2,96,1536]{2,1,0:T(8,128)(2,1)S(1)} %dynamic-slice_bitcast_fusion.2), channel_id=1, source_target_pairs={{0,16},{4,20},{8,24},{12,28},{16,0},{20,4},{24,8},{28,12},{1,17},{... | collective-permute-start | bytes 1769480 | tf_op jit(solution)/shard_map/ppermute | solution.py:192
  384.1 15.4 %collective-permute-start.38 = (bf16[2,96,1536]{2,1,0:T(8,128)(2,1)S(1)}, bf16[2,96,1536]{2,1,0:T(8,128)(2,1)S(1)}, u32[]{:S(2)}, u32[]{:S(2)}) collective-permute-start(bf16[2,96,1536]{2,1,0:T(8,128)(2,1)S(1)} %dynamic-slice_bitcast_fusion.1), channel_id=1, source_target_pairs={{0,8},{4,12},{8,0},{12,4},{16,24},{20,28},{24,16},{28,20},{1,9},{5... | collective-permute-start | bytes 1769480 | tf_op jit(solution)/shard_map/ppermute | solution.py:192
  387.2 1.2 collective-permute-start.46
  387.4 24.2 %copy-start.36 = (bf16[96,768]{1,0:T(8,128)(2,1)S(1)}, bf16[96,768]{1,0:T(8,128)(2,1)}, u32[]{:S(2)}) copy-start(bf16[96,768]{1,0:T(8,128)(2,1)} %copy-done.35) | copy-start | bytes 442372
  387.4 20.5 %collective-permute-start.41 = (bf16[1,256,768]{2,1,0:T(8,128)(2,1)S(1)}, bf16[1,256,768]{2,1,0:T(8,128)(2,1)S(1)}, u32[]{:S(2)}, u32[]{:S(2)}) collective-permute-start(bf16[1,256,768]{2,1,0:T(8,128)(2,1)S(1)} %get-tuple-element.243), channel_id=1, source_target_pairs={{0,2},{1,3},{2,0},{3,1},{4,6},{5,7},{6,4},{7,5},{8,10},{9,11},{10,... | collective-permute-start | bytes 1179656 | tf_op jit(solution)/shard_map/ppermute | solution.py:177
  388.4 23.1 %collective-permute-start.47 = (f32[1536]{0:T(1024)S(1)}, f32[1536]{0:T(1024)S(1)}, u32[]{:S(2)}, u32[]{:S(2)}) collective-permute-start(f32[1536]{0:T(1024)S(1)} %add.461), channel_id=1, source_target_pairs={{0,8},{4,12},{8,0},{12,4},{16,24},{20,28},{24,16},{28,20},{1,9},{5... | collective-permute-start | bytes 18440 | tf_op jit(solution)/shard_map/ppermute | solution.py:192
  408.0 9.2 %collective-permute-start.43 = (bf16[96,1536]{1,0:T(8,128)(2,1)S(1)}, bf16[96,1536]{1,0:T(8,128)(2,1)S(1)}, u32[]{:S(2)}, u32[]{:S(2)}) collective-permute-start(bf16[96,1536]{1,0:T(8,128)(2,1)S(1)} %dynamic-slice_bitcast_fusion.5), channel_id=1, source_target_pairs={{0,16},{4,20},{8,24},{12,28},{16,0},{20,4},{24,8},{28,12},{1,17},{... | collective-permute-start | bytes 884744 | tf_op jit(solution)/shard_map/ppermute | solution.py:192
  408.8 8.8 %collective-permute-start.42 = (bf16[96,1536]{1,0:T(8,128)(2,1)S(1)}, bf16[96,1536]{1,0:T(8,128)(2,1)S(1)}, u32[]{:S(2)}, u32[]{:S(2)}) collective-permute-start(bf16[96,1536]{1,0:T(8,128)(2,1)S(1)} %dynamic-slice_bitcast_fusion.6), channel_id=1, source_target_pairs={{0,8},{4,12},{8,0},{12,4},{16,24},{20,28},{24,16},{28,20},{1,9},{5... | collective-permute-start | bytes 884744 | tf_op jit(solution)/shard_map/ppermute | solution.py:192
  411.5 25.9 %copy-start.11 = (bf16[1,256,768]{2,1,0:T(8,128)(2,1)S(1)}, bf16[1,256,768]{2,1,0:T(8,128)(2,1)}, u32[]{:S(2)}) copy-start(bf16[1,256,768]{2,1,0:T(8,128)(2,1)} %get-tuple-element.125) | copy-start | bytes 1179652
  411.5 5.8 %collective-permute-start.48 = (f32[1536]{0:T(1024)S(1)}, f32[1536]{0:T(1024)S(1)}, u32[]{:S(2)}, u32[]{:S(2)}) collective-permute-start(f32[1536]{0:T(1024)S(1)} %add.462), channel_id=1, source_target_pairs={{0,16},{4,20},{8,24},{12,28},{16,0},{20,4},{24,8},{28,12},{1,17},{... | collective-permute-start | bytes 18440 | tf_op jit(solution)/shard_map/ppermute | solution.py:192
  413.3 13.8 %collective-permute-start.45 = (bf16[1,256,768]{2,1,0:T(8,128)(2,1)S(1)}, bf16[1,256,768]{2,1,0:T(8,128)(2,1)S(1)}, u32[]{:S(2)}, u32[]{:S(2)}) collective-permute-start(bf16[1,256,768]{2,1,0:T(8,128)(2,1)S(1)} %get-tuple-element.240), channel_id=1, source_target_pairs={{0,1},{1,2},{2,3},{3,0},{4,5},{5,6},{6,7},{7,4},{8,9},{9,10},{10,1... | collective-permute-start | bytes 1179656 | tf_op jit(solution)/shard_map/ppermute | solution.py:177
  413.3 19.0 %collective-permute-start.44 = (bf16[1,256,768]{2,1,0:T(8,128)(2,1)S(1)}, bf16[1,256,768]{2,1,0:T(8,128)(2,1)S(1)}, u32[]{:S(2)}, u32[]{:S(2)}) collective-permute-start(bf16[1,256,768]{2,1,0:T(8,128)(2,1)S(1)} %get-tuple-element.242), channel_id=1, source_target_pairs={{0,3},{1,0},{2,1},{3,2},{4,7},{5,4},{6,5},{7,6},{8,11},{9,8},{10,9... | collective-permute-start | bytes 1179656 | tf_op jit(solution)/shard_map/ppermute | solution.py:177
  432.6 10.6 %collective-permute-start.49 = (bf16[96,768]{1,0:T(8,128)(2,1)S(1)}, bf16[96,768]{1,0:T(8,128)(2,1)S(1)}, u32[]{:S(2)}, u32[]{:S(2)}) collective-permute-start(bf16[96,768]{1,0:T(8,128)(2,1)S(1)} %pad_maximum_fusion.6), channel_id=1, source_target_pairs={{0,3},{1,0},{2,1},{3,2},{4,7},{5,4},{6,5},{7,6},{8,11},{9,8},{10,9... | collective-permute-start | bytes 442376 | tf_op jit(solution)/shard_map/ppermute | solution.py:177
  434.8 12.8 %collective-permute-start.50 = (bf16[96,768]{1,0:T(8,128)(2,1)S(1)}, bf16[96,768]{1,0:T(8,128)(2,1)S(1)}, u32[]{:S(2)}, u32[]{:S(2)}) collective-permute-start(bf16[96,768]{1,0:T(8,128)(2,1)S(1)} %pad_maximum_fusion.7), channel_id=1, source_target_pairs={{0,2},{1,3},{2,0},{3,1},{4,6},{5,7},{6,4},{7,5},{8,10},{9,11},{10,... | collective-permute-start | bytes 442376 | tf_op jit(solution)/shard_map/ppermute | solution.py:177
  435.3 12.3 %collective-permute-start.51 = (bf16[96,768]{1,0:T(8,128)(2,1)S(1)}, bf16[96,768]{1,0:T(8,128)(2,1)S(1)}, u32[]{:S(2)}, u32[]{:S(2)}) collective-permute-start(bf16[96,768]{1,0:T(8,128)(2,1)S(1)} %pad_maximum_fusion.8), channel_id=1, source_target_pairs={{0,1},{1,2},{2,3},{3,0},{4,5},{5,6},{6,7},{7,4},{8,9},{9,10},{10,1... | collective-permute-start | bytes 442376 | tf_op jit(solution)/shard_map/ppermute | solution.py:177
  (58 other events, 363.1 us)
Sparse Core Ops, SparseCore 0:
  65.3 64.8 all-gather.1
  210.4 53.3 reduce-scatter.1

commit v5 on v4

--- a/solution.py
+++ b/solution.py
@@ -108,7 +108,7 @@
             bytes_accessed=8 * count * width * length,
         ),
         name="attend",
-    )(queries, keys_all, values, ids[:, None, :], ids[:, :, None])
+    )(queries, keys_all, values, *ids)
 
 
 def attend_back(queries, keys_all, values, grad_context, logsum, ids, earlier, part):
@@ -117,7 +117,7 @@
     first = pairs // 2 * part
     rows, as_row, as_col, sums = attention_specs(length, first)
     body = functools.partial(attend_back_kernel, scaling=HDIM ** (-0.5))
-    operands = [queries, keys_all, values, grad_context, logsum, ids[:, None, :], ids[:, :, None]]
+    operands = [queries, keys_all, values, grad_context, logsum, *ids]
     in_specs = [rows, rows, rows, rows, sums, as_row, as_col]
     aliases = {}
     if earlier is not None:
@@ -206,56 +206,57 @@
     ]
 
 
-def gather_rows(members, block, before, beyond):
+def together(*groups):
+    return lax.optimization_barrier(tuple(list(group) for group in groups))
+
+
+def gather_rows(members, block, before, beyond, fillers):
     if members != 8:
-        return lax.all_gather(block, "fsdp", axis=0, tiled=True), before, beyond
+        return lax.all_gather(block, "fsdp", axis=0, tiled=True), before, beyond, fillers
     rows, cols = block.shape
     first, second = block[:, : cols // 2], block[:, cols // 2 :]
-    (over_x, over_y), beyond = meet(
-        (flip("fsdp", members, 2, first), flip("fsdp", members, 4, second)), beyond, (2, 3)
-    )
-    first, second = beside(2, first, over_x, 0), beside(4, second, over_y, 0)
-    (over_y, over_x), before = meet(
-        (flip("fsdp", members, 4, first), flip("fsdp", members, 2, second)), before, (1, 2)
-    )
-    both = jnp.concatenate([beside(4, first, over_y, 0), beside(2, second, over_x, 1)], axis=3)
-    other, before = meet(flip("fsdp", members, 1, both), before, (3,))
-    return beside(1, both, other, 2).reshape(members * rows, cols), before, beyond
+    near = (flip("fsdp", members, 2, first), flip("fsdp", members, 4, second))
+    near, beyond, fillers = together(near, beyond, fillers)
+    first, second = beside(2, first, near[0], 0), beside(4, second, near[1], 0)
+    far = (flip("fsdp", members, 4, first), flip("fsdp", members, 2, second))
+    far, before[:3] = together(far, before[:3])
+    both = jnp.concatenate([beside(4, first, far[0], 0), beside(2, second, far[1], 1)], axis=3)
+    (other,), before[3:] = together((flip("fsdp", members, 1, both),), before[3:])
+    return beside(1, both, other, 2).reshape(members * rows, cols), before, beyond, fillers
 
 
 def add_low(kept, moved):
     return (kept.astype(WIDE) + moved.astype(WIDE)).astype(LOW)
 
 
-def scatter_core(grad):
+def scatter_core(grad, others=()):
     if lax.axis_size("fsdp") != 8:
-        return lax.psum_scatter(grad, "fsdp", scatter_dimension=0, tiled=True)
+        return lax.psum_scatter(grad, "fsdp", scatter_dimension=0, tiled=True), others
     total_rows, cols = grad.shape
     kept, theirs = entries(1, grad.reshape(2, 2, 2, total_rows // 8, cols), 2)
-    return add_low(kept, flip("fsdp", 8, 1, theirs))
-
-
-def scatter_near(grad):
+    (moved,), others = together((flip("fsdp", 8, 1, theirs),), others)
+    return add_low(kept, moved), others
+
+
+def scatter_near(grad, others=()):
     if lax.axis_size("fsdp") != 8:
-        return grad
+        return grad, others
     half = grad.shape[-1] // 2
     first, first_out = entries(4, grad[..., :half], 0)
     second, second_out = entries(2, grad[..., half:], 1)
-    over_y, over_x = lax.optimization_barrier(
-        (flip("fsdp", 8, 4, first_out), flip("fsdp", 8, 2, second_out))
-    )
-    return add_low(first, over_y), add_low(second, over_x)
-
-
-def scatter_far(grad):
+    moved = (flip("fsdp", 8, 4, first_out), flip("fsdp", 8, 2, second_out))
+    moved, others = together(moved, others)
+    return (add_low(first, moved[0]), add_low(second, moved[1])), others
+
+
+def scatter_far(grad, others=()):
     if lax.axis_size("fsdp") != 8:
-        return grad
+        return grad, others
     first, first_out = entries(2, grad[0], 0)
     second, second_out = entries(4, grad[1], 0)
-    over_x, over_y = lax.optimization_barrier(
-        (flip("fsdp", 8, 2, first_out), flip("fsdp", 8, 4, second_out))
-    )
-    return jnp.concatenate([add_low(first, over_x), add_low(second, over_y)], axis=1)
+    moved = (flip("fsdp", 8, 2, first_out), flip("fsdp", 8, 4, second_out))
+    moved, others = together(moved, others)
+    return jnp.concatenate([add_low(first, moved[0]), add_low(second, moved[1])], axis=1), others
 
 
 def total_over_tp(vector):
@@ -373,15 +374,6 @@
     query_bias_full = jnp.concatenate([part[:head_cols] for part in biases])
     value_bias_full = jnp.concatenate([part[head_cols : 2 * head_cols] for part in biases])
     inner_bias_full = jnp.concatenate([part[2 * head_cols :] for part in biases])
-    heads, rows, rest = gather_rows(fsdp, columns(heads, (head_cols,) * 4), rows, rest)
-    query_full, key_full, value_full, output_turned = (
-        heads[:, i * width : (i + 1) * width] for i in range(4)
-    )
-    rows = whole_rows(rows)
-    rows, out_grad = lax.optimization_barrier((rows, out_grad))
-    rest = lax.all_gather(columns(rest, (unit_cols, unit_cols)), "fsdp", axis=0, tiled=True)
-    inner_full, outer_turned = rest[:, : tp * unit_cols], rest[:, tp * unit_cols :]
-
     first = rank * count
     segment = lax.dynamic_slice_in_dim(segment_ids, first, count, 0)
     live = lax.dynamic_slice_in_dim(live_mask, first, count, 0)
@@ -389,6 +381,19 @@
     ids = jnp.where(live == 1, segment, length + spots).reshape(count, tp, places)
     ids = [lax.dynamic_slice_in_dim(ids, (rank - step) % tp, 1, 1) for step in range(tp)]
     ids = jnp.concatenate(ids, axis=1).reshape(count, length)
+    ids = (ids[:, None, :], ids[:, :, None])
+    fillers = (*ids, query_bias_full, value_bias_full, inner_bias_full)
+    heads, rows, rest, fillers = gather_rows(
+        fsdp, columns(heads, (head_cols,) * 4), rows, rest, fillers
+    )
+    *ids, query_bias_full, value_bias_full, inner_bias_full = fillers
+    query_full, key_full, value_full, output_turned = (
+        heads[:, i * width : (i + 1) * width] for i in range(4)
+    )
+    rows = whole_rows(rows)
+    rows, out_grad = lax.optimization_barrier((rows, out_grad))
+    rest = lax.all_gather(columns(rest, (unit_cols, unit_cols)), "fsdp", axis=0, tiled=True)
+    inner_full, outer_turned = rest[:, : tp * unit_cols], rest[:, tp * unit_cols :]
 
     shape = (count, length, width)
     queries = (dot(rows, query_full, BY_ROWS) + query_bias_full).astype(LOW).reshape(shape)
@@ -422,9 +427,10 @@
     outer_share = lax.psum_scatter(outer_grad, "fsdp", scatter_dimension=0, tiled=True)
     grad_activ = dot(grad_branch, outer_turned, BY_ROWS)
     grad_pre = (grad_activ * slope).astype(LOW)
-    grad_pre, layer_out = meet(grad_pre, layer_out, (2,))
     inner_bias_grad = jnp.sum(grad_pre.astype(WIDE), axis=0)
-    inner_share = scatter_core(dot(first_low, grad_pre, BY_FIRST).astype(LOW))
+    inner_share, layer_out[:3] = scatter_core(
+        dot(first_low, grad_pre, BY_FIRST).astype(LOW), layer_out[:3]
+    )
     grad_first = grad_second + dot(grad_pre, inner_full, BY_LAST)
     grad_mixed, first_gain_grad, first_shift_grad = normalize_back(
         grad_first, first_normed, first_scaling, first_gain.astype(WIDE)
@@ -447,10 +453,10 @@
         )
     )
     grad_context, inner_share, output_grad, layer_out, early = lax.optimization_barrier(
-        (grad_context, scatter_near(inner_share), output_grad, layer_out, early)
+        (grad_context, scatter_near(inner_share)[0], output_grad, layer_out, early)
     )
     early = total_over_fsdp(early)
-    inner_share = scatter_far(inner_share)
+    inner_share, _ = scatter_far(inner_share)
     back = functools.partial(attend_back, queries, keys_all, values, grad_context, logsum, ids)
     halfway = back(None, 0)
     halfway, inner_share, outer_share, early = lax.optimization_barrier(
@@ -468,28 +474,28 @@
     query_rows_grad, key_rows_grad, value_rows_grad = (
         array.reshape(count * length, width) for array in rows_grads
     )
-    query_bias_grad = jnp.sum(query_rows_grad.astype(WIDE), axis=0)
-    value_bias_grad = jnp.sum(value_rows_grad.astype(WIDE), axis=0)
-    late = total_over_tp(
-        jnp.concatenate([by_rank(query_bias_grad), by_rank(value_bias_grad)])
-    )
     head_grads = [
         dot(rows, grad, BY_FIRST).astype(LOW)
         for grad in (query_rows_grad, key_rows_grad, value_rows_grad)
     ]
-    heads_share = scatter_core(jnp.concatenate(head_grads + [output_grad], axis=1))
     tokens_grad = (
         grad_mixed
         + dot(query_rows_grad, query_full, BY_LAST)
         + dot(key_rows_grad, key_full, BY_LAST)
         + dot(value_rows_grad, value_full, BY_LAST)
     ).astype(LOW)
-    tokens_grad, late = lax.optimization_barrier((tokens_grad, late))
+    late = [by_rank(jnp.sum(grad.astype(WIDE), axis=0)) for grad in (query_rows_grad, value_rows_grad)]
+    heads_share, (tokens_grad, late) = scatter_core(
+        jnp.concatenate(head_grads + [output_grad], axis=1), (tokens_grad, jnp.concatenate(late))
+    )
     tokens_grad = to_owners(tokens_grad)
-    late = total_over_fsdp(late)
-    heads_share, tokens_grad = meet(scatter_near(heads_share), tokens_grad, (2,))
-    heads_share, tokens_grad = meet(scatter_far(heads_share), tokens_grad, (1, 3))
-    heads_share, late = lax.optimization_barrier((heads_share, late))
+    late = late + flip("fsdp", fsdp, 1, late) if fsdp == 8 else lax.psum(late, "fsdp")
+    heads_share, tokens_grad[:3] = scatter_near(heads_share, tokens_grad[:3])
+    late = late + flip("fsdp", fsdp, 2, late) if fsdp == 8 else late
+    heads_share, tokens_grad[3:] = scatter_far(heads_share, tokens_grad[3:])
+    late = late + flip("fsdp", fsdp, 4, late) if fsdp == 8 else late
+    late = spread(late)
+    late = jnp.sum(by_source(late[:1] + late[:0:-1]), axis=0)
     query_share, key_share, value_share, output_share = summed(
         own_columns(heads_share, (head_cols,) * 4), (head_cols,) * 4
     )

time: 465 us -> 449 us (0.966)
  waiting for transfers between devices: 132 us -> 94 us
  starting transfers between devices: 61.5 us -> 82.8 us
  matrix products: 80.1 us -> 88.2 us
  local copies, waits for them, and re-layouts: 42.3 us -> 35.7 us
    ppermute x15, waiting for transfers between devices: 46.6 us -> 18.5 us  [sent_back(): moved.append(lax.ppermute(parts[step], 'tp', pairs))]
    ppermute x6 -> x9, starting transfers between devices: 11 us -> 26.2 us  [spread(): return [block] + [lax.ppermute(block, 'tp', pairs) for pairs in rank_pairs]]
    ppermute x25 -> x23, waiting for transfers between devices: 19.5 us -> 8.21 us  [flip(): return lax.ppermute(block, axis, [(i, i ^ bit) for i in range(members)])]
    ppermute x15, starting transfers between devices: 21.8 us -> 31.3 us  [sent_back(): moved.append(lax.ppermute(parts[step], 'tp', pairs))]
    dot_general x18, matrix products: 80.1 us -> 88.2 us  [dot(): return lax.dot_general(left, right, dims, preferred_element_type=WIDE)]
    ppermute x6 -> x9, waiting for transfers between devices: 34 us -> 38.5 us  [spread(): return [block] + [lax.ppermute(block, 'tp', pairs) for pairs in rank_pairs]]
    ppermute x25 -> x23, starting transfers between devices: 26 us -> 22.4 us  [flip(): return lax.ppermute(block, axis, [(i, i ^ bit) for i in range(members)])]
    unnamed x161 -> x136, local copies, waits for them, and re-layouts: 13.2 us -> 12.9 us
  transfers between devices with their start and end apart: 54 -> 55, of which waited for: 21 -> 19; matrix products, arithmetic and copies ran while one was open for 27% -> 23% of each run, Pallas kernels for 17% -> 17%
where the time goes in v5:
time: 449 us; the launch traced here: 441 us
  waiting for transfers between devices  94 us (21%)
  matrix products  88.2 us (20%)
  starting transfers between devices  82.8 us (18%)
  Pallas kernels  76.6 us (17%)
  other arithmetic  48 us (11%)
  local copies, waits for them, and re-layouts  35.7 us (8%)
  between operations  16.1 us (4%)
    dot_general x18, matrix products, dot(): return lax.dot_general(left, right, dims, preferred_element_type=WIDE)  88.2 us
    pallas_call x2, Pallas kernels, attend_back(): pl.pallas_call(body, grid=(count, pairs - first if part else pairs // 2),...  46.6 us
    ppermute x9, waiting for transfers between devices, spread(): return [block] + [lax.ppermute(block, 'tp', pairs) for pairs in rank_pairs]  38.5 us
    ppermute x15, starting transfers between devices, sent_back(): moved.append(lax.ppermute(parts[step], 'tp', pairs))  31.3 us
    pallas_call x1, Pallas kernels, attend(): pl.pallas_call(functools.partial(attend_kernel, scaling=scaling), grid=(c...  30 us
    ppermute x6, waiting for transfers between devices, dealt(): parts.append(lax.ppermute(block, 'tp', pairs) if step else block)  28.6 us
    ppermute x9, starting transfers between devices, spread(): return [block] + [lax.ppermute(block, 'tp', pairs) for pairs in rank_pairs]  26.2 us
    ppermute x23, starting transfers between devices, flip(): return lax.ppermute(block, axis, [(i, i ^ bit) for i in range(members)])  22.4 us
  transfers between devices with their start and end apart: 55, of which 19 were waited for; matrix products, arithmetic and copies ran while one was open for 23% of the time, Pallas kernels for 17%

profile of v5, /device:TPU:0, one launch (start us, length us, event | category | flops | bytes accessed | tf_op | source)
XLA Modules:
  0.0 441.4 jit_solution(9367436217887328523)
XLA Ops:
  7.2 2.1 concatenate.81
  13.2 5.1 %collective-permute-start.2 = (bf16[99,768]{0,1:T(8,128)(2,1)S(1)}, bf16[99,768]{0,1:T(8,128)(2,1)S(1)}, u32[]{:S(2)}, u32[]{:S(2)}) collective-permute-start(bf16[99,768]{0,1:T(8,128)(2,1)S(1)} %fusion.94), channel_id=1, source_target_pairs={{0,3},{1,0},{2,1},{3,2},{4,7},{5,4},{6,5},{7,6},{8,11},{9,8},{10,9... | collective-permute-start | bytes 456200 | tf_op jit(solution)/shard_map/ppermute | solution.py:159
  21.8 1.8 collective-permute-done.2
  23.7 11.4 %collective-permute-done.1 = bf16[99,768]{0,1:T(8,128)(2,1)S(1)} collective-permute-done((bf16[99,768]{0,1:T(8,128)(2,1)S(1)}, bf16[99,768]{0,1:T(8,128)(2,1)S(1)}, u32[]{:S(2)}, u32[]{:S(2)}) %collective-permute-start.1) | collective-permute-done | bytes 152096 | tf_op jit(solution)/shard_map/ppermute | solution.py:159
  35.7 2.6 collective-permute-start.6
  38.3 1.9 collective-permute-start.5
  41.7 1.6 collective-permute-start.4
  46.7 12.0 %collective-permute-done.5 = bf16[96,1536]{1,0:T(8,128)(2,1)} collective-permute-done((bf16[96,1536]{1,0:T(8,128)(2,1)S(1)}, bf16[96,1536]{1,0:T(8,128)(2,1)}, u32[]{:S(2)}, u32[]{:S(2)}) %collective-permute-start.5) | collective-permute-done | bytes 294944 | tf_op jit(solution)/shard_map/ppermute | solution.py:159
  58.7 4.9 %collective-permute-done.6 = bf16[96,1536]{1,0:T(8,128)(2,1)S(1)} collective-permute-done((bf16[96,1536]{1,0:T(8,128)(2,1)S(1)}, bf16[96,1536]{1,0:T(8,128)(2,1)S(1)}, u32[]{:S(2)}, u32[]{:S(2)}) %collective-permute-start.6) | collective-permute-done | bytes 294944 | tf_op jit(solution)/shard_map/ppermute | solution.py:159
  72.5 1.6 collective-permute-start.8
  75.0 25.6 %collective-permute-done.11 = bf16[1,256,768]{2,1,0:T(8,128)(2,1)S(1)} collective-permute-done((bf16[1,256,768]{2,1,0:T(8,128)(2,1)S(1)}, bf16[1,256,768]{2,1,0:T(8,128)(2,1)S(1)}, u32[]{:S(2)}, u32[]{:S(2)}) %collective-permute-start.11) | collective-permute-done | bytes 393248 | tf_op jit(solution)/shard_map/ppermute | solution.py:168
  112.6 3.0 collective-permute-done.13
  117.8 2.1 collective-permute-start.16
  120.5 2.2 bitcast_select_fusion
  122.7 2.8 fusion.65.k_ref.refs_1_
  125.4 2.6 fusion.37.v_ref.refs_2_
  128.0 2.5 fusion.36.q_ref.refs_0_
  130.6 30.0 %attend.1 = (bf16[1,1024,768]{2,1,0:T(8,128)(2,1)}, f32[1,6,2,1024]{3,2,1,0:T(2,128)}) custom-call(bf16[1,1024,768]{2,1,0:T(8,128)(2,1)} %fusion.36.q_ref.refs_0_, bf16[1,1024,768]{2,1,0:T(8,128)(2,1)} %fusion.65.k_ref.refs_1_, bf16[1,1024,768]{2,1,0:T(8,128)(2,1)} %fusion.37.v_ref.refs_2_, s32[1,1,1024]{2,1,0:T(1,128)} %broadcast_in_dim_reshape.6.row_ref.refs_5_, ...), custom_call_target="tpu_custom_call" | custom-call | flops 22548578304 | bytes 6291456 | tf_op jit(solution)/shard_map/attend/pallas_call | solution.py:96
  161.4 3.8 fusion.114
  165.7 11.3 %multiply_convert_fusion = (bf16[1024,3072]{1,0:T(8,128)(2,1)S(1)}, f32[1024,3072]{1,0:T(8,128)}) fusion(f32[3072]{0:T(1024)} %pad_maximum_fusion.9, bf16[768,6144]{1,0:T(8,128)(2,1)} %all-gather.2.cloned.1.call-done, f32[1024,768]{1,0:T(8,128)S(1)} %get-tuple-element.362, f32[768]{0:T(1024)} %convert_element_type.284, f32[768]{0:T(1024)S(1)} %convert_element_type.283, ...), kind=kOutput, calls=%fused_computation.8 | convolution fusion | flops 4854644736 | bytes 26766336 | tf_op jit(solution)/shard_map/dot_general | solution.py:22
  177.2 5.4 %fusion.115 = (f32[1024]{0:T(1024)S(1)}, f32[1024,768]{1,0:T(8,128)S(1)}) fusion(f32[768]{0:T(1024)S(1)} %copy-done.39, bf16[1024,3072]{1,0:T(8,128)(2,1)S(1)} %get-tuple-element.129, bf16[768,6144]{1,0:T(8,128)(2,1)S(1)} %copy-done.46, f32[768]{0:T(1024)S(1)} %copy-done.38, f32[768]{0:T(1024)S(1)} %convert_element_type.283, ...), kind=kOutput, calls=%fused_computation.265 | convolution fusion | flops 4837342208 | bytes 17326080 | tf_op jit(solution)/shard_map/dot_general | solution.py:22
  183.6 5.3 %fusion.29 = (f32[768]{0:T(1024)}, f32[1024]{0:T(1024)S(1)}, f32[1024]{0:T(1024)S(1)}, bf16[1024,768]{1,0:T(8,128)(2,1)}) fusion(f32[1024,768]{1,0:T(8,128)S(1)} %get-tuple-element.366, f32[1024]{0:T(1024)S(1)} %add_rsqrt_fusion, f32[1024]{0:T(1024)S(1)} %broadcast_multiply_fusion.4, bf16[1,256,768]{2,1,0:T(8,128)(2,1)} %collective-permute-done.16, ...), kind=kLoop, calls=%fused_computation.44 | loop fusion | flops 14939392 | bytes 6317056 | tf_op jit(solution)/shard_map/reduce_sum | solution.py:288
  188.9 4.7 %fusion.99 = (f32[768]{0:T(1024)}, f32[1024,768]{1,0:T(8,128)}) fusion(f32[1024]{0:T(1024)S(1)} %broadcast_multiply_fusion.2, f32[1024,768]{1,0:T(8,128)S(1)} %get-tuple-element.366, f32[1024]{0:T(1024)S(1)} %broadcast_multiply_fusion.4, f32[1024]{0:T(1024)S(1)} %broadcast_multiply_fusion.3, f32[768]{0:T(1024)S(1)} %convert_element_type.290, ...), kind=kLoop, calls=%fused_computation.250 | loop fusion | flops 12582144 | bytes 7886848 | tf_op jit(solution)/shard_map/reduce_sum | solution.py:424
  193.6 8.8 %convolution_convert_fusion = bf16[768,3072]{1,0:T(8,128)(2,1)} fusion(bf16[1024,3072]{1,0:T(8,128)(2,1)S(1)} %get-tuple-element.129, f32[1024,768]{1,0:T(8,128)} %get-tuple-element.261), kind=kOutput, calls=%fused_computation.13 | convolution fusion | flops 4834983936 | bytes 14155776 | tf_op jit(solution)/shard_map/dot_general | solution.py:22
  202.4 15.5 %convert_reduce_fusion = (f32[3072]{0:T(1024)}, bf16[1024,3072]{1,0:T(8,128)(2,1)}) fusion(f32[1024,3072]{1,0:T(8,128)} %get-tuple-element.364, f32[3072]{0:T(1024)S(1)} %copy-done.37, bf16[768,6144]{1,0:T(8,128)(2,1)} %all-gather.2.cloned.1.call-done, f32[1024,768]{1,0:T(8,128)} %get-tuple-element.261), kind=kOutput, calls=%fused_computation.7 | convolution fusion | flops 4873516032 | bytes 26763264 | tf_op jit(solution)/shard_map/dot_general | solution.py:22
  220.0 8.7 %convolution_convert_fusion.1 = bf16[768,3072]{1,0:T(8,128)(2,1)S(1)} fusion(bf16[1024,3072]{1,0:T(8,128)(2,1)} %get-tuple-element.369, f32[1024,768]{1,0:T(8,128)S(1)} %get-tuple-element.362, f32[768]{0:T(1024)} %convert_element_type.284, f32[768]{0:T(1024)} %copy-done.30, f32[1024]{0:T(1024)} %copy-done.32, f32[1024]{0:T(1024)S(1)} %broadcast_multiply_fusion.5), kind=kOutput, calls=%fused_computation.14 | convolution fusion | flops 4838129664 | bytes 14170112 | tf_op jit(solution)/shard_map/dot_general | solution.py:22
  229.6 2.3 collective-permute-start.19
  231.9 3.7 collective-permute-start.18
  237.2 9.3 %multiply_reduce_fusion = (f32[768]{0:T(1024)S(1)}, f32[1024]{0:T(1024)S(1)}, f32[1024]{0:T(1024)S(1)}, f32[768]{0:T(1024)S(1)}, f32[1024,768]{1,0:T(8,128)S(1)}) fusion(f32[1024,768]{1,0:T(8,128)S(1)} %get-tuple-element.362, f32[1024]{0:T(1024)S(1)} %copy-done.33, f32[1024]{0:T(1024)S(1)} %broadcast_multiply_fusion.5, f32[768]{0:T(1024)S(1)} %copy-done.31, ...), kind=kOutput, calls=%fused_computation.48 | convolution fusion | flops 4839698432 | bytes 20472832 | tf_op jit(solution)/shard_map/dot_general | solution.py:22
  248.0 2.0 convert_reduce_fusion.1
  254.8 6.4 %collective-permute-start.24 = (f32[7680]{0:T(1024)S(1)}, f32[7680]{0:T(1024)S(1)}, u32[]{:S(2)}, u32[]{:S(2)}) collective-permute-start(f32[7680]{0:T(1024)S(1)} %add.443), channel_id=1, source_target_pairs={{0,2},{1,3},{2,0},{3,1},{4,6},{5,7},{6,4},{7,5},{8,10},{9,11},{10,... | collective-permute-start | bytes 92168 | tf_op jit(solution)/shard_map/ppermute | solution.py:192
  261.2 3.8 fusion.66.g_ref.refs_3_
  265.0 4.4 %collective-permute-start.22 = (bf16[1,256,768]{2,1,0:T(8,128)(2,1)S(1)}, bf16[1,256,768]{2,1,0:T(8,128)(2,1)}, u32[]{:S(2)}, u32[]{:S(2)}) collective-permute-start(bf16[1,256,768]{2,1,0:T(8,128)(2,1)S(1)} %get-tuple-element.275), channel_id=1, source_target_pairs={{0,1},{1,2},{2,3},{3,0},{4,5},{5,6},{6,7},{7,4},{8,9},{9,10},{10,1... | collective-permute-start | bytes 1179656 | tf_op jit(solution)/shard_map/ppermute | solution.py:177
  269.4 3.3 collective-permute-done.20
  273.1 5.1 %collective-permute-done.22 = bf16[1,256,768]{2,1,0:T(8,128)(2,1)} collective-permute-done((bf16[1,256,768]{2,1,0:T(8,128)(2,1)S(1)}, bf16[1,256,768]{2,1,0:T(8,128)(2,1)}, u32[]{:S(2)}, u32[]{:S(2)}) %collective-permute-start.22) | collective-permute-done | bytes 393248 | tf_op jit(solution)/shard_map/ppermute | solution.py:177
  281.0 1.7 collective-permute-start.26
  284.3 23.1 %attend_back.2 = (bf16[1,1024,768]{2,1,0:T(8,128)(2,1)}, bf16[1,1024,768]{2,1,0:T(8,128)(2,1)}, bf16[1,1024,768]{2,1,0:T(8,128)(2,1)}) custom-call(bf16[1,1024,768]{2,1,0:T(8,128)(2,1)} %fusion.36.q_ref.refs_0_, bf16[1,1024,768]{2,1,0:T(8,128)(2,1)} %fusion.65.k_ref.refs_1_, bf16[1,1024,768]{2,1,0:T(8,128)(2,1)} %fusion.37.v_ref.refs_2_, ...), custom_call_target="tpu_custom_call" | custom-call | flops 19327352832 | bytes 5505024 | tf_op jit(solution)/shard_map/attend_back/pallas_call | solution.py:131
  308.4 4.5 %collective-permute-start.32 = (bf16[96,768]{1,0:T(8,128)(2,1)}, bf16[96,768]{1,0:T(8,128)(2,1)}, u32[]{:S(2)}, u32[]{:S(2)}) collective-permute-start(bf16[96,768]{1,0:T(8,128)(2,1)} %get-tuple-element.291), channel_id=1, source_target_pairs={{0,1},{1,2},{2,3},{3,0},{4,5},{5,6},{6,7},{7,4},{8,9},{9,10},{10,1... | collective-permute-start | bytes 442376 | tf_op jit(solution)/shard_map/ppermute | solution.py:177
  312.9 3.4 collective-permute-start.31
  316.3 1.9 fusion.104
  318.2 2.0 collective-permute-start.35
  320.3 23.5 %attend_back.3 = (bf16[1,1024,768]{2,1,0:T(8,128)(2,1)}, bf16[1,1024,768]{2,1,0:T(8,128)(2,1)}, bf16[1,1024,768]{2,1,0:T(8,128)(2,1)}) custom-call(bf16[1,1024,768]{2,1,0:T(8,128)(2,1)} %fusion.36.q_ref.refs_0_, bf16[1,1024,768]{2,1,0:T(8,128)(2,1)} %fusion.65.k_ref.refs_1_, ...), custom_call_target="tpu_custom_call", output_to_operand_aliasing={{0}: (7, {}), {1}: (8, {}), {2}: (9, {})} | custom-call | flops 19327352832 | bytes 5505024 | tf_op jit(solution)/shard_map/attend_back/pallas_call | solution.py:131
  343.7 2.3 collective-permute-start.33
  346.7 2.4 collective-permute-done.33
  349.8 3.0 fusion.59
  356.7 2.2 copy-done
  358.9 1.6 dynamic-slice_bitcast_fusion
  361.5 3.3 fusion.46
  368.5 2.6 fusion.6
  372.6 2.6 collective-permute-start.40
  375.2 1.8 collective-permute-start.39
  378.0 2.7 collective-permute-done.49
  380.7 2.9 collective-permute-start.52
  384.7 8.4 %collective-permute-done.52 = f32[1536]{0:T(1024)S(1)} collective-permute-done((f32[1536]{0:T(1024)S(1)}, f32[1536]{0:T(1024)S(1)}, u32[]{:S(2)}, u32[]{:S(2)}) %collective-permute-start.52) | collective-permute-done | bytes 6176 | tf_op jit(solution)/shard_map/ppermute | solution.py:159
  393.1 8.6 %collective-permute-start.51 = (f32[1536]{0:T(1024)S(1)}, f32[1536]{0:T(1024)S(1)}, u32[]{:S(2)}, u32[]{:S(2)}) collective-permute-start(f32[1536]{0:T(1024)S(1)} %add.463), channel_id=1, source_target_pairs={{0,2},{1,3},{2,0},{3,1},{4,6},{5,7},{6,4},{7,5},{8,10},{9,11},{10,... | collective-permute-start | bytes 18440 | tf_op jit(solution)/shard_map/ppermute | solution.py:159
  401.6 1.8 convert_add_fusion.10
  403.5 3.7 collective-permute-start.50
  407.2 1.8 add_bitcast_fusion
  409.0 2.0 collective-permute-start.43
  412.2 1.7 collective-permute-start.41
  415.3 5.7 %collective-permute-done.43 = bf16[1,256,768]{2,1,0:T(8,128)(2,1)S(1)} collective-permute-done((bf16[1,256,768]{2,1,0:T(8,128)(2,1)S(1)}, bf16[1,256,768]{2,1,0:T(8,128)(2,1)S(1)}, u32[]{:S(2)}, u32[]{:S(2)}) %collective-permute-start.43) | collective-permute-done | bytes 393248 | tf_op jit(solution)/shard_map/ppermute | solution.py:177
  421.9 2.1 collective-permute-start.46
  424.0 4.0 fusion.38
  428.3 4.1 collective-permute-done.45
  (357 shorter events, 74.1 us)
Async XLA Ops:
  7.2 34.3 %copy-start.26 = (bf16[192,96]{1,0:T(8,128)(2,1)S(1)}, bf16[192,96]{1,0:T(8,128)(2,1)}, u32[]{:S(2)}) copy-start(bf16[192,96]{1,0:T(8,128)(2,1)} %param.27) | copy-start | bytes 110596
  7.2 158.5 %all-gather.2.cloned.1.call-start = ((), (), s32[]{:S(2)}) async-start(), calls=%async_computation.1 | async-start | bytes 10616832 | tf_op jit(solution)/shard_map/all_gather | solution.py:395
  13.2 10.5 %collective-permute-start.2 = (bf16[99,768]{0,1:T(8,128)(2,1)S(1)}, bf16[99,768]{0,1:T(8,128)(2,1)S(1)}, u32[]{:S(2)}, u32[]{:S(2)}) collective-permute-start(bf16[99,768]{0,1:T(8,128)(2,1)S(1)} %fusion.94), channel_id=1, source_target_pairs={{0,3},{1,0},{2,1},{3,2},{4,7},{5,4},{6,5},{7,6},{8,11},{9,8},{10,9... | collective-permute-start | bytes 456200 | tf_op jit(solution)/shard_map/ppermute | solution.py:159
  18.3 16.7 %collective-permute-start.1 = (bf16[99,768]{0,1:T(8,128)(2,1)S(1)}, bf16[99,768]{0,1:T(8,128)(2,1)S(1)}, u32[]{:S(2)}, u32[]{:S(2)}) collective-permute-start(bf16[99,768]{0,1:T(8,128)(2,1)S(1)} %fusion.94), channel_id=1, source_target_pairs={{0,2},{1,3},{2,0},{3,1},{4,6},{5,7},{6,4},{7,5},{8,10},{9,11},{10,... | collective-permute-start | bytes 456200 | tf_op jit(solution)/shard_map/ppermute | solution.py:159
  18.3 16.7 %collective-permute-start = (bf16[99,768]{0,1:T(8,128)(2,1)S(1)}, bf16[99,768]{0,1:T(8,128)(2,1)S(1)}, u32[]{:S(2)}, u32[]{:S(2)}) collective-permute-start(bf16[99,768]{0,1:T(8,128)(2,1)S(1)} %fusion.94), channel_id=1, source_target_pairs={{0,1},{1,2},{2,3},{3,0},{4,5},{5,6},{6,7},{7,4},{8,9},{9,10},{10,1... | collective-permute-start | bytes 456200 | tf_op jit(solution)/shard_map/ppermute | solution.py:159
  35.4 23.3 %collective-permute-start.7 = (bf16[96,1536]{1,0:T(8,128)(2,1)S(1)}, bf16[96,1536]{1,0:T(8,128)(2,1)S(1)}, u32[]{:S(2)}, u32[]{:S(2)}) collective-permute-start(bf16[96,1536]{1,0:T(8,128)(2,1)S(1)} %pad_maximum_fusion.4), channel_id=1, source_target_pairs={{0,3},{1,0},{2,1},{3,2},{4,7},{5,4},{6,5},{7,6},{8,11},{9,8},{10,9... | collective-permute-start | bytes 884744 | tf_op jit(solution)/shard_map/ppermute | solution.py:159
  35.7 27.9 %collective-permute-start.6 = (bf16[96,1536]{1,0:T(8,128)(2,1)S(1)}, bf16[96,1536]{1,0:T(8,128)(2,1)S(1)}, u32[]{:S(2)}, u32[]{:S(2)}) collective-permute-start(bf16[96,1536]{1,0:T(8,128)(2,1)S(1)} %pad_maximum_fusion.4), channel_id=1, source_target_pairs={{0,2},{1,3},{2,0},{3,1},{4,6},{5,7},{6,4},{7,5},{8,10},{9,11},{10,... | collective-permute-start | bytes 884744 | tf_op jit(solution)/shard_map/ppermute | solution.py:159
  38.3 20.4 %collective-permute-start.5 = (bf16[96,1536]{1,0:T(8,128)(2,1)S(1)}, bf16[96,1536]{1,0:T(8,128)(2,1)}, u32[]{:S(2)}, u32[]{:S(2)}) collective-permute-start(bf16[96,1536]{1,0:T(8,128)(2,1)S(1)} %pad_maximum_fusion.4), channel_id=1, source_target_pairs={{0,1},{1,2},{2,3},{3,0},{4,5},{5,6},{6,7},{7,4},{8,9},{9,10},{10,1... | collective-permute-start | bytes 884744 | tf_op jit(solution)/shard_map/ppermute | solution.py:159
  41.7 22.0 %collective-permute-start.4 = (bf16[96,1536]{0,1:T(8,128)(2,1)S(1)}, bf16[96,1536]{0,1:T(8,128)(2,1)S(1)}, u32[]{:S(2)}, u32[]{:S(2)}) collective-permute-start(bf16[96,1536]{0,1:T(8,128)(2,1)S(1)} %get-tuple-element.315), channel_id=1, source_target_pairs={{0,16},{4,20},{8,24},{12,28},{16,0},{20,4},{24,8},{28,12},{1,17},{... | collective-permute-start | bytes 884744 | tf_op jit(solution)/shard_map/ppermute | solution.py:192
  43.2 20.4 %collective-permute-start.3 = (bf16[96,1536]{0,1:T(8,128)(2,1)S(1)}, bf16[96,1536]{0,1:T(8,128)(2,1)S(1)}, u32[]{:S(2)}, u32[]{:S(2)}) collective-permute-start(bf16[96,1536]{0,1:T(8,128)(2,1)S(1)} %get-tuple-element.316), channel_id=1, source_target_pairs={{0,8},{4,12},{8,0},{12,4},{16,24},{20,28},{24,16},{28,20},{1,9},{5... | collective-permute-start | bytes 884744 | tf_op jit(solution)/shard_map/ppermute | solution.py:192
  66.9 240.9 %reduce-scatter.2.cloned.1.call-start = ((), (), s32[]{:S(2)}) async-start(), calls=%async_computation.2 | async-start | bytes 5308416 | tf_op jit(solution)/shard_map/reduce_scatter | solution.py:427
  70.8 29.9 %collective-permute-start.9 = (bf16[2,96,1536]{2,1,0:T(8,128)(2,1)S(1)}, bf16[2,96,1536]{2,1,0:T(8,128)(2,1)}, u32[]{:S(2)}, u32[]{:S(2)}) collective-permute-start(bf16[2,96,1536]{2,1,0:T(8,128)(2,1)S(1)} %broadcast_select_fusion.2), channel_id=1, source_target_pairs={{0,8},{4,12},{8,0},{12,4},{16,24},{20,28},{24,16},{28,20},{1,9},{5... | collective-permute-start | bytes 1769480 | tf_op jit(solution)/shard_map/ppermute | solution.py:192
  72.5 28.2 %collective-permute-start.8 = (bf16[2,96,1536]{2,1,0:T(8,128)(2,1)S(1)}, bf16[2,96,1536]{2,1,0:T(8,128)(2,1)}, u32[]{:S(2)}, u32[]{:S(2)}) collective-permute-start(bf16[2,96,1536]{2,1,0:T(8,128)(2,1)S(1)} %broadcast_select_fusion.3), channel_id=1, source_target_pairs={{0,16},{4,20},{8,24},{12,28},{16,0},{20,4},{24,8},{28,12},{1,17},{... | collective-permute-start | bytes 1769480 | tf_op jit(solution)/shard_map/ppermute | solution.py:192
  74.9 25.8 %collective-permute-start.11 = (bf16[1,256,768]{2,1,0:T(8,128)(2,1)S(1)}, bf16[1,256,768]{2,1,0:T(8,128)(2,1)S(1)}, u32[]{:S(2)}, u32[]{:S(2)}) collective-permute-start(bf16[1,256,768]{2,1,0:T(8,128)(2,1)S(1)} %get-tuple-element.284), channel_id=1, source_target_pairs={{0,2},{1,3},{2,0},{3,1},{4,6},{5,7},{6,4},{7,5},{8,10},{9,11},{10,... | collective-permute-start | bytes 1179656 | tf_op jit(solution)/shard_map/ppermute | solution.py:168
  75.0 25.6 %collective-permute-start.10 = (bf16[1,256,768]{2,1,0:T(8,128)(2,1)S(1)}, bf16[1,256,768]{2,1,0:T(8,128)(2,1)S(1)}, u32[]{:S(2)}, u32[]{:S(2)}) collective-permute-start(bf16[1,256,768]{2,1,0:T(8,128)(2,1)S(1)} %get-tuple-element.285), channel_id=1, source_target_pairs={{0,1},{1,2},{2,3},{3,0},{4,5},{5,6},{6,7},{7,4},{8,9},{9,10},{10,1... | collective-permute-start | bytes 1179656 | tf_op jit(solution)/shard_map/ppermute | solution.py:168
  103.7 11.9 %collective-permute-start.12 = (bf16[2,2,96,3072]{3,2,1,0:T(8,128)(2,1)S(1)}, bf16[2,2,96,3072]{3,2,1,0:T(8,128)(2,1)}, u32[]{:S(2)}, u32[]{:S(2)}) collective-permute-start(bf16[2,2,96,3072]{3,2,1,0:T(8,128)(2,1)S(1)} %pad_maximum_fusion.1), channel_id=1, source_target_pairs={{0,4},{4,0},{8,12},{12,8},{16,20},{20,16},{24,28},{28,24},{1,5},{5... | collective-permute-start | bytes 7077896 | tf_op jit(solution)/shard_map/ppermute | solution.py:192
  103.7 11.8 %collective-permute-start.13 = (bf16[1,256,768]{2,1,0:T(8,128)(2,1)}, bf16[1,256,768]{2,1,0:T(8,128)(2,1)}, u32[]{:S(2)}, u32[]{:S(2)}) collective-permute-start(bf16[1,256,768]{2,1,0:T(8,128)(2,1)} %get-tuple-element.283), channel_id=1, source_target_pairs={{0,3},{1,0},{2,1},{3,2},{4,7},{5,4},{6,5},{7,6},{8,11},{9,8},{10,9... | collective-permute-start | bytes 1179656 | tf_op jit(solution)/shard_map/ppermute | solution.py:168
  104.7 72.4 %copy-start.30 = (f32[768]{0:T(1024)}, f32[768]{0:T(1024)S(1)}, u32[]{:S(2)}) copy-start(f32[768]{0:T(1024)S(1)} %convert_element_type.283) | copy-start | bytes 9220
  117.8 59.3 %collective-permute-start.16 = (bf16[1,256,768]{2,1,0:T(8,128)(2,1)}, bf16[1,256,768]{2,1,0:T(8,128)(2,1)}, u32[]{:S(2)}, u32[]{:S(2)}) collective-permute-start(bf16[1,256,768]{2,1,0:T(8,128)(2,1)} %get-tuple-element.280), channel_id=1, source_target_pairs={{0,3},{1,0},{2,1},{3,2},{4,7},{5,4},{6,5},{7,6},{8,11},{9,8},{10,9... | collective-permute-start | bytes 1179656 | tf_op jit(solution)/shard_map/ppermute | solution.py:168
  119.9 57.2 %collective-permute-start.15 = (bf16[1,256,768]{2,1,0:T(8,128)(2,1)}, bf16[1,256,768]{2,1,0:T(8,128)(2,1)}, u32[]{:S(2)}, u32[]{:S(2)}) collective-permute-start(bf16[1,256,768]{2,1,0:T(8,128)(2,1)} %get-tuple-element.281), channel_id=1, source_target_pairs={{0,1},{1,2},{2,3},{3,0},{4,5},{5,6},{6,7},{7,4},{8,9},{9,10},{10,1... | collective-permute-start | bytes 1179656 | tf_op jit(solution)/shard_map/ppermute | solution.py:168
  119.9 40.7 %collective-permute-start.14 = (bf16[1,256,768]{2,1,0:T(8,128)(2,1)S(1)}, bf16[1,256,768]{2,1,0:T(8,128)(2,1)S(1)}, u32[]{:S(2)}, u32[]{:S(2)}) collective-permute-start(bf16[1,256,768]{2,1,0:T(8,128)(2,1)S(1)} %get-tuple-element.282), channel_id=1, source_target_pairs={{0,2},{1,3},{2,0},{3,1},{4,6},{5,7},{6,4},{7,5},{8,10},{9,11},{10,... | collective-permute-start | bytes 1179656 | tf_op jit(solution)/shard_map/ppermute | solution.py:168
  130.6 30.8 %copy-start.40 = (f32[768]{0:T(1024)S(1)}, f32[768]{0:T(1024)}, u32[]{:S(2)}) copy-start(f32[768]{0:T(1024)} %convert_element_type.282) | copy-start | bytes 9220
  229.6 21.3 %collective-permute-start.19 = (bf16[1,256,768]{2,1,0:T(8,128)(2,1)S(1)}, bf16[1,256,768]{2,1,0:T(8,128)(2,1)S(1)}, u32[]{:S(2)}, u32[]{:S(2)}) collective-permute-start(bf16[1,256,768]{2,1,0:T(8,128)(2,1)S(1)} %get-tuple-element.276), channel_id=1, source_target_pairs={{0,2},{1,3},{2,0},{3,1},{4,6},{5,7},{6,4},{7,5},{8,10},{9,11},{10,... | collective-permute-start | bytes 1179656 | tf_op jit(solution)/shard_map/ppermute | solution.py:177
  231.9 19.0 %collective-permute-start.18 = (bf16[1,256,768]{2,1,0:T(8,128)(2,1)S(1)}, bf16[1,256,768]{2,1,0:T(8,128)(2,1)S(1)}, u32[]{:S(2)}, u32[]{:S(2)}) collective-permute-start(bf16[1,256,768]{2,1,0:T(8,128)(2,1)S(1)} %get-tuple-element.277), channel_id=1, source_target_pairs={{0,3},{1,0},{2,1},{3,2},{4,7},{5,4},{6,5},{7,6},{8,11},{9,8},{10,9... | collective-permute-start | bytes 1179656 | tf_op jit(solution)/shard_map/ppermute | solution.py:177
  236.3 14.6 %collective-permute-start.17 = (bf16[2,2,96,3072]{3,2,0,1:T(8,128)(2,1)S(1)}, bf16[2,2,96,3072]{3,2,0,1:T(8,128)(2,1)S(1)}, u32[]{:S(2)}, u32[]{:S(2)}) collective-permute-start(bf16[2,2,96,3072]{3,2,0,1:T(8,128)(2,1)S(1)} %bitcast.176), channel_id=1, source_target_pairs={{0,4},{4,0},{8,12},{12,8},{16,20},{20,16},{24,28},{28,24},{1,5},{5... | collective-permute-start | bytes 7077896 | tf_op jit(solution)/shard_map/ppermute | solution.py:192
  250.0 4.8 %collective-permute-start.23 = (f32[7680]{0:T(1024)S(1)}, f32[7680]{0:T(1024)S(1)}, u32[]{:S(2)}, u32[]{:S(2)}) collective-permute-start(f32[7680]{0:T(1024)S(1)} %constant_dynamic-update-slice_fusion.18), channel_id=1, source_target_pairs={{0,1},{1,0},{2,3},{3,2},{4,5},{5,4},{6,7},{7,6},{8,9},{9,8},{10,11... | collective-permute-start | bytes 92168 | tf_op jit(solution)/shard_map/ppermute | solution.py:192
  252.1 20.6 %collective-permute-start.20 = (bf16[2,96,1536]{2,1,0:T(8,128)(2,1)S(1)}, bf16[2,96,1536]{2,1,0:T(8,128)(2,1)S(1)}, u32[]{:S(2)}, u32[]{:S(2)}) collective-permute-start(bf16[2,96,1536]{2,1,0:T(8,128)(2,1)S(1)} %dynamic-slice_bitcast_fusion.4), channel_id=1, source_target_pairs={{0,16},{4,20},{8,24},{12,28},{16,0},{20,4},{24,8},{28,12},{1,17},{... | collective-permute-start | bytes 1769480 | tf_op jit(solution)/shard_map/ppermute | solution.py:192
  252.6 20.2 %collective-permute-start.21 = (bf16[2,96,1536]{2,1,0:T(8,128)(2,1)S(1)}, bf16[2,96,1536]{2,1,0:T(8,128)(2,1)S(1)}, u32[]{:S(2)}, u32[]{:S(2)}) collective-permute-start(bf16[2,96,1536]{2,1,0:T(8,128)(2,1)S(1)} %dynamic-slice_bitcast_fusion.3), channel_id=1, source_target_pairs={{0,8},{4,12},{8,0},{12,4},{16,24},{20,28},{24,16},{28,20},{1,9},{5... | collective-permute-start | bytes 1769480 | tf_op jit(solution)/shard_map/ppermute | solution.py:192
  254.8 14.6 %collective-permute-start.24 = (f32[7680]{0:T(1024)S(1)}, f32[7680]{0:T(1024)S(1)}, u32[]{:S(2)}, u32[]{:S(2)}) collective-permute-start(f32[7680]{0:T(1024)S(1)} %add.443), channel_id=1, source_target_pairs={{0,2},{1,3},{2,0},{3,1},{4,6},{5,7},{6,4},{7,5},{8,10},{9,11},{10,... | collective-permute-start | bytes 92168 | tf_op jit(solution)/shard_map/ppermute | solution.py:192
  265.0 13.2 %collective-permute-start.22 = (bf16[1,256,768]{2,1,0:T(8,128)(2,1)S(1)}, bf16[1,256,768]{2,1,0:T(8,128)(2,1)}, u32[]{:S(2)}, u32[]{:S(2)}) collective-permute-start(bf16[1,256,768]{2,1,0:T(8,128)(2,1)S(1)} %get-tuple-element.275), channel_id=1, source_target_pairs={{0,1},{1,2},{2,3},{3,0},{4,5},{5,6},{6,7},{7,4},{8,9},{9,10},{10,1... | collective-permute-start | bytes 1179656 | tf_op jit(solution)/shard_map/ppermute | solution.py:177
  278.2 1.2 collective-permute-start.27
  279.4 3.9 collective-permute-start.28
  281.0 26.5 %collective-permute-start.26 = (bf16[96,1536]{1,0:T(8,128)(2,1)}, bf16[96,1536]{1,0:T(8,128)(2,1)S(1)}, u32[]{:S(2)}, u32[]{:S(2)}) collective-permute-start(bf16[96,1536]{1,0:T(8,128)(2,1)} %dynamic-slice_bitcast_fusion.7), channel_id=1, source_target_pairs={{0,16},{4,20},{8,24},{12,28},{16,0},{20,4},{24,8},{28,12},{1,17},{... | collective-permute-start | bytes 884744 | tf_op jit(solution)/shard_map/ppermute | solution.py:192
  282.7 24.8 %collective-permute-start.25 = (bf16[96,1536]{1,0:T(8,128)(2,1)S(1)}, bf16[96,1536]{1,0:T(8,128)(2,1)S(1)}, u32[]{:S(2)}, u32[]{:S(2)}) collective-permute-start(bf16[96,1536]{1,0:T(8,128)(2,1)S(1)} %dynamic-slice_bitcast_fusion.8), channel_id=1, source_target_pairs={{0,8},{4,12},{8,0},{12,4},{16,24},{20,28},{24,16},{28,20},{1,9},{5... | collective-permute-start | bytes 884744 | tf_op jit(solution)/shard_map/ppermute | solution.py:192
  283.3 24.1 %collective-permute-start.29 = (f32[7680]{0:T(1024)S(1)}, f32[7680]{0:T(1024)S(1)}, u32[]{:S(2)}, u32[]{:S(2)}) collective-permute-start(f32[7680]{0:T(1024)S(1)} %add.448), channel_id=1, source_target_pairs={{0,16},{4,20},{8,24},{12,28},{16,0},{20,4},{24,8},{28,12},{1,17},{... | collective-permute-start | bytes 92168 | tf_op jit(solution)/shard_map/ppermute | solution.py:192
  307.4 38.6 %copy-start.25 = (f32[7680]{0:T(1024)}, f32[7680]{0:T(1024)S(1)}, u32[]{:S(2)}) copy-start(f32[7680]{0:T(1024)S(1)} %add.449) | copy-start | bytes 92164
  308.4 35.3 %collective-permute-start.32 = (bf16[96,768]{1,0:T(8,128)(2,1)}, bf16[96,768]{1,0:T(8,128)(2,1)}, u32[]{:S(2)}, u32[]{:S(2)}) collective-permute-start(bf16[96,768]{1,0:T(8,128)(2,1)} %get-tuple-element.291), channel_id=1, source_target_pairs={{0,1},{1,2},{2,3},{3,0},{4,5},{5,6},{6,7},{7,4},{8,9},{9,10},{10,1... | collective-permute-start | bytes 442376 | tf_op jit(solution)/shard_map/ppermute | solution.py:177
  312.9 33.7 %collective-permute-start.31 = (bf16[96,768]{1,0:T(8,128)(2,1)S(1)}, bf16[96,768]{1,0:T(8,128)(2,1)}, u32[]{:S(2)}, u32[]{:S(2)}) collective-permute-start(bf16[96,768]{1,0:T(8,128)(2,1)S(1)} %get-tuple-element.292), channel_id=1, source_target_pairs={{0,2},{1,3},{2,0},{3,1},{4,6},{5,7},{6,4},{7,5},{8,10},{9,11},{10,... | collective-permute-start | bytes 442376 | tf_op jit(solution)/shard_map/ppermute | solution.py:177
  316.3 30.4 %collective-permute-start.30 = (bf16[96,768]{1,0:T(8,128)(2,1)S(1)}, bf16[96,768]{1,0:T(8,128)(2,1)}, u32[]{:S(2)}, u32[]{:S(2)}) collective-permute-start(bf16[96,768]{1,0:T(8,128)(2,1)S(1)} %get-tuple-element.293), channel_id=1, source_target_pairs={{0,3},{1,0},{2,1},{3,2},{4,7},{5,4},{6,5},{7,6},{8,11},{9,8},{10,9... | collective-permute-start | bytes 442376 | tf_op jit(solution)/shard_map/ppermute | solution.py:177
  318.2 28.5 %collective-permute-start.35 = (bf16[96,768]{1,0:T(8,128)(2,1)}, bf16[96,768]{1,0:T(8,128)(2,1)}, u32[]{:S(2)}, u32[]{:S(2)}) collective-permute-start(bf16[96,768]{1,0:T(8,128)(2,1)} %get-tuple-element.287), channel_id=1, source_target_pairs={{0,1},{1,2},{2,3},{3,0},{4,5},{5,6},{6,7},{7,4},{8,9},{9,10},{10,1... | collective-permute-start | bytes 442376 | tf_op jit(solution)/shard_map/ppermute | solution.py:177
  320.2 26.5 %collective-permute-start.34 = (bf16[96,768]{1,0:T(8,128)(2,1)}, bf16[96,768]{1,0:T(8,128)(2,1)}, u32[]{:S(2)}, u32[]{:S(2)}) collective-permute-start(bf16[96,768]{1,0:T(8,128)(2,1)} %get-tuple-element.288), channel_id=1, source_target_pairs={{0,2},{1,3},{2,0},{3,1},{4,6},{5,7},{6,4},{7,5},{8,10},{9,11},{10,... | collective-permute-start | bytes 442376 | tf_op jit(solution)/shard_map/ppermute | solution.py:177
  343.7 5.4 %collective-permute-start.33 = (bf16[96,768]{1,0:T(8,128)(2,1)S(1)}, bf16[96,768]{1,0:T(8,128)(2,1)S(1)}, u32[]{:S(2)}, u32[]{:S(2)}) collective-permute-start(bf16[96,768]{1,0:T(8,128)(2,1)S(1)} %get-tuple-element.289), channel_id=1, source_target_pairs={{0,3},{1,0},{2,1},{3,2},{4,7},{5,4},{6,5},{7,6},{8,11},{9,8},{10,9... | collective-permute-start | bytes 442376 | tf_op jit(solution)/shard_map/ppermute | solution.py:177
  360.5 7.9 %collective-permute-start.36 = (bf16[2,2,96,3072]{3,2,1,0:T(8,128)(2,1)}, bf16[2,2,96,3072]{3,2,1,0:T(8,128)(2,1)}, u32[]{:S(2)}, u32[]{:S(2)}) collective-permute-start(bf16[2,2,96,3072]{3,2,1,0:T(8,128)(2,1)} %dynamic-slice_bitcast_fusion), channel_id=1, source_target_pairs={{0,4},{4,0},{8,12},{12,8},{16,20},{20,16},{24,28},{28,24},{1,5},{5... | collective-permute-start | bytes 7077896 | tf_op jit(solution)/shard_map/ppermute | solution.py:192
  371.0 1.4 collective-permute-start.47
  372.4 4.6 %collective-permute-start.48 = (f32[1536]{0:T(1024)S(1)}, f32[1536]{0:T(1024)S(1)}, u32[]{:S(2)}, u32[]{:S(2)}) collective-permute-start(f32[1536]{0:T(1024)S(1)} %add.461), channel_id=1, source_target_pairs={{0,8},{4,12},{8,0},{12,4},{16,24},{20,28},{24,16},{28,20},{1,9},{5... | collective-permute-start | bytes 18440 | tf_op jit(solution)/shard_map/ppermute | solution.py:192
  372.4 34.8 %copy-start.17 = (bf16[96,768]{1,0:T(8,128)(2,1)S(1)}, bf16[96,768]{1,0:T(8,128)(2,1)}, u32[]{:S(2)}) copy-start(bf16[96,768]{1,0:T(8,128)(2,1)} %get-tuple-element.181) | copy-start | bytes 442372
  372.4 34.8 %copy-start.28 = (bf16[96,768]{1,0:T(8,128)(2,1)S(1)}, bf16[96,768]{1,0:T(8,128)(2,1)}, u32[]{:S(2)}) copy-start(bf16[96,768]{1,0:T(8,128)(2,1)} %copy-done.27) | copy-start | bytes 442372
  372.4 38.5 %copy-start.43 = (pred[4]{0:T(512)(128)(4,1)S(1)}, pred[4]{0:T(512)(128)(4,1)}, u32[]{:S(2)}) copy-start(pred[4]{0:T(512)(128)(4,1)} %compare_and_fusion) | copy-start | bytes 16
  372.5 38.5 %copy-start.44 = (s32[4]{0:T(128)S(1)}, s32[4]{0:T(128)}, u32[]{:S(2)}) copy-start(s32[4]{0:T(128)} %get-tuple-element.374) | copy-start | bytes 52
  372.5 38.5 %copy-start.45 = (s32[4]{0:T(128)S(1)}, s32[4]{0:T(128)}, u32[]{:S(2)}) copy-start(s32[4]{0:T(128)} %get-tuple-element.375) | copy-start | bytes 52
  372.6 38.5 %collective-permute-start.40 = (bf16[1,256,768]{2,1,0:T(8,128)(2,1)S(1)}, bf16[1,256,768]{2,1,0:T(8,128)(2,1)S(1)}, u32[]{:S(2)}, u32[]{:S(2)}) collective-permute-start(bf16[1,256,768]{2,1,0:T(8,128)(2,1)S(1)} %get-tuple-element.272), channel_id=1, source_target_pairs={{0,2},{1,3},{2,0},{3,1},{4,6},{5,7},{6,4},{7,5},{8,10},{9,11},{10,... | collective-permute-start | bytes 1179656 | tf_op jit(solution)/shard_map/ppermute | solution.py:177
  375.2 35.8 %collective-permute-start.39 = (bf16[1,256,768]{2,1,0:T(8,128)(2,1)S(1)}, bf16[1,256,768]{2,1,0:T(8,128)(2,1)S(1)}, u32[]{:S(2)}, u32[]{:S(2)}) collective-permute-start(bf16[1,256,768]{2,1,0:T(8,128)(2,1)S(1)} %get-tuple-element.273), channel_id=1, source_target_pairs={{0,3},{1,0},{2,1},{3,2},{4,7},{5,4},{6,5},{7,6},{8,11},{9,8},{10,9... | collective-permute-start | bytes 1179656 | tf_op jit(solution)/shard_map/ppermute | solution.py:177
  377.0 3.7 collective-permute-start.49
  380.7 12.4 %collective-permute-start.52 = (f32[1536]{0:T(1024)S(1)}, f32[1536]{0:T(1024)S(1)}, u32[]{:S(2)}, u32[]{:S(2)}) collective-permute-start(f32[1536]{0:T(1024)S(1)} %add.463), channel_id=1, source_target_pairs={{0,3},{1,0},{2,1},{3,2},{4,7},{5,4},{6,5},{7,6},{8,11},{9,8},{10,9... | collective-permute-start | bytes 18440 | tf_op jit(solution)/shard_map/ppermute | solution.py:159
  383.7 27.4 %collective-permute-start.37 = (bf16[2,96,1536]{2,1,0:T(8,128)(2,1)S(1)}, bf16[2,96,1536]{2,1,0:T(8,128)(2,1)S(1)}, u32[]{:S(2)}, u32[]{:S(2)}) collective-permute-start(bf16[2,96,1536]{2,1,0:T(8,128)(2,1)S(1)} %dynamic-slice_bitcast_fusion.2), channel_id=1, source_target_pairs={{0,16},{4,20},{8,24},{12,28},{16,0},{20,4},{24,8},{28,12},{1,17},{... | collective-permute-start | bytes 1769480 | tf_op jit(solution)/shard_map/ppermute | solution.py:192
  384.4 26.7 %collective-permute-start.38 = (bf16[2,96,1536]{2,1,0:T(8,128)(2,1)S(1)}, bf16[2,96,1536]{2,1,0:T(8,128)(2,1)S(1)}, u32[]{:S(2)}, u32[]{:S(2)}) collective-permute-start(bf16[2,96,1536]{2,1,0:T(8,128)(2,1)S(1)} %dynamic-slice_bitcast_fusion.1), channel_id=1, source_target_pairs={{0,8},{4,12},{8,0},{12,4},{16,24},{20,28},{24,16},{28,20},{1,9},{5... | collective-permute-start | bytes 1769480 | tf_op jit(solution)/shard_map/ppermute | solution.py:192
  393.1 10.4 %collective-permute-start.51 = (f32[1536]{0:T(1024)S(1)}, f32[1536]{0:T(1024)S(1)}, u32[]{:S(2)}, u32[]{:S(2)}) collective-permute-start(f32[1536]{0:T(1024)S(1)} %add.463), channel_id=1, source_target_pairs={{0,2},{1,3},{2,0},{3,1},{4,6},{5,7},{6,4},{7,5},{8,10},{9,11},{10,... | collective-permute-start | bytes 18440 | tf_op jit(solution)/shard_map/ppermute | solution.py:159
  403.5 5.5 %collective-permute-start.50 = (f32[1536]{0:T(1024)S(1)}, f32[1536]{0:T(1024)S(1)}, u32[]{:S(2)}, u32[]{:S(2)}) collective-permute-start(f32[1536]{0:T(1024)S(1)} %add.463), channel_id=1, source_target_pairs={{0,1},{1,2},{2,3},{3,0},{4,5},{5,6},{6,7},{7,4},{8,9},{9,10},{10,1... | collective-permute-start | bytes 18440 | tf_op jit(solution)/shard_map/ppermute | solution.py:159
  409.0 12.0 %collective-permute-start.43 = (bf16[1,256,768]{2,1,0:T(8,128)(2,1)S(1)}, bf16[1,256,768]{2,1,0:T(8,128)(2,1)S(1)}, u32[]{:S(2)}, u32[]{:S(2)}) collective-permute-start(bf16[1,256,768]{2,1,0:T(8,128)(2,1)S(1)} %get-tuple-element.271), channel_id=1, source_target_pairs={{0,1},{1,2},{2,3},{3,0},{4,5},{5,6},{6,7},{7,4},{8,9},{9,10},{10,1... | collective-permute-start | bytes 1179656 | tf_op jit(solution)/shard_map/ppermute | solution.py:177
  411.5 9.5 %collective-permute-start.42 = (bf16[96,1536]{1,0:T(8,128)(2,1)S(1)}, bf16[96,1536]{1,0:T(8,128)(2,1)S(1)}, u32[]{:S(2)}, u32[]{:S(2)}) collective-permute-start(bf16[96,1536]{1,0:T(8,128)(2,1)S(1)} %dynamic-slice_bitcast_fusion.5), channel_id=1, source_target_pairs={{0,16},{4,20},{8,24},{12,28},{16,0},{20,4},{24,8},{28,12},{1,17},{... | collective-permute-start | bytes 884744 | tf_op jit(solution)/shard_map/ppermute | solution.py:192
  412.2 8.8 %collective-permute-start.41 = (bf16[96,1536]{1,0:T(8,128)(2,1)S(1)}, bf16[96,1536]{1,0:T(8,128)(2,1)S(1)}, u32[]{:S(2)}, u32[]{:S(2)}) collective-permute-start(bf16[96,1536]{1,0:T(8,128)(2,1)S(1)} %dynamic-slice_bitcast_fusion.6), channel_id=1, source_target_pairs={{0,8},{4,12},{8,0},{12,4},{16,24},{20,28},{24,16},{28,20},{1,9},{5... | collective-permute-start | bytes 884744 | tf_op jit(solution)/shard_map/ppermute | solution.py:192
  421.5 6.8 %collective-permute-start.44 = (bf16[96,768]{1,0:T(8,128)(2,1)S(1)}, bf16[96,768]{1,0:T(8,128)(2,1)S(1)}, u32[]{:S(2)}, u32[]{:S(2)}) collective-permute-start(bf16[96,768]{1,0:T(8,128)(2,1)S(1)} %pad_maximum_fusion.5), channel_id=1, source_target_pairs={{0,3},{1,0},{2,1},{3,2},{4,7},{5,4},{6,5},{7,6},{8,11},{9,8},{10,9... | collective-permute-start | bytes 442376 | tf_op jit(solution)/shard_map/ppermute | solution.py:177
  421.7 10.7 %collective-permute-start.45 = (bf16[96,768]{1,0:T(8,128)(2,1)S(1)}, bf16[96,768]{1,0:T(8,128)(2,1)S(1)}, u32[]{:S(2)}, u32[]{:S(2)}) collective-permute-start(bf16[96,768]{1,0:T(8,128)(2,1)S(1)} %pad_maximum_fusion.6), channel_id=1, source_target_pairs={{0,2},{1,3},{2,0},{3,1},{4,6},{5,7},{6,4},{7,5},{8,10},{9,11},{10,... | collective-permute-start | bytes 442376 | tf_op jit(solution)/shard_map/ppermute | solution.py:177
  421.9 10.5 %collective-permute-start.46 = (bf16[96,768]{1,0:T(8,128)(2,1)S(1)}, bf16[96,768]{1,0:T(8,128)(2,1)S(1)}, u32[]{:S(2)}, u32[]{:S(2)}) collective-permute-start(bf16[96,768]{1,0:T(8,128)(2,1)S(1)} %pad_maximum_fusion.7), channel_id=1, source_target_pairs={{0,1},{1,2},{2,3},{3,0},{4,5},{5,6},{6,7},{7,4},{8,9},{9,10},{10,1... | collective-permute-start | bytes 442376 | tf_op jit(solution)/shard_map/ppermute | solution.py:177
  (47 other events, 289.0 us)
Sparse Core Ops, SparseCore 0:
  67.0 64.8 all-gather.1
  220.1 56.9 reduce-scatter.1

commit v6 on v5

--- a/solution.py
+++ b/solution.py
@@ -22,34 +22,30 @@
     return lax.dot_general(left, right, dims, preferred_element_type=WIDE)
 
 
-def halves(pair):
+def halves(pair, fill=0):
     lane = lax.broadcasted_iota(jnp.int32, (1, PAIR), 1)
-    zero = jnp.zeros((), pair.dtype)
-    return jnp.where(lane < HDIM, pair, zero), jnp.where(lane < HDIM, zero, pair)
+    other = jnp.full((), fill, pair.dtype)
+    return jnp.where(lane < HDIM, pair, other), jnp.where(lane < HDIM, other, pair)
 
 
 def attend_kernel(q_ref, k_ref, v_ref, row_ref, col_ref, context_ref, logsum_ref, *, scaling):
     keys_all = k_ref[0]
-    turned = [half.T for half in halves(v_ref[0])]
-    key_ids = col_ref[0]
-    for start in range(0, q_ref.shape[1], BLOCK):
-        part = slice(start, start + BLOCK)
-        seen = key_ids == row_ref[0, :, part]
-        total = None
-        for head, queries in enumerate(halves(q_ref[0, part, :] * scaling)):
-            scores = jnp.where(seen, dot(keys_all, queries, BY_LAST), MASKED)
-            highest = jnp.max(scores, axis=0, keepdims=True)
-            weights = jnp.exp(scores - highest)
-            sums = jnp.sum(weights, axis=0, keepdims=True)
-            probs = (weights * (1.0 / sums)).astype(LOW)
-            logsum_ref[0, 0, head : head + 1, part] = highest + jnp.log(sums)
-            piece = dot(turned[head], probs, BY_ROWS)
-            total = piece if total is None else total + piece
-        context_ref[0, part, :] = total.T.astype(LOW)
+    turned = [half.T for half in halves(v_ref[0], 1)]
+    seen = col_ref[0] == row_ref[0]
+    pieces = []
+    for head, queries in enumerate(halves(q_ref[0] * scaling)):
+        scores = jnp.where(seen, dot(keys_all, queries, BY_LAST), MASKED)
+        highest = jnp.max(scores, axis=0, keepdims=True)
+        piece = dot(turned[head], jnp.exp(scores - highest).astype(LOW), BY_ROWS)
+        mine, ones = (piece[:HDIM], piece[HDIM:]) if head == 0 else (piece[HDIM:], piece[:HDIM])
+        sums = ones[:1]
+        logsum_ref[0, 0, head : head + 1, :] = highest + jnp.log(sums)
+        pieces.append(mine * (1.0 / sums))
+    context_ref[0] = jnp.concatenate(pieces, axis=0).T.astype(LOW)
 
 
 def attend_back_kernel(
-    q_ref, k_ref, v_ref, g_ref, logsum_ref, row_ref, col_ref, dq_ref, dk_ref, dv_ref, *, scaling
+    q_ref, k_ref, v_ref, g_ref, c_ref, logsum_ref, row_ref, col_ref, dq_ref, dk_ref, dv_ref, *, scaling
 ):
     keys_all = k_ref[0]
     values = v_ref[0]
@@ -64,13 +60,14 @@
         total = None
         queries_of = halves(q_ref[0, part, :] * scaling)
         grads_of = halves(g_ref[0, part, :])
+        products = g_ref[0, part, :].astype(WIDE).T * c_ref[0, part, :].astype(WIDE).T
         for head in range(2):
             queries, grads = queries_of[head], grads_of[head]
+            level = jnp.sum(products[head * HDIM : (head + 1) * HDIM], axis=0, keepdims=True)
             scores = jnp.where(seen, dot(keys_all, queries, BY_LAST), MASKED)
             probs = jnp.exp(scores - logsum_ref[0, 0, head : head + 1, part])
             grad_probs = dot(values, grads, BY_LAST)
             value_grad = value_grad + dot(probs.astype(LOW), grads, BY_ROWS)
-            level = jnp.sum(probs * grad_probs, axis=0, keepdims=True)
             grad_scores = (probs * (grad_probs - level)).astype(LOW)
             key_grad = key_grad + dot(grad_scores, queries, BY_ROWS)
             piece = dot(turned[head], grad_scores, BY_ROWS)
@@ -111,21 +108,21 @@
     )(queries, keys_all, values, *ids)
 
 
-def attend_back(queries, keys_all, values, grad_context, logsum, ids, earlier, part):
+def attend_back(queries, keys_all, values, grad_context, context, logsum, ids, earlier, part):
     count, length, width = queries.shape
     pairs = width // PAIR
     first = pairs // 2 * part
     rows, as_row, as_col, sums = attention_specs(length, first)
     body = functools.partial(attend_back_kernel, scaling=HDIM ** (-0.5))
-    operands = [queries, keys_all, values, grad_context, logsum, *ids]
-    in_specs = [rows, rows, rows, rows, sums, as_row, as_col]
+    operands = [queries, keys_all, values, grad_context, context, logsum, *ids]
+    in_specs = [rows] * 5 + [sums, as_row, as_col]
     aliases = {}
     if earlier is not None:
 
         def body(*refs):
-            attend_back_kernel(*refs[:7], *refs[10:], scaling=HDIM ** (-0.5))
-
-        aliases = {7 + i: i for i in range(3)}
+            attend_back_kernel(*refs[:8], *refs[11:], scaling=HDIM ** (-0.5))
+
+        aliases = {8 + i: i for i in range(3)}
         operands += list(earlier)
         in_specs += [pl.BlockSpec(memory_space=pl.ANY)] * 3
     return pl.pallas_call(
@@ -257,22 +254,6 @@
     moved = (flip("fsdp", 8, 2, first_out), flip("fsdp", 8, 4, second_out))
     moved, others = together(moved, others)
     return jnp.concatenate([add_low(first, moved[0]), add_low(second, moved[1])], axis=1), others
-
-
-def total_over_tp(vector):
-    bit = 1
-    while bit < lax.axis_size("tp"):
-        vector = vector + flip("tp", lax.axis_size("tp"), bit, vector)
-        bit *= 2
-    return vector
-
-
-def total_over_fsdp(vector):
-    bit = 1
-    while bit < lax.axis_size("fsdp"):
-        vector = vector + flip("fsdp", lax.axis_size("fsdp"), bit, vector)
-        bit *= 2
-    return vector
 
 
 def normalize(token_rows):
@@ -439,38 +420,22 @@
     grad_mixed_low = grad_mixed.astype(LOW)
     output_grad = dot(grad_mixed_low, context, BY_FIRST).astype(LOW)
     grad_context = dot(grad_mixed_low, output_turned, BY_ROWS).astype(LOW).reshape(shape)
-    early = total_over_tp(
-        jnp.concatenate(
-            [
-                output_bias_grad,
-                first_gain_grad,
-                first_shift_grad,
-                outer_bias_grad,
-                second_gain_grad,
-                second_shift_grad,
-                by_rank(inner_bias_grad),
-            ]
-        )
-    )
-    grad_context, inner_share, output_grad, layer_out, early = lax.optimization_barrier(
-        (grad_context, scatter_near(inner_share)[0], output_grad, layer_out, early)
-    )
-    early = total_over_fsdp(early)
+    grad_context, inner_share, output_grad, layer_out = lax.optimization_barrier(
+        (grad_context, scatter_near(inner_share)[0], output_grad, layer_out)
+    )
     inner_share, _ = scatter_far(inner_share)
-    back = functools.partial(attend_back, queries, keys_all, values, grad_context, logsum, ids)
+    back = functools.partial(
+        attend_back, queries, keys_all, values, grad_context, context.reshape(shape), logsum, ids
+    )
     halfway = back(None, 0)
-    halfway, inner_share, outer_share, early = lax.optimization_barrier(
-        (halfway, inner_share, outer_share, early)
+    halfway, inner_share, outer_share = lax.optimization_barrier(
+        (halfway, inner_share, outer_share)
     )
     layer_out = own_places(layer_out)
-    inner_parts = own_columns(inner_share, (unit_cols,))
-    outer_parts = own_columns(outer_share, (unit_cols,))
-    rows_grads = back(halfway, 1)
-    rows_grads, inner_parts, outer_parts = lax.optimization_barrier(
-        (rows_grads, inner_parts, outer_parts)
-    )
-    (inner_share,) = summed(inner_parts, (unit_cols,))
-    (outer_share,) = summed(outer_parts, (unit_cols,))
+    units = (unit_cols, unit_cols)
+    unit_parts = own_columns(jnp.concatenate([inner_share, outer_share], axis=1), units)
+    rows_grads, unit_parts = lax.optimization_barrier((back(halfway, 1), unit_parts))
+    inner_share, outer_share = summed(unit_parts, units)
     query_rows_grad, key_rows_grad, value_rows_grad = (
         array.reshape(count * length, width) for array in rows_grads
     )
@@ -484,23 +449,31 @@
         + dot(key_rows_grad, key_full, BY_LAST)
         + dot(value_rows_grad, value_full, BY_LAST)
     ).astype(LOW)
-    late = [by_rank(jnp.sum(grad.astype(WIDE), axis=0)) for grad in (query_rows_grad, value_rows_grad)]
-    heads_share, (tokens_grad, late) = scatter_core(
-        jnp.concatenate(head_grads + [output_grad], axis=1), (tokens_grad, jnp.concatenate(late))
+    vectors = [
+        output_bias_grad,
+        first_gain_grad,
+        first_shift_grad,
+        outer_bias_grad,
+        second_gain_grad,
+        second_shift_grad,
+        by_rank(jnp.sum(query_rows_grad.astype(WIDE), axis=0)),
+        by_rank(jnp.sum(value_rows_grad.astype(WIDE), axis=0)),
+        by_rank(inner_bias_grad),
+    ]
+    vectors = jnp.concatenate(vectors).reshape(-1, 128)
+    vectors = lax.all_gather(vectors, ("tp", "fsdp"), axis=0)
+    heads_share, (tokens_grad,) = scatter_core(
+        jnp.concatenate(head_grads + [output_grad], axis=1), (tokens_grad,)
     )
     tokens_grad = to_owners(tokens_grad)
-    late = late + flip("fsdp", fsdp, 1, late) if fsdp == 8 else lax.psum(late, "fsdp")
     heads_share, tokens_grad[:3] = scatter_near(heads_share, tokens_grad[:3])
-    late = late + flip("fsdp", fsdp, 2, late) if fsdp == 8 else late
     heads_share, tokens_grad[3:] = scatter_far(heads_share, tokens_grad[3:])
-    late = late + flip("fsdp", fsdp, 4, late) if fsdp == 8 else late
-    late = spread(late)
-    late = jnp.sum(by_source(late[:1] + late[:0:-1]), axis=0)
+    heads_share, vectors = lax.optimization_barrier((heads_share, vectors))
+    totals = jnp.sum(vectors, axis=0).reshape(-1)
     query_share, key_share, value_share, output_share = summed(
         own_columns(heads_share, (head_cols,) * 4), (head_cols,) * 4
     )
     tokens_grad = own_places(tokens_grad).astype(WIDE)
-    totals = jnp.concatenate([early[: 6 * width], late, early[6 * width :]])
     rowwise = [totals[i * width : (i + 1) * width] for i in range(6)]
     query_bias_total = lax.dynamic_slice_in_dim(totals, 6 * width + rank * head_cols, head_cols)
     value_bias_total = lax.dynamic_slice_in_dim(totals, 7 * width + rank * head_cols, head_cols)

time: 449 us -> 467 us (1.040)
  waiting for transfers between devices: 94 us -> 125 us
  starting transfers between devices: 82.8 us -> 56.1 us
  local copies, waits for them, and re-layouts: 35.7 us -> 55.3 us
  Pallas kernels: 76.6 us -> 60.4 us
  other arithmetic: 48 us -> 61.8 us
    ppermute x15 -> x12, waiting for transfers between devices: 18.5 us -> 49.2 us  [sent_back(): moved.append(lax.ppermute(parts[step], 'tp', pairs))]
    ppermute x9 -> x6, waiting for transfers between devices: 38.5 us -> 15.4 us  [spread(): return [block] + [lax.ppermute(block, 'tp', pairs) for pairs in rank_pairs]]
    all_gather x0 -> x1, waiting for transfers between devices: none -> 16.9 us  [on_device(): vectors = lax.all_gather(vectors, ('tp', 'fsdp'), axis=0)]
    ppermute x15 -> x12, starting transfers between devices: 31.3 us -> 14.5 us  [sent_back(): moved.append(lax.ppermute(parts[step], 'tp', pairs))]
    ppermute x9 -> x6, starting transfers between devices: 26.2 us -> 14.2 us  [spread(): return [block] + [lax.ppermute(block, 'tp', pairs) for pairs in rank_pairs]]
    ppermute x6, starting transfers between devices: 2.82 us -> 14.3 us  [dealt(): parts.append(lax.ppermute(block, 'tp', pairs) if step else block)]
    unnamed x136 -> x148, local copies, waits for them, and re-layouts: 12.9 us -> 22.3 us
    ppermute x23 -> x15, starting transfers between devices: 22.4 us -> 12.9 us  [flip(): return lax.ppermute(block, axis, [(i, i ^ bit) for i in range(members)])]
  transfers between devices with their start and end apart: 55 -> 42, of which waited for: 19 -> 18; matrix products, arithmetic and copies ran while one was open for 23% -> 32% of each run, Pallas kernels for 17% -> 13%
where the time goes in v6:
time: 467 us; the launch traced here: 461 us
  waiting for transfers between devices  125 us (27%)
  matrix products  87.4 us (19%)
  other arithmetic  61.8 us (13%)
  Pallas kernels  60.4 us (13%)
  starting transfers between devices  56.1 us (12%)
  local copies, waits for them, and re-layouts  55.3 us (12%)
  between operations  15.3 us (3%)
    dot_general x18, matrix products, dot(): return lax.dot_general(left, right, dims, preferred_element_type=WIDE)  87.4 us
    ppermute x12, waiting for transfers between devices, sent_back(): moved.append(lax.ppermute(parts[step], 'tp', pairs))  49.2 us
    pallas_call x2, Pallas kernels, attend_back(): pl.pallas_call(body, grid=(count, pairs - first if part else pairs // 2),...  37.5 us
    ppermute x6, waiting for transfers between devices, dealt(): parts.append(lax.ppermute(block, 'tp', pairs) if step else block)  27 us
    pallas_call x1, Pallas kernels, attend(): pl.pallas_call(functools.partial(attend_kernel, scaling=scaling), grid=(c...  22.8 us
    unnamed x148, local copies, waits for them, and re-layouts  22.3 us
    all_gather x1, waiting for transfers between devices, on_device(): vectors = lax.all_gather(vectors, ('tp', 'fsdp'), axis=0)  16.9 us
    ppermute x15, waiting for transfers between devices, flip(): return lax.ppermute(block, axis, [(i, i ^ bit) for i in range(members)])  16.3 us
  transfers between devices with their start and end apart: 42, of which 18 were waited for; matrix products, arithmetic and copies ran while one was open for 32% of the time, Pallas kernels for 13%

profile of v6, /device:TPU:0, one launch (start us, length us, event | category | flops | bytes accessed | tf_op | source)
XLA Modules:
  0.0 461.2 jit_solution(7499954605948442779)
XLA Ops:
  7.2 2.1 concatenate.90
  13.2 3.1 collective-permute-start
  16.3 2.6 collective-permute-start.1
  24.2 7.6 %collective-permute-done.1 = bf16[99,768]{0,1:T(8,128)(2,1)S(1)} collective-permute-done((bf16[99,768]{0,1:T(8,128)(2,1)S(1)}, bf16[99,768]{0,1:T(8,128)(2,1)S(1)}, u32[]{:S(2)}, u32[]{:S(2)}) %collective-permute-start.1) | collective-permute-done | bytes 152096 | tf_op jit(solution)/shard_map/ppermute | solution.py:156
  32.7 4.7 %collective-permute-start.5 = (bf16[96,1536]{1,0:T(8,128)(2,1)S(1)}, bf16[96,1536]{1,0:T(8,128)(2,1)S(1)}, u32[]{:S(2)}, u32[]{:S(2)}) collective-permute-start(bf16[96,1536]{1,0:T(8,128)(2,1)S(1)} %pad_maximum_fusion.5), channel_id=1, source_target_pairs={{0,1},{1,2},{2,3},{3,0},{4,5},{5,6},{6,7},{7,4},{8,9},{9,10},{10,1... | collective-permute-start | bytes 884744 | tf_op jit(solution)/shard_map/ppermute | solution.py:156
  37.4 1.6 collective-permute-start.6
  40.1 1.5 collective-permute-start.3
  41.6 1.5 collective-permute-start.4
  46.5 4.1 collective-permute-done.3
  51.8 5.6 %collective-permute-done.6 = bf16[96,1536]{1,0:T(8,128)(2,1)S(1)} collective-permute-done((bf16[96,1536]{1,0:T(8,128)(2,1)S(1)}, bf16[96,1536]{1,0:T(8,128)(2,1)S(1)}, u32[]{:S(2)}, u32[]{:S(2)}) %collective-permute-start.6) | collective-permute-done | bytes 294944 | tf_op jit(solution)/shard_map/ppermute | solution.py:156
  63.2 1.6 collective-permute-start.9
  66.1 1.6 collective-permute-start.8
  68.5 6.9 %collective-permute-start.10 = (bf16[1,256,768]{2,1,0:T(8,128)(2,1)S(1)}, bf16[1,256,768]{2,1,0:T(8,128)(2,1)S(1)}, u32[]{:S(2)}, u32[]{:S(2)}) collective-permute-start(bf16[1,256,768]{2,1,0:T(8,128)(2,1)S(1)} %get-tuple-element.258), channel_id=1, source_target_pairs={{0,1},{1,2},{2,3},{3,0},{4,5},{5,6},{6,7},{7,4},{8,9},{9,10},{10,1... | collective-permute-start | bytes 1179656 | tf_op jit(solution)/shard_map/ppermute | solution.py:165
  75.4 2.2 collective-permute-start.11
  77.6 9.5 %collective-permute-done.10 = bf16[1,256,768]{2,1,0:T(8,128)(2,1)S(1)} collective-permute-done((bf16[1,256,768]{2,1,0:T(8,128)(2,1)S(1)}, bf16[1,256,768]{2,1,0:T(8,128)(2,1)S(1)}, u32[]{:S(2)}, u32[]{:S(2)}) %collective-permute-start.10) | collective-permute-done | bytes 393248 | tf_op jit(solution)/shard_map/ppermute | solution.py:165
  87.1 14.9 %collective-permute-done.11 = bf16[1,256,768]{2,1,0:T(8,128)(2,1)S(1)} collective-permute-done((bf16[1,256,768]{2,1,0:T(8,128)(2,1)S(1)}, bf16[1,256,768]{2,1,0:T(8,128)(2,1)S(1)}, u32[]{:S(2)}, u32[]{:S(2)}) %collective-permute-start.11) | collective-permute-done | bytes 393248 | tf_op jit(solution)/shard_map/ppermute | solution.py:165
  114.5 2.6 collective-permute-done.13
  119.4 3.5 collective-permute-start.15
  123.5 2.2 bitcast_select_fusion
  125.7 2.7 fusion.65.k_ref.refs_1_
  128.3 2.6 fusion.37.v_ref.refs_2_
  130.9 2.5 fusion.36.q_ref.refs_0_
  133.5 22.8 %attend.1 = (bf16[1,1024,768]{2,1,0:T(8,128)(2,1)}, f32[1,6,2,1024]{3,2,1,0:T(2,128)}) custom-call(bf16[1,1024,768]{2,1,0:T(8,128)(2,1)} %fusion.36.q_ref.refs_0_, bf16[1,1024,768]{2,1,0:T(8,128)(2,1)} %fusion.65.k_ref.refs_1_, bf16[1,1024,768]{2,1,0:T(8,128)(2,1)} %fusion.37.v_ref.refs_2_, s32[1,1,1024]{2,1,0:T(1,128)} %broadcast_in_dim_reshape.6.row_ref.refs_6_, ...), custom_call_target="tpu_custom_call" | custom-call | flops 22548578304 | bytes 6291456 | tf_op jit(solution)/shard_map/attend/pallas_call | solution.py:93
  157.1 3.8 fusion.112
  161.5 11.4 %multiply_convert_fusion = (bf16[1024,3072]{1,0:T(8,128)(2,1)S(1)}, f32[1024,3072]{1,0:T(8,128)}) fusion(f32[3072]{0:T(1024)} %pad_maximum_fusion.13, bf16[768,6144]{1,0:T(8,128)(2,1)} %all-gather.3.cloned.1.call-done, f32[1024,768]{1,0:T(8,128)S(1)} %get-tuple-element.337, f32[768]{0:T(1024)} %convert_element_type.272, f32[768]{0:T(1024)S(1)} %convert_element_type.271, ...), kind=kOutput, calls=%fused_computation.8 | convolution fusion | flops 4854644736 | bytes 26766336 | tf_op jit(solution)/shard_map/dot_general | solution.py:22
  173.0 5.4 %fusion.113 = (f32[1024]{0:T(1024)S(1)}, f32[1024,768]{1,0:T(8,128)S(1)}) fusion(f32[768]{0:T(1024)S(1)} %copy-done.42, bf16[1024,3072]{1,0:T(8,128)(2,1)S(1)} %get-tuple-element.124, bf16[768,6144]{1,0:T(8,128)(2,1)S(1)} %copy-done.52, f32[768]{0:T(1024)S(1)} %copy-done.40, f32[768]{0:T(1024)S(1)} %convert_element_type.271, ...), kind=kOutput, calls=%fused_computation.270 | convolution fusion | flops 4837342208 | bytes 17326080 | tf_op jit(solution)/shard_map/dot_general | solution.py:22
  179.4 5.3 %fusion.29 = (f32[768]{0:T(1024)}, f32[1024]{0:T(1024)S(1)}, f32[1024]{0:T(1024)S(1)}, bf16[1024,768]{1,0:T(8,128)(2,1)}) fusion(f32[1024,768]{1,0:T(8,128)S(1)} %get-tuple-element.341, f32[1024]{0:T(1024)S(1)} %add_rsqrt_fusion, f32[1024]{0:T(1024)S(1)} %broadcast_multiply_fusion.4, bf16[1,256,768]{2,1,0:T(8,128)(2,1)} %collective-permute-done.16, ...), kind=kLoop, calls=%fused_computation.44 | loop fusion | flops 14939392 | bytes 6317056 | tf_op jit(solution)/shard_map/reduce_sum | solution.py:269
  184.7 4.1 fusion.99
  188.8 1.7 copy-done.14
  190.5 6.9 %convolution_convert_fusion = bf16[768,3072]{1,0:T(8,128)(2,1)} fusion(bf16[1024,3072]{1,0:T(8,128)(2,1)S(1)} %get-tuple-element.124, f32[1024,768]{1,0:T(8,128)S(1)} %get-tuple-element.234), kind=kOutput, calls=%fused_computation.13 | convolution fusion | flops 4834983936 | bytes 14155776 | tf_op jit(solution)/shard_map/dot_general | solution.py:22
  197.5 14.0 %convert_reduce_fusion = (f32[3072]{0:T(1024)}, bf16[1024,3072]{1,0:T(8,128)(2,1)S(1)}) fusion(f32[1024,3072]{1,0:T(8,128)} %get-tuple-element.339, f32[3072]{0:T(1024)} %pad_maximum_fusion.13, bf16[768,6144]{1,0:T(8,128)(2,1)} %all-gather.3.cloned.1.call-done, f32[1024,768]{1,0:T(8,128)} %copy-done.14), kind=kOutput, calls=%fused_computation.7 | convolution fusion | flops 4873516032 | bytes 26763264 | tf_op jit(solution)/shard_map/dot_general | solution.py:22
  211.4 6.5 %convolution_convert_fusion.1 = bf16[768,3072]{1,0:T(8,128)(2,1)S(1)} fusion(bf16[1024,3072]{1,0:T(8,128)(2,1)S(1)} %get-tuple-element.344, f32[1024,768]{1,0:T(8,128)S(1)} %get-tuple-element.337, f32[768]{0:T(1024)S(1)} %copy-done.41, f32[768]{0:T(1024)S(1)} %convert_element_type.271, f32[1024]{0:T(1024)S(1)} %copy-done.37, ...), kind=kOutput, calls=%fused_computation.14 | convolution fusion | flops 4838129664 | bytes 14170112 | tf_op jit(solution)/shard_map/dot_general | solution.py:22
  217.9 1.7 constant_dynamic-slice_fusion.13
  219.7 1.6 copy.126
  224.1 1.9 collective-permute-start.19
  226.1 8.1 %multiply_reduce_fusion = (f32[768]{0:T(1024)}, f32[1024]{0:T(1024)}, f32[1024]{0:T(1024)}, f32[768]{0:T(1024)}, f32[1024,768]{1,0:T(8,128)}) fusion(f32[1024,768]{1,0:T(8,128)S(1)} %get-tuple-element.337, f32[1024]{0:T(1024)S(1)} %copy-done.37, f32[1024]{0:T(1024)S(1)} %broadcast_multiply_fusion.5, f32[768]{0:T(1024)S(1)} %convert_element_type.271, ...), kind=kOutput, calls=%fused_computation.47 | convolution fusion | flops 4839698432 | bytes 20473856 | tf_op jit(solution)/shard_map/dot_general | solution.py:22
  236.4 2.9 fusion.101
  239.3 1.6 constant_dynamic-update-slice_fusion.16
  244.1 4.0 fusion.66.g_ref.refs_3_
  248.1 12.5 %collective-permute-done.19 = bf16[1,256,768]{2,1,0:T(8,128)(2,1)} collective-permute-done((bf16[1,256,768]{2,1,0:T(8,128)(2,1)}, bf16[1,256,768]{2,1,0:T(8,128)(2,1)}, u32[]{:S(2)}, u32[]{:S(2)}) %collective-permute-start.19) | collective-permute-done | bytes 393248 | tf_op jit(solution)/shard_map/ppermute | solution.py:174
  260.6 2.6 fusion.7
  268.1 1.5 convert_reduce_fusion.1
  269.7 4.0 fusion.53
  273.7 5.3 %collective-permute-done.21 = bf16[2,96,1536]{2,1,0:T(8,128)(2,1)} collective-permute-done((bf16[2,96,1536]{2,1,0:T(8,128)(2,1)}, bf16[2,96,1536]{2,1,0:T(8,128)(2,1)}, u32[]{:S(2)}, u32[]{:S(2)}) %collective-permute-start.21) | collective-permute-done | bytes 589856 | tf_op jit(solution)/shard_map/ppermute | solution.py:189
  286.3 18.5 %attend_back.2 = (bf16[1,1024,768]{2,1,0:T(8,128)(2,1)}, bf16[1,1024,768]{2,1,0:T(8,128)(2,1)}, bf16[1,1024,768]{2,1,0:T(8,128)(2,1)}) custom-call(bf16[1,1024,768]{2,1,0:T(8,128)(2,1)} %fusion.36.q_ref.refs_0_, bf16[1,1024,768]{2,1,0:T(8,128)(2,1)} %fusion.65.k_ref.refs_1_, bf16[1,1024,768]{2,1,0:T(8,128)(2,1)} %fusion.37.v_ref.refs_2_, ...), custom_call_target="tpu_custom_call" | custom-call | flops 19327352832 | bytes 5505024 | tf_op jit(solution)/shard_map/attend_back/pallas_call | solution.py:128
  312.5 3.8 collective-permute-start.25
  316.3 19.0 %attend_back.3 = (bf16[1,1024,768]{2,1,0:T(8,128)(2,1)}, bf16[1,1024,768]{2,1,0:T(8,128)(2,1)}, bf16[1,1024,768]{2,1,0:T(8,128)(2,1)}) custom-call(bf16[1,1024,768]{2,1,0:T(8,128)(2,1)} %fusion.36.q_ref.refs_0_, bf16[1,1024,768]{2,1,0:T(8,128)(2,1)} %fusion.65.k_ref.refs_1_, ...), custom_call_target="tpu_custom_call", output_to_operand_aliasing={{0}: (8, {}), {1}: (9, {}), {2}: (10, {})} | custom-call | flops 19327352832 | bytes 5505024 | tf_op jit(solution)/shard_map/attend_back/pallas_call | solution.py:128
  336.0 3.5 fusion.56
  343.3 2.2 copy-done
  345.6 1.6 dynamic-slice_bitcast_fusion
  350.2 1.7 convert_reduce_fusion.3
  352.0 3.3 fusion.46
  355.3 2.8 fusion.42
  358.2 2.9 add_convert_fusion
  361.2 2.6 fusion.6
  366.2 1.7 collective-permute-start.29
  370.4 3.0 collective-permute-start.32
  376.8 4.6 collective-permute-done.31
  381.4 27.4 %collective-permute-done.32 = bf16[1,256,768]{2,1,0:T(8,128)(2,1)} collective-permute-done((bf16[1,256,768]{2,1,0:T(8,128)(2,1)}, bf16[1,256,768]{2,1,0:T(8,128)(2,1)}, u32[]{:S(2)}, u32[]{:S(2)}) %collective-permute-start.32) | collective-permute-done | bytes 393248 | tf_op jit(solution)/shard_map/ppermute | solution.py:174
  415.1 2.9 collective-permute-done.34
  419.8 16.9 %all-gather.5.cloned.1.call-done = f32[32,72,128]{2,1,0:T(8,128)} async-done(((f32[1,72,128]{2,1,0:T(8,128)}), f32[32,72,128]{2,1,0:T(8,128)}) %all-gather.5.cloned.1.call-update) | async-done | bytes 1179664 | tf_op jit(solution)/shard_map/all_gather | solution.py:464
  437.0 2.3 collective-permute-start.36
  441.8 4.3 fusion.38
  448.0 4.7 %collective-permute-done.37 = bf16[96,768]{1,0:T(8,128)(2,1)S(1)} collective-permute-done((bf16[96,768]{1,0:T(8,128)(2,1)}, bf16[96,768]{1,0:T(8,128)(2,1)S(1)}, u32[]{:S(2)}, u32[]{:S(2)}) %collective-permute-start.37) | collective-permute-done | bytes 147488 | tf_op jit(solution)/shard_map/ppermute | solution.py:174
  (334 shorter events, 99.4 us)
Async XLA Ops:
  7.2 32.8 %copy-start.33 = (bf16[192,96]{1,0:T(8,128)(2,1)S(1)}, bf16[192,96]{1,0:T(8,128)(2,1)}, u32[]{:S(2)}) copy-start(bf16[192,96]{1,0:T(8,128)(2,1)} %param.27) | copy-start | bytes 110596
  7.2 154.2 %all-gather.3.cloned.1.call-start = ((), (), s32[]{:S(2)}) async-start(), calls=%async_computation.1 | async-start | bytes 10616832 | tf_op jit(solution)/shard_map/all_gather | solution.py:376
  13.2 11.0 %collective-permute-start = (bf16[99,768]{0,1:T(8,128)(2,1)S(1)}, bf16[99,768]{0,1:T(8,128)(2,1)S(1)}, u32[]{:S(2)}, u32[]{:S(2)}) collective-permute-start(bf16[99,768]{0,1:T(8,128)(2,1)S(1)} %fusion.94), channel_id=1, source_target_pairs={{0,1},{1,2},{2,3},{3,0},{4,5},{5,6},{6,7},{7,4},{8,9},{9,10},{10,1... | collective-permute-start | bytes 456200 | tf_op jit(solution)/shard_map/ppermute | solution.py:156
  16.3 15.5 %collective-permute-start.1 = (bf16[99,768]{0,1:T(8,128)(2,1)S(1)}, bf16[99,768]{0,1:T(8,128)(2,1)S(1)}, u32[]{:S(2)}, u32[]{:S(2)}) collective-permute-start(bf16[99,768]{0,1:T(8,128)(2,1)S(1)} %fusion.94), channel_id=1, source_target_pairs={{0,2},{1,3},{2,0},{3,1},{4,6},{5,7},{6,4},{7,5},{8,10},{9,11},{10,... | collective-permute-start | bytes 456200 | tf_op jit(solution)/shard_map/ppermute | solution.py:156
  18.9 12.9 %collective-permute-start.2 = (bf16[99,768]{0,1:T(8,128)(2,1)S(1)}, bf16[99,768]{0,1:T(8,128)(2,1)S(1)}, u32[]{:S(2)}, u32[]{:S(2)}) collective-permute-start(bf16[99,768]{0,1:T(8,128)(2,1)S(1)} %fusion.94), channel_id=1, source_target_pairs={{0,3},{1,0},{2,1},{3,2},{4,7},{5,4},{6,5},{7,6},{8,11},{9,8},{10,9... | collective-permute-start | bytes 456200 | tf_op jit(solution)/shard_map/ppermute | solution.py:156
  32.7 13.8 %collective-permute-start.5 = (bf16[96,1536]{1,0:T(8,128)(2,1)S(1)}, bf16[96,1536]{1,0:T(8,128)(2,1)S(1)}, u32[]{:S(2)}, u32[]{:S(2)}) collective-permute-start(bf16[96,1536]{1,0:T(8,128)(2,1)S(1)} %pad_maximum_fusion.5), channel_id=1, source_target_pairs={{0,1},{1,2},{2,3},{3,0},{4,5},{5,6},{6,7},{7,4},{8,9},{9,10},{10,1... | collective-permute-start | bytes 884744 | tf_op jit(solution)/shard_map/ppermute | solution.py:156
  37.4 20.0 %collective-permute-start.6 = (bf16[96,1536]{1,0:T(8,128)(2,1)S(1)}, bf16[96,1536]{1,0:T(8,128)(2,1)S(1)}, u32[]{:S(2)}, u32[]{:S(2)}) collective-permute-start(bf16[96,1536]{1,0:T(8,128)(2,1)S(1)} %pad_maximum_fusion.5), channel_id=1, source_target_pairs={{0,2},{1,3},{2,0},{3,1},{4,6},{5,7},{6,4},{7,5},{8,10},{9,11},{10,... | collective-permute-start | bytes 884744 | tf_op jit(solution)/shard_map/ppermute | solution.py:156
  39.1 18.4 %collective-permute-start.7 = (bf16[96,1536]{1,0:T(8,128)(2,1)S(1)}, bf16[96,1536]{1,0:T(8,128)(2,1)}, u32[]{:S(2)}, u32[]{:S(2)}) collective-permute-start(bf16[96,1536]{1,0:T(8,128)(2,1)S(1)} %pad_maximum_fusion.5), channel_id=1, source_target_pairs={{0,3},{1,0},{2,1},{3,2},{4,7},{5,4},{6,5},{7,6},{8,11},{9,8},{10,9... | collective-permute-start | bytes 884744 | tf_op jit(solution)/shard_map/ppermute | solution.py:156
  40.1 17.4 %copy-start.27 = (bf16[96,1536]{0,1:T(8,128)(2,1)}, bf16[96,1536]{0,1:T(8,128)(2,1)S(1)}, u32[]{:S(2)}) copy-start(bf16[96,1536]{0,1:T(8,128)(2,1)S(1)} %get-tuple-element.290) | copy-start | bytes 884740
  40.1 10.5 %collective-permute-start.3 = (bf16[96,1536]{0,1:T(8,128)(2,1)S(1)}, bf16[96,1536]{0,1:T(8,128)(2,1)S(1)}, u32[]{:S(2)}, u32[]{:S(2)}) collective-permute-start(bf16[96,1536]{0,1:T(8,128)(2,1)S(1)} %get-tuple-element.291), channel_id=1, source_target_pairs={{0,8},{4,12},{8,0},{12,4},{16,24},{20,28},{24,16},{28,20},{1,9},{5... | collective-permute-start | bytes 884744 | tf_op jit(solution)/shard_map/ppermute | solution.py:189
  41.6 10.2 %collective-permute-start.4 = (bf16[96,1536]{0,1:T(8,128)(2,1)S(1)}, bf16[96,1536]{0,1:T(8,128)(2,1)S(1)}, u32[]{:S(2)}, u32[]{:S(2)}) collective-permute-start(bf16[96,1536]{0,1:T(8,128)(2,1)S(1)} %get-tuple-element.290), channel_id=1, source_target_pairs={{0,16},{4,20},{8,24},{12,28},{16,0},{20,4},{24,8},{28,12},{1,17},{... | collective-permute-start | bytes 884744 | tf_op jit(solution)/shard_map/ppermute | solution.py:189
  60.4 247.5 %reduce-scatter.2.cloned.1.call-start = ((), (), s32[]{:S(2)}) async-start(), calls=%async_computation.2 | async-start | bytes 5308416 | tf_op jit(solution)/shard_map/reduce_scatter | solution.py:408
  63.2 38.8 %collective-permute-start.9 = (bf16[2,96,1536]{2,1,0:T(8,128)(2,1)S(1)}, bf16[2,96,1536]{2,1,0:T(8,128)(2,1)}, u32[]{:S(2)}, u32[]{:S(2)}) collective-permute-start(bf16[2,96,1536]{2,1,0:T(8,128)(2,1)S(1)} %broadcast_select_fusion.2), channel_id=1, source_target_pairs={{0,8},{4,12},{8,0},{12,4},{16,24},{20,28},{24,16},{28,20},{1,9},{5... | collective-permute-start | bytes 1769480 | tf_op jit(solution)/shard_map/ppermute | solution.py:189
  66.1 36.0 %collective-permute-start.8 = (bf16[2,96,1536]{2,1,0:T(8,128)(2,1)S(1)}, bf16[2,96,1536]{2,1,0:T(8,128)(2,1)}, u32[]{:S(2)}, u32[]{:S(2)}) collective-permute-start(bf16[2,96,1536]{2,1,0:T(8,128)(2,1)S(1)} %broadcast_select_fusion.3), channel_id=1, source_target_pairs={{0,16},{4,20},{8,24},{12,28},{16,0},{20,4},{24,8},{28,12},{1,17},{... | collective-permute-start | bytes 1769480 | tf_op jit(solution)/shard_map/ppermute | solution.py:189
  68.5 18.6 %collective-permute-start.10 = (bf16[1,256,768]{2,1,0:T(8,128)(2,1)S(1)}, bf16[1,256,768]{2,1,0:T(8,128)(2,1)S(1)}, u32[]{:S(2)}, u32[]{:S(2)}) collective-permute-start(bf16[1,256,768]{2,1,0:T(8,128)(2,1)S(1)} %get-tuple-element.258), channel_id=1, source_target_pairs={{0,1},{1,2},{2,3},{3,0},{4,5},{5,6},{6,7},{7,4},{8,9},{9,10},{10,1... | collective-permute-start | bytes 1179656 | tf_op jit(solution)/shard_map/ppermute | solution.py:165
  75.4 26.6 %collective-permute-start.11 = (bf16[1,256,768]{2,1,0:T(8,128)(2,1)S(1)}, bf16[1,256,768]{2,1,0:T(8,128)(2,1)S(1)}, u32[]{:S(2)}, u32[]{:S(2)}) collective-permute-start(bf16[1,256,768]{2,1,0:T(8,128)(2,1)S(1)} %get-tuple-element.257), channel_id=1, source_target_pairs={{0,2},{1,3},{2,0},{3,1},{4,6},{5,7},{6,4},{7,5},{8,10},{9,11},{10,... | collective-permute-start | bytes 1179656 | tf_op jit(solution)/shard_map/ppermute | solution.py:165
  104.9 12.2 %copy-start.30 = (bf16[1,256,768]{2,1,0:T(8,128)(2,1)S(1)}, bf16[1,256,768]{2,1,0:T(8,128)(2,1)}, u32[]{:S(2)}) copy-start(bf16[1,256,768]{2,1,0:T(8,128)(2,1)} %copy-done.29) | copy-start | bytes 1179652
  105.2 11.9 %collective-permute-start.12 = (bf16[2,2,96,3072]{3,2,1,0:T(8,128)(2,1)S(1)}, bf16[2,2,96,3072]{3,2,1,0:T(8,128)(2,1)}, u32[]{:S(2)}, u32[]{:S(2)}) collective-permute-start(bf16[2,2,96,3072]{3,2,1,0:T(8,128)(2,1)S(1)} %pad_maximum_fusion.1), channel_id=1, source_target_pairs={{0,4},{4,0},{8,12},{12,8},{16,20},{20,16},{24,28},{28,24},{1,5},{5... | collective-permute-start | bytes 7077896 | tf_op jit(solution)/shard_map/ppermute | solution.py:189
  105.3 11.8 %collective-permute-start.13 = (bf16[1,256,768]{2,1,0:T(8,128)(2,1)}, bf16[1,256,768]{2,1,0:T(8,128)(2,1)}, u32[]{:S(2)}, u32[]{:S(2)}) collective-permute-start(bf16[1,256,768]{2,1,0:T(8,128)(2,1)} %get-tuple-element.256), channel_id=1, source_target_pairs={{0,3},{1,0},{2,1},{3,2},{4,7},{5,4},{6,5},{7,6},{8,11},{9,8},{10,9... | collective-permute-start | bytes 1179656 | tf_op jit(solution)/shard_map/ppermute | solution.py:165
  107.9 118.2 %copy-start.34 = (f32[768]{0:T(1024)}, f32[768]{0:T(1024)S(1)}, u32[]{:S(2)}) copy-start(f32[768]{0:T(1024)S(1)} %convert_element_type.271) | copy-start | bytes 9220
  118.2 12.7 %copy-start.19 = (bf16[1024,768]{1,0:T(8,128)(2,1)}, bf16[1024,768]{1,0:T(8,128)(2,1)S(1)}, u32[]{:S(2)}) copy-start(bf16[1024,768]{1,0:T(8,128)(2,1)S(1)} %maximum_bitcast_fusion) | copy-start | bytes 4718596
  119.4 37.0 %collective-permute-start.14 = (bf16[1,256,768]{2,1,0:T(8,128)(2,1)S(1)}, bf16[1,256,768]{2,1,0:T(8,128)(2,1)S(1)}, u32[]{:S(2)}, u32[]{:S(2)}) collective-permute-start(bf16[1,256,768]{2,1,0:T(8,128)(2,1)S(1)} %get-tuple-element.255), channel_id=1, source_target_pairs={{0,2},{1,3},{2,0},{3,1},{4,6},{5,7},{6,4},{7,5},{8,10},{9,11},{10,... | collective-permute-start | bytes 1179656 | tf_op jit(solution)/shard_map/ppermute | solution.py:165
  119.4 53.5 %collective-permute-start.15 = (bf16[1,256,768]{2,1,0:T(8,128)(2,1)}, bf16[1,256,768]{2,1,0:T(8,128)(2,1)}, u32[]{:S(2)}, u32[]{:S(2)}) collective-permute-start(bf16[1,256,768]{2,1,0:T(8,128)(2,1)} %get-tuple-element.254), channel_id=1, source_target_pairs={{0,1},{1,2},{2,3},{3,0},{4,5},{5,6},{6,7},{7,4},{8,9},{9,10},{10,1... | collective-permute-start | bytes 1179656 | tf_op jit(solution)/shard_map/ppermute | solution.py:165
  122.9 50.0 %collective-permute-start.16 = (bf16[1,256,768]{2,1,0:T(8,128)(2,1)}, bf16[1,256,768]{2,1,0:T(8,128)(2,1)}, u32[]{:S(2)}, u32[]{:S(2)}) collective-permute-start(bf16[1,256,768]{2,1,0:T(8,128)(2,1)} %get-tuple-element.253), channel_id=1, source_target_pairs={{0,3},{1,0},{2,1},{3,2},{4,7},{5,4},{6,5},{7,6},{8,11},{9,8},{10,9... | collective-permute-start | bytes 1179656 | tf_op jit(solution)/shard_map/ppermute | solution.py:165
  133.5 23.6 %copy-start.43 = (f32[768]{0:T(1024)S(1)}, f32[768]{0:T(1024)}, u32[]{:S(2)}) copy-start(f32[768]{0:T(1024)} %convert_element_type.270) | copy-start | bytes 9220
  161.4 11.5 %copy-start.36 = (f32[1024]{0:T(1024)}, f32[1024]{0:T(1024)S(1)}, u32[]{:S(2)}) copy-start(f32[1024]{0:T(1024)S(1)} %add_rsqrt_fusion.1) | copy-start | bytes 12292
  161.4 11.5 %copy-start.40 = (f32[768]{0:T(1024)S(1)}, f32[768]{0:T(1024)}, u32[]{:S(2)}) copy-start(f32[768]{0:T(1024)} %convert_element_type.272) | copy-start | bytes 9220
  161.5 11.5 %copy-start.42 = (f32[768]{0:T(1024)S(1)}, f32[768]{0:T(1024)}, u32[]{:S(2)}) copy-start(f32[768]{0:T(1024)} %convert_element_type.275) | copy-start | bytes 9220
  161.5 11.5 %copy-start.52 = (bf16[768,6144]{1,0:T(8,128)(2,1)S(1)}, bf16[768,6144]{1,0:T(8,128)(2,1)}, u32[]{:S(2)}) copy-start(bf16[768,6144]{1,0:T(8,128)(2,1)} %all-gather.3.cloned.1.call-done) | copy-start | bytes 28311556
  197.4 239.3 %all-gather.5.cloned.1.call-start = ((), (), s32[]{:S(2)}) async-start(), calls=%async_computation.3 | async-start | bytes 1216512 | tf_op jit(solution)/shard_map/all_gather | solution.py:464
  197.5 14.0 %copy-start.37 = (f32[1024]{0:T(1024)S(1)}, f32[1024]{0:T(1024)}, u32[]{:S(2)}) copy-start(f32[1024]{0:T(1024)} %copy-done.36) | copy-start | bytes 12292
  197.5 14.0 %copy-start.41 = (f32[768]{0:T(1024)S(1)}, f32[768]{0:T(1024)}, u32[]{:S(2)}) copy-start(f32[768]{0:T(1024)} %convert_element_type.272) | copy-start | bytes 9220
  211.4 14.7 %slice-start.2 = ((s8[9437184]{0:T(1024)(128)(4,1)}), s8[4194304]{0:T(1024)(128)(4,1)S(1)}, s32[]{:S(2)}) async-start(s8[9437184]{0:T(1024)(128)(4,1)} %bitcast.196), calls=%async_computation.6 | async-start | bytes 8388608
  211.4 14.7 %slice-start.3 = ((s8[9437184]{0:T(1024)(128)(4,1)}), s8[4194304]{0:T(1024)(128)(4,1)S(1)}, s32[]{:S(2)}) async-start(s8[9437184]{0:T(1024)(128)(4,1)} %bitcast.196), calls=%async_computation.7 | async-start | bytes 8388608
  221.3 39.3 %collective-permute-start.17 = (bf16[2,2,96,3072]{3,2,0,1:T(8,128)(2,1)}, bf16[2,2,96,3072]{3,2,0,1:T(8,128)(2,1)}, u32[]{:S(2)}, u32[]{:S(2)}) collective-permute-start(bf16[2,2,96,3072]{3,2,0,1:T(8,128)(2,1)} %bitcast.180), channel_id=1, source_target_pairs={{0,4},{4,0},{8,12},{12,8},{16,20},{20,16},{24,28},{28,24},{1,5},{5... | collective-permute-start | bytes 7077896 | tf_op jit(solution)/shard_map/ppermute | solution.py:189
  223.0 25.1 %collective-permute-start.18 = (bf16[1,256,768]{2,1,0:T(8,128)(2,1)}, bf16[1,256,768]{2,1,0:T(8,128)(2,1)}, u32[]{:S(2)}, u32[]{:S(2)}) collective-permute-start(bf16[1,256,768]{2,1,0:T(8,128)(2,1)} %get-tuple-element.250), channel_id=1, source_target_pairs={{0,3},{1,0},{2,1},{3,2},{4,7},{5,4},{6,5},{7,6},{8,11},{9,8},{10,9... | collective-permute-start | bytes 1179656 | tf_op jit(solution)/shard_map/ppermute | solution.py:174
  224.1 36.5 %collective-permute-start.19 = (bf16[1,256,768]{2,1,0:T(8,128)(2,1)}, bf16[1,256,768]{2,1,0:T(8,128)(2,1)}, u32[]{:S(2)}, u32[]{:S(2)}) collective-permute-start(bf16[1,256,768]{2,1,0:T(8,128)(2,1)} %get-tuple-element.249), channel_id=1, source_target_pairs={{0,2},{1,3},{2,0},{3,1},{4,6},{5,7},{6,4},{7,5},{8,10},{9,11},{10,... | collective-permute-start | bytes 1179656 | tf_op jit(solution)/shard_map/ppermute | solution.py:174
  226.0 56.9 %collective-permute-start.22 = (bf16[1,256,768]{2,1,0:T(8,128)(2,1)}, bf16[1,256,768]{2,1,0:T(8,128)(2,1)}, u32[]{:S(2)}, u32[]{:S(2)}) collective-permute-start(bf16[1,256,768]{2,1,0:T(8,128)(2,1)} %get-tuple-element.248), channel_id=1, source_target_pairs={{0,1},{1,2},{2,3},{3,0},{4,5},{5,6},{6,7},{7,4},{8,9},{9,10},{10,1... | collective-permute-start | bytes 1179656 | tf_op jit(solution)/shard_map/ppermute | solution.py:174
  244.1 16.5 %copy-start.3 = (bf16[2,2,1,96,3072]{4,3,2,1,0:T(8,128)(2,1)S(1)}, bf16[2,2,1,96,3072]{4,3,2,1,0:T(8,128)(2,1)}, u32[]{:S(2)}) copy-start(bf16[2,2,1,96,3072]{4,3,2,1,0:T(8,128)(2,1)} %get-tuple-element.237) | copy-start | bytes 7077892
  264.4 14.7 %collective-permute-start.21 = (bf16[2,96,1536]{2,1,0:T(8,128)(2,1)}, bf16[2,96,1536]{2,1,0:T(8,128)(2,1)}, u32[]{:S(2)}, u32[]{:S(2)}) collective-permute-start(bf16[2,96,1536]{2,1,0:T(8,128)(2,1)} %dynamic-slice_bitcast_fusion.3), channel_id=1, source_target_pairs={{0,8},{4,12},{8,0},{12,4},{16,24},{20,28},{24,16},{28,20},{1,9},{5... | collective-permute-start | bytes 1769480 | tf_op jit(solution)/shard_map/ppermute | solution.py:189
  265.7 14.6 %collective-permute-start.20 = (bf16[2,96,1536]{2,1,0:T(8,128)(2,1)}, bf16[2,96,1536]{2,1,0:T(8,128)(2,1)}, u32[]{:S(2)}, u32[]{:S(2)}) collective-permute-start(bf16[2,96,1536]{2,1,0:T(8,128)(2,1)} %dynamic-slice_bitcast_fusion.4), channel_id=1, source_target_pairs={{0,16},{4,20},{8,24},{12,28},{16,0},{20,4},{24,8},{28,12},{1,17},{... | collective-permute-start | bytes 1769480 | tf_op jit(solution)/shard_map/ppermute | solution.py:189
  269.7 10.6 %copy-start.11 = (bf16[2,2,96,1536]{3,2,0,1:T(8,128)(2,1)S(1)}, bf16[2,2,96,1536]{3,2,0,1:T(8,128)(2,1)}, u32[]{:S(2)}) copy-start(bf16[2,2,96,1536]{3,2,0,1:T(8,128)(2,1)} %copy-done.10) | copy-start | bytes 3538948
  269.7 11.8 %copy-start.9 = (bf16[2,2,96,1536]{3,2,0,1:T(8,128)(2,1)S(1)}, bf16[2,2,96,1536]{3,2,0,1:T(8,128)(2,1)}, u32[]{:S(2)}) copy-start(bf16[2,2,96,1536]{3,2,0,1:T(8,128)(2,1)} %copy-done.8) | copy-start | bytes 3538948
  283.8 21.1 %collective-permute-start.24 = (bf16[96,1536]{1,0:T(8,128)(2,1)}, bf16[96,1536]{1,0:T(8,128)(2,1)S(1)}, u32[]{:S(2)}, u32[]{:S(2)}) collective-permute-start(bf16[96,1536]{1,0:T(8,128)(2,1)} %dynamic-slice_bitcast_fusion.7), channel_id=1, source_target_pairs={{0,16},{4,20},{8,24},{12,28},{16,0},{20,4},{24,8},{28,12},{1,17},{... | collective-permute-start | bytes 884744 | tf_op jit(solution)/shard_map/ppermute | solution.py:189
  284.9 20.0 %collective-permute-start.23 = (bf16[96,1536]{1,0:T(8,128)(2,1)}, bf16[96,1536]{1,0:T(8,128)(2,1)}, u32[]{:S(2)}, u32[]{:S(2)}) collective-permute-start(bf16[96,1536]{1,0:T(8,128)(2,1)} %dynamic-slice_bitcast_fusion.8), channel_id=1, source_target_pairs={{0,8},{4,12},{8,0},{12,4},{16,24},{20,28},{24,16},{28,20},{1,9},{5... | collective-permute-start | bytes 884744 | tf_op jit(solution)/shard_map/ppermute | solution.py:189
  311.0 25.0 %collective-permute-start.27 = (bf16[96,1536]{1,0:T(8,128)(2,1)}, bf16[96,1536]{1,0:T(8,128)(2,1)}, u32[]{:S(2)}, u32[]{:S(2)}) collective-permute-start(bf16[96,1536]{1,0:T(8,128)(2,1)} %pad_maximum_fusion.9), channel_id=1, source_target_pairs={{0,1},{1,2},{2,3},{3,0},{4,5},{5,6},{6,7},{7,4},{8,9},{9,10},{10,1... | collective-permute-start | bytes 884744 | tf_op jit(solution)/shard_map/ppermute | solution.py:174
  311.7 24.3 %collective-permute-start.26 = (bf16[96,1536]{1,0:T(8,128)(2,1)}, bf16[96,1536]{1,0:T(8,128)(2,1)}, u32[]{:S(2)}, u32[]{:S(2)}) collective-permute-start(bf16[96,1536]{1,0:T(8,128)(2,1)} %pad_maximum_fusion.8), channel_id=1, source_target_pairs={{0,2},{1,3},{2,0},{3,1},{4,6},{5,7},{6,4},{7,5},{8,10},{9,11},{10,... | collective-permute-start | bytes 884744 | tf_op jit(solution)/shard_map/ppermute | solution.py:174
  312.5 23.5 %collective-permute-start.25 = (bf16[96,1536]{1,0:T(8,128)(2,1)}, bf16[96,1536]{1,0:T(8,128)(2,1)}, u32[]{:S(2)}, u32[]{:S(2)}) collective-permute-start(bf16[96,1536]{1,0:T(8,128)(2,1)} %pad_maximum_fusion.7), channel_id=1, source_target_pairs={{0,3},{1,0},{2,1},{3,2},{4,7},{5,4},{6,5},{7,6},{8,11},{9,8},{10,9... | collective-permute-start | bytes 884744 | tf_op jit(solution)/shard_map/ppermute | solution.py:174
  347.1 14.0 %collective-permute-start.28 = (bf16[2,2,96,3072]{3,2,1,0:T(8,128)(2,1)}, bf16[2,2,96,3072]{3,2,1,0:T(8,128)(2,1)}, u32[]{:S(2)}, u32[]{:S(2)}) collective-permute-start(bf16[2,2,96,3072]{3,2,1,0:T(8,128)(2,1)} %dynamic-slice_bitcast_fusion), channel_id=1, source_target_pairs={{0,4},{4,0},{8,12},{12,8},{16,20},{20,16},{24,28},{28,24},{1,5},{5... | collective-permute-start | bytes 7077896 | tf_op jit(solution)/shard_map/ppermute | solution.py:189
  364.8 44.0 %collective-permute-start.30 = (bf16[2,96,1536]{2,1,0:T(8,128)(2,1)}, bf16[2,96,1536]{2,1,0:T(8,128)(2,1)}, u32[]{:S(2)}, u32[]{:S(2)}) collective-permute-start(bf16[2,96,1536]{2,1,0:T(8,128)(2,1)} %dynamic-slice_bitcast_fusion.1), channel_id=1, source_target_pairs={{0,8},{4,12},{8,0},{12,4},{16,24},{20,28},{24,16},{28,20},{1,9},{5... | collective-permute-start | bytes 1769480 | tf_op jit(solution)/shard_map/ppermute | solution.py:189
  366.2 42.5 %collective-permute-start.29 = (bf16[2,96,1536]{2,1,0:T(8,128)(2,1)}, bf16[2,96,1536]{2,1,0:T(8,128)(2,1)}, u32[]{:S(2)}, u32[]{:S(2)}) collective-permute-start(bf16[2,96,1536]{2,1,0:T(8,128)(2,1)} %dynamic-slice_bitcast_fusion.2), channel_id=1, source_target_pairs={{0,16},{4,20},{8,24},{12,28},{16,0},{20,4},{24,8},{28,12},{1,17},{... | collective-permute-start | bytes 1769480 | tf_op jit(solution)/shard_map/ppermute | solution.py:189
  369.0 44.0 %copy-start.25 = (bf16[96,1536]{1,0:T(8,128)(2,1)S(1)}, bf16[96,1536]{1,0:T(8,128)(2,1)}, u32[]{:S(2)}) copy-start(bf16[96,1536]{1,0:T(8,128)(2,1)} %pad_maximum_fusion.6) | copy-start | bytes 884740
  369.0 12.4 %collective-permute-start.31 = (bf16[1,256,768]{2,1,0:T(8,128)(2,1)}, bf16[1,256,768]{2,1,0:T(8,128)(2,1)S(1)}, u32[]{:S(2)}, u32[]{:S(2)}) collective-permute-start(bf16[1,256,768]{2,1,0:T(8,128)(2,1)} %get-tuple-element.246), channel_id=1, source_target_pairs={{0,3},{1,0},{2,1},{3,2},{4,7},{5,4},{6,5},{7,6},{8,11},{9,8},{10,9... | collective-permute-start | bytes 1179656 | tf_op jit(solution)/shard_map/ppermute | solution.py:174
  370.4 38.3 %collective-permute-start.32 = (bf16[1,256,768]{2,1,0:T(8,128)(2,1)}, bf16[1,256,768]{2,1,0:T(8,128)(2,1)}, u32[]{:S(2)}, u32[]{:S(2)}) collective-permute-start(bf16[1,256,768]{2,1,0:T(8,128)(2,1)} %get-tuple-element.245), channel_id=1, source_target_pairs={{0,2},{1,3},{2,0},{3,1},{4,6},{5,7},{6,4},{7,5},{8,10},{9,11},{10,... | collective-permute-start | bytes 1179656 | tf_op jit(solution)/shard_map/ppermute | solution.py:174
  376.8 38.4 %collective-permute-start.35 = (bf16[1,256,768]{2,1,0:T(8,128)(2,1)}, bf16[1,256,768]{2,1,0:T(8,128)(2,1)S(1)}, u32[]{:S(2)}, u32[]{:S(2)}) collective-permute-start(bf16[1,256,768]{2,1,0:T(8,128)(2,1)} %get-tuple-element.244), channel_id=1, source_target_pairs={{0,1},{1,2},{2,3},{3,0},{4,5},{5,6},{6,7},{7,4},{8,9},{9,10},{10,1... | collective-permute-start | bytes 1179656 | tf_op jit(solution)/shard_map/ppermute | solution.py:174
  410.0 8.1 %collective-permute-start.34 = (bf16[96,1536]{1,0:T(8,128)(2,1)S(1)}, bf16[96,1536]{1,0:T(8,128)(2,1)S(1)}, u32[]{:S(2)}, u32[]{:S(2)}) collective-permute-start(bf16[96,1536]{1,0:T(8,128)(2,1)S(1)} %dynamic-slice_bitcast_fusion.5), channel_id=1, source_target_pairs={{0,16},{4,20},{8,24},{12,28},{16,0},{20,4},{24,8},{28,12},{1,17},{... | collective-permute-start | bytes 884744 | tf_op jit(solution)/shard_map/ppermute | solution.py:189
  411.7 7.8 %collective-permute-start.33 = (bf16[96,1536]{1,0:T(8,128)(2,1)S(1)}, bf16[96,1536]{1,0:T(8,128)(2,1)S(1)}, u32[]{:S(2)}, u32[]{:S(2)}) collective-permute-start(bf16[96,1536]{1,0:T(8,128)(2,1)S(1)} %dynamic-slice_bitcast_fusion.6), channel_id=1, source_target_pairs={{0,8},{4,12},{8,0},{12,4},{16,24},{20,28},{24,16},{28,20},{1,9},{5... | collective-permute-start | bytes 884744 | tf_op jit(solution)/shard_map/ppermute | solution.py:189
  419.6 22.1 %copy-start.18 = (bf16[1,256,768]{2,1,0:T(8,128)(2,1)S(1)}, bf16[1,256,768]{2,1,0:T(8,128)(2,1)}, u32[]{:S(2)}) copy-start(bf16[1,256,768]{2,1,0:T(8,128)(2,1)} %get-tuple-element.137) | copy-start | bytes 1179652
  419.6 22.1 %copy-start.49 = (pred[4]{0:T(512)(128)(4,1)S(1)}, pred[4]{0:T(512)(128)(4,1)}, u32[]{:S(2)}) copy-start(pred[4]{0:T(512)(128)(4,1)} %compare_and_fusion) | copy-start | bytes 16
  419.6 22.1 %copy-start.50 = (s32[4]{0:T(128)S(1)}, s32[4]{0:T(128)}, u32[]{:S(2)}) copy-start(s32[4]{0:T(128)} %get-tuple-element.349) | copy-start | bytes 52
  419.6 22.1 %copy-start.51 = (s32[4]{0:T(128)S(1)}, s32[4]{0:T(128)}, u32[]{:S(2)}) copy-start(s32[4]{0:T(128)} %get-tuple-element.350) | copy-start | bytes 52
  437.0 11.0 %collective-permute-start.36 = (bf16[96,768]{1,0:T(8,128)(2,1)S(1)}, bf16[96,768]{1,0:T(8,128)(2,1)S(1)}, u32[]{:S(2)}, u32[]{:S(2)}) collective-permute-start(bf16[96,768]{1,0:T(8,128)(2,1)S(1)} %pad_maximum_fusion.10), channel_id=1, source_target_pairs={{0,3},{1,0},{2,1},{3,2},{4,7},{5,4},{6,5},{7,6},{8,11},{9,8},{10,9... | collective-permute-start | bytes 442376 | tf_op jit(solution)/shard_map/ppermute | solution.py:174
  440.0 12.7 %collective-permute-start.37 = (bf16[96,768]{1,0:T(8,128)(2,1)}, bf16[96,768]{1,0:T(8,128)(2,1)S(1)}, u32[]{:S(2)}, u32[]{:S(2)}) collective-permute-start(bf16[96,768]{1,0:T(8,128)(2,1)} %pad_maximum_fusion.11), channel_id=1, source_target_pairs={{0,2},{1,3},{2,0},{3,1},{4,6},{5,7},{6,4},{7,5},{8,10},{9,11},{10,... | collective-permute-start | bytes 442376 | tf_op jit(solution)/shard_map/ppermute | solution.py:174
  440.8 12.0 %collective-permute-start.38 = (bf16[96,768]{1,0:T(8,128)(2,1)}, bf16[96,768]{1,0:T(8,128)(2,1)S(1)}, u32[]{:S(2)}, u32[]{:S(2)}) collective-permute-start(bf16[96,768]{1,0:T(8,128)(2,1)} %pad_maximum_fusion.12), channel_id=1, source_target_pairs={{0,1},{1,2},{2,3},{3,0},{4,5},{5,6},{6,7},{7,4},{8,9},{9,10},{10,1... | collective-permute-start | bytes 442376 | tf_op jit(solution)/shard_map/ppermute | solution.py:174
  (38 other events, 141.0 us)
Sparse Core Ops, SparseCore 0:
  60.5 72.6 all-gather.2
  197.5 51.2 reduce-scatter.1
  376.9 59.7 all-gather.4

commit v7 on v6

--- a/solution.py
+++ b/solution.py
@@ -166,12 +166,12 @@
     return parts
 
 
-def sent_back(parts):
+def sent_back(parts, steps=None):
     members = lax.axis_size("tp")
-    moved = [parts[0]]
-    for step in range(1, members):
+    moved = list(parts)
+    for step in range(1, members) if steps is None else steps:
         pairs = [(i, (i - step) % members) for i in range(members)]
-        moved.append(lax.ppermute(parts[step], "tp", pairs))
+        moved[step] = lax.ppermute(parts[step], "tp", pairs)
     return moved
 
 
@@ -254,6 +254,14 @@
     moved = (flip("fsdp", 8, 2, first_out), flip("fsdp", 8, 4, second_out))
     moved, others = together(moved, others)
     return jnp.concatenate([add_low(first, moved[0]), add_low(second, moved[1])], axis=1), others
+
+
+def total_over_fsdp(vector):
+    members, bit = lax.axis_size("fsdp"), 1
+    while bit < members:
+        vector = vector + flip("fsdp", members, bit, vector)
+        bit *= 2
+    return vector
 
 
 def normalize(token_rows):
@@ -306,9 +314,9 @@
     def by_member(array):
         return array.reshape(tp, count, places, width)
 
-    def to_owners(array):
+    def by_arrival(array):
         parts = array.reshape(count, tp, places, width)
-        return sent_back([parts[:, step] for step in range(tp)])
+        return [parts[:, step] for step in range(tp)]
 
     def own_places(parts):
         return by_source(parts).reshape(sequences, places, width)
@@ -363,11 +371,18 @@
     ids = [lax.dynamic_slice_in_dim(ids, (rank - step) % tp, 1, 1) for step in range(tp)]
     ids = jnp.concatenate(ids, axis=1).reshape(count, length)
     ids = (ids[:, None, :], ids[:, :, None])
-    fillers = (*ids, query_bias_full, value_bias_full, inner_bias_full)
+    fillers = (
+        *ids,
+        *(vector.astype(WIDE) for vector in (output_bias, first_gain, first_shift)),
+        *(vector.astype(WIDE) for vector in (outer_bias, second_gain, second_shift)),
+        *(query_bias_full, value_bias_full, inner_bias_full),
+    )
     heads, rows, rest, fillers = gather_rows(
         fsdp, columns(heads, (head_cols,) * 4), rows, rest, fillers
     )
-    *ids, query_bias_full, value_bias_full, inner_bias_full = fillers
+    ids = fillers[:2]
+    output_bias, first_gain, first_shift, outer_bias, second_gain, second_shift = fillers[2:8]
+    query_bias_full, value_bias_full, inner_bias_full = fillers[8:]
     query_full, key_full, value_full, output_turned = (
         heads[:, i * width : (i + 1) * width] for i in range(4)
     )
@@ -383,9 +398,9 @@
     context, logsum = attend(queries, keys_all, values, ids)
     context, grad_out = meet(context, dealt(by_member(out_grad)), (2,))
     context = context.reshape(count * length, width)
-    mixed = dot(context, output_turned, BY_LAST) + output_bias.astype(WIDE)
+    mixed = dot(context, output_turned, BY_LAST) + output_bias
     first_normed, first_scaling = normalize(rows.astype(WIDE) + mixed)
-    first_rows = first_normed * first_gain.astype(WIDE) + first_shift.astype(WIDE)
+    first_rows = first_normed * first_gain + first_shift
     first_low = first_rows.astype(LOW)
     preactivation = dot(first_low, inner_full, BY_ROWS) + inner_bias_full
     cumulative = 0.5 * (1.0 + lax.erf(preactivation * 0.7071067811865476))
@@ -394,13 +409,13 @@
     slope = cumulative + preactivation * density
     activation_rows, grad_out = meet(activation_rows, grad_out, (1, 3))
     branch = dot(activation_rows, outer_turned, BY_LAST)
-    second_normed, second_scaling = normalize(first_rows + branch + outer_bias.astype(WIDE))
-    second_rows = second_normed * second_gain.astype(WIDE) + second_shift.astype(WIDE)
-    layer_out = to_owners(second_rows.astype(LOW))
+    second_normed, second_scaling = normalize(first_rows + branch + outer_bias)
+    second_rows = second_normed * second_gain + second_shift
+    layer_out = by_arrival(second_rows.astype(LOW))
 
     grad_out = whole_rows(grad_out).astype(WIDE)
     grad_second, second_gain_grad, second_shift_grad = normalize_back(
-        grad_out, second_normed, second_scaling, second_gain.astype(WIDE)
+        grad_out, second_normed, second_scaling, second_gain
     )
     outer_bias_grad = jnp.sum(grad_second, axis=0)
     grad_branch = grad_second.astype(LOW)
@@ -409,32 +424,50 @@
     grad_activ = dot(grad_branch, outer_turned, BY_ROWS)
     grad_pre = (grad_activ * slope).astype(LOW)
     inner_bias_grad = jnp.sum(grad_pre.astype(WIDE), axis=0)
-    inner_share, layer_out[:3] = scatter_core(
-        dot(first_low, grad_pre, BY_FIRST).astype(LOW), layer_out[:3]
-    )
+    layer_out = sent_back(layer_out, range(2, 3))
+    inner_share, layer_out[2:3] = scatter_core(
+        dot(first_low, grad_pre, BY_FIRST).astype(LOW), layer_out[2:3]
+    )
+    inner_share, layer_out = lax.optimization_barrier((inner_share, layer_out))
+    layer_out = sent_back(layer_out, [step for step in range(1, tp) if step != 2])
     grad_first = grad_second + dot(grad_pre, inner_full, BY_LAST)
     grad_mixed, first_gain_grad, first_shift_grad = normalize_back(
-        grad_first, first_normed, first_scaling, first_gain.astype(WIDE)
+        grad_first, first_normed, first_scaling, first_gain
     )
     output_bias_grad = jnp.sum(grad_mixed, axis=0)
     grad_mixed_low = grad_mixed.astype(LOW)
     output_grad = dot(grad_mixed_low, context, BY_FIRST).astype(LOW)
     grad_context = dot(grad_mixed_low, output_turned, BY_ROWS).astype(LOW).reshape(shape)
-    grad_context, inner_share, output_grad, layer_out = lax.optimization_barrier(
-        (grad_context, scatter_near(inner_share)[0], output_grad, layer_out)
-    )
+    vectors = [
+        output_bias_grad,
+        first_gain_grad,
+        first_shift_grad,
+        outer_bias_grad,
+        second_gain_grad,
+        second_shift_grad,
+        by_rank(jnp.sum(grad_context.astype(WIDE), axis=(0, 1))),
+        *jnp.split(by_rank(inner_bias_grad), inner_bias_grad.shape[0] // width),
+    ]
+    (inner_share, _), vectors = scatter_near(inner_share), vectors
+    grad_context, inner_share, output_grad, vectors = lax.optimization_barrier(
+        (grad_context, inner_share, output_grad, vectors)
+    )
+    vectors = lax.all_gather(jnp.stack(vectors), ("tp", "fsdp"), axis=0)
     inner_share, _ = scatter_far(inner_share)
     back = functools.partial(
         attend_back, queries, keys_all, values, grad_context, context.reshape(shape), logsum, ids
     )
     halfway = back(None, 0)
-    halfway, inner_share, outer_share = lax.optimization_barrier(
-        (halfway, inner_share, outer_share)
+    halfway, inner_share, outer_share, layer_out = lax.optimization_barrier(
+        (halfway, inner_share, outer_share, layer_out)
     )
     layer_out = own_places(layer_out)
     units = (unit_cols, unit_cols)
     unit_parts = own_columns(jnp.concatenate([inner_share, outer_share], axis=1), units)
-    rows_grads, unit_parts = lax.optimization_barrier((back(halfway, 1), unit_parts))
+    rows_grads, unit_parts, vectors = lax.optimization_barrier(
+        (back(halfway, 1), unit_parts, vectors)
+    )
+    totals = jnp.sum(vectors, axis=0).reshape(-1)
     inner_share, outer_share = summed(unit_parts, units)
     query_rows_grad, key_rows_grad, value_rows_grad = (
         array.reshape(count * length, width) for array in rows_grads
@@ -449,35 +482,28 @@
         + dot(key_rows_grad, key_full, BY_LAST)
         + dot(value_rows_grad, value_full, BY_LAST)
     ).astype(LOW)
-    vectors = [
-        output_bias_grad,
-        first_gain_grad,
-        first_shift_grad,
-        outer_bias_grad,
-        second_gain_grad,
-        second_shift_grad,
-        by_rank(jnp.sum(query_rows_grad.astype(WIDE), axis=0)),
-        by_rank(jnp.sum(value_rows_grad.astype(WIDE), axis=0)),
-        by_rank(inner_bias_grad),
-    ]
-    vectors = jnp.concatenate(vectors).reshape(-1, 128)
-    vectors = lax.all_gather(vectors, ("tp", "fsdp"), axis=0)
-    heads_share, (tokens_grad,) = scatter_core(
-        jnp.concatenate(head_grads + [output_grad], axis=1), (tokens_grad,)
-    )
-    tokens_grad = to_owners(tokens_grad)
+    late = jnp.sum(query_rows_grad.astype(WIDE), axis=0)
+    heads_share, (tokens_grad, late) = scatter_core(
+        jnp.concatenate(head_grads + [output_grad], axis=1), (tokens_grad, late)
+    )
+    late = total_over_fsdp(late)
+    tokens_grad = sent_back(by_arrival(tokens_grad))
     heads_share, tokens_grad[:3] = scatter_near(heads_share, tokens_grad[:3])
     heads_share, tokens_grad[3:] = scatter_far(heads_share, tokens_grad[3:])
-    heads_share, vectors = lax.optimization_barrier((heads_share, vectors))
-    totals = jnp.sum(vectors, axis=0).reshape(-1)
-    query_share, key_share, value_share, output_share = summed(
-        own_columns(heads_share, (head_cols,) * 4), (head_cols,) * 4
+    heads_share, late = lax.optimization_barrier((heads_share, late))
+    high = late.astype(LOW)
+    late = jnp.concatenate([high, (late - high.astype(WIDE)).astype(LOW)])
+    late = jnp.pad(late, (0, heads_share.shape[1] - late.shape[0]))[None]
+    heads_share = own_columns(jnp.concatenate([heads_share, late], axis=0), (head_cols,) * 4)
+    heads_share = summed(heads_share, (head_cols,) * 4)
+    query_bias_total = heads_share[0][shard_rows] + heads_share[1][shard_rows]
+    query_share, key_share, value_share, output_share = (
+        share[:shard_rows] for share in heads_share
     )
     tokens_grad = own_places(tokens_grad).astype(WIDE)
     rowwise = [totals[i * width : (i + 1) * width] for i in range(6)]
-    query_bias_total = lax.dynamic_slice_in_dim(totals, 6 * width + rank * head_cols, head_cols)
-    value_bias_total = lax.dynamic_slice_in_dim(totals, 7 * width + rank * head_cols, head_cols)
-    inner_bias_total = lax.dynamic_slice_in_dim(totals, 8 * width + rank * unit_cols, unit_cols)
+    value_bias_total = lax.dynamic_slice_in_dim(totals, 6 * width + rank * head_cols, head_cols)
+    inner_bias_total = lax.dynamic_slice_in_dim(totals, 7 * width + rank * unit_cols, unit_cols)
     return (
         layer_out,
         tokens_grad,

time: 467 us -> 449 us (0.961)
  waiting for transfers between devices: 125 us -> 101 us
  starting transfers between devices: 56.1 us -> 62.1 us
    ppermute x12, waiting for transfers between devices: 49.2 us -> 25.6 us  [sent_back(): moved[step] = lax.ppermute(parts[step], 'tp', pairs)]
    ppermute x12, starting transfers between devices: 14.5 us -> 32.1 us  [sent_back(): moved[step] = lax.ppermute(parts[step], 'tp', pairs)]
    ppermute x15 -> x18, waiting for transfers between devices: 16.3 us -> 2.81 us  [flip(): return lax.ppermute(block, axis, [(i, i ^ bit) for i in range(members)])]
    ppermute x6, starting transfers between devices: 14.3 us -> 2.96 us  [dealt(): parts.append(lax.ppermute(block, 'tp', pairs) if step else block)]
    ppermute x6, waiting for transfers between devices: 27 us -> 35.6 us  [dealt(): parts.append(lax.ppermute(block, 'tp', pairs) if step else block)]
    ppermute x6, waiting for transfers between devices: 15.4 us -> 23.7 us  [spread(): return [block] + [lax.ppermute(block, 'tp', pairs) for pairs in rank_pairs]]
    unnamed x148 -> x145, local copies, waits for them, and re-layouts: 22.3 us -> 14.3 us
    another operation x0 -> x12, local copies, waits for them, and re-layouts: none -> 6.84 us  [on_device(): vectors = lax.all_gather(jnp.stack(vectors), ('tp', 'fsdp'), axis=0)]
  transfers between devices with their start and end apart: 42 -> 45, of which waited for: 18 -> 10; matrix products, arithmetic and copies ran while one was open for 32% -> 34% of each run, Pallas kernels for 13% -> 14%
where the time goes in v7:
time: 449 us; the launch traced here: 443 us
  waiting for transfers between devices  101 us (22%)
  matrix products  88.7 us (20%)
  starting transfers between devices  62.1 us (14%)
  Pallas kernels  60.2 us (13%)
  other arithmetic  58.9 us (13%)
  local copies, waits for them, and re-layouts  56.3 us (13%)
  between operations  15.6 us (3%)
    dot_general x18, matrix products, dot(): return lax.dot_general(left, right, dims, preferred_element_type=WIDE)  88.7 us
    pallas_call x2, Pallas kernels, attend_back(): pl.pallas_call(body, grid=(count, pairs - first if part else pairs // 2),...  37.4 us
    ppermute x6, waiting for transfers between devices, dealt(): parts.append(lax.ppermute(block, 'tp', pairs) if step else block)  35.6 us
    ppermute x12, starting transfers between devices, sent_back(): moved[step] = lax.ppermute(parts[step], 'tp', pairs)  32.1 us
    ppermute x12, waiting for transfers between devices, sent_back(): moved[step] = lax.ppermute(parts[step], 'tp', pairs)  25.6 us
    ppermute x6, waiting for transfers between devices, spread(): return [block] + [lax.ppermute(block, 'tp', pairs) for pairs in rank_pairs]  23.7 us
    pallas_call x1, Pallas kernels, attend(): pl.pallas_call(functools.partial(attend_kernel, scaling=scaling), grid=(c...  22.9 us
    ppermute x18, starting transfers between devices, flip(): return lax.ppermute(block, axis, [(i, i ^ bit) for i in range(members)])  15.9 us
  transfers between devices with their start and end apart: 45, of which 10 were waited for; matrix products, arithmetic and copies ran while one was open for 34% of the time, Pallas kernels for 14%

profile of v7, /device:TPU:0, one launch (start us, length us, event | category | flops | bytes accessed | tf_op | source)
XLA Modules:
  0.0 443.2 jit_solution(8129822747205148689)
XLA Ops:
  7.2 2.1 concatenate.88
  13.2 5.1 %collective-permute-start.2 = (bf16[99,768]{0,1:T(8,128)(2,1)S(1)}, bf16[99,768]{0,1:T(8,128)(2,1)S(1)}, u32[]{:S(2)}, u32[]{:S(2)}) collective-permute-start(bf16[99,768]{0,1:T(8,128)(2,1)S(1)} %fusion.91), channel_id=1, source_target_pairs={{0,3},{1,0},{2,1},{3,2},{4,7},{5,4},{6,5},{7,6},{8,11},{9,8},{10,9... | collective-permute-start | bytes 456200 | tf_op jit(solution)/shard_map/ppermute | solution.py:156
  28.3 6.7 %collective-permute-done.1 = bf16[99,768]{0,1:T(8,128)(2,1)S(1)} collective-permute-done((bf16[99,768]{0,1:T(8,128)(2,1)S(1)}, bf16[99,768]{0,1:T(8,128)(2,1)S(1)}, u32[]{:S(2)}, u32[]{:S(2)}) %collective-permute-start.1) | collective-permute-done | bytes 152096 | tf_op jit(solution)/shard_map/ppermute | solution.py:156
  35.7 2.6 collective-permute-start.6
  38.3 1.9 collective-permute-start.5
  41.7 1.6 collective-permute-start.4
  43.2 1.5 collective-permute-start.3
  46.7 12.0 %collective-permute-done.5 = bf16[96,1536]{1,0:T(8,128)(2,1)} collective-permute-done((bf16[96,1536]{1,0:T(8,128)(2,1)S(1)}, bf16[96,1536]{1,0:T(8,128)(2,1)}, u32[]{:S(2)}, u32[]{:S(2)}) %collective-permute-start.5) | collective-permute-done | bytes 294944 | tf_op jit(solution)/shard_map/ppermute | solution.py:156
  58.7 4.9 %collective-permute-done.6 = bf16[96,1536]{1,0:T(8,128)(2,1)S(1)} collective-permute-done((bf16[96,1536]{1,0:T(8,128)(2,1)S(1)}, bf16[96,1536]{1,0:T(8,128)(2,1)S(1)}, u32[]{:S(2)}, u32[]{:S(2)}) %collective-permute-start.6) | collective-permute-done | bytes 294944 | tf_op jit(solution)/shard_map/ppermute | solution.py:156
  70.8 1.6 collective-permute-start.9
  72.5 1.6 collective-permute-start.8
  75.0 25.6 %collective-permute-done.11 = bf16[1,256,768]{2,1,0:T(8,128)(2,1)S(1)} collective-permute-done((bf16[1,256,768]{2,1,0:T(8,128)(2,1)S(1)}, bf16[1,256,768]{2,1,0:T(8,128)(2,1)S(1)}, u32[]{:S(2)}, u32[]{:S(2)}) %collective-permute-start.11) | collective-permute-done | bytes 393248 | tf_op jit(solution)/shard_map/ppermute | solution.py:165
  105.7 9.9 %collective-permute-done.13 = bf16[1,256,768]{2,1,0:T(8,128)(2,1)} collective-permute-done((bf16[1,256,768]{2,1,0:T(8,128)(2,1)}, bf16[1,256,768]{2,1,0:T(8,128)(2,1)}, u32[]{:S(2)}, u32[]{:S(2)}) %collective-permute-start.13) | collective-permute-done | bytes 393248 | tf_op jit(solution)/shard_map/ppermute | solution.py:165
  117.9 2.1 collective-permute-start.16
  120.7 2.2 bitcast_select_fusion
  122.9 2.7 fusion.63.k_ref.refs_1_
  125.6 2.5 fusion.35.v_ref.refs_2_
  128.2 2.5 fusion.34.q_ref.refs_0_
  130.7 22.9 %attend.1 = (bf16[1,1024,768]{2,1,0:T(8,128)(2,1)}, f32[1,6,2,1024]{3,2,1,0:T(2,128)}) custom-call(bf16[1,1024,768]{2,1,0:T(8,128)(2,1)} %fusion.34.q_ref.refs_0_, bf16[1,1024,768]{2,1,0:T(8,128)(2,1)} %fusion.63.k_ref.refs_1_, bf16[1,1024,768]{2,1,0:T(8,128)(2,1)} %fusion.35.v_ref.refs_2_, s32[1,1,1024]{2,1,0:T(1,128)} %broadcast_in_dim_reshape.6.row_ref.refs_6_, ...), custom_call_target="tpu_custom_call" | custom-call | flops 22548578304 | bytes 6291456 | tf_op jit(solution)/shard_map/attend/pallas_call | solution.py:93
  154.4 3.8 fusion.116
  158.8 11.1 %multiply_convert_fusion = (bf16[1024,3072]{1,0:T(8,128)(2,1)S(1)}, f32[1024,3072]{1,0:T(8,128)}) fusion(f32[3072]{0:T(1024)} %pad_maximum_fusion.13, bf16[768,6144]{1,0:T(8,128)(2,1)} %all-gather.5.cloned.1.call-done, f32[1024,768]{1,0:T(8,128)S(1)} %get-tuple-element.379, f32[768]{0:T(1024)} %convert_element_type.271, f32[768]{0:T(1024)S(1)} %convert_element_type.270, ...), kind=kOutput, calls=%fused_computation.8 | convolution fusion | flops 4854644736 | bytes 26766336 | tf_op jit(solution)/shard_map/dot_general | solution.py:22
  169.9 5.4 %fusion.106 = (f32[1024]{0:T(1024)S(1)}, f32[1024,768]{1,0:T(8,128)S(1)}) fusion(f32[768]{0:T(1024)S(1)} %copy-done.48, f32[768]{0:T(1024)S(1)} %copy-done.46, f32[768]{0:T(1024)S(1)} %convert_element_type.270, f32[1024]{0:T(1024)S(1)} %add_rsqrt_fusion.1, f32[1024,768]{1,0:T(8,128)S(1)} %get-tuple-element.379, f32[1024]{0:T(1024)S(1)} %broadcast_multiply_fusion.5, ...), kind=kOutput, calls=%fused_computation.255 | convolution fusion | flops 4837342208 | bytes 17326080 | tf_op jit(solution)/shard_map/dot_general | solution.py:22
  176.4 5.4 %fusion.29 = (f32[768]{0:T(1024)}, f32[1024]{0:T(1024)S(1)}, f32[1024]{0:T(1024)S(1)}, bf16[1024,768]{1,0:T(8,128)(2,1)}) fusion(f32[1024,768]{1,0:T(8,128)S(1)} %get-tuple-element.294, f32[1024]{0:T(1024)S(1)} %add_rsqrt_fusion, f32[1024]{0:T(1024)S(1)} %broadcast_multiply_fusion.4, bf16[1,256,768]{2,1,0:T(8,128)(2,1)} %collective-permute-done.16, ...), kind=kLoop, calls=%fused_computation.44 | loop fusion | flops 14939392 | bytes 6317056 | tf_op jit(solution)/shard_map/reduce_sum | solution.py:277
  181.7 3.5 fusion.103
  185.2 1.7 copy-done.12
  186.9 7.0 %convolution_convert_fusion = bf16[768,3072]{1,0:T(8,128)(2,1)} fusion(bf16[1024,3072]{1,0:T(8,128)(2,1)S(1)} %get-tuple-element.149, f32[1024,768]{1,0:T(8,128)S(1)} %get-tuple-element.290), kind=kOutput, calls=%fused_computation.13 | convolution fusion | flops 4834983936 | bytes 14155776 | tf_op jit(solution)/shard_map/dot_general | solution.py:22
  193.9 13.9 %convert_reduce_fusion = (f32[3072]{0:T(1024)}, bf16[1024,3072]{1,0:T(8,128)(2,1)S(1)}) fusion(f32[1024,3072]{1,0:T(8,128)} %get-tuple-element.381, f32[3072]{0:T(1024)} %pad_maximum_fusion.13, bf16[768,6144]{1,0:T(8,128)(2,1)} %all-gather.5.cloned.1.call-done, f32[1024,768]{1,0:T(8,128)} %copy-done.12), kind=kOutput, calls=%fused_computation.7 | convolution fusion | flops 4873516032 | bytes 26763264 | tf_op jit(solution)/shard_map/dot_general | solution.py:22
  207.8 6.5 %convolution_convert_fusion.1 = bf16[768,3072]{1,0:T(8,128)(2,1)S(1)} fusion(bf16[1024,3072]{1,0:T(8,128)(2,1)S(1)} %get-tuple-element.386, f32[1024,768]{1,0:T(8,128)S(1)} %get-tuple-element.379, f32[768]{0:T(1024)S(1)} %copy-done.47, f32[768]{0:T(1024)S(1)} %convert_element_type.270, f32[1024]{0:T(1024)S(1)} %copy-done.39, ...), kind=kOutput, calls=%fused_computation.14 | convolution fusion | flops 4838129664 | bytes 14170112 | tf_op jit(solution)/shard_map/dot_general | solution.py:22
  215.5 2.4 collective-permute-start.18
  217.9 1.8 constant_dynamic-slice_fusion.9
  219.7 1.6 copy.127
  222.5 8.9 %multiply_reduce_fusion = (f32[768]{0:T(1024)}, f32[1024]{0:T(1024)S(1)}, f32[1024]{0:T(1024)S(1)}, f32[768]{0:T(1024)}, f32[1024,768]{1,0:T(8,128)S(1)}) fusion(f32[1024,768]{1,0:T(8,128)S(1)} %get-tuple-element.379, f32[1024]{0:T(1024)S(1)} %copy-done.39, f32[1024]{0:T(1024)S(1)} %broadcast_multiply_fusion.5, f32[768]{0:T(1024)S(1)} %convert_element_type.270, ...), kind=kOutput, calls=%fused_computation.48 | convolution fusion | flops 4839698432 | bytes 20473856 | tf_op jit(solution)/shard_map/dot_general | solution.py:22
  231.4 1.7 fusion.105
  233.1 5.0 %convert_reduce_fusion.3 = (f32[768]{0:T(1024)S(1)}, bf16[1024,768]{1,0:T(8,128)(2,1)}) fusion(bf16[768,3072]{1,0:T(8,128)(2,1)} %copy-done.4, f32[1024,768]{1,0:T(8,128)S(1)} %get-tuple-element.292), kind=kOutput, calls=%fused_computation.47 | convolution fusion | flops 1211104512 | bytes 5901312 | tf_op jit(solution)/shard_map/dot_general | solution.py:22
  238.2 2.5 fusion.7
  247.2 1.5 convert_reduce_fusion.1
  248.8 4.0 fusion.51
  252.8 3.9 collective-permute-start.23
  256.7 2.0 collective-permute-done.19
  266.3 1.7 collective-permute-start.22
  269.1 2.7 stack.47
  271.8 18.6 %attend_back.2 = (bf16[1,1024,768]{2,1,0:T(8,128)(2,1)}, bf16[1,1024,768]{2,1,0:T(8,128)(2,1)}, bf16[1,1024,768]{2,1,0:T(8,128)(2,1)}) custom-call(bf16[1,1024,768]{2,1,0:T(8,128)(2,1)} %fusion.34.q_ref.refs_0_, bf16[1,1024,768]{2,1,0:T(8,128)(2,1)} %fusion.63.k_ref.refs_1_, bf16[1,1024,768]{2,1,0:T(8,128)(2,1)} %fusion.35.v_ref.refs_2_, ...), custom_call_target="tpu_custom_call" | custom-call | flops 19327352832 | bytes 5505024 | tf_op jit(solution)/shard_map/attend_back/pallas_call | solution.py:128
  293.6 1.9 fusion.110
  295.6 1.8 fusion.111
  298.1 3.9 collective-permute-start.25
  304.1 18.8 %attend_back.3 = (bf16[1,1024,768]{2,1,0:T(8,128)(2,1)}, bf16[1,1024,768]{2,1,0:T(8,128)(2,1)}, bf16[1,1024,768]{2,1,0:T(8,128)(2,1)}) custom-call(bf16[1,1024,768]{2,1,0:T(8,128)(2,1)} %fusion.34.q_ref.refs_0_, bf16[1,1024,768]{2,1,0:T(8,128)(2,1)} %fusion.63.k_ref.refs_1_, ...), custom_call_target="tpu_custom_call", output_to_operand_aliasing={{0}: (8, {}), {1}: (9, {}), {2}: (10, {})} | custom-call | flops 19327352832 | bytes 5505024 | tf_op jit(solution)/shard_map/attend_back/pallas_call | solution.py:128
  323.9 13.6 %all-gather.7.cloned.1.call-done = f32[32,11,768]{2,1,0:T(8,128)} async-done(((f32[1,11,768]{2,1,0:T(8,128)}), f32[32,11,768]{2,1,0:T(8,128)}) %all-gather.7.cloned.1.call-update) | async-done | bytes 1081360 | tf_op jit(solution)/shard_map/all_gather | solution.py:455
  337.5 3.5 fusion.57
  341.0 1.5 fusion.60
  344.9 2.2 copy-done
  347.1 1.6 dynamic-slice_bitcast_fusion
  349.4 1.7 convert_reduce_fusion.2
  351.1 3.3 fusion.44
  354.4 2.8 fusion.40
  357.3 2.9 add_convert_fusion
  360.2 2.6 fusion.6
  363.1 1.5 collective-permute-start.29
  367.3 2.3 collective-permute-start.31
  370.9 17.1 %collective-permute-done.32 = bf16[1,256,768]{2,1,0:T(8,128)(2,1)S(1)} collective-permute-done((bf16[1,256,768]{2,1,0:T(8,128)(2,1)S(1)}, bf16[1,256,768]{2,1,0:T(8,128)(2,1)S(1)}, u32[]{:S(2)}, u32[]{:S(2)}) %collective-permute-start.32) | collective-permute-done | bytes 393248 | tf_op jit(solution)/shard_map/ppermute | solution.py:174
  395.5 1.6 slice_reduce_fusion
  402.7 9.8 %collective-permute-start.39 = (bf16[97,768]{1,0:T(8,128)(2,1)S(1)}, bf16[97,768]{1,0:T(8,128)(2,1)S(1)}, u32[]{:S(2)}, u32[]{:S(2)}) collective-permute-start(bf16[97,768]{1,0:T(8,128)(2,1)S(1)} %pad_maximum_fusion.10), channel_id=1, source_target_pairs={{0,3},{1,0},{2,1},{3,2},{4,7},{5,4},{6,5},{7,6},{8,11},{9,8},{10,9... | collective-permute-start | bytes 446984 | tf_op jit(solution)/shard_map/ppermute | solution.py:174
  412.6 8.4 %collective-permute-start.40 = (bf16[97,768]{1,0:T(8,128)(2,1)S(1)}, bf16[97,768]{1,0:T(8,128)(2,1)S(1)}, u32[]{:S(2)}, u32[]{:S(2)}) collective-permute-start(bf16[97,768]{1,0:T(8,128)(2,1)S(1)} %pad_maximum_fusion.11), channel_id=1, source_target_pairs={{0,2},{1,3},{2,0},{3,1},{4,6},{5,7},{6,4},{7,5},{8,10},{9,11},{10,... | collective-permute-start | bytes 446984 | tf_op jit(solution)/shard_map/ppermute | solution.py:174
  421.3 4.3 fusion.36
  425.6 8.5 %collective-permute-done.40 = bf16[97,768]{1,0:T(8,128)(2,1)S(1)} collective-permute-done((bf16[97,768]{1,0:T(8,128)(2,1)S(1)}, bf16[97,768]{1,0:T(8,128)(2,1)S(1)}, u32[]{:S(2)}, u32[]{:S(2)}) %collective-permute-start.40) | collective-permute-done | bytes 149024 | tf_op jit(solution)/shard_map/ppermute | solution.py:174
  (348 shorter events, 83.5 us)
Async XLA Ops:
  7.2 34.3 %copy-start.36 = (bf16[192,96]{1,0:T(8,128)(2,1)S(1)}, bf16[192,96]{1,0:T(8,128)(2,1)}, u32[]{:S(2)}) copy-start(bf16[192,96]{1,0:T(8,128)(2,1)} %param.27) | copy-start | bytes 110596
  7.2 151.5 %all-gather.5.cloned.1.call-start = ((), (), s32[]{:S(2)}) async-start(), calls=%async_computation.1 | async-start | bytes 10616832 | tf_op jit(solution)/shard_map/all_gather | solution.py:391
  13.2 15.1 %collective-permute-start.2 = (bf16[99,768]{0,1:T(8,128)(2,1)S(1)}, bf16[99,768]{0,1:T(8,128)(2,1)S(1)}, u32[]{:S(2)}, u32[]{:S(2)}) collective-permute-start(bf16[99,768]{0,1:T(8,128)(2,1)S(1)} %fusion.91), channel_id=1, source_target_pairs={{0,3},{1,0},{2,1},{3,2},{4,7},{5,4},{6,5},{7,6},{8,11},{9,8},{10,9... | collective-permute-start | bytes 456200 | tf_op jit(solution)/shard_map/ppermute | solution.py:156
  18.3 16.7 %collective-permute-start.1 = (bf16[99,768]{0,1:T(8,128)(2,1)S(1)}, bf16[99,768]{0,1:T(8,128)(2,1)S(1)}, u32[]{:S(2)}, u32[]{:S(2)}) collective-permute-start(bf16[99,768]{0,1:T(8,128)(2,1)S(1)} %fusion.91), channel_id=1, source_target_pairs={{0,2},{1,3},{2,0},{3,1},{4,6},{5,7},{6,4},{7,5},{8,10},{9,11},{10,... | collective-permute-start | bytes 456200 | tf_op jit(solution)/shard_map/ppermute | solution.py:156
  18.3 16.7 %collective-permute-start = (bf16[99,768]{0,1:T(8,128)(2,1)S(1)}, bf16[99,768]{0,1:T(8,128)(2,1)S(1)}, u32[]{:S(2)}, u32[]{:S(2)}) collective-permute-start(bf16[99,768]{0,1:T(8,128)(2,1)S(1)} %fusion.91), channel_id=1, source_target_pairs={{0,1},{1,2},{2,3},{3,0},{4,5},{5,6},{6,7},{7,4},{8,9},{9,10},{10,1... | collective-permute-start | bytes 456200 | tf_op jit(solution)/shard_map/ppermute | solution.py:156
  35.4 23.3 %collective-permute-start.7 = (bf16[96,1536]{1,0:T(8,128)(2,1)S(1)}, bf16[96,1536]{1,0:T(8,128)(2,1)S(1)}, u32[]{:S(2)}, u32[]{:S(2)}) collective-permute-start(bf16[96,1536]{1,0:T(8,128)(2,1)S(1)} %pad_maximum_fusion.5), channel_id=1, source_target_pairs={{0,3},{1,0},{2,1},{3,2},{4,7},{5,4},{6,5},{7,6},{8,11},{9,8},{10,9... | collective-permute-start | bytes 884744 | tf_op jit(solution)/shard_map/ppermute | solution.py:156
  35.7 27.9 %collective-permute-start.6 = (bf16[96,1536]{1,0:T(8,128)(2,1)S(1)}, bf16[96,1536]{1,0:T(8,128)(2,1)S(1)}, u32[]{:S(2)}, u32[]{:S(2)}) collective-permute-start(bf16[96,1536]{1,0:T(8,128)(2,1)S(1)} %pad_maximum_fusion.5), channel_id=1, source_target_pairs={{0,2},{1,3},{2,0},{3,1},{4,6},{5,7},{6,4},{7,5},{8,10},{9,11},{10,... | collective-permute-start | bytes 884744 | tf_op jit(solution)/shard_map/ppermute | solution.py:156
  38.3 20.4 %collective-permute-start.5 = (bf16[96,1536]{1,0:T(8,128)(2,1)S(1)}, bf16[96,1536]{1,0:T(8,128)(2,1)}, u32[]{:S(2)}, u32[]{:S(2)}) collective-permute-start(bf16[96,1536]{1,0:T(8,128)(2,1)S(1)} %pad_maximum_fusion.5), channel_id=1, source_target_pairs={{0,1},{1,2},{2,3},{3,0},{4,5},{5,6},{6,7},{7,4},{8,9},{9,10},{10,1... | collective-permute-start | bytes 884744 | tf_op jit(solution)/shard_map/ppermute | solution.py:156
  41.6 22.0 %copy-start.27 = (bf16[96,1536]{0,1:T(8,128)(2,1)}, bf16[96,1536]{0,1:T(8,128)(2,1)S(1)}, u32[]{:S(2)}) copy-start(bf16[96,1536]{0,1:T(8,128)(2,1)S(1)} %get-tuple-element.348) | copy-start | bytes 884740
  41.7 22.0 %collective-permute-start.4 = (bf16[96,1536]{0,1:T(8,128)(2,1)S(1)}, bf16[96,1536]{0,1:T(8,128)(2,1)S(1)}, u32[]{:S(2)}, u32[]{:S(2)}) collective-permute-start(bf16[96,1536]{0,1:T(8,128)(2,1)S(1)} %get-tuple-element.348), channel_id=1, source_target_pairs={{0,16},{4,20},{8,24},{12,28},{16,0},{20,4},{24,8},{28,12},{1,17},{... | collective-permute-start | bytes 884744 | tf_op jit(solution)/shard_map/ppermute | solution.py:189
  43.2 20.4 %collective-permute-start.3 = (bf16[96,1536]{0,1:T(8,128)(2,1)S(1)}, bf16[96,1536]{0,1:T(8,128)(2,1)S(1)}, u32[]{:S(2)}, u32[]{:S(2)}) collective-permute-start(bf16[96,1536]{0,1:T(8,128)(2,1)S(1)} %get-tuple-element.349), channel_id=1, source_target_pairs={{0,8},{4,12},{8,0},{12,4},{16,24},{20,28},{24,16},{28,20},{1,9},{5... | collective-permute-start | bytes 884744 | tf_op jit(solution)/shard_map/ppermute | solution.py:189
  66.9 226.7 %reduce-scatter.2.cloned.1.call-start = ((), (), s32[]{:S(2)}) async-start(), calls=%async_computation.2 | async-start | bytes 5308416 | tf_op jit(solution)/shard_map/reduce_scatter | solution.py:423
  70.8 29.9 %collective-permute-start.9 = (bf16[2,96,1536]{2,1,0:T(8,128)(2,1)S(1)}, bf16[2,96,1536]{2,1,0:T(8,128)(2,1)}, u32[]{:S(2)}, u32[]{:S(2)}) collective-permute-start(bf16[2,96,1536]{2,1,0:T(8,128)(2,1)S(1)} %broadcast_select_fusion.2), channel_id=1, source_target_pairs={{0,8},{4,12},{8,0},{12,4},{16,24},{20,28},{24,16},{28,20},{1,9},{5... | collective-permute-start | bytes 1769480 | tf_op jit(solution)/shard_map/ppermute | solution.py:189
  72.5 28.2 %collective-permute-start.8 = (bf16[2,96,1536]{2,1,0:T(8,128)(2,1)S(1)}, bf16[2,96,1536]{2,1,0:T(8,128)(2,1)}, u32[]{:S(2)}, u32[]{:S(2)}) collective-permute-start(bf16[2,96,1536]{2,1,0:T(8,128)(2,1)S(1)} %broadcast_select_fusion.3), channel_id=1, source_target_pairs={{0,16},{4,20},{8,24},{12,28},{16,0},{20,4},{24,8},{28,12},{1,17},{... | collective-permute-start | bytes 1769480 | tf_op jit(solution)/shard_map/ppermute | solution.py:189
  74.9 25.8 %collective-permute-start.11 = (bf16[1,256,768]{2,1,0:T(8,128)(2,1)S(1)}, bf16[1,256,768]{2,1,0:T(8,128)(2,1)S(1)}, u32[]{:S(2)}, u32[]{:S(2)}) collective-permute-start(bf16[1,256,768]{2,1,0:T(8,128)(2,1)S(1)} %get-tuple-element.315), channel_id=1, source_target_pairs={{0,2},{1,3},{2,0},{3,1},{4,6},{5,7},{6,4},{7,5},{8,10},{9,11},{10,... | collective-permute-start | bytes 1179656 | tf_op jit(solution)/shard_map/ppermute | solution.py:165
  75.0 25.6 %collective-permute-start.10 = (bf16[1,256,768]{2,1,0:T(8,128)(2,1)S(1)}, bf16[1,256,768]{2,1,0:T(8,128)(2,1)S(1)}, u32[]{:S(2)}, u32[]{:S(2)}) collective-permute-start(bf16[1,256,768]{2,1,0:T(8,128)(2,1)S(1)} %get-tuple-element.316), channel_id=1, source_target_pairs={{0,1},{1,2},{2,3},{3,0},{4,5},{5,6},{6,7},{7,4},{8,9},{9,10},{10,1... | collective-permute-start | bytes 1179656 | tf_op jit(solution)/shard_map/ppermute | solution.py:165
  103.7 11.9 %collective-permute-start.12 = (bf16[2,2,96,3072]{3,2,1,0:T(8,128)(2,1)S(1)}, bf16[2,2,96,3072]{3,2,1,0:T(8,128)(2,1)}, u32[]{:S(2)}, u32[]{:S(2)}) collective-permute-start(bf16[2,2,96,3072]{3,2,1,0:T(8,128)(2,1)S(1)} %pad_maximum_fusion.1), channel_id=1, source_target_pairs={{0,4},{4,0},{8,12},{12,8},{16,20},{20,16},{24,28},{28,24},{1,5},{5... | collective-permute-start | bytes 7077896 | tf_op jit(solution)/shard_map/ppermute | solution.py:189
  103.8 11.8 %collective-permute-start.13 = (bf16[1,256,768]{2,1,0:T(8,128)(2,1)}, bf16[1,256,768]{2,1,0:T(8,128)(2,1)}, u32[]{:S(2)}, u32[]{:S(2)}) collective-permute-start(bf16[1,256,768]{2,1,0:T(8,128)(2,1)} %get-tuple-element.314), channel_id=1, source_target_pairs={{0,3},{1,0},{2,1},{3,2},{4,7},{5,4},{6,5},{7,6},{8,11},{9,8},{10,9... | collective-permute-start | bytes 1179656 | tf_op jit(solution)/shard_map/ppermute | solution.py:165
  105.7 15.0 %copy-start.43 = (pred[768]{0:T(1024)(128)(4,1)S(1)}, pred[768]{0:T(1024)(128)(4,1)}, u32[]{:S(2)}) copy-start(pred[768]{0:T(1024)(128)(4,1)} %iota.60) | copy-start | bytes 2308
  116.7 11.5 %copy-start.17 = (bf16[1024,768]{1,0:T(8,128)(2,1)}, bf16[1024,768]{1,0:T(8,128)(2,1)S(1)}, u32[]{:S(2)}) copy-start(bf16[1024,768]{1,0:T(8,128)(2,1)S(1)} %maximum_bitcast_fusion) | copy-start | bytes 4718596
  117.9 52.0 %collective-permute-start.16 = (bf16[1,256,768]{2,1,0:T(8,128)(2,1)}, bf16[1,256,768]{2,1,0:T(8,128)(2,1)}, u32[]{:S(2)}, u32[]{:S(2)}) collective-permute-start(bf16[1,256,768]{2,1,0:T(8,128)(2,1)} %get-tuple-element.311), channel_id=1, source_target_pairs={{0,3},{1,0},{2,1},{3,2},{4,7},{5,4},{6,5},{7,6},{8,11},{9,8},{10,9... | collective-permute-start | bytes 1179656 | tf_op jit(solution)/shard_map/ppermute | solution.py:165
  119.9 49.9 %collective-permute-start.15 = (bf16[1,256,768]{2,1,0:T(8,128)(2,1)}, bf16[1,256,768]{2,1,0:T(8,128)(2,1)}, u32[]{:S(2)}, u32[]{:S(2)}) collective-permute-start(bf16[1,256,768]{2,1,0:T(8,128)(2,1)} %get-tuple-element.312), channel_id=1, source_target_pairs={{0,1},{1,2},{2,3},{3,0},{4,5},{5,6},{6,7},{7,4},{8,9},{9,10},{10,1... | collective-permute-start | bytes 1179656 | tf_op jit(solution)/shard_map/ppermute | solution.py:165
  120.1 33.5 %collective-permute-start.14 = (bf16[1,256,768]{2,1,0:T(8,128)(2,1)S(1)}, bf16[1,256,768]{2,1,0:T(8,128)(2,1)S(1)}, u32[]{:S(2)}, u32[]{:S(2)}) collective-permute-start(bf16[1,256,768]{2,1,0:T(8,128)(2,1)S(1)} %get-tuple-element.313), channel_id=1, source_target_pairs={{0,2},{1,3},{2,0},{3,1},{4,6},{5,7},{6,4},{7,5},{8,10},{9,11},{10,... | collective-permute-start | bytes 1179656 | tf_op jit(solution)/shard_map/ppermute | solution.py:165
  130.7 23.6 %copy-start.49 = (f32[768]{0:T(1024)S(1)}, f32[768]{0:T(1024)}, u32[]{:S(2)}) copy-start(f32[768]{0:T(1024)} %convert_element_type.269) | copy-start | bytes 9220
  158.7 11.2 %copy-start.38 = (f32[1024]{0:T(1024)}, f32[1024]{0:T(1024)S(1)}, u32[]{:S(2)}) copy-start(f32[1024]{0:T(1024)S(1)} %add_rsqrt_fusion.1) | copy-start | bytes 12292
  158.7 11.2 %copy-start.46 = (f32[768]{0:T(1024)S(1)}, f32[768]{0:T(1024)}, u32[]{:S(2)}) copy-start(f32[768]{0:T(1024)} %convert_element_type.271) | copy-start | bytes 9220
  158.7 11.2 %copy-start.48 = (f32[768]{0:T(1024)S(1)}, f32[768]{0:T(1024)}, u32[]{:S(2)}) copy-start(f32[768]{0:T(1024)} %convert_element_type.272) | copy-start | bytes 9220
  193.9 143.6 %all-gather.7.cloned.1.call-start = ((), (), s32[]{:S(2)}) async-start(), calls=%async_computation.3 | async-start | bytes 1622016 | tf_op jit(solution)/shard_map/all_gather | solution.py:455
  193.9 13.9 %copy-start.39 = (f32[1024]{0:T(1024)S(1)}, f32[1024]{0:T(1024)}, u32[]{:S(2)}) copy-start(f32[1024]{0:T(1024)} %copy-done.38) | copy-start | bytes 12292
  193.9 13.9 %copy-start.47 = (f32[768]{0:T(1024)S(1)}, f32[768]{0:T(1024)}, u32[]{:S(2)}) copy-start(f32[768]{0:T(1024)} %convert_element_type.271) | copy-start | bytes 9220
  207.8 13.5 %slice-start.2 = ((s8[9437184]{0:T(1024)(128)(4,1)}), s8[4194304]{0:T(1024)(128)(4,1)S(1)}, s32[]{:S(2)}) async-start(s8[9437184]{0:T(1024)(128)(4,1)} %bitcast.184), calls=%async_computation.6 | async-start | bytes 8388608
  207.8 13.5 %slice-start.3 = ((s8[9437184]{0:T(1024)(128)(4,1)}), s8[4194304]{0:T(1024)(128)(4,1)S(1)}, s32[]{:S(2)}) async-start(s8[9437184]{0:T(1024)(128)(4,1)} %bitcast.184), calls=%async_computation.7 | async-start | bytes 8388608
  215.5 22.6 %collective-permute-start.18 = (bf16[1,256,768]{2,1,0:T(8,128)(2,1)}, bf16[1,256,768]{2,1,0:T(8,128)(2,1)}, u32[]{:S(2)}, u32[]{:S(2)}) collective-permute-start(bf16[1,256,768]{2,1,0:T(8,128)(2,1)} %get-tuple-element.309), channel_id=1, source_target_pairs={{0,2},{1,3},{2,0},{3,1},{4,6},{5,7},{6,4},{7,5},{8,10},{9,11},{10,... | collective-permute-start | bytes 1179656 | tf_op jit(solution)/shard_map/ppermute | solution.py:174
  221.3 16.9 %collective-permute-start.17 = (bf16[2,2,96,3072]{3,2,0,1:T(8,128)(2,1)}, bf16[2,2,96,3072]{3,2,0,1:T(8,128)(2,1)}, u32[]{:S(2)}, u32[]{:S(2)}) collective-permute-start(bf16[2,2,96,3072]{3,2,0,1:T(8,128)(2,1)} %bitcast.166), channel_id=1, source_target_pairs={{0,4},{4,0},{8,12},{12,8},{16,20},{20,16},{24,28},{28,24},{1,5},{5... | collective-permute-start | bytes 7077896 | tf_op jit(solution)/shard_map/ppermute | solution.py:189
  242.8 15.9 %collective-permute-start.19 = (bf16[2,96,1536]{2,1,0:T(8,128)(2,1)}, bf16[2,96,1536]{2,1,0:T(8,128)(2,1)}, u32[]{:S(2)}, u32[]{:S(2)}) collective-permute-start(bf16[2,96,1536]{2,1,0:T(8,128)(2,1)} %dynamic-slice_bitcast_fusion.4), channel_id=1, source_target_pairs={{0,16},{4,20},{8,24},{12,28},{16,0},{20,4},{24,8},{28,12},{1,17},{... | collective-permute-start | bytes 1769480 | tf_op jit(solution)/shard_map/ppermute | solution.py:189
  244.3 14.4 %collective-permute-start.20 = (bf16[2,96,1536]{2,1,0:T(8,128)(2,1)}, bf16[2,96,1536]{2,1,0:T(8,128)(2,1)}, u32[]{:S(2)}, u32[]{:S(2)}) collective-permute-start(bf16[2,96,1536]{2,1,0:T(8,128)(2,1)} %dynamic-slice_bitcast_fusion.3), channel_id=1, source_target_pairs={{0,8},{4,12},{8,0},{12,4},{16,24},{20,28},{24,16},{28,20},{1,9},{5... | collective-permute-start | bytes 1769480 | tf_op jit(solution)/shard_map/ppermute | solution.py:189
  252.8 40.7 %collective-permute-start.23 = (bf16[1,256,768]{2,1,0:T(8,128)(2,1)}, bf16[1,256,768]{2,1,0:T(8,128)(2,1)S(1)}, u32[]{:S(2)}, u32[]{:S(2)}) collective-permute-start(bf16[1,256,768]{2,1,0:T(8,128)(2,1)} %get-tuple-element.171), channel_id=1, source_target_pairs={{0,3},{1,0},{2,1},{3,2},{4,7},{5,4},{6,5},{7,6},{8,11},{9,8},{10,9... | collective-permute-start | bytes 1179656 | tf_op jit(solution)/shard_map/ppermute | solution.py:174
  256.7 36.9 %collective-permute-start.24 = (bf16[1,256,768]{2,1,0:T(8,128)(2,1)}, bf16[1,256,768]{2,1,0:T(8,128)(2,1)}, u32[]{:S(2)}, u32[]{:S(2)}) collective-permute-start(bf16[1,256,768]{2,1,0:T(8,128)(2,1)} %get-tuple-element.173), channel_id=1, source_target_pairs={{0,1},{1,2},{2,3},{3,0},{4,5},{5,6},{6,7},{7,4},{8,9},{9,10},{10,1... | collective-permute-start | bytes 1179656 | tf_op jit(solution)/shard_map/ppermute | solution.py:174
  266.3 24.1 %collective-permute-start.22 = (bf16[96,1536]{1,0:T(8,128)(2,1)}, bf16[96,1536]{1,0:T(8,128)(2,1)}, u32[]{:S(2)}, u32[]{:S(2)}) collective-permute-start(bf16[96,1536]{1,0:T(8,128)(2,1)} %dynamic-slice_bitcast_fusion.7), channel_id=1, source_target_pairs={{0,16},{4,20},{8,24},{12,28},{16,0},{20,4},{24,8},{28,12},{1,17},{... | collective-permute-start | bytes 884744 | tf_op jit(solution)/shard_map/ppermute | solution.py:189
  268.8 21.6 %collective-permute-start.21 = (bf16[96,1536]{1,0:T(8,128)(2,1)}, bf16[96,1536]{1,0:T(8,128)(2,1)}, u32[]{:S(2)}, u32[]{:S(2)}) collective-permute-start(bf16[96,1536]{1,0:T(8,128)(2,1)} %dynamic-slice_bitcast_fusion.8), channel_id=1, source_target_pairs={{0,8},{4,12},{8,0},{12,4},{16,24},{20,28},{24,16},{28,20},{1,9},{5... | collective-permute-start | bytes 884744 | tf_op jit(solution)/shard_map/ppermute | solution.py:189
  293.6 29.3 %copy-start.28 = (bf16[1,256,768]{2,1,0:T(8,128)(2,1)}, bf16[1,256,768]{2,1,0:T(8,128)(2,1)S(1)}, u32[]{:S(2)}) copy-start(bf16[1,256,768]{2,1,0:T(8,128)(2,1)S(1)} %collective-permute-done.23) | copy-start | bytes 1179652
  298.1 39.4 %collective-permute-start.25 = (bf16[96,1536]{1,0:T(8,128)(2,1)}, bf16[96,1536]{1,0:T(8,128)(2,1)}, u32[]{:S(2)}, u32[]{:S(2)}) collective-permute-start(bf16[96,1536]{1,0:T(8,128)(2,1)} %pad_maximum_fusion.7), channel_id=1, source_target_pairs={{0,3},{1,0},{2,1},{3,2},{4,7},{5,4},{6,5},{7,6},{8,11},{9,8},{10,9... | collective-permute-start | bytes 884744 | tf_op jit(solution)/shard_map/ppermute | solution.py:174
  302.8 34.7 %collective-permute-start.26 = (bf16[96,1536]{1,0:T(8,128)(2,1)}, bf16[96,1536]{1,0:T(8,128)(2,1)}, u32[]{:S(2)}, u32[]{:S(2)}) collective-permute-start(bf16[96,1536]{1,0:T(8,128)(2,1)} %pad_maximum_fusion.8), channel_id=1, source_target_pairs={{0,2},{1,3},{2,0},{3,1},{4,6},{5,7},{6,4},{7,5},{8,10},{9,11},{10,... | collective-permute-start | bytes 884744 | tf_op jit(solution)/shard_map/ppermute | solution.py:174
  303.5 34.0 %collective-permute-start.27 = (bf16[96,1536]{1,0:T(8,128)(2,1)}, bf16[96,1536]{1,0:T(8,128)(2,1)}, u32[]{:S(2)}, u32[]{:S(2)}) collective-permute-start(bf16[96,1536]{1,0:T(8,128)(2,1)} %pad_maximum_fusion.9), channel_id=1, source_target_pairs={{0,1},{1,2},{2,3},{3,0},{4,5},{5,6},{6,7},{7,4},{8,9},{9,10},{10,1... | collective-permute-start | bytes 884744 | tf_op jit(solution)/shard_map/ppermute | solution.py:174
  348.6 11.6 %collective-permute-start.28 = (bf16[2,2,96,3072]{3,2,1,0:T(8,128)(2,1)}, bf16[2,2,96,3072]{3,2,1,0:T(8,128)(2,1)}, u32[]{:S(2)}, u32[]{:S(2)}) collective-permute-start(bf16[2,2,96,3072]{3,2,1,0:T(8,128)(2,1)} %dynamic-slice_bitcast_fusion), channel_id=1, source_target_pairs={{0,4},{4,0},{8,12},{12,8},{16,20},{20,16},{24,28},{28,24},{1,5},{5... | collective-permute-start | bytes 7077896 | tf_op jit(solution)/shard_map/ppermute | solution.py:189
  363.1 26.0 %collective-permute-start.29 = (bf16[2,96,1536]{2,1,0:T(8,128)(2,1)S(1)}, bf16[2,96,1536]{2,1,0:T(8,128)(2,1)S(1)}, u32[]{:S(2)}, u32[]{:S(2)}) collective-permute-start(bf16[2,96,1536]{2,1,0:T(8,128)(2,1)S(1)} %dynamic-slice_bitcast_fusion.2), channel_id=1, source_target_pairs={{0,16},{4,20},{8,24},{12,28},{16,0},{20,4},{24,8},{28,12},{1,17},{... | collective-permute-start | bytes 1769480 | tf_op jit(solution)/shard_map/ppermute | solution.py:189
  364.7 24.4 %collective-permute-start.30 = (bf16[2,96,1536]{2,1,0:T(8,128)(2,1)S(1)}, bf16[2,96,1536]{2,1,0:T(8,128)(2,1)S(1)}, u32[]{:S(2)}, u32[]{:S(2)}) collective-permute-start(bf16[2,96,1536]{2,1,0:T(8,128)(2,1)S(1)} %dynamic-slice_bitcast_fusion.1), channel_id=1, source_target_pairs={{0,8},{4,12},{8,0},{12,4},{16,24},{20,28},{24,16},{28,20},{1,9},{5... | collective-permute-start | bytes 1769480 | tf_op jit(solution)/shard_map/ppermute | solution.py:189
  366.5 4.4 collective-permute-start.36
  366.5 21.6 %collective-permute-start.32 = (bf16[1,256,768]{2,1,0:T(8,128)(2,1)S(1)}, bf16[1,256,768]{2,1,0:T(8,128)(2,1)S(1)}, u32[]{:S(2)}, u32[]{:S(2)}) collective-permute-start(bf16[1,256,768]{2,1,0:T(8,128)(2,1)S(1)} %get-tuple-element.303), channel_id=1, source_target_pairs={{0,2},{1,3},{2,0},{3,1},{4,6},{5,7},{6,4},{7,5},{8,10},{9,11},{10,... | collective-permute-start | bytes 1179656 | tf_op jit(solution)/shard_map/ppermute | solution.py:174
  367.3 21.8 %collective-permute-start.31 = (bf16[1,256,768]{2,1,0:T(8,128)(2,1)S(1)}, bf16[1,256,768]{2,1,0:T(8,128)(2,1)S(1)}, u32[]{:S(2)}, u32[]{:S(2)}) collective-permute-start(bf16[1,256,768]{2,1,0:T(8,128)(2,1)S(1)} %get-tuple-element.304), channel_id=1, source_target_pairs={{0,3},{1,0},{2,1},{3,2},{4,7},{5,4},{6,5},{7,6},{8,11},{9,8},{10,9... | collective-permute-start | bytes 1179656 | tf_op jit(solution)/shard_map/ppermute | solution.py:174
  370.8 22.7 %copy-start.19 = (f32[32,11,768]{2,1,0:T(8,128)S(1)}, f32[32,11,768]{2,1,0:T(8,128)}, u32[]{:S(2)}) copy-start(f32[32,11,768]{2,1,0:T(8,128)} %all-gather.7.cloned.1.call-done) | copy-start | bytes 3244036
  370.9 28.4 %collective-permute-start.35 = (bf16[1,256,768]{2,1,0:T(8,128)(2,1)}, bf16[1,256,768]{2,1,0:T(8,128)(2,1)S(1)}, u32[]{:S(2)}, u32[]{:S(2)}) collective-permute-start(bf16[1,256,768]{2,1,0:T(8,128)(2,1)} %get-tuple-element.302), channel_id=1, source_target_pairs={{0,1},{1,2},{2,3},{3,0},{4,5},{5,6},{6,7},{7,4},{8,9},{9,10},{10,1... | collective-permute-start | bytes 1179656 | tf_op jit(solution)/shard_map/ppermute | solution.py:174
  388.1 6.2 %collective-permute-start.37 = (f32[768]{0:T(1024)S(1)}, f32[768]{0:T(1024)S(1)}, u32[]{:S(2)}, u32[]{:S(2)}) collective-permute-start(f32[768]{0:T(1024)S(1)} %add.419), channel_id=1, source_target_pairs={{0,8},{4,12},{8,0},{12,4},{16,24},{20,28},{24,16},{28,20},{1,9},{5... | collective-permute-start | bytes 9224 | tf_op jit(solution)/shard_map/ppermute | solution.py:189
  390.9 8.4 %collective-permute-start.34 = (bf16[96,1536]{1,0:T(8,128)(2,1)}, bf16[96,1536]{1,0:T(8,128)(2,1)}, u32[]{:S(2)}, u32[]{:S(2)}) collective-permute-start(bf16[96,1536]{1,0:T(8,128)(2,1)} %dynamic-slice_bitcast_fusion.5), channel_id=1, source_target_pairs={{0,16},{4,20},{8,24},{12,28},{16,0},{20,4},{24,8},{28,12},{1,17},{... | collective-permute-start | bytes 884744 | tf_op jit(solution)/shard_map/ppermute | solution.py:189
  391.5 8.6 %collective-permute-start.33 = (bf16[96,1536]{1,0:T(8,128)(2,1)}, bf16[96,1536]{1,0:T(8,128)(2,1)}, u32[]{:S(2)}, u32[]{:S(2)}) collective-permute-start(bf16[96,1536]{1,0:T(8,128)(2,1)} %dynamic-slice_bitcast_fusion.6), channel_id=1, source_target_pairs={{0,8},{4,12},{8,0},{12,4},{16,24},{20,28},{24,16},{28,20},{1,9},{5... | collective-permute-start | bytes 884744 | tf_op jit(solution)/shard_map/ppermute | solution.py:189
  394.3 4.9 %collective-permute-start.38 = (f32[768]{0:T(1024)S(1)}, f32[768]{0:T(1024)S(1)}, u32[]{:S(2)}, u32[]{:S(2)}) collective-permute-start(f32[768]{0:T(1024)S(1)} %add.420), channel_id=1, source_target_pairs={{0,16},{4,20},{8,24},{12,28},{16,0},{20,4},{24,8},{28,12},{1,17},{... | collective-permute-start | bytes 9224 | tf_op jit(solution)/shard_map/ppermute | solution.py:189
  401.0 20.2 %copy-start.16 = (bf16[1,256,768]{2,1,0:T(8,128)(2,1)S(1)}, bf16[1,256,768]{2,1,0:T(8,128)(2,1)}, u32[]{:S(2)}) copy-start(bf16[1,256,768]{2,1,0:T(8,128)(2,1)} %get-tuple-element.177) | copy-start | bytes 1179652
  401.1 20.2 %copy-start.29 = (bf16[1,256,768]{2,1,0:T(8,128)(2,1)S(1)}, bf16[1,256,768]{2,1,0:T(8,128)(2,1)}, u32[]{:S(2)}) copy-start(bf16[1,256,768]{2,1,0:T(8,128)(2,1)} %copy-done.28) | copy-start | bytes 1179652
  401.1 20.2 %copy-start.31 = (bf16[1,256,768]{2,1,0:T(8,128)(2,1)S(1)}, bf16[1,256,768]{2,1,0:T(8,128)(2,1)}, u32[]{:S(2)}) copy-start(bf16[1,256,768]{2,1,0:T(8,128)(2,1)} %copy-done.30) | copy-start | bytes 1179652
  401.1 20.2 %copy-start.33 = (bf16[1,256,768]{2,1,0:T(8,128)(2,1)S(1)}, bf16[1,256,768]{2,1,0:T(8,128)(2,1)}, u32[]{:S(2)}) copy-start(bf16[1,256,768]{2,1,0:T(8,128)(2,1)} %copy-done.32) | copy-start | bytes 1179652
  401.1 20.2 %copy-start.53 = (s32[4]{0:T(128)S(1)}, s32[4]{0:T(128)}, u32[]{:S(2)}) copy-start(s32[4]{0:T(128)} %get-tuple-element.392) | copy-start | bytes 52
  402.7 22.9 %collective-permute-start.39 = (bf16[97,768]{1,0:T(8,128)(2,1)S(1)}, bf16[97,768]{1,0:T(8,128)(2,1)S(1)}, u32[]{:S(2)}, u32[]{:S(2)}) collective-permute-start(bf16[97,768]{1,0:T(8,128)(2,1)S(1)} %pad_maximum_fusion.10), channel_id=1, source_target_pairs={{0,3},{1,0},{2,1},{3,2},{4,7},{5,4},{6,5},{7,6},{8,11},{9,8},{10,9... | collective-permute-start | bytes 446984 | tf_op jit(solution)/shard_map/ppermute | solution.py:174
  412.6 21.4 %collective-permute-start.40 = (bf16[97,768]{1,0:T(8,128)(2,1)S(1)}, bf16[97,768]{1,0:T(8,128)(2,1)S(1)}, u32[]{:S(2)}, u32[]{:S(2)}) collective-permute-start(bf16[97,768]{1,0:T(8,128)(2,1)S(1)} %pad_maximum_fusion.11), channel_id=1, source_target_pairs={{0,2},{1,3},{2,0},{3,1},{4,6},{5,7},{6,4},{7,5},{8,10},{9,11},{10,... | collective-permute-start | bytes 446984 | tf_op jit(solution)/shard_map/ppermute | solution.py:174
  421.1 12.9 %collective-permute-start.41 = (bf16[97,768]{1,0:T(8,128)(2,1)S(1)}, bf16[97,768]{1,0:T(8,128)(2,1)S(1)}, u32[]{:S(2)}, u32[]{:S(2)}) collective-permute-start(bf16[97,768]{1,0:T(8,128)(2,1)S(1)} %pad_maximum_fusion.12), channel_id=1, source_target_pairs={{0,1},{1,2},{2,3},{3,0},{4,5},{5,6},{6,7},{7,4},{8,9},{9,10},{10,1... | collective-permute-start | bytes 446984 | tf_op jit(solution)/shard_map/ppermute | solution.py:174
  (43 other events, 210.8 us)
Sparse Core Ops, SparseCore 0:
  67.0 64.8 all-gather.4
  194.0 53.7 reduce-scatter.1
  271.9 65.5 all-gather.6

commit v8 on v7

--- a/solution.py
+++ b/solution.py
@@ -445,18 +445,22 @@
         outer_bias_grad,
         second_gain_grad,
         second_shift_grad,
-        by_rank(jnp.sum(grad_context.astype(WIDE), axis=(0, 1))),
         *jnp.split(by_rank(inner_bias_grad), inner_bias_grad.shape[0] // width),
+        jnp.zeros((width,), WIDE),
+        jnp.zeros((width,), WIDE),
     ]
-    (inner_share, _), vectors = scatter_near(inner_share), vectors
-    grad_context, inner_share, output_grad, vectors = lax.optimization_barrier(
-        (grad_context, inner_share, output_grad, vectors)
-    )
-    vectors = lax.all_gather(jnp.stack(vectors), ("tp", "fsdp"), axis=0)
+    vectors = lax.all_gather(
+        jnp.stack(lax.optimization_barrier(vectors)), ("tp", "fsdp"), axis=0
+    )
+    inner_share, _ = scatter_near(inner_share)
+    grad_context, inner_share, output_grad = lax.optimization_barrier(
+        (grad_context, inner_share, output_grad)
+    )
     inner_share, _ = scatter_far(inner_share)
     back = functools.partial(
         attend_back, queries, keys_all, values, grad_context, context.reshape(shape), logsum, ids
     )
+    value_bias_grad = jnp.sum(grad_context.astype(WIDE), axis=(0, 1))
     halfway = back(None, 0)
     halfway, inner_share, outer_share, layer_out = lax.optimization_barrier(
         (halfway, inner_share, outer_share, layer_out)
@@ -467,7 +471,7 @@
     rows_grads, unit_parts, vectors = lax.optimization_barrier(
         (back(halfway, 1), unit_parts, vectors)
     )
-    totals = jnp.sum(vectors, axis=0).reshape(-1)
+    totals = jnp.sum(vectors, axis=0).reshape(-1)[: -2 * width]
     inner_share, outer_share = summed(unit_parts, units)
     query_rows_grad, key_rows_grad, value_rows_grad = (
         array.reshape(count * length, width) for array in rows_grads
@@ -482,7 +486,8 @@
         + dot(key_rows_grad, key_full, BY_LAST)
         + dot(value_rows_grad, value_full, BY_LAST)
     ).astype(LOW)
-    late = jnp.sum(query_rows_grad.astype(WIDE), axis=0)
+    late = [jnp.sum(query_rows_grad.astype(WIDE), axis=0), value_bias_grad]
+    late = jnp.concatenate(late)
     heads_share, (tokens_grad, late) = scatter_core(
         jnp.concatenate(head_grads + [output_grad], axis=1), (tokens_grad, late)
     )
@@ -492,18 +497,18 @@
     heads_share, tokens_grad[3:] = scatter_far(heads_share, tokens_grad[3:])
     heads_share, late = lax.optimization_barrier((heads_share, late))
     high = late.astype(LOW)
-    late = jnp.concatenate([high, (late - high.astype(WIDE)).astype(LOW)])
-    late = jnp.pad(late, (0, heads_share.shape[1] - late.shape[0]))[None]
+    late = jnp.stack([high, (late - high.astype(WIDE)).astype(LOW)]).reshape(2, 2, width)
+    late = late.transpose(1, 0, 2).reshape(1, 4 * width)
     heads_share = own_columns(jnp.concatenate([heads_share, late], axis=0), (head_cols,) * 4)
     heads_share = summed(heads_share, (head_cols,) * 4)
     query_bias_total = heads_share[0][shard_rows] + heads_share[1][shard_rows]
+    value_bias_total = heads_share[2][shard_rows] + heads_share[3][shard_rows]
     query_share, key_share, value_share, output_share = (
         share[:shard_rows] for share in heads_share
     )
     tokens_grad = own_places(tokens_grad).astype(WIDE)
     rowwise = [totals[i * width : (i + 1) * width] for i in range(6)]
-    value_bias_total = lax.dynamic_slice_in_dim(totals, 6 * width + rank * head_cols, head_cols)
-    inner_bias_total = lax.dynamic_slice_in_dim(totals, 7 * width + rank * unit_cols, unit_cols)
+    inner_bias_total = lax.dynamic_slice_in_dim(totals, 6 * width + rank * unit_cols, unit_cols)
     return (
         layer_out,
         tokens_grad,

time: 449 us -> 431 us (0.960)
  local copies, waits for them, and re-layouts: 56.3 us -> 41 us
  waiting for transfers between devices: 101 us -> 113 us
  other arithmetic: 58.9 us -> 50.3 us
    ppermute x12, waiting for transfers between devices: 25.6 us -> 45.1 us  [sent_back(): moved[step] = lax.ppermute(parts[step], 'tp', pairs)]
    ppermute x12, starting transfers between devices: 32.1 us -> 14.2 us  [sent_back(): moved[step] = lax.ppermute(parts[step], 'tp', pairs)]
    ppermute x6, waiting for transfers between devices: 23.7 us -> 8.97 us  [spread(): return [block] + [lax.ppermute(block, 'tp', pairs) for pairs in rank_pairs]]
    ppermute x6, starting transfers between devices: 2.96 us -> 14.2 us  [dealt(): parts.append(lax.ppermute(block, 'tp', pairs) if step else block)]
    ppermute x18, waiting for transfers between devices: 2.81 us -> 8.6 us  [flip(): return lax.ppermute(block, axis, [(i, i ^ bit) for i in range(members)])]
    convert_element_type x10, other arithmetic: 12.5 us -> 6.86 us  [add_low(): return (kept.astype(WIDE) + moved.astype(WIDE)).astype(LOW)]
    another operation x12 -> x16, local copies, waits for them, and re-layouts: 6.84 us -> 1.37 us  [the longest x13 1.33 us: on_device(): jnp.stack(lax.optimization_barrier(vectors))]
    unnamed x145 -> x147, local copies, waits for them, and re-layouts: 14.3 us -> 13.3 us
  transfers between devices with their start and end apart: 45 -> 45, of which waited for: 10 -> 15; matrix products, arithmetic and copies ran while one was open for 34% -> 29% of each run, Pallas kernels for 14% -> 14%
where the time goes in v8:
time: 431 us; the launch traced here: 426 us
  waiting for transfers between devices  113 us (26%)
  matrix products  86.2 us (20%)
  Pallas kernels  60.2 us (14%)
  starting transfers between devices  59 us (14%)
  other arithmetic  50.3 us (12%)
  local copies, waits for them, and re-layouts  41 us (10%)
  between operations  15.6 us (4%)
    dot_general x18, matrix products, dot(): return lax.dot_general(left, right, dims, preferred_element_type=WIDE)  86.2 us
    ppermute x12, waiting for transfers between devices, sent_back(): moved[step] = lax.ppermute(parts[step], 'tp', pairs)  45.1 us
    pallas_call x2, Pallas kernels, attend_back(): pl.pallas_call(body, grid=(count, pairs - first if part else pairs // 2),...  37.3 us
    ppermute x6, waiting for transfers between devices, dealt(): parts.append(lax.ppermute(block, 'tp', pairs) if step else block)  33.3 us
    pallas_call x1, Pallas kernels, attend(): pl.pallas_call(functools.partial(attend_kernel, scaling=scaling), grid=(c...  22.9 us
    all_gather x1, waiting for transfers between devices, on_device(): lax.all_gather(jnp.stack(lax.optimization_barrier(vectors)), ('tp', 'fsdp...  17.2 us
    ppermute x18, starting transfers between devices, flip(): return lax.ppermute(block, axis, [(i, i ^ bit) for i in range(members)])  16.2 us
    ppermute x6, starting transfers between devices, dealt(): parts.append(lax.ppermute(block, 'tp', pairs) if step else block)  14.2 us
  transfers between devices with their start and end apart: 45, of which 15 were waited for; matrix products, arithmetic and copies ran while one was open for 29% of the time, Pallas kernels for 14%

profile of v8, /device:TPU:0, one launch (start us, length us, event | category | flops | bytes accessed | tf_op | source)
XLA Modules:
  0.0 425.6 jit_solution(135895092211076635)
XLA Ops:
  7.2 2.1 concatenate.86
  13.2 3.1 collective-permute-start
  16.3 2.6 collective-permute-start.1
  29.2 2.6 collective-permute-done.1
  32.7 4.7 %collective-permute-start.5 = (bf16[96,1536]{1,0:T(8,128)(2,1)S(1)}, bf16[96,1536]{1,0:T(8,128)(2,1)S(1)}, u32[]{:S(2)}, u32[]{:S(2)}) collective-permute-start(bf16[96,1536]{1,0:T(8,128)(2,1)S(1)} %pad_maximum_fusion.5), channel_id=1, source_target_pairs={{0,1},{1,2},{2,3},{3,0},{4,5},{5,6},{6,7},{7,4},{8,9},{9,10},{10,1... | collective-permute-start | bytes 884744 | tf_op jit(solution)/shard_map/ppermute | solution.py:156
  37.4 1.6 collective-permute-start.6
  40.1 1.5 collective-permute-start.3
  41.6 1.5 collective-permute-start.4
  46.5 4.1 collective-permute-done.3
  51.8 5.6 %collective-permute-done.6 = bf16[96,1536]{1,0:T(8,128)(2,1)S(1)} collective-permute-done((bf16[96,1536]{1,0:T(8,128)(2,1)S(1)}, bf16[96,1536]{1,0:T(8,128)(2,1)S(1)}, u32[]{:S(2)}, u32[]{:S(2)}) %collective-permute-start.6) | collective-permute-done | bytes 294944 | tf_op jit(solution)/shard_map/ppermute | solution.py:156
  63.2 1.6 collective-permute-start.9
  66.1 1.6 collective-permute-start.8
  68.5 6.9 %collective-permute-start.10 = (bf16[1,256,768]{2,1,0:T(8,128)(2,1)S(1)}, bf16[1,256,768]{2,1,0:T(8,128)(2,1)S(1)}, u32[]{:S(2)}, u32[]{:S(2)}) collective-permute-start(bf16[1,256,768]{2,1,0:T(8,128)(2,1)S(1)} %get-tuple-element.318), channel_id=1, source_target_pairs={{0,1},{1,2},{2,3},{3,0},{4,5},{5,6},{6,7},{7,4},{8,9},{9,10},{10,1... | collective-permute-start | bytes 1179656 | tf_op jit(solution)/shard_map/ppermute | solution.py:165
  75.4 2.2 collective-permute-start.11
  77.6 9.5 %collective-permute-done.10 = bf16[1,256,768]{2,1,0:T(8,128)(2,1)S(1)} collective-permute-done((bf16[1,256,768]{2,1,0:T(8,128)(2,1)S(1)}, bf16[1,256,768]{2,1,0:T(8,128)(2,1)S(1)}, u32[]{:S(2)}, u32[]{:S(2)}) %collective-permute-start.10) | collective-permute-done | bytes 393248 | tf_op jit(solution)/shard_map/ppermute | solution.py:165
  87.1 14.9 %collective-permute-done.11 = bf16[1,256,768]{2,1,0:T(8,128)(2,1)S(1)} collective-permute-done((bf16[1,256,768]{2,1,0:T(8,128)(2,1)S(1)}, bf16[1,256,768]{2,1,0:T(8,128)(2,1)S(1)}, u32[]{:S(2)}, u32[]{:S(2)}) %collective-permute-start.11) | collective-permute-done | bytes 393248 | tf_op jit(solution)/shard_map/ppermute | solution.py:165
  108.2 8.9 %collective-permute-done.13 = bf16[1,256,768]{2,1,0:T(8,128)(2,1)} collective-permute-done((bf16[1,256,768]{2,1,0:T(8,128)(2,1)}, bf16[1,256,768]{2,1,0:T(8,128)(2,1)}, u32[]{:S(2)}, u32[]{:S(2)}) %collective-permute-start.13) | collective-permute-done | bytes 393248 | tf_op jit(solution)/shard_map/ppermute | solution.py:165
  119.3 3.5 collective-permute-start.15
  123.3 2.2 bitcast_select_fusion
  125.5 2.6 fusion.63.k_ref.refs_1_
  128.1 2.6 fusion.35.v_ref.refs_2_
  130.7 2.5 fusion.34.q_ref.refs_0_
  133.2 22.9 %attend.1 = (bf16[1,1024,768]{2,1,0:T(8,128)(2,1)}, f32[1,6,2,1024]{3,2,1,0:T(2,128)}) custom-call(bf16[1,1024,768]{2,1,0:T(8,128)(2,1)} %fusion.34.q_ref.refs_0_, bf16[1,1024,768]{2,1,0:T(8,128)(2,1)} %fusion.63.k_ref.refs_1_, bf16[1,1024,768]{2,1,0:T(8,128)(2,1)} %fusion.35.v_ref.refs_2_, s32[1,1,1024]{2,1,0:T(1,128)} %broadcast_in_dim_reshape.6.row_ref.refs_6_, ...), custom_call_target="tpu_custom_call" | custom-call | flops 22548578304 | bytes 6291456 | tf_op jit(solution)/shard_map/attend/pallas_call | solution.py:93
  156.9 3.8 fusion.114
  161.2 11.1 %multiply_convert_fusion = (bf16[1024,3072]{1,0:T(8,128)(2,1)S(1)}, f32[1024,3072]{1,0:T(8,128)}) fusion(f32[3072]{0:T(1024)} %pad_maximum_fusion.13, bf16[768,6144]{1,0:T(8,128)(2,1)} %all-gather.5.cloned.1.call-done, f32[1024,768]{1,0:T(8,128)S(1)} %get-tuple-element.379, f32[768]{0:T(1024)} %convert_element_type.268, f32[768]{0:T(1024)S(1)} %convert_element_type.267, ...), kind=kOutput, calls=%fused_computation.8 | convolution fusion | flops 4854644736 | bytes 26766336 | tf_op jit(solution)/shard_map/dot_general | solution.py:22
  172.4 5.4 %fusion.104 = (f32[1024]{0:T(1024)S(1)}, f32[1024,768]{1,0:T(8,128)S(1)}) fusion(f32[768]{0:T(1024)S(1)} %copy-done.47, f32[768]{0:T(1024)S(1)} %copy-done.45, f32[768]{0:T(1024)S(1)} %convert_element_type.267, f32[1024]{0:T(1024)S(1)} %add_rsqrt_fusion.1, f32[1024,768]{1,0:T(8,128)S(1)} %get-tuple-element.379, f32[1024]{0:T(1024)S(1)} %broadcast_multiply_fusion.5, ...), kind=kOutput, calls=%fused_computation.250 | convolution fusion | flops 4837342208 | bytes 17326080 | tf_op jit(solution)/shard_map/dot_general | solution.py:22
  178.8 5.3 %fusion.29 = (f32[768]{0:T(1024)}, f32[1024]{0:T(1024)S(1)}, f32[1024]{0:T(1024)S(1)}, bf16[1024,768]{1,0:T(8,128)(2,1)}) fusion(f32[1024,768]{1,0:T(8,128)S(1)} %get-tuple-element.296, f32[1024]{0:T(1024)S(1)} %add_rsqrt_fusion, f32[1024]{0:T(1024)S(1)} %broadcast_multiply_fusion.4, bf16[1,256,768]{2,1,0:T(8,128)(2,1)} %collective-permute-done.16, ...), kind=kLoop, calls=%fused_computation.44 | loop fusion | flops 14939392 | bytes 6317056 | tf_op jit(solution)/shard_map/reduce_sum | solution.py:277
  184.2 3.5 fusion.101
  187.7 1.7 copy-done.8
  189.3 6.9 %convolution_convert_fusion = bf16[768,3072]{1,0:T(8,128)(2,1)} fusion(bf16[1024,3072]{1,0:T(8,128)(2,1)S(1)} %get-tuple-element.150, f32[1024,768]{1,0:T(8,128)S(1)} %get-tuple-element.292), kind=kOutput, calls=%fused_computation.13 | convolution fusion | flops 4834983936 | bytes 14155776 | tf_op jit(solution)/shard_map/dot_general | solution.py:22
  196.3 14.2 %convert_reduce_fusion = (f32[3072]{0:T(1024)}, bf16[1024,3072]{1,0:T(8,128)(2,1)S(1)}) fusion(f32[1024,3072]{1,0:T(8,128)} %get-tuple-element.381, f32[3072]{0:T(1024)} %pad_maximum_fusion.13, bf16[768,6144]{1,0:T(8,128)(2,1)} %all-gather.5.cloned.1.call-done, f32[1024,768]{1,0:T(8,128)} %copy-done.8), kind=kOutput, calls=%fused_computation.7 | convolution fusion | flops 4873516032 | bytes 26763264 | tf_op jit(solution)/shard_map/dot_general | solution.py:22
  210.5 6.3 %convolution_convert_fusion.1 = bf16[768,3072]{1,0:T(8,128)(2,1)S(1)} fusion(bf16[1024,3072]{1,0:T(8,128)(2,1)S(1)} %get-tuple-element.384, f32[1024,768]{1,0:T(8,128)S(1)} %get-tuple-element.379, f32[768]{0:T(1024)S(1)} %copy-done.46, f32[768]{0:T(1024)S(1)} %convert_element_type.267, f32[1024]{0:T(1024)S(1)} %copy-done.38, ...), kind=kOutput, calls=%fused_computation.14 | convolution fusion | flops 4838129664 | bytes 14170112 | tf_op jit(solution)/shard_map/dot_general | solution.py:22
  221.1 10.3 %multiply_reduce_fusion = (f32[768]{0:T(1024)}, f32[1024]{0:T(1024)S(1)}, f32[1024]{0:T(1024)S(1)}, f32[768]{0:T(1024)}, f32[1024,768]{1,0:T(8,128)S(1)}) fusion(f32[1024,768]{1,0:T(8,128)S(1)} %get-tuple-element.379, f32[1024]{0:T(1024)S(1)} %copy-done.38, f32[1024]{0:T(1024)S(1)} %broadcast_multiply_fusion.5, f32[768]{0:T(1024)S(1)} %convert_element_type.267, ...), kind=kOutput, calls=%fused_computation.48 | convolution fusion | flops 4839698432 | bytes 20472832 | tf_op jit(solution)/shard_map/dot_general | solution.py:22
  232.7 6.8 %collective-permute-done.18 = bf16[1,256,768]{2,1,0:T(8,128)(2,1)S(1)} collective-permute-done((bf16[1,256,768]{2,1,0:T(8,128)(2,1)S(1)}, bf16[1,256,768]{2,1,0:T(8,128)(2,1)S(1)}, u32[]{:S(2)}, u32[]{:S(2)}) %collective-permute-start.18) | collective-permute-done | bytes 393248 | tf_op jit(solution)/shard_map/ppermute | solution.py:174
  243.2 3.9 fusion.64.g_ref.refs_3_
  247.1 1.4 convert_reduce_fusion.1
  250.0 4.9 %fusion.51 = bf16[768,768]{1,0:T(8,128)(2,1)} fusion(bf16[1,1024,768]{2,1,0:T(8,128)(2,1)} %get-tuple-element.141.c_ref.refs_4_, f32[1024,768]{1,0:T(8,128)} %copy-done.1), kind=kOutput, calls=%fused_computation.89 | convolution fusion | flops 1209335808 | bytes 5898240 | tf_op jit(solution)/shard_map/dot_general | solution.py:22
  254.9 1.5 collective-permute-start.23
  256.9 2.2 collective-permute-done.20
  261.5 1.5 collective-permute-start.22
  263.7 18.6 %attend_back.2 = (bf16[1,1024,768]{2,1,0:T(8,128)(2,1)}, bf16[1,1024,768]{2,1,0:T(8,128)(2,1)}, bf16[1,1024,768]{2,1,0:T(8,128)(2,1)}) custom-call(bf16[1,1024,768]{2,1,0:T(8,128)(2,1)} %fusion.34.q_ref.refs_0_, bf16[1,1024,768]{2,1,0:T(8,128)(2,1)} %fusion.63.k_ref.refs_1_, bf16[1,1024,768]{2,1,0:T(8,128)(2,1)} %fusion.35.v_ref.refs_2_, ...), custom_call_target="tpu_custom_call" | custom-call | flops 19327352832 | bytes 5505024 | tf_op jit(solution)/shard_map/attend_back/pallas_call | solution.py:128
  283.8 1.5 collective-permute-start.27
  286.1 2.4 collective-permute-start.26
  290.7 18.8 %attend_back.3 = (bf16[1,1024,768]{2,1,0:T(8,128)(2,1)}, bf16[1,1024,768]{2,1,0:T(8,128)(2,1)}, bf16[1,1024,768]{2,1,0:T(8,128)(2,1)}) custom-call(bf16[1,1024,768]{2,1,0:T(8,128)(2,1)} %fusion.34.q_ref.refs_0_, bf16[1,1024,768]{2,1,0:T(8,128)(2,1)} %fusion.63.k_ref.refs_1_, ...), custom_call_target="tpu_custom_call", output_to_operand_aliasing={{0}: (8, {}), {1}: (9, {}), {2}: (10, {})} | custom-call | flops 19327352832 | bytes 5505024 | tf_op jit(solution)/shard_map/attend_back/pallas_call | solution.py:128
  309.5 17.2 %all-gather.7.cloned.1.call-done = f32[32,12,768]{2,1,0:T(8,128)} async-done(((f32[1,12,768]{2,1,0:T(8,128)}), f32[32,12,768]{2,1,0:T(8,128)}) %all-gather.7.cloned.1.call-update) | async-done | bytes 1179664 | tf_op jit(solution)/shard_map/all_gather | solution.py:452
  326.7 3.1 fusion.54
  329.9 1.5 fusion.57
  331.3 1.5 fusion.60
  333.7 2.2 copy-done
  335.9 1.6 dynamic-slice_bitcast_fusion
  338.7 1.7 convert_reduce_fusion.2
  340.4 1.7 convert_reduce_fusion.3
  342.1 2.8 fusion.44
  345.1 1.4 fusion.40
  347.5 1.5 add_convert_fusion
  350.5 1.5 collective-permute-start.30
  353.6 2.3 collective-permute-start.31
  357.1 8.3 %collective-permute-done.31 = bf16[1,256,768]{2,1,0:T(8,128)(2,1)S(1)} collective-permute-done((bf16[1,256,768]{2,1,0:T(8,128)(2,1)S(1)}, bf16[1,256,768]{2,1,0:T(8,128)(2,1)S(1)}, u32[]{:S(2)}, u32[]{:S(2)}) %collective-permute-start.31) | collective-permute-done | bytes 393248 | tf_op jit(solution)/shard_map/ppermute | solution.py:174
  366.9 23.3 %collective-permute-done.32 = bf16[1,256,768]{2,1,0:T(8,128)(2,1)S(1)} collective-permute-done((bf16[1,256,768]{2,1,0:T(8,128)(2,1)S(1)}, bf16[1,256,768]{2,1,0:T(8,128)(2,1)S(1)}, u32[]{:S(2)}, u32[]{:S(2)}) %collective-permute-start.32) | collective-permute-done | bytes 393248 | tf_op jit(solution)/shard_map/ppermute | solution.py:174
  394.9 1.5 collective-permute-start.38
  396.4 1.6 slice_reduce_fusion
  403.7 2.1 collective-permute-start.41
  405.8 4.0 fusion.36
  409.8 6.7 %collective-permute-done.40 = bf16[97,768]{1,0:T(8,128)(2,1)S(1)} collective-permute-done((bf16[97,768]{1,0:T(8,128)(2,1)S(1)}, bf16[97,768]{1,0:T(8,128)(2,1)S(1)}, u32[]{:S(2)}, u32[]{:S(2)}) %collective-permute-start.40) | collective-permute-done | bytes 149024 | tf_op jit(solution)/shard_map/ppermute | solution.py:174
  (353 shorter events, 79.6 us)
Async XLA Ops:
  7.2 32.8 %copy-start.36 = (bf16[192,96]{1,0:T(8,128)(2,1)S(1)}, bf16[192,96]{1,0:T(8,128)(2,1)}, u32[]{:S(2)}) copy-start(bf16[192,96]{1,0:T(8,128)(2,1)} %param.27) | copy-start | bytes 110596
  7.2 154.0 %all-gather.5.cloned.1.call-start = ((), (), s32[]{:S(2)}) async-start(), calls=%async_computation.1 | async-start | bytes 10616832 | tf_op jit(solution)/shard_map/all_gather | solution.py:391
  13.2 16.0 %collective-permute-start = (bf16[99,768]{0,1:T(8,128)(2,1)S(1)}, bf16[99,768]{0,1:T(8,128)(2,1)S(1)}, u32[]{:S(2)}, u32[]{:S(2)}) collective-permute-start(bf16[99,768]{0,1:T(8,128)(2,1)S(1)} %fusion.92), channel_id=1, source_target_pairs={{0,1},{1,2},{2,3},{3,0},{4,5},{5,6},{6,7},{7,4},{8,9},{9,10},{10,1... | collective-permute-start | bytes 456200 | tf_op jit(solution)/shard_map/ppermute | solution.py:156
  16.3 15.5 %collective-permute-start.1 = (bf16[99,768]{0,1:T(8,128)(2,1)S(1)}, bf16[99,768]{0,1:T(8,128)(2,1)S(1)}, u32[]{:S(2)}, u32[]{:S(2)}) collective-permute-start(bf16[99,768]{0,1:T(8,128)(2,1)S(1)} %fusion.92), channel_id=1, source_target_pairs={{0,2},{1,3},{2,0},{3,1},{4,6},{5,7},{6,4},{7,5},{8,10},{9,11},{10,... | collective-permute-start | bytes 456200 | tf_op jit(solution)/shard_map/ppermute | solution.py:156
  18.9 12.9 %collective-permute-start.2 = (bf16[99,768]{0,1:T(8,128)(2,1)S(1)}, bf16[99,768]{0,1:T(8,128)(2,1)S(1)}, u32[]{:S(2)}, u32[]{:S(2)}) collective-permute-start(bf16[99,768]{0,1:T(8,128)(2,1)S(1)} %fusion.92), channel_id=1, source_target_pairs={{0,3},{1,0},{2,1},{3,2},{4,7},{5,4},{6,5},{7,6},{8,11},{9,8},{10,9... | collective-permute-start | bytes 456200 | tf_op jit(solution)/shard_map/ppermute | solution.py:156
  32.7 13.8 %collective-permute-start.5 = (bf16[96,1536]{1,0:T(8,128)(2,1)S(1)}, bf16[96,1536]{1,0:T(8,128)(2,1)S(1)}, u32[]{:S(2)}, u32[]{:S(2)}) collective-permute-start(bf16[96,1536]{1,0:T(8,128)(2,1)S(1)} %pad_maximum_fusion.5), channel_id=1, source_target_pairs={{0,1},{1,2},{2,3},{3,0},{4,5},{5,6},{6,7},{7,4},{8,9},{9,10},{10,1... | collective-permute-start | bytes 884744 | tf_op jit(solution)/shard_map/ppermute | solution.py:156
  37.4 20.0 %collective-permute-start.6 = (bf16[96,1536]{1,0:T(8,128)(2,1)S(1)}, bf16[96,1536]{1,0:T(8,128)(2,1)S(1)}, u32[]{:S(2)}, u32[]{:S(2)}) collective-permute-start(bf16[96,1536]{1,0:T(8,128)(2,1)S(1)} %pad_maximum_fusion.5), channel_id=1, source_target_pairs={{0,2},{1,3},{2,0},{3,1},{4,6},{5,7},{6,4},{7,5},{8,10},{9,11},{10,... | collective-permute-start | bytes 884744 | tf_op jit(solution)/shard_map/ppermute | solution.py:156
  39.1 18.4 %collective-permute-start.7 = (bf16[96,1536]{1,0:T(8,128)(2,1)S(1)}, bf16[96,1536]{1,0:T(8,128)(2,1)}, u32[]{:S(2)}, u32[]{:S(2)}) collective-permute-start(bf16[96,1536]{1,0:T(8,128)(2,1)S(1)} %pad_maximum_fusion.5), channel_id=1, source_target_pairs={{0,3},{1,0},{2,1},{3,2},{4,7},{5,4},{6,5},{7,6},{8,11},{9,8},{10,9... | collective-permute-start | bytes 884744 | tf_op jit(solution)/shard_map/ppermute | solution.py:156
  40.1 17.4 %copy-start.21 = (bf16[96,1536]{0,1:T(8,128)(2,1)}, bf16[96,1536]{0,1:T(8,128)(2,1)S(1)}, u32[]{:S(2)}) copy-start(bf16[96,1536]{0,1:T(8,128)(2,1)S(1)} %get-tuple-element.352) | copy-start | bytes 884740
  40.1 10.5 %collective-permute-start.3 = (bf16[96,1536]{0,1:T(8,128)(2,1)S(1)}, bf16[96,1536]{0,1:T(8,128)(2,1)S(1)}, u32[]{:S(2)}, u32[]{:S(2)}) collective-permute-start(bf16[96,1536]{0,1:T(8,128)(2,1)S(1)} %get-tuple-element.353), channel_id=1, source_target_pairs={{0,8},{4,12},{8,0},{12,4},{16,24},{20,28},{24,16},{28,20},{1,9},{5... | collective-permute-start | bytes 884744 | tf_op jit(solution)/shard_map/ppermute | solution.py:189
  41.6 10.2 %collective-permute-start.4 = (bf16[96,1536]{0,1:T(8,128)(2,1)S(1)}, bf16[96,1536]{0,1:T(8,128)(2,1)S(1)}, u32[]{:S(2)}, u32[]{:S(2)}) collective-permute-start(bf16[96,1536]{0,1:T(8,128)(2,1)S(1)} %get-tuple-element.352), channel_id=1, source_target_pairs={{0,16},{4,20},{8,24},{12,28},{16,0},{20,4},{24,8},{28,12},{1,17},{... | collective-permute-start | bytes 884744 | tf_op jit(solution)/shard_map/ppermute | solution.py:189
  50.6 8.8 %copy-start.30 = (bf16[96,1536]{0,1:T(8,128)(2,1)}, bf16[96,1536]{0,1:T(8,128)(2,1)S(1)}, u32[]{:S(2)}) copy-start(bf16[96,1536]{0,1:T(8,128)(2,1)S(1)} %collective-permute-done.3) | copy-start | bytes 884740
  60.4 222.2 %reduce-scatter.2.cloned.1.call-start = ((), (), s32[]{:S(2)}) async-start(), calls=%async_computation.2 | async-start | bytes 5308416 | tf_op jit(solution)/shard_map/reduce_scatter | solution.py:423
  63.2 38.8 %collective-permute-start.9 = (bf16[2,96,1536]{2,1,0:T(8,128)(2,1)S(1)}, bf16[2,96,1536]{2,1,0:T(8,128)(2,1)}, u32[]{:S(2)}, u32[]{:S(2)}) collective-permute-start(bf16[2,96,1536]{2,1,0:T(8,128)(2,1)S(1)} %broadcast_select_fusion.2), channel_id=1, source_target_pairs={{0,8},{4,12},{8,0},{12,4},{16,24},{20,28},{24,16},{28,20},{1,9},{5... | collective-permute-start | bytes 1769480 | tf_op jit(solution)/shard_map/ppermute | solution.py:189
  66.1 36.0 %collective-permute-start.8 = (bf16[2,96,1536]{2,1,0:T(8,128)(2,1)S(1)}, bf16[2,96,1536]{2,1,0:T(8,128)(2,1)}, u32[]{:S(2)}, u32[]{:S(2)}) collective-permute-start(bf16[2,96,1536]{2,1,0:T(8,128)(2,1)S(1)} %broadcast_select_fusion.3), channel_id=1, source_target_pairs={{0,16},{4,20},{8,24},{12,28},{16,0},{20,4},{24,8},{28,12},{1,17},{... | collective-permute-start | bytes 1769480 | tf_op jit(solution)/shard_map/ppermute | solution.py:189
  68.5 18.6 %collective-permute-start.10 = (bf16[1,256,768]{2,1,0:T(8,128)(2,1)S(1)}, bf16[1,256,768]{2,1,0:T(8,128)(2,1)S(1)}, u32[]{:S(2)}, u32[]{:S(2)}) collective-permute-start(bf16[1,256,768]{2,1,0:T(8,128)(2,1)S(1)} %get-tuple-element.318), channel_id=1, source_target_pairs={{0,1},{1,2},{2,3},{3,0},{4,5},{5,6},{6,7},{7,4},{8,9},{9,10},{10,1... | collective-permute-start | bytes 1179656 | tf_op jit(solution)/shard_map/ppermute | solution.py:165
  75.4 26.6 %collective-permute-start.11 = (bf16[1,256,768]{2,1,0:T(8,128)(2,1)S(1)}, bf16[1,256,768]{2,1,0:T(8,128)(2,1)S(1)}, u32[]{:S(2)}, u32[]{:S(2)}) collective-permute-start(bf16[1,256,768]{2,1,0:T(8,128)(2,1)S(1)} %get-tuple-element.317), channel_id=1, source_target_pairs={{0,2},{1,3},{2,0},{3,1},{4,6},{5,7},{6,4},{7,5},{8,10},{9,11},{10,... | collective-permute-start | bytes 1179656 | tf_op jit(solution)/shard_map/ppermute | solution.py:165
  104.9 12.2 %copy-start.29 = (bf16[1,256,768]{2,1,0:T(8,128)(2,1)S(1)}, bf16[1,256,768]{2,1,0:T(8,128)(2,1)}, u32[]{:S(2)}) copy-start(bf16[1,256,768]{2,1,0:T(8,128)(2,1)} %copy-done.28) | copy-start | bytes 1179652
  105.2 11.9 %collective-permute-start.12 = (bf16[2,2,96,3072]{3,2,1,0:T(8,128)(2,1)S(1)}, bf16[2,2,96,3072]{3,2,1,0:T(8,128)(2,1)}, u32[]{:S(2)}, u32[]{:S(2)}) collective-permute-start(bf16[2,2,96,3072]{3,2,1,0:T(8,128)(2,1)S(1)} %pad_maximum_fusion.1), channel_id=1, source_target_pairs={{0,4},{4,0},{8,12},{12,8},{16,20},{20,16},{24,28},{28,24},{1,5},{5... | collective-permute-start | bytes 7077896 | tf_op jit(solution)/shard_map/ppermute | solution.py:189
  105.3 11.8 %collective-permute-start.13 = (bf16[1,256,768]{2,1,0:T(8,128)(2,1)}, bf16[1,256,768]{2,1,0:T(8,128)(2,1)}, u32[]{:S(2)}, u32[]{:S(2)}) collective-permute-start(bf16[1,256,768]{2,1,0:T(8,128)(2,1)} %get-tuple-element.316), channel_id=1, source_target_pairs={{0,3},{1,0},{2,1},{3,2},{4,7},{5,4},{6,5},{7,6},{8,11},{9,8},{10,9... | collective-permute-start | bytes 1179656 | tf_op jit(solution)/shard_map/ppermute | solution.py:165
  108.2 10.0 %copy-start.16 = (bf16[4,256,768]{2,1,0:T(8,128)(2,1)S(1)}, bf16[4,256,768]{2,1,0:T(8,128)(2,1)}, u32[]{:S(2)}) copy-start(bf16[4,256,768]{2,1,0:T(8,128)(2,1)} %param.37) | copy-start | bytes 4718596
  108.2 15.1 %copy-start.42 = (pred[768]{0:T(1024)(128)(4,1)S(1)}, pred[768]{0:T(1024)(128)(4,1)}, u32[]{:S(2)}) copy-start(pred[768]{0:T(1024)(128)(4,1)} %iota.60) | copy-start | bytes 2308
  118.2 12.4 %copy-start.11 = (bf16[1024,768]{1,0:T(8,128)(2,1)}, bf16[1024,768]{1,0:T(8,128)(2,1)S(1)}, u32[]{:S(2)}) copy-start(bf16[1024,768]{1,0:T(8,128)(2,1)S(1)} %maximum_bitcast_fusion) | copy-start | bytes 4718596
  119.3 36.8 %collective-permute-start.14 = (bf16[1,256,768]{2,1,0:T(8,128)(2,1)S(1)}, bf16[1,256,768]{2,1,0:T(8,128)(2,1)S(1)}, u32[]{:S(2)}, u32[]{:S(2)}) collective-permute-start(bf16[1,256,768]{2,1,0:T(8,128)(2,1)S(1)} %get-tuple-element.315), channel_id=1, source_target_pairs={{0,2},{1,3},{2,0},{3,1},{4,6},{5,7},{6,4},{7,5},{8,10},{9,11},{10,... | collective-permute-start | bytes 1179656 | tf_op jit(solution)/shard_map/ppermute | solution.py:165
  119.3 53.0 %collective-permute-start.15 = (bf16[1,256,768]{2,1,0:T(8,128)(2,1)}, bf16[1,256,768]{2,1,0:T(8,128)(2,1)}, u32[]{:S(2)}, u32[]{:S(2)}) collective-permute-start(bf16[1,256,768]{2,1,0:T(8,128)(2,1)} %get-tuple-element.314), channel_id=1, source_target_pairs={{0,1},{1,2},{2,3},{3,0},{4,5},{5,6},{6,7},{7,4},{8,9},{9,10},{10,1... | collective-permute-start | bytes 1179656 | tf_op jit(solution)/shard_map/ppermute | solution.py:165
  122.8 49.5 %collective-permute-start.16 = (bf16[1,256,768]{2,1,0:T(8,128)(2,1)}, bf16[1,256,768]{2,1,0:T(8,128)(2,1)}, u32[]{:S(2)}, u32[]{:S(2)}) collective-permute-start(bf16[1,256,768]{2,1,0:T(8,128)(2,1)} %get-tuple-element.313), channel_id=1, source_target_pairs={{0,3},{1,0},{2,1},{3,2},{4,7},{5,4},{6,5},{7,6},{8,11},{9,8},{10,9... | collective-permute-start | bytes 1179656 | tf_op jit(solution)/shard_map/ppermute | solution.py:165
  133.2 23.6 %copy-start.48 = (f32[768]{0:T(1024)S(1)}, f32[768]{0:T(1024)}, u32[]{:S(2)}) copy-start(f32[768]{0:T(1024)} %convert_element_type.266) | copy-start | bytes 9220
  161.1 11.2 %copy-start.37 = (f32[1024]{0:T(1024)}, f32[1024]{0:T(1024)S(1)}, u32[]{:S(2)}) copy-start(f32[1024]{0:T(1024)S(1)} %add_rsqrt_fusion.1) | copy-start | bytes 12292
  161.2 11.2 %copy-start.45 = (f32[768]{0:T(1024)S(1)}, f32[768]{0:T(1024)}, u32[]{:S(2)}) copy-start(f32[768]{0:T(1024)} %convert_element_type.268) | copy-start | bytes 9220
  161.2 11.2 %copy-start.47 = (f32[768]{0:T(1024)S(1)}, f32[768]{0:T(1024)}, u32[]{:S(2)}) copy-start(f32[768]{0:T(1024)} %convert_element_type.269) | copy-start | bytes 9220
  161.2 11.2 %copy-start.55 = (bf16[768,6144]{1,0:T(8,128)(2,1)S(1)}, bf16[768,6144]{1,0:T(8,128)(2,1)}, u32[]{:S(2)}) copy-start(bf16[768,6144]{1,0:T(8,128)(2,1)} %all-gather.5.cloned.1.call-done) | copy-start | bytes 28311556
  196.2 130.4 %all-gather.7.cloned.1.call-start = ((), (), s32[]{:S(2)}) async-start(), calls=%async_computation.3 | async-start | bytes 1622016 | tf_op jit(solution)/shard_map/all_gather | solution.py:452
  196.3 14.2 %copy-start.38 = (f32[1024]{0:T(1024)S(1)}, f32[1024]{0:T(1024)}, u32[]{:S(2)}) copy-start(f32[1024]{0:T(1024)} %copy-done.37) | copy-start | bytes 12292
  196.3 14.2 %copy-start.46 = (f32[768]{0:T(1024)S(1)}, f32[768]{0:T(1024)}, u32[]{:S(2)}) copy-start(f32[768]{0:T(1024)} %convert_element_type.268) | copy-start | bytes 9220
  217.5 22.0 %collective-permute-start.17 = (bf16[2,2,96,3072]{3,2,0,1:T(8,128)(2,1)S(1)}, bf16[2,2,96,3072]{3,2,0,1:T(8,128)(2,1)S(1)}, u32[]{:S(2)}, u32[]{:S(2)}) collective-permute-start(bf16[2,2,96,3072]{3,2,0,1:T(8,128)(2,1)S(1)} %bitcast.181), channel_id=1, source_target_pairs={{0,4},{4,0},{8,12},{12,8},{16,20},{20,16},{24,28},{28,24},{1,5},{5... | collective-permute-start | bytes 7077896 | tf_op jit(solution)/shard_map/ppermute | solution.py:189
  219.8 19.7 %collective-permute-start.18 = (bf16[1,256,768]{2,1,0:T(8,128)(2,1)S(1)}, bf16[1,256,768]{2,1,0:T(8,128)(2,1)S(1)}, u32[]{:S(2)}, u32[]{:S(2)}) collective-permute-start(bf16[1,256,768]{2,1,0:T(8,128)(2,1)S(1)} %get-tuple-element.311), channel_id=1, source_target_pairs={{0,2},{1,3},{2,0},{3,1},{4,6},{5,7},{6,4},{7,5},{8,10},{9,11},{10,... | collective-permute-start | bytes 1179656 | tf_op jit(solution)/shard_map/ppermute | solution.py:174
  232.7 10.4 %copy-start.1 = (f32[1024,768]{1,0:T(8,128)}, f32[1024,768]{1,0:T(8,128)S(1)}, u32[]{:S(2)}) copy-start(f32[1024,768]{1,0:T(8,128)S(1)} %get-tuple-element.294) | copy-start | bytes 9437188
  241.5 17.6 %collective-permute-start.20 = (bf16[2,96,1536]{2,1,0:T(8,128)(2,1)}, bf16[2,96,1536]{2,1,0:T(8,128)(2,1)}, u32[]{:S(2)}, u32[]{:S(2)}) collective-permute-start(bf16[2,96,1536]{2,1,0:T(8,128)(2,1)} %dynamic-slice_bitcast_fusion.3), channel_id=1, source_target_pairs={{0,8},{4,12},{8,0},{12,4},{16,24},{20,28},{24,16},{28,20},{1,9},{5... | collective-permute-start | bytes 1769480 | tf_op jit(solution)/shard_map/ppermute | solution.py:189
  242.6 16.5 %collective-permute-start.19 = (bf16[2,96,1536]{2,1,0:T(8,128)(2,1)}, bf16[2,96,1536]{2,1,0:T(8,128)(2,1)}, u32[]{:S(2)}, u32[]{:S(2)}) collective-permute-start(bf16[2,96,1536]{2,1,0:T(8,128)(2,1)} %dynamic-slice_bitcast_fusion.4), channel_id=1, source_target_pairs={{0,16},{4,20},{8,24},{12,28},{16,0},{20,4},{24,8},{28,12},{1,17},{... | collective-permute-start | bytes 1769480 | tf_op jit(solution)/shard_map/ppermute | solution.py:189
  254.9 27.7 %collective-permute-start.23 = (bf16[1,256,768]{2,1,0:T(8,128)(2,1)}, bf16[1,256,768]{2,1,0:T(8,128)(2,1)}, u32[]{:S(2)}, u32[]{:S(2)}) collective-permute-start(bf16[1,256,768]{2,1,0:T(8,128)(2,1)} %get-tuple-element.172), channel_id=1, source_target_pairs={{0,3},{1,0},{2,1},{3,2},{4,7},{5,4},{6,5},{7,6},{8,11},{9,8},{10,9... | collective-permute-start | bytes 1179656 | tf_op jit(solution)/shard_map/ppermute | solution.py:174
  256.3 26.2 %collective-permute-start.24 = (bf16[1,256,768]{2,1,0:T(8,128)(2,1)}, bf16[1,256,768]{2,1,0:T(8,128)(2,1)}, u32[]{:S(2)}, u32[]{:S(2)}) collective-permute-start(bf16[1,256,768]{2,1,0:T(8,128)(2,1)} %get-tuple-element.174), channel_id=1, source_target_pairs={{0,1},{1,2},{2,3},{3,0},{4,5},{5,6},{6,7},{7,4},{8,9},{9,10},{10,1... | collective-permute-start | bytes 1179656 | tf_op jit(solution)/shard_map/ppermute | solution.py:174
  261.5 20.8 %collective-permute-start.22 = (bf16[96,1536]{1,0:T(8,128)(2,1)S(1)}, bf16[96,1536]{1,0:T(8,128)(2,1)S(1)}, u32[]{:S(2)}, u32[]{:S(2)}) collective-permute-start(bf16[96,1536]{1,0:T(8,128)(2,1)S(1)} %dynamic-slice_bitcast_fusion.7), channel_id=1, source_target_pairs={{0,16},{4,20},{8,24},{12,28},{16,0},{20,4},{24,8},{28,12},{1,17},{... | collective-permute-start | bytes 884744 | tf_op jit(solution)/shard_map/ppermute | solution.py:189
  263.1 19.2 %collective-permute-start.21 = (bf16[96,1536]{1,0:T(8,128)(2,1)S(1)}, bf16[96,1536]{1,0:T(8,128)(2,1)S(1)}, u32[]{:S(2)}, u32[]{:S(2)}) collective-permute-start(bf16[96,1536]{1,0:T(8,128)(2,1)S(1)} %dynamic-slice_bitcast_fusion.8), channel_id=1, source_target_pairs={{0,8},{4,12},{8,0},{12,4},{16,24},{20,28},{24,16},{28,20},{1,9},{5... | collective-permute-start | bytes 884744 | tf_op jit(solution)/shard_map/ppermute | solution.py:189
  283.8 42.8 %collective-permute-start.27 = (bf16[96,1536]{1,0:T(8,128)(2,1)S(1)}, bf16[96,1536]{1,0:T(8,128)(2,1)S(1)}, u32[]{:S(2)}, u32[]{:S(2)}) collective-permute-start(bf16[96,1536]{1,0:T(8,128)(2,1)S(1)} %pad_maximum_fusion.9), channel_id=1, source_target_pairs={{0,1},{1,2},{2,3},{3,0},{4,5},{5,6},{6,7},{7,4},{8,9},{9,10},{10,1... | collective-permute-start | bytes 884744 | tf_op jit(solution)/shard_map/ppermute | solution.py:174
  286.1 40.6 %collective-permute-start.26 = (bf16[96,1536]{1,0:T(8,128)(2,1)}, bf16[96,1536]{1,0:T(8,128)(2,1)S(1)}, u32[]{:S(2)}, u32[]{:S(2)}) collective-permute-start(bf16[96,1536]{1,0:T(8,128)(2,1)} %pad_maximum_fusion.8), channel_id=1, source_target_pairs={{0,2},{1,3},{2,0},{3,1},{4,6},{5,7},{6,4},{7,5},{8,10},{9,11},{10,... | collective-permute-start | bytes 884744 | tf_op jit(solution)/shard_map/ppermute | solution.py:174
  289.2 37.5 %copy-start.12 = (bf16[1024,768]{1,0:T(8,128)(2,1)S(1)}, bf16[1024,768]{1,0:T(8,128)(2,1)}, u32[]{:S(2)}) copy-start(bf16[1024,768]{1,0:T(8,128)(2,1)} %copy-done.11) | copy-start | bytes 4718596
  289.3 37.4 %collective-permute-start.25 = (bf16[96,1536]{1,0:T(8,128)(2,1)}, bf16[96,1536]{1,0:T(8,128)(2,1)S(1)}, u32[]{:S(2)}, u32[]{:S(2)}) collective-permute-start(bf16[96,1536]{1,0:T(8,128)(2,1)} %pad_maximum_fusion.7), channel_id=1, source_target_pairs={{0,3},{1,0},{2,1},{3,2},{4,7},{5,4},{6,5},{7,6},{8,11},{9,8},{10,9... | collective-permute-start | bytes 884744 | tf_op jit(solution)/shard_map/ppermute | solution.py:174
  335.9 9.1 %slice-start.2 = ((s8[4718592]{0:T(1024)(128)(4,1)}), s8[524288]{0:T(1024)(128)(4,1)S(1)}, s32[]{:S(2)}) async-start(s8[4718592]{0:T(1024)(128)(4,1)} %bitcast.176), calls=%async_computation.6 | async-start | bytes 1048576
  337.4 11.6 %collective-permute-start.28 = (bf16[2,2,96,3072]{3,2,1,0:T(8,128)(2,1)}, bf16[2,2,96,3072]{3,2,1,0:T(8,128)(2,1)S(1)}, u32[]{:S(2)}, u32[]{:S(2)}) collective-permute-start(bf16[2,2,96,3072]{3,2,1,0:T(8,128)(2,1)} %dynamic-slice_bitcast_fusion), channel_id=1, source_target_pairs={{0,4},{4,0},{8,12},{12,8},{16,20},{20,16},{24,28},{28,24},{1,5},{5... | collective-permute-start | bytes 7077896 | tf_op jit(solution)/shard_map/ppermute | solution.py:189
  349.0 7.3 %collective-permute-start.36 = (f32[1536]{0:T(1024)S(1)}, f32[1536]{0:T(1024)S(1)}, u32[]{:S(2)}, u32[]{:S(2)}) collective-permute-start(f32[1536]{0:T(1024)S(1)} %pad_maximum_fusion.14), channel_id=1, source_target_pairs={{0,4},{4,0},{8,12},{12,8},{16,20},{20,16},{24,28},{28,24},{1,5},{5... | collective-permute-start | bytes 18440 | tf_op jit(solution)/shard_map/ppermute | solution.py:189
  350.5 39.6 %collective-permute-start.30 = (bf16[2,96,1536]{2,1,0:T(8,128)(2,1)S(1)}, bf16[2,96,1536]{2,1,0:T(8,128)(2,1)S(1)}, u32[]{:S(2)}, u32[]{:S(2)}) collective-permute-start(bf16[2,96,1536]{2,1,0:T(8,128)(2,1)S(1)} %dynamic-slice_bitcast_fusion.1), channel_id=1, source_target_pairs={{0,8},{4,12},{8,0},{12,4},{16,24},{20,28},{24,16},{28,20},{1,9},{5... | collective-permute-start | bytes 1769480 | tf_op jit(solution)/shard_map/ppermute | solution.py:189
  352.1 38.0 %collective-permute-start.29 = (bf16[2,96,1536]{2,1,0:T(8,128)(2,1)S(1)}, bf16[2,96,1536]{2,1,0:T(8,128)(2,1)S(1)}, u32[]{:S(2)}, u32[]{:S(2)}) collective-permute-start(bf16[2,96,1536]{2,1,0:T(8,128)(2,1)S(1)} %dynamic-slice_bitcast_fusion.2), channel_id=1, source_target_pairs={{0,16},{4,20},{8,24},{12,28},{16,0},{20,4},{24,8},{28,12},{1,17},{... | collective-permute-start | bytes 1769480 | tf_op jit(solution)/shard_map/ppermute | solution.py:189
  353.6 11.8 %collective-permute-start.31 = (bf16[1,256,768]{2,1,0:T(8,128)(2,1)S(1)}, bf16[1,256,768]{2,1,0:T(8,128)(2,1)S(1)}, u32[]{:S(2)}, u32[]{:S(2)}) collective-permute-start(bf16[1,256,768]{2,1,0:T(8,128)(2,1)S(1)} %get-tuple-element.306), channel_id=1, source_target_pairs={{0,3},{1,0},{2,1},{3,2},{4,7},{5,4},{6,5},{7,6},{8,11},{9,8},{10,9... | collective-permute-start | bytes 1179656 | tf_op jit(solution)/shard_map/ppermute | solution.py:174
  355.9 34.2 %collective-permute-start.32 = (bf16[1,256,768]{2,1,0:T(8,128)(2,1)S(1)}, bf16[1,256,768]{2,1,0:T(8,128)(2,1)S(1)}, u32[]{:S(2)}, u32[]{:S(2)}) collective-permute-start(bf16[1,256,768]{2,1,0:T(8,128)(2,1)S(1)} %get-tuple-element.305), channel_id=1, source_target_pairs={{0,2},{1,3},{2,0},{3,1},{4,6},{5,7},{6,4},{7,5},{8,10},{9,11},{10,... | collective-permute-start | bytes 1179656 | tf_op jit(solution)/shard_map/ppermute | solution.py:174
  356.3 37.8 %copy-start.13 = (f32[32,12,768]{2,1,0:T(8,128)S(1)}, f32[32,12,768]{2,1,0:T(8,128)}, u32[]{:S(2)}) copy-start(f32[32,12,768]{2,1,0:T(8,128)} %all-gather.7.cloned.1.call-done) | copy-start | bytes 3538948
  356.3 43.1 %collective-permute-start.35 = (bf16[1,256,768]{2,1,0:T(8,128)(2,1)}, bf16[1,256,768]{2,1,0:T(8,128)(2,1)S(1)}, u32[]{:S(2)}, u32[]{:S(2)}) collective-permute-start(bf16[1,256,768]{2,1,0:T(8,128)(2,1)} %get-tuple-element.304), channel_id=1, source_target_pairs={{0,1},{1,2},{2,3},{3,0},{4,5},{5,6},{6,7},{7,4},{8,9},{9,10},{10,1... | collective-permute-start | bytes 1179656 | tf_op jit(solution)/shard_map/ppermute | solution.py:174
  365.5 26.5 %copy-start.24 = (bf16[1,256,768]{2,1,0:T(8,128)(2,1)}, bf16[1,256,768]{2,1,0:T(8,128)(2,1)S(1)}, u32[]{:S(2)}) copy-start(bf16[1,256,768]{2,1,0:T(8,128)(2,1)S(1)} %collective-permute-done.31) | copy-start | bytes 1179652
  365.5 29.4 %collective-permute-start.37 = (f32[1536]{0:T(1024)S(1)}, f32[1536]{0:T(1024)S(1)}, u32[]{:S(2)}, u32[]{:S(2)}) collective-permute-start(f32[1536]{0:T(1024)S(1)} %add.410), channel_id=1, source_target_pairs={{0,8},{4,12},{8,0},{12,4},{16,24},{20,28},{24,16},{28,20},{1,9},{5... | collective-permute-start | bytes 18440 | tf_op jit(solution)/shard_map/ppermute | solution.py:189
  391.1 8.4 %collective-permute-start.34 = (bf16[96,1536]{1,0:T(8,128)(2,1)}, bf16[96,1536]{1,0:T(8,128)(2,1)}, u32[]{:S(2)}, u32[]{:S(2)}) collective-permute-start(bf16[96,1536]{1,0:T(8,128)(2,1)} %dynamic-slice_bitcast_fusion.5), channel_id=1, source_target_pairs={{0,16},{4,20},{8,24},{12,28},{16,0},{20,4},{24,8},{28,12},{1,17},{... | collective-permute-start | bytes 884744 | tf_op jit(solution)/shard_map/ppermute | solution.py:189
  392.8 7.8 %collective-permute-start.33 = (bf16[96,1536]{1,0:T(8,128)(2,1)}, bf16[96,1536]{1,0:T(8,128)(2,1)}, u32[]{:S(2)}, u32[]{:S(2)}) collective-permute-start(bf16[96,1536]{1,0:T(8,128)(2,1)} %dynamic-slice_bitcast_fusion.6), channel_id=1, source_target_pairs={{0,8},{4,12},{8,0},{12,4},{16,24},{20,28},{24,16},{28,20},{1,9},{5... | collective-permute-start | bytes 884744 | tf_op jit(solution)/shard_map/ppermute | solution.py:189
  394.9 4.6 %collective-permute-start.38 = (f32[1536]{0:T(1024)S(1)}, f32[1536]{0:T(1024)S(1)}, u32[]{:S(2)}, u32[]{:S(2)}) collective-permute-start(f32[1536]{0:T(1024)S(1)} %add.411), channel_id=1, source_target_pairs={{0,16},{4,20},{8,24},{12,28},{16,0},{20,4},{24,8},{28,12},{1,17},{... | collective-permute-start | bytes 18440 | tf_op jit(solution)/shard_map/ppermute | solution.py:189
  403.3 6.5 %collective-permute-start.39 = (bf16[97,768]{1,0:T(8,128)(2,1)S(1)}, bf16[97,768]{1,0:T(8,128)(2,1)S(1)}, u32[]{:S(2)}, u32[]{:S(2)}) collective-permute-start(bf16[97,768]{1,0:T(8,128)(2,1)S(1)} %pad_maximum_fusion.10), channel_id=1, source_target_pairs={{0,3},{1,0},{2,1},{3,2},{4,7},{5,4},{6,5},{7,6},{8,11},{9,8},{10,9... | collective-permute-start | bytes 446984 | tf_op jit(solution)/shard_map/ppermute | solution.py:174
  403.5 12.9 %collective-permute-start.40 = (bf16[97,768]{1,0:T(8,128)(2,1)S(1)}, bf16[97,768]{1,0:T(8,128)(2,1)S(1)}, u32[]{:S(2)}, u32[]{:S(2)}) collective-permute-start(bf16[97,768]{1,0:T(8,128)(2,1)S(1)} %pad_maximum_fusion.11), channel_id=1, source_target_pairs={{0,2},{1,3},{2,0},{3,1},{4,6},{5,7},{6,4},{7,5},{8,10},{9,11},{10,... | collective-permute-start | bytes 446984 | tf_op jit(solution)/shard_map/ppermute | solution.py:174
  403.7 12.8 %collective-permute-start.41 = (bf16[97,768]{1,0:T(8,128)(2,1)S(1)}, bf16[97,768]{1,0:T(8,128)(2,1)S(1)}, u32[]{:S(2)}, u32[]{:S(2)}) collective-permute-start(bf16[97,768]{1,0:T(8,128)(2,1)S(1)} %pad_maximum_fusion.12), channel_id=1, source_target_pairs={{0,1},{1,2},{2,3},{3,0},{4,5},{5,6},{6,7},{7,4},{8,9},{9,10},{10,1... | collective-permute-start | bytes 446984 | tf_op jit(solution)/shard_map/ppermute | solution.py:174
  (44 other events, 156.1 us)
Sparse Core Ops, SparseCore 0:
  60.5 72.7 all-gather.4
  196.4 53.9 reduce-scatter.1
  253.8 72.8 all-gather.6

commit v9 on v8

--- a/solution.py
+++ b/solution.py
@@ -328,14 +328,15 @@
             first += cols
         return jnp.concatenate(pieces, axis=1)
 
-    def own_columns(share, widths):
+    def own_columns(share, widths, shared=None):
         parts = []
         for step in range(tp):
             pieces, first = [], 0
             for cols in widths:
                 pieces.append(share[:, first + step * cols : first + (step + 1) * cols])
                 first += tp * cols
-            parts.append(jnp.concatenate(pieces, axis=1))
+            part = jnp.concatenate(pieces, axis=1)
+            parts.append(part if shared is None else jnp.concatenate([part, shared], axis=0))
         return sent_back(parts)
 
     def summed(parts, widths):
@@ -446,15 +447,10 @@
         second_gain_grad,
         second_shift_grad,
         *jnp.split(by_rank(inner_bias_grad), inner_bias_grad.shape[0] // width),
-        jnp.zeros((width,), WIDE),
-        jnp.zeros((width,), WIDE),
     ]
-    vectors = lax.all_gather(
-        jnp.stack(lax.optimization_barrier(vectors)), ("tp", "fsdp"), axis=0
-    )
     inner_share, _ = scatter_near(inner_share)
-    grad_context, inner_share, output_grad = lax.optimization_barrier(
-        (grad_context, inner_share, output_grad)
+    grad_context, inner_share, output_grad, vectors = lax.optimization_barrier(
+        (grad_context, inner_share, output_grad, vectors)
     )
     inner_share, _ = scatter_far(inner_share)
     back = functools.partial(
@@ -468,10 +464,7 @@
     layer_out = own_places(layer_out)
     units = (unit_cols, unit_cols)
     unit_parts = own_columns(jnp.concatenate([inner_share, outer_share], axis=1), units)
-    rows_grads, unit_parts, vectors = lax.optimization_barrier(
-        (back(halfway, 1), unit_parts, vectors)
-    )
-    totals = jnp.sum(vectors, axis=0).reshape(-1)[: -2 * width]
+    rows_grads, unit_parts = lax.optimization_barrier((back(halfway, 1), unit_parts))
     inner_share, outer_share = summed(unit_parts, units)
     query_rows_grad, key_rows_grad, value_rows_grad = (
         array.reshape(count * length, width) for array in rows_grads
@@ -487,7 +480,7 @@
         + dot(value_rows_grad, value_full, BY_LAST)
     ).astype(LOW)
     late = [jnp.sum(query_rows_grad.astype(WIDE), axis=0), value_bias_grad]
-    late = jnp.concatenate(late)
+    late = jnp.stack(late + vectors)
     heads_share, (tokens_grad, late) = scatter_core(
         jnp.concatenate(head_grads + [output_grad], axis=1), (tokens_grad, late)
     )
@@ -497,10 +490,18 @@
     heads_share, tokens_grad[3:] = scatter_far(heads_share, tokens_grad[3:])
     heads_share, late = lax.optimization_barrier((heads_share, late))
     high = late.astype(LOW)
-    late = jnp.stack([high, (late - high.astype(WIDE)).astype(LOW)]).reshape(2, 2, width)
-    late = late.transpose(1, 0, 2).reshape(1, 4 * width)
-    heads_share = own_columns(jnp.concatenate([heads_share, late], axis=0), (head_cols,) * 4)
-    heads_share = summed(heads_share, (head_cols,) * 4)
+    lower = (late - high.astype(WIDE)).astype(LOW)
+    heads_parts = own_columns(
+        jnp.concatenate(
+            [heads_share, jnp.stack([high[0], lower[0], high[1], lower[1]]).reshape(1, -1)], axis=0
+        ),
+        (head_cols,) * 4,
+        jnp.concatenate([high[2:], lower[2:]], axis=0),
+    )
+    totals = by_source([part[shard_rows + 1 :] for part in heads_parts]).astype(WIDE)
+    totals = totals[:, : len(vectors)] + totals[:, len(vectors) :]
+    totals = jnp.sum(totals, axis=0).reshape(-1)
+    heads_share = summed([part[: shard_rows + 1] for part in heads_parts], (head_cols,) * 4)
     query_bias_total = heads_share[0][shard_rows] + heads_share[1][shard_rows]
     value_bias_total = heads_share[2][shard_rows] + heads_share[3][shard_rows]
     query_share, key_share, value_share, output_share = (

time: 431 us -> 420 us (0.974)
  waiting for transfers between devices: 113 us -> 100 us
    all_gather x1 -> x0, waiting for transfers between devices: 17.2 us -> none  [on_device(): lax.all_gather(jnp.stack(lax.optimization_barrier(vectors)), ('tp', 'fsdp...]
    ppermute x18, waiting for transfers between devices: 8.6 us -> 14.3 us  [flip(): return lax.ppermute(block, axis, [(i, i ^ bit) for i in range(members)])]
    unnamed x147 -> x134, local copies, waits for them, and re-layouts: 13.3 us -> 12.7 us
  transfers between devices with their start and end apart: 45 -> 44, of which waited for: 15 -> 17; matrix products, arithmetic and copies ran while one was open for 29% -> 29% of each run, Pallas kernels for 14% -> 15%
where the time goes in v9:
time: 420 us; the launch traced here: 414 us
  waiting for transfers between devices  100 us (24%)
  matrix products  86.7 us (21%)
  starting transfers between devices  62.8 us (15%)
  Pallas kernels  60.2 us (14%)
  other arithmetic  46.2 us (11%)
  local copies, waits for them, and re-layouts  41.6 us (10%)
  between operations  15.9 us (4%)
    dot_general x18, matrix products, dot(): return lax.dot_general(left, right, dims, preferred_element_type=WIDE)  86.7 us
    ppermute x12, waiting for transfers between devices, sent_back(): moved[step] = lax.ppermute(parts[step], 'tp', pairs)  43.8 us
    pallas_call x2, Pallas kernels, attend_back(): pl.pallas_call(body, grid=(count, pairs - first if part else pairs // 2),...  37.3 us
    ppermute x6, waiting for transfers between devices, dealt(): parts.append(lax.ppermute(block, 'tp', pairs) if step else block)  33.3 us
    pallas_call x1, Pallas kernels, attend(): pl.pallas_call(functools.partial(attend_kernel, scaling=scaling), grid=(c...  22.8 us
    ppermute x12, starting transfers between devices, sent_back(): moved[step] = lax.ppermute(parts[step], 'tp', pairs)  17.8 us
    ppermute x18, starting transfers between devices, flip(): return lax.ppermute(block, axis, [(i, i ^ bit) for i in range(members)])  16.4 us
    ppermute x18, waiting for transfers between devices, flip(): return lax.ppermute(block, axis, [(i, i ^ bit) for i in range(members)])  14.3 us
  transfers between devices with their start and end apart: 44, of which 17 were waited for; matrix products, arithmetic and copies ran while one was open for 29% of the time, Pallas kernels for 15%

profile of v9, /device:TPU:0, one launch (start us, length us, event | category | flops | bytes accessed | tf_op | source)
XLA Modules:
  0.0 413.8 jit_solution(1850118665676435992)
XLA Ops:
  7.2 2.1 concatenate.97
  13.2 3.1 collective-permute-start
  16.3 2.6 collective-permute-start.1
  29.2 2.6 collective-permute-done.1
  32.7 4.7 %collective-permute-start.5 = (bf16[96,1536]{1,0:T(8,128)(2,1)S(1)}, bf16[96,1536]{1,0:T(8,128)(2,1)S(1)}, u32[]{:S(2)}, u32[]{:S(2)}) collective-permute-start(bf16[96,1536]{1,0:T(8,128)(2,1)S(1)} %pad_maximum_fusion.11), channel_id=1, source_target_pairs={{0,1},{1,2},{2,3},{3,0},{4,5},{5,6},{6,7},{7,4},{8,9},{9,10},{10,1... | collective-permute-start | bytes 884744 | tf_op jit(solution)/shard_map/ppermute | solution.py:156
  37.4 1.6 collective-permute-start.6
  40.1 1.5 collective-permute-start.3
  41.6 1.5 collective-permute-start.4
  46.5 4.1 collective-permute-done.3
  51.8 5.6 %collective-permute-done.6 = bf16[96,1536]{1,0:T(8,128)(2,1)S(1)} collective-permute-done((bf16[96,1536]{1,0:T(8,128)(2,1)S(1)}, bf16[96,1536]{1,0:T(8,128)(2,1)S(1)}, u32[]{:S(2)}, u32[]{:S(2)}) %collective-permute-start.6) | collective-permute-done | bytes 294944 | tf_op jit(solution)/shard_map/ppermute | solution.py:156
  63.2 1.6 collective-permute-start.9
  66.1 1.6 collective-permute-start.8
  68.5 6.9 %collective-permute-start.10 = (bf16[1,256,768]{2,1,0:T(8,128)(2,1)S(1)}, bf16[1,256,768]{2,1,0:T(8,128)(2,1)S(1)}, u32[]{:S(2)}, u32[]{:S(2)}) collective-permute-start(bf16[1,256,768]{2,1,0:T(8,128)(2,1)S(1)} %get-tuple-element.329), channel_id=1, source_target_pairs={{0,1},{1,2},{2,3},{3,0},{4,5},{5,6},{6,7},{7,4},{8,9},{9,10},{10,1... | collective-permute-start | bytes 1179656 | tf_op jit(solution)/shard_map/ppermute | solution.py:165
  75.4 2.2 collective-permute-start.11
  77.6 9.5 %collective-permute-done.10 = bf16[1,256,768]{2,1,0:T(8,128)(2,1)S(1)} collective-permute-done((bf16[1,256,768]{2,1,0:T(8,128)(2,1)S(1)}, bf16[1,256,768]{2,1,0:T(8,128)(2,1)S(1)}, u32[]{:S(2)}, u32[]{:S(2)}) %collective-permute-start.10) | collective-permute-done | bytes 393248 | tf_op jit(solution)/shard_map/ppermute | solution.py:165
  87.1 14.9 %collective-permute-done.11 = bf16[1,256,768]{2,1,0:T(8,128)(2,1)S(1)} collective-permute-done((bf16[1,256,768]{2,1,0:T(8,128)(2,1)S(1)}, bf16[1,256,768]{2,1,0:T(8,128)(2,1)S(1)}, u32[]{:S(2)}, u32[]{:S(2)}) %collective-permute-start.11) | collective-permute-done | bytes 393248 | tf_op jit(solution)/shard_map/ppermute | solution.py:165
  108.2 8.9 %collective-permute-done.13 = bf16[1,256,768]{2,1,0:T(8,128)(2,1)} collective-permute-done((bf16[1,256,768]{2,1,0:T(8,128)(2,1)}, bf16[1,256,768]{2,1,0:T(8,128)(2,1)}, u32[]{:S(2)}, u32[]{:S(2)}) %collective-permute-start.13) | collective-permute-done | bytes 393248 | tf_op jit(solution)/shard_map/ppermute | solution.py:165
  119.3 3.5 collective-permute-start.15
  123.3 2.2 bitcast_select_fusion
  125.5 2.6 fusion.63.k_ref.refs_1_
  128.1 2.5 fusion.35.v_ref.refs_2_
  130.7 2.5 fusion.34.q_ref.refs_0_
  133.2 22.8 %attend.1 = (bf16[1,1024,768]{2,1,0:T(8,128)(2,1)}, f32[1,6,2,1024]{3,2,1,0:T(2,128)}) custom-call(bf16[1,1024,768]{2,1,0:T(8,128)(2,1)} %fusion.34.q_ref.refs_0_, bf16[1,1024,768]{2,1,0:T(8,128)(2,1)} %fusion.63.k_ref.refs_1_, bf16[1,1024,768]{2,1,0:T(8,128)(2,1)} %fusion.35.v_ref.refs_2_, s32[1,1,1024]{2,1,0:T(1,128)} %broadcast_in_dim_reshape.6.row_ref.refs_6_, ...), custom_call_target="tpu_custom_call" | custom-call | flops 22548578304 | bytes 6291456 | tf_op jit(solution)/shard_map/attend/pallas_call | solution.py:93
  156.8 3.8 fusion.121
  161.2 11.2 %multiply_convert_fusion = (bf16[1024,3072]{1,0:T(8,128)(2,1)S(1)}, f32[1024,3072]{1,0:T(8,128)}) fusion(f32[3072]{0:T(1024)} %pad_maximum_fusion.17, bf16[768,6144]{1,0:T(8,128)(2,1)} %all-gather.2.cloned.1.call-done, f32[1024,768]{1,0:T(8,128)S(1)} %get-tuple-element.397, f32[768]{0:T(1024)} %convert_element_type.271, f32[768]{0:T(1024)S(1)} %convert_element_type.270, ...), kind=kOutput, calls=%fused_computation.8 | convolution fusion | flops 4854644736 | bytes 26766336 | tf_op jit(solution)/shard_map/dot_general | solution.py:22
  172.5 5.4 %fusion.109 = (f32[1024]{0:T(1024)S(1)}, f32[1024,768]{1,0:T(8,128)S(1)}) fusion(f32[768]{0:T(1024)S(1)} %copy-done.43, f32[768]{0:T(1024)S(1)} %copy-done.41, f32[768]{0:T(1024)S(1)} %convert_element_type.270, f32[1024]{0:T(1024)S(1)} %add_rsqrt_fusion.1, f32[1024,768]{1,0:T(8,128)S(1)} %get-tuple-element.397, f32[1024]{0:T(1024)S(1)} %broadcast_multiply_fusion.5, ...), kind=kOutput, calls=%fused_computation.262 | convolution fusion | flops 4837342208 | bytes 17326080 | tf_op jit(solution)/shard_map/dot_general | solution.py:22
  178.9 5.3 %fusion.29 = (f32[768]{0:T(1024)}, f32[1024]{0:T(1024)S(1)}, f32[1024]{0:T(1024)S(1)}, bf16[1024,768]{1,0:T(8,128)(2,1)}) fusion(f32[1024,768]{1,0:T(8,128)S(1)} %get-tuple-element.307, f32[1024]{0:T(1024)S(1)} %add_rsqrt_fusion, f32[1024]{0:T(1024)S(1)} %broadcast_multiply_fusion.4, bf16[1,256,768]{2,1,0:T(8,128)(2,1)} %collective-permute-done.16, ...), kind=kLoop, calls=%fused_computation.44 | loop fusion | flops 14939392 | bytes 6317056 | tf_op jit(solution)/shard_map/reduce_sum | solution.py:277
  184.2 3.5 fusion.106
  187.7 1.7 copy-done.8
  189.4 6.9 %convolution_convert_fusion = bf16[768,3072]{1,0:T(8,128)(2,1)} fusion(bf16[1024,3072]{1,0:T(8,128)(2,1)S(1)} %get-tuple-element.147, f32[1024,768]{1,0:T(8,128)S(1)} %get-tuple-element.303), kind=kOutput, calls=%fused_computation.13 | convolution fusion | flops 4834983936 | bytes 14155776 | tf_op jit(solution)/shard_map/dot_general | solution.py:22
  196.4 13.6 %convert_reduce_fusion = (f32[3072]{0:T(1024)}, bf16[1024,3072]{1,0:T(8,128)(2,1)S(1)}) fusion(f32[1024,3072]{1,0:T(8,128)} %get-tuple-element.399, f32[3072]{0:T(1024)} %pad_maximum_fusion.17, bf16[768,6144]{1,0:T(8,128)(2,1)} %all-gather.2.cloned.1.call-done, f32[1024,768]{1,0:T(8,128)} %copy-done.8), kind=kOutput, calls=%fused_computation.7 | convolution fusion | flops 4873516032 | bytes 26763264 | tf_op jit(solution)/shard_map/dot_general | solution.py:22
  209.9 6.8 %convolution_convert_fusion.1 = bf16[768,3072]{1,0:T(8,128)(2,1)S(1)} fusion(bf16[1024,3072]{1,0:T(8,128)(2,1)S(1)} %get-tuple-element.402, f32[1024,768]{1,0:T(8,128)S(1)} %get-tuple-element.397, f32[768]{0:T(1024)S(1)} %copy-done.42, f32[768]{0:T(1024)S(1)} %convert_element_type.270, f32[1024]{0:T(1024)S(1)} %copy-done.34, ...), kind=kOutput, calls=%fused_computation.14 | convolution fusion | flops 4838129664 | bytes 14170112 | tf_op jit(solution)/shard_map/dot_general | solution.py:22
  219.7 1.5 collective-permute-start.18
  221.2 10.3 %multiply_reduce_fusion = (f32[768]{0:T(1024)}, f32[1024]{0:T(1024)S(1)}, f32[1024]{0:T(1024)S(1)}, f32[768]{0:T(1024)}, f32[1024,768]{1,0:T(8,128)S(1)}) fusion(f32[1024,768]{1,0:T(8,128)S(1)} %get-tuple-element.397, f32[1024]{0:T(1024)S(1)} %copy-done.34, f32[1024]{0:T(1024)S(1)} %broadcast_multiply_fusion.5, f32[768]{0:T(1024)S(1)} %convert_element_type.270, ...), kind=kOutput, calls=%fused_computation.48 | convolution fusion | flops 4839698432 | bytes 20472832 | tf_op jit(solution)/shard_map/dot_general | solution.py:22
  232.6 6.8 %collective-permute-done.18 = bf16[1,256,768]{2,1,0:T(8,128)(2,1)S(1)} collective-permute-done((bf16[1,256,768]{2,1,0:T(8,128)(2,1)S(1)}, bf16[1,256,768]{2,1,0:T(8,128)(2,1)S(1)}, u32[]{:S(2)}, u32[]{:S(2)}) %collective-permute-start.18) | collective-permute-done | bytes 393248 | tf_op jit(solution)/shard_map/ppermute | solution.py:174
  243.2 4.0 fusion.64.g_ref.refs_3_
  247.2 1.4 convert_reduce_fusion.1
  248.7 4.9 %fusion.51 = bf16[768,768]{1,0:T(8,128)(2,1)} fusion(bf16[1,1024,768]{2,1,0:T(8,128)(2,1)} %get-tuple-element.138.c_ref.refs_4_, f32[1024,768]{1,0:T(8,128)} %copy-done.1), kind=kOutput, calls=%fused_computation.89 | convolution fusion | flops 1209335808 | bytes 5898240 | tf_op jit(solution)/shard_map/dot_general | solution.py:22
  255.6 3.6 collective-permute-done.20
  261.7 1.5 collective-permute-start.22
  263.9 18.7 %attend_back.2 = (bf16[1,1024,768]{2,1,0:T(8,128)(2,1)}, bf16[1,1024,768]{2,1,0:T(8,128)(2,1)}, bf16[1,1024,768]{2,1,0:T(8,128)(2,1)}) custom-call(bf16[1,1024,768]{2,1,0:T(8,128)(2,1)} %fusion.34.q_ref.refs_0_, bf16[1,1024,768]{2,1,0:T(8,128)(2,1)} %fusion.63.k_ref.refs_1_, bf16[1,1024,768]{2,1,0:T(8,128)(2,1)} %fusion.35.v_ref.refs_2_, ...), custom_call_target="tpu_custom_call" | custom-call | flops 19327352832 | bytes 5505024 | tf_op jit(solution)/shard_map/attend_back/pallas_call | solution.py:128
  284.1 1.5 collective-permute-start.27
  286.4 2.4 collective-permute-start.26
  289.5 1.4 collective-permute-start.25
  290.9 18.6 %attend_back.3 = (bf16[1,1024,768]{2,1,0:T(8,128)(2,1)}, bf16[1,1024,768]{2,1,0:T(8,128)(2,1)}, bf16[1,1024,768]{2,1,0:T(8,128)(2,1)}) custom-call(bf16[1,1024,768]{2,1,0:T(8,128)(2,1)} %fusion.34.q_ref.refs_0_, bf16[1,1024,768]{2,1,0:T(8,128)(2,1)} %fusion.63.k_ref.refs_1_, ...), custom_call_target="tpu_custom_call", output_to_operand_aliasing={{0}: (8, {}), {1}: (9, {}), {2}: (10, {})} | custom-call | flops 19327352832 | bytes 5505024 | tf_op jit(solution)/shard_map/attend_back/pallas_call | solution.py:128
  309.7 3.1 fusion.54
  312.8 1.5 fusion.57
  314.3 1.5 fusion.60
  316.7 1.6 dynamic-slice_bitcast_fusion
  322.8 1.5 stack.54
  324.3 3.3 fusion.44
  327.8 1.4 fusion.40
  330.2 1.5 add_convert_fusion
  335.1 1.5 collective-permute-start.29
  337.6 4.5 %collective-permute-start.31 = (bf16[1,256,768]{2,1,0:T(8,128)(2,1)}, bf16[1,256,768]{2,1,0:T(8,128)(2,1)}, u32[]{:S(2)}, u32[]{:S(2)}) collective-permute-start(bf16[1,256,768]{2,1,0:T(8,128)(2,1)} %get-tuple-element.317), channel_id=1, source_target_pairs={{0,3},{1,0},{2,1},{3,2},{4,7},{5,4},{6,5},{7,6},{8,11},{9,8},{10,9... | collective-permute-start | bytes 1179656 | tf_op jit(solution)/shard_map/ppermute | solution.py:174
  344.0 8.1 %collective-permute-done.31 = bf16[1,256,768]{2,1,0:T(8,128)(2,1)} collective-permute-done((bf16[1,256,768]{2,1,0:T(8,128)(2,1)}, bf16[1,256,768]{2,1,0:T(8,128)(2,1)}, u32[]{:S(2)}, u32[]{:S(2)}) %collective-permute-start.31) | collective-permute-done | bytes 393248 | tf_op jit(solution)/shard_map/ppermute | solution.py:174
  352.0 1.4 collective-permute-start.37
  353.4 23.3 %collective-permute-done.32 = bf16[1,256,768]{2,1,0:T(8,128)(2,1)} collective-permute-done((bf16[1,256,768]{2,1,0:T(8,128)(2,1)}, bf16[1,256,768]{2,1,0:T(8,128)(2,1)}, u32[]{:S(2)}, u32[]{:S(2)}) %collective-permute-start.32) | collective-permute-done | bytes 393248 | tf_op jit(solution)/shard_map/ppermute | solution.py:174
  378.0 1.5 collective-permute-start.34
  381.5 1.5 collective-permute-start.38
  383.8 2.8 collective-permute-done.38
  389.0 3.7 collective-permute-start.39
  392.7 4.4 %fusion.36 = (f32[4,256,768]{2,1,0:T(8,128)}, bf16[4,256,768]{2,1,0:T(8,128)(2,1)}) fusion(s32[4]{0:T(128)S(1)} %get-tuple-element.407, s32[4]{0:T(128)S(1)} %get-tuple-element.408, pred[4]{0:T(512)(128)(4,1)S(1)} %compare_and_fusion, bf16[256,768]{1,0:T(8,128)(2,1)S(1)} %bitcast.183, bf16[256,768]{1,0:T(8,128)(2,1)} %bitcast.50, ...), kind=kLoop, calls=%fused_computation.72 | loop fusion | flops 8650752 | bytes 7864356 | tf_op jit(solution)/shard_map/convert_element_type | solution.py:510
  398.3 4.5 %collective-permute-done.40 = bf16[117,768]{1,0:T(8,128)(2,1)S(1)} collective-permute-done((bf16[117,768]{1,0:T(8,128)(2,1)S(1)}, bf16[117,768]{1,0:T(8,128)(2,1)S(1)}, u32[]{:S(2)}, u32[]{:S(2)}) %collective-permute-start.40) | collective-permute-done | bytes 179744 | tf_op jit(solution)/shard_map/ppermute | solution.py:174
  (338 shorter events, 79.5 us)
Async XLA Ops:
  7.2 32.8 %copy-start.32 = (bf16[192,96]{1,0:T(8,128)(2,1)S(1)}, bf16[192,96]{1,0:T(8,128)(2,1)}, u32[]{:S(2)}) copy-start(bf16[192,96]{1,0:T(8,128)(2,1)} %param.27) | copy-start | bytes 110596
  7.2 153.9 %all-gather.2.cloned.1.call-start = ((), (), s32[]{:S(2)}) async-start(), calls=%async_computation.1 | async-start | bytes 10616832 | tf_op jit(solution)/shard_map/all_gather | solution.py:392
  13.2 16.0 %collective-permute-start = (bf16[99,768]{0,1:T(8,128)(2,1)S(1)}, bf16[99,768]{0,1:T(8,128)(2,1)S(1)}, u32[]{:S(2)}, u32[]{:S(2)}) collective-permute-start(bf16[99,768]{0,1:T(8,128)(2,1)S(1)} %fusion.95), channel_id=1, source_target_pairs={{0,1},{1,2},{2,3},{3,0},{4,5},{5,6},{6,7},{7,4},{8,9},{9,10},{10,1... | collective-permute-start | bytes 456200 | tf_op jit(solution)/shard_map/ppermute | solution.py:156
  16.3 15.5 %collective-permute-start.1 = (bf16[99,768]{0,1:T(8,128)(2,1)S(1)}, bf16[99,768]{0,1:T(8,128)(2,1)S(1)}, u32[]{:S(2)}, u32[]{:S(2)}) collective-permute-start(bf16[99,768]{0,1:T(8,128)(2,1)S(1)} %fusion.95), channel_id=1, source_target_pairs={{0,2},{1,3},{2,0},{3,1},{4,6},{5,7},{6,4},{7,5},{8,10},{9,11},{10,... | collective-permute-start | bytes 456200 | tf_op jit(solution)/shard_map/ppermute | solution.py:156
  18.9 12.9 %collective-permute-start.2 = (bf16[99,768]{0,1:T(8,128)(2,1)S(1)}, bf16[99,768]{0,1:T(8,128)(2,1)S(1)}, u32[]{:S(2)}, u32[]{:S(2)}) collective-permute-start(bf16[99,768]{0,1:T(8,128)(2,1)S(1)} %fusion.95), channel_id=1, source_target_pairs={{0,3},{1,0},{2,1},{3,2},{4,7},{5,4},{6,5},{7,6},{8,11},{9,8},{10,9... | collective-permute-start | bytes 456200 | tf_op jit(solution)/shard_map/ppermute | solution.py:156
  32.7 13.8 %collective-permute-start.5 = (bf16[96,1536]{1,0:T(8,128)(2,1)S(1)}, bf16[96,1536]{1,0:T(8,128)(2,1)S(1)}, u32[]{:S(2)}, u32[]{:S(2)}) collective-permute-start(bf16[96,1536]{1,0:T(8,128)(2,1)S(1)} %pad_maximum_fusion.11), channel_id=1, source_target_pairs={{0,1},{1,2},{2,3},{3,0},{4,5},{5,6},{6,7},{7,4},{8,9},{9,10},{10,1... | collective-permute-start | bytes 884744 | tf_op jit(solution)/shard_map/ppermute | solution.py:156
  37.4 20.0 %collective-permute-start.6 = (bf16[96,1536]{1,0:T(8,128)(2,1)S(1)}, bf16[96,1536]{1,0:T(8,128)(2,1)S(1)}, u32[]{:S(2)}, u32[]{:S(2)}) collective-permute-start(bf16[96,1536]{1,0:T(8,128)(2,1)S(1)} %pad_maximum_fusion.11), channel_id=1, source_target_pairs={{0,2},{1,3},{2,0},{3,1},{4,6},{5,7},{6,4},{7,5},{8,10},{9,11},{10,... | collective-permute-start | bytes 884744 | tf_op jit(solution)/shard_map/ppermute | solution.py:156
  39.1 18.4 %collective-permute-start.7 = (bf16[96,1536]{1,0:T(8,128)(2,1)S(1)}, bf16[96,1536]{1,0:T(8,128)(2,1)}, u32[]{:S(2)}, u32[]{:S(2)}) collective-permute-start(bf16[96,1536]{1,0:T(8,128)(2,1)S(1)} %pad_maximum_fusion.11), channel_id=1, source_target_pairs={{0,3},{1,0},{2,1},{3,2},{4,7},{5,4},{6,5},{7,6},{8,11},{9,8},{10,9... | collective-permute-start | bytes 884744 | tf_op jit(solution)/shard_map/ppermute | solution.py:156
  40.1 17.4 %copy-start.21 = (bf16[96,1536]{0,1:T(8,128)(2,1)}, bf16[96,1536]{0,1:T(8,128)(2,1)S(1)}, u32[]{:S(2)}) copy-start(bf16[96,1536]{0,1:T(8,128)(2,1)S(1)} %get-tuple-element.363) | copy-start | bytes 884740
  40.1 10.5 %collective-permute-start.3 = (bf16[96,1536]{0,1:T(8,128)(2,1)S(1)}, bf16[96,1536]{0,1:T(8,128)(2,1)S(1)}, u32[]{:S(2)}, u32[]{:S(2)}) collective-permute-start(bf16[96,1536]{0,1:T(8,128)(2,1)S(1)} %get-tuple-element.364), channel_id=1, source_target_pairs={{0,8},{4,12},{8,0},{12,4},{16,24},{20,28},{24,16},{28,20},{1,9},{5... | collective-permute-start | bytes 884744 | tf_op jit(solution)/shard_map/ppermute | solution.py:189
  41.6 10.2 %collective-permute-start.4 = (bf16[96,1536]{0,1:T(8,128)(2,1)S(1)}, bf16[96,1536]{0,1:T(8,128)(2,1)S(1)}, u32[]{:S(2)}, u32[]{:S(2)}) collective-permute-start(bf16[96,1536]{0,1:T(8,128)(2,1)S(1)} %get-tuple-element.363), channel_id=1, source_target_pairs={{0,16},{4,20},{8,24},{12,28},{16,0},{20,4},{24,8},{28,12},{1,17},{... | collective-permute-start | bytes 884744 | tf_op jit(solution)/shard_map/ppermute | solution.py:189
  50.6 8.8 %copy-start.26 = (bf16[96,1536]{0,1:T(8,128)(2,1)}, bf16[96,1536]{0,1:T(8,128)(2,1)S(1)}, u32[]{:S(2)}) copy-start(bf16[96,1536]{0,1:T(8,128)(2,1)S(1)} %collective-permute-done.3) | copy-start | bytes 884740
  59.4 8.2 %copy-start.15 = (bf16[4,256,768]{2,1,0:T(8,128)(2,1)S(1)}, bf16[4,256,768]{2,1,0:T(8,128)(2,1)}, u32[]{:S(2)}) copy-start(bf16[4,256,768]{2,1,0:T(8,128)(2,1)} %param.19) | copy-start | bytes 4718596
  60.4 222.4 %reduce-scatter.2.cloned.1.call-start = ((), (), s32[]{:S(2)}) async-start(), calls=%async_computation.2 | async-start | bytes 5308416 | tf_op jit(solution)/shard_map/reduce_scatter | solution.py:424
  63.2 38.8 %collective-permute-start.9 = (bf16[2,96,1536]{2,1,0:T(8,128)(2,1)S(1)}, bf16[2,96,1536]{2,1,0:T(8,128)(2,1)}, u32[]{:S(2)}, u32[]{:S(2)}) collective-permute-start(bf16[2,96,1536]{2,1,0:T(8,128)(2,1)S(1)} %broadcast_select_fusion.2), channel_id=1, source_target_pairs={{0,8},{4,12},{8,0},{12,4},{16,24},{20,28},{24,16},{28,20},{1,9},{5... | collective-permute-start | bytes 1769480 | tf_op jit(solution)/shard_map/ppermute | solution.py:189
  66.1 36.0 %collective-permute-start.8 = (bf16[2,96,1536]{2,1,0:T(8,128)(2,1)S(1)}, bf16[2,96,1536]{2,1,0:T(8,128)(2,1)}, u32[]{:S(2)}, u32[]{:S(2)}) collective-permute-start(bf16[2,96,1536]{2,1,0:T(8,128)(2,1)S(1)} %broadcast_select_fusion.3), channel_id=1, source_target_pairs={{0,16},{4,20},{8,24},{12,28},{16,0},{20,4},{24,8},{28,12},{1,17},{... | collective-permute-start | bytes 1769480 | tf_op jit(solution)/shard_map/ppermute | solution.py:189
  68.5 18.6 %collective-permute-start.10 = (bf16[1,256,768]{2,1,0:T(8,128)(2,1)S(1)}, bf16[1,256,768]{2,1,0:T(8,128)(2,1)S(1)}, u32[]{:S(2)}, u32[]{:S(2)}) collective-permute-start(bf16[1,256,768]{2,1,0:T(8,128)(2,1)S(1)} %get-tuple-element.329), channel_id=1, source_target_pairs={{0,1},{1,2},{2,3},{3,0},{4,5},{5,6},{6,7},{7,4},{8,9},{9,10},{10,1... | collective-permute-start | bytes 1179656 | tf_op jit(solution)/shard_map/ppermute | solution.py:165
  75.4 26.6 %collective-permute-start.11 = (bf16[1,256,768]{2,1,0:T(8,128)(2,1)S(1)}, bf16[1,256,768]{2,1,0:T(8,128)(2,1)S(1)}, u32[]{:S(2)}, u32[]{:S(2)}) collective-permute-start(bf16[1,256,768]{2,1,0:T(8,128)(2,1)S(1)} %get-tuple-element.328), channel_id=1, source_target_pairs={{0,2},{1,3},{2,0},{3,1},{4,6},{5,7},{6,4},{7,5},{8,10},{9,11},{10,... | collective-permute-start | bytes 1179656 | tf_op jit(solution)/shard_map/ppermute | solution.py:165
  104.9 12.2 %copy-start.25 = (bf16[1,256,768]{2,1,0:T(8,128)(2,1)S(1)}, bf16[1,256,768]{2,1,0:T(8,128)(2,1)}, u32[]{:S(2)}) copy-start(bf16[1,256,768]{2,1,0:T(8,128)(2,1)} %copy-done.24) | copy-start | bytes 1179652
  105.2 11.9 %collective-permute-start.12 = (bf16[2,2,96,3072]{3,2,1,0:T(8,128)(2,1)S(1)}, bf16[2,2,96,3072]{3,2,1,0:T(8,128)(2,1)}, u32[]{:S(2)}, u32[]{:S(2)}) collective-permute-start(bf16[2,2,96,3072]{3,2,1,0:T(8,128)(2,1)S(1)} %pad_maximum_fusion.1), channel_id=1, source_target_pairs={{0,4},{4,0},{8,12},{12,8},{16,20},{20,16},{24,28},{28,24},{1,5},{5... | collective-permute-start | bytes 7077896 | tf_op jit(solution)/shard_map/ppermute | solution.py:189
  105.3 11.8 %collective-permute-start.13 = (bf16[1,256,768]{2,1,0:T(8,128)(2,1)}, bf16[1,256,768]{2,1,0:T(8,128)(2,1)}, u32[]{:S(2)}, u32[]{:S(2)}) collective-permute-start(bf16[1,256,768]{2,1,0:T(8,128)(2,1)} %get-tuple-element.327), channel_id=1, source_target_pairs={{0,3},{1,0},{2,1},{3,2},{4,7},{5,4},{6,5},{7,6},{8,11},{9,8},{10,9... | collective-permute-start | bytes 1179656 | tf_op jit(solution)/shard_map/ppermute | solution.py:165
  108.2 10.0 %copy-start.16 = (bf16[4,256,768]{2,1,0:T(8,128)(2,1)S(1)}, bf16[4,256,768]{2,1,0:T(8,128)(2,1)}, u32[]{:S(2)}) copy-start(bf16[4,256,768]{2,1,0:T(8,128)(2,1)} %param.37) | copy-start | bytes 4718596
  108.2 15.1 %copy-start.38 = (pred[768]{0:T(1024)(128)(4,1)S(1)}, pred[768]{0:T(1024)(128)(4,1)}, u32[]{:S(2)}) copy-start(pred[768]{0:T(1024)(128)(4,1)} %iota.68) | copy-start | bytes 2308
  118.2 12.4 %copy-start.11 = (bf16[1024,768]{1,0:T(8,128)(2,1)}, bf16[1024,768]{1,0:T(8,128)(2,1)S(1)}, u32[]{:S(2)}) copy-start(bf16[1024,768]{1,0:T(8,128)(2,1)S(1)} %maximum_bitcast_fusion) | copy-start | bytes 4718596
  119.3 36.7 %collective-permute-start.14 = (bf16[1,256,768]{2,1,0:T(8,128)(2,1)S(1)}, bf16[1,256,768]{2,1,0:T(8,128)(2,1)S(1)}, u32[]{:S(2)}, u32[]{:S(2)}) collective-permute-start(bf16[1,256,768]{2,1,0:T(8,128)(2,1)S(1)} %get-tuple-element.326), channel_id=1, source_target_pairs={{0,2},{1,3},{2,0},{3,1},{4,6},{5,7},{6,4},{7,5},{8,10},{9,11},{10,... | collective-permute-start | bytes 1179656 | tf_op jit(solution)/shard_map/ppermute | solution.py:165
  119.3 53.1 %collective-permute-start.15 = (bf16[1,256,768]{2,1,0:T(8,128)(2,1)}, bf16[1,256,768]{2,1,0:T(8,128)(2,1)}, u32[]{:S(2)}, u32[]{:S(2)}) collective-permute-start(bf16[1,256,768]{2,1,0:T(8,128)(2,1)} %get-tuple-element.325), channel_id=1, source_target_pairs={{0,1},{1,2},{2,3},{3,0},{4,5},{5,6},{6,7},{7,4},{8,9},{9,10},{10,1... | collective-permute-start | bytes 1179656 | tf_op jit(solution)/shard_map/ppermute | solution.py:165
  122.8 49.6 %collective-permute-start.16 = (bf16[1,256,768]{2,1,0:T(8,128)(2,1)}, bf16[1,256,768]{2,1,0:T(8,128)(2,1)}, u32[]{:S(2)}, u32[]{:S(2)}) collective-permute-start(bf16[1,256,768]{2,1,0:T(8,128)(2,1)} %get-tuple-element.324), channel_id=1, source_target_pairs={{0,3},{1,0},{2,1},{3,2},{4,7},{5,4},{6,5},{7,6},{8,11},{9,8},{10,9... | collective-permute-start | bytes 1179656 | tf_op jit(solution)/shard_map/ppermute | solution.py:165
  133.2 23.6 %copy-start.44 = (f32[768]{0:T(1024)S(1)}, f32[768]{0:T(1024)}, u32[]{:S(2)}) copy-start(f32[768]{0:T(1024)} %convert_element_type.269) | copy-start | bytes 9220
  161.1 11.3 %copy-start.33 = (f32[1024]{0:T(1024)}, f32[1024]{0:T(1024)S(1)}, u32[]{:S(2)}) copy-start(f32[1024]{0:T(1024)S(1)} %add_rsqrt_fusion.1) | copy-start | bytes 12292
  161.2 11.3 %copy-start.41 = (f32[768]{0:T(1024)S(1)}, f32[768]{0:T(1024)}, u32[]{:S(2)}) copy-start(f32[768]{0:T(1024)} %convert_element_type.271) | copy-start | bytes 9220
  161.2 11.3 %copy-start.43 = (f32[768]{0:T(1024)S(1)}, f32[768]{0:T(1024)}, u32[]{:S(2)}) copy-start(f32[768]{0:T(1024)} %convert_element_type.272) | copy-start | bytes 9220
  161.2 11.3 %copy-start.48 = (bf16[768,6144]{1,0:T(8,128)(2,1)S(1)}, bf16[768,6144]{1,0:T(8,128)(2,1)}, u32[]{:S(2)}) copy-start(bf16[768,6144]{1,0:T(8,128)(2,1)} %all-gather.2.cloned.1.call-done) | copy-start | bytes 28311556
  196.3 13.6 %copy-start.34 = (f32[1024]{0:T(1024)S(1)}, f32[1024]{0:T(1024)}, u32[]{:S(2)}) copy-start(f32[1024]{0:T(1024)} %copy-done.33) | copy-start | bytes 12292
  196.3 13.6 %copy-start.42 = (f32[768]{0:T(1024)S(1)}, f32[768]{0:T(1024)}, u32[]{:S(2)}) copy-start(f32[768]{0:T(1024)} %convert_element_type.271) | copy-start | bytes 9220
  217.4 22.1 %collective-permute-start.17 = (bf16[2,2,96,3072]{3,2,0,1:T(8,128)(2,1)S(1)}, bf16[2,2,96,3072]{3,2,0,1:T(8,128)(2,1)S(1)}, u32[]{:S(2)}, u32[]{:S(2)}) collective-permute-start(bf16[2,2,96,3072]{3,2,0,1:T(8,128)(2,1)S(1)} %bitcast.181), channel_id=1, source_target_pairs={{0,4},{4,0},{8,12},{12,8},{16,20},{20,16},{24,28},{28,24},{1,5},{5... | collective-permute-start | bytes 7077896 | tf_op jit(solution)/shard_map/ppermute | solution.py:189
  219.7 19.7 %collective-permute-start.18 = (bf16[1,256,768]{2,1,0:T(8,128)(2,1)S(1)}, bf16[1,256,768]{2,1,0:T(8,128)(2,1)S(1)}, u32[]{:S(2)}, u32[]{:S(2)}) collective-permute-start(bf16[1,256,768]{2,1,0:T(8,128)(2,1)S(1)} %get-tuple-element.322), channel_id=1, source_target_pairs={{0,2},{1,3},{2,0},{3,1},{4,6},{5,7},{6,4},{7,5},{8,10},{9,11},{10,... | collective-permute-start | bytes 1179656 | tf_op jit(solution)/shard_map/ppermute | solution.py:174
  232.6 10.6 %copy-start.1 = (f32[1024,768]{1,0:T(8,128)}, f32[1024,768]{1,0:T(8,128)S(1)}, u32[]{:S(2)}) copy-start(f32[1024,768]{1,0:T(8,128)S(1)} %get-tuple-element.305) | copy-start | bytes 9437188
  241.5 17.8 %collective-permute-start.20 = (bf16[2,96,1536]{2,1,0:T(8,128)(2,1)}, bf16[2,96,1536]{2,1,0:T(8,128)(2,1)}, u32[]{:S(2)}, u32[]{:S(2)}) collective-permute-start(bf16[2,96,1536]{2,1,0:T(8,128)(2,1)} %dynamic-slice_bitcast_fusion.3), channel_id=1, source_target_pairs={{0,8},{4,12},{8,0},{12,4},{16,24},{20,28},{24,16},{28,20},{1,9},{5... | collective-permute-start | bytes 1769480 | tf_op jit(solution)/shard_map/ppermute | solution.py:189
  242.7 16.5 %collective-permute-start.19 = (bf16[2,96,1536]{2,1,0:T(8,128)(2,1)}, bf16[2,96,1536]{2,1,0:T(8,128)(2,1)}, u32[]{:S(2)}, u32[]{:S(2)}) collective-permute-start(bf16[2,96,1536]{2,1,0:T(8,128)(2,1)} %dynamic-slice_bitcast_fusion.4), channel_id=1, source_target_pairs={{0,16},{4,20},{8,24},{12,28},{16,0},{20,4},{24,8},{28,12},{1,17},{... | collective-permute-start | bytes 1769480 | tf_op jit(solution)/shard_map/ppermute | solution.py:189
  253.6 29.3 %collective-permute-start.23 = (bf16[1,256,768]{2,1,0:T(8,128)(2,1)}, bf16[1,256,768]{2,1,0:T(8,128)(2,1)}, u32[]{:S(2)}, u32[]{:S(2)}) collective-permute-start(bf16[1,256,768]{2,1,0:T(8,128)(2,1)} %get-tuple-element.169), channel_id=1, source_target_pairs={{0,3},{1,0},{2,1},{3,2},{4,7},{5,4},{6,5},{7,6},{8,11},{9,8},{10,9... | collective-permute-start | bytes 1179656 | tf_op jit(solution)/shard_map/ppermute | solution.py:174
  255.0 27.9 %collective-permute-start.24 = (bf16[1,256,768]{2,1,0:T(8,128)(2,1)}, bf16[1,256,768]{2,1,0:T(8,128)(2,1)}, u32[]{:S(2)}, u32[]{:S(2)}) collective-permute-start(bf16[1,256,768]{2,1,0:T(8,128)(2,1)} %get-tuple-element.171), channel_id=1, source_target_pairs={{0,1},{1,2},{2,3},{3,0},{4,5},{5,6},{6,7},{7,4},{8,9},{9,10},{10,1... | collective-permute-start | bytes 1179656 | tf_op jit(solution)/shard_map/ppermute | solution.py:174
  261.7 20.9 %collective-permute-start.22 = (bf16[96,1536]{1,0:T(8,128)(2,1)S(1)}, bf16[96,1536]{1,0:T(8,128)(2,1)S(1)}, u32[]{:S(2)}, u32[]{:S(2)}) collective-permute-start(bf16[96,1536]{1,0:T(8,128)(2,1)S(1)} %dynamic-slice_bitcast_fusion.7), channel_id=1, source_target_pairs={{0,16},{4,20},{8,24},{12,28},{16,0},{20,4},{24,8},{28,12},{1,17},{... | collective-permute-start | bytes 884744 | tf_op jit(solution)/shard_map/ppermute | solution.py:189
  263.2 19.4 %collective-permute-start.21 = (bf16[96,1536]{1,0:T(8,128)(2,1)S(1)}, bf16[96,1536]{1,0:T(8,128)(2,1)S(1)}, u32[]{:S(2)}, u32[]{:S(2)}) collective-permute-start(bf16[96,1536]{1,0:T(8,128)(2,1)S(1)} %dynamic-slice_bitcast_fusion.8), channel_id=1, source_target_pairs={{0,8},{4,12},{8,0},{12,4},{16,24},{20,28},{24,16},{28,20},{1,9},{5... | collective-permute-start | bytes 884744 | tf_op jit(solution)/shard_map/ppermute | solution.py:189
  284.1 25.5 %collective-permute-start.27 = (bf16[96,1536]{1,0:T(8,128)(2,1)S(1)}, bf16[96,1536]{1,0:T(8,128)(2,1)S(1)}, u32[]{:S(2)}, u32[]{:S(2)}) collective-permute-start(bf16[96,1536]{1,0:T(8,128)(2,1)S(1)} %pad_maximum_fusion.15), channel_id=1, source_target_pairs={{0,1},{1,2},{2,3},{3,0},{4,5},{5,6},{6,7},{7,4},{8,9},{9,10},{10,1... | collective-permute-start | bytes 884744 | tf_op jit(solution)/shard_map/ppermute | solution.py:174
  286.4 23.2 %collective-permute-start.26 = (bf16[96,1536]{1,0:T(8,128)(2,1)}, bf16[96,1536]{1,0:T(8,128)(2,1)S(1)}, u32[]{:S(2)}, u32[]{:S(2)}) collective-permute-start(bf16[96,1536]{1,0:T(8,128)(2,1)} %pad_maximum_fusion.14), channel_id=1, source_target_pairs={{0,2},{1,3},{2,0},{3,1},{4,6},{5,7},{6,4},{7,5},{8,10},{9,11},{10,... | collective-permute-start | bytes 884744 | tf_op jit(solution)/shard_map/ppermute | solution.py:174
  289.5 20.1 %copy-start.12 = (bf16[1024,768]{1,0:T(8,128)(2,1)S(1)}, bf16[1024,768]{1,0:T(8,128)(2,1)}, u32[]{:S(2)}) copy-start(bf16[1024,768]{1,0:T(8,128)(2,1)} %copy-done.11) | copy-start | bytes 4718596
  289.5 20.1 %collective-permute-start.25 = (bf16[96,1536]{1,0:T(8,128)(2,1)}, bf16[96,1536]{1,0:T(8,128)(2,1)S(1)}, u32[]{:S(2)}, u32[]{:S(2)}) collective-permute-start(bf16[96,1536]{1,0:T(8,128)(2,1)} %pad_maximum_fusion.13), channel_id=1, source_target_pairs={{0,3},{1,0},{2,1},{3,2},{4,7},{5,4},{6,5},{7,6},{8,11},{9,8},{10,9... | collective-permute-start | bytes 884744 | tf_op jit(solution)/shard_map/ppermute | solution.py:174
  316.7 11.0 %slice-start.2 = ((s8[4718592]{0:T(1024)(128)(4,1)}), s8[524288]{0:T(1024)(128)(4,1)S(1)}, s32[]{:S(2)}) async-start(s8[4718592]{0:T(1024)(128)(4,1)} %bitcast.176), calls=%async_computation.5 | async-start | bytes 1048576
  318.2 13.4 %collective-permute-start.28 = (bf16[2,2,96,3072]{3,2,1,0:T(8,128)(2,1)}, bf16[2,2,96,3072]{3,2,1,0:T(8,128)(2,1)S(1)}, u32[]{:S(2)}, u32[]{:S(2)}) collective-permute-start(bf16[2,2,96,3072]{3,2,1,0:T(8,128)(2,1)} %dynamic-slice_bitcast_fusion), channel_id=1, source_target_pairs={{0,4},{4,0},{8,12},{12,8},{16,20},{20,16},{24,28},{28,24},{1,5},{5... | collective-permute-start | bytes 7077896 | tf_op jit(solution)/shard_map/ppermute | solution.py:189
  333.7 43.0 %collective-permute-start.30 = (bf16[2,96,1536]{2,1,0:T(8,128)(2,1)}, bf16[2,96,1536]{2,1,0:T(8,128)(2,1)}, u32[]{:S(2)}, u32[]{:S(2)}) collective-permute-start(bf16[2,96,1536]{2,1,0:T(8,128)(2,1)} %dynamic-slice_bitcast_fusion.1), channel_id=1, source_target_pairs={{0,8},{4,12},{8,0},{12,4},{16,24},{20,28},{24,16},{28,20},{1,9},{5... | collective-permute-start | bytes 1769480 | tf_op jit(solution)/shard_map/ppermute | solution.py:189
  335.1 41.6 %collective-permute-start.29 = (bf16[2,96,1536]{2,1,0:T(8,128)(2,1)}, bf16[2,96,1536]{2,1,0:T(8,128)(2,1)}, u32[]{:S(2)}, u32[]{:S(2)}) collective-permute-start(bf16[2,96,1536]{2,1,0:T(8,128)(2,1)} %dynamic-slice_bitcast_fusion.2), channel_id=1, source_target_pairs={{0,16},{4,20},{8,24},{12,28},{16,0},{20,4},{24,8},{28,12},{1,17},{... | collective-permute-start | bytes 1769480 | tf_op jit(solution)/shard_map/ppermute | solution.py:189
  337.6 14.4 %collective-permute-start.31 = (bf16[1,256,768]{2,1,0:T(8,128)(2,1)}, bf16[1,256,768]{2,1,0:T(8,128)(2,1)}, u32[]{:S(2)}, u32[]{:S(2)}) collective-permute-start(bf16[1,256,768]{2,1,0:T(8,128)(2,1)} %get-tuple-element.317), channel_id=1, source_target_pairs={{0,3},{1,0},{2,1},{3,2},{4,7},{5,4},{6,5},{7,6},{8,11},{9,8},{10,9... | collective-permute-start | bytes 1179656 | tf_op jit(solution)/shard_map/ppermute | solution.py:174
  342.1 34.6 %collective-permute-start.32 = (bf16[1,256,768]{2,1,0:T(8,128)(2,1)}, bf16[1,256,768]{2,1,0:T(8,128)(2,1)}, u32[]{:S(2)}, u32[]{:S(2)}) collective-permute-start(bf16[1,256,768]{2,1,0:T(8,128)(2,1)} %get-tuple-element.316), channel_id=1, source_target_pairs={{0,2},{1,3},{2,0},{3,1},{4,6},{5,7},{6,4},{7,5},{8,10},{9,11},{10,... | collective-permute-start | bytes 1179656 | tf_op jit(solution)/shard_map/ppermute | solution.py:174
  342.7 1.2 collective-permute-start.36
  342.7 38.6 %copy-start.29 = (bf16[96,1536]{1,0:T(8,128)(2,1)S(1)}, bf16[96,1536]{1,0:T(8,128)(2,1)}, u32[]{:S(2)}) copy-start(bf16[96,1536]{1,0:T(8,128)(2,1)} %copy-done.28) | copy-start | bytes 884740
  342.7 38.6 %copy-start.31 = (bf16[96,1536]{1,0:T(8,128)(2,1)S(1)}, bf16[96,1536]{1,0:T(8,128)(2,1)}, u32[]{:S(2)}) copy-start(bf16[96,1536]{1,0:T(8,128)(2,1)} %copy-done.30) | copy-start | bytes 884740
  343.9 42.7 %collective-permute-start.35 = (bf16[1,256,768]{2,1,0:T(8,128)(2,1)}, bf16[1,256,768]{2,1,0:T(8,128)(2,1)S(1)}, u32[]{:S(2)}, u32[]{:S(2)}) collective-permute-start(bf16[1,256,768]{2,1,0:T(8,128)(2,1)} %get-tuple-element.315), channel_id=1, source_target_pairs={{0,1},{1,2},{2,3},{3,0},{4,5},{5,6},{6,7},{7,4},{8,9},{9,10},{10,1... | collective-permute-start | bytes 1179656 | tf_op jit(solution)/shard_map/ppermute | solution.py:174
  352.0 29.5 %collective-permute-start.37 = (f32[12,768]{1,0:T(8,128)S(1)}, f32[12,768]{1,0:T(8,128)S(1)}, u32[]{:S(2)}, u32[]{:S(2)}) collective-permute-start(f32[12,768]{1,0:T(8,128)S(1)} %add.418), channel_id=1, source_target_pairs={{0,8},{4,12},{8,0},{12,4},{16,24},{20,28},{24,16},{28,20},{1,9},{5... | collective-permute-start | bytes 110600 | tf_op jit(solution)/shard_map/ppermute | solution.py:189
  378.0 8.6 %collective-permute-start.34 = (bf16[96,1536]{1,0:T(8,128)(2,1)S(1)}, bf16[96,1536]{1,0:T(8,128)(2,1)S(1)}, u32[]{:S(2)}, u32[]{:S(2)}) collective-permute-start(bf16[96,1536]{1,0:T(8,128)(2,1)S(1)} %dynamic-slice_bitcast_fusion.5), channel_id=1, source_target_pairs={{0,16},{4,20},{8,24},{12,28},{16,0},{20,4},{24,8},{28,12},{1,17},{... | collective-permute-start | bytes 884744 | tf_op jit(solution)/shard_map/ppermute | solution.py:189
  380.7 7.3 %collective-permute-start.33 = (bf16[96,1536]{1,0:T(8,128)(2,1)S(1)}, bf16[96,1536]{1,0:T(8,128)(2,1)S(1)}, u32[]{:S(2)}, u32[]{:S(2)}) collective-permute-start(bf16[96,1536]{1,0:T(8,128)(2,1)S(1)} %dynamic-slice_bitcast_fusion.6), channel_id=1, source_target_pairs={{0,8},{4,12},{8,0},{12,4},{16,24},{20,28},{24,16},{28,20},{1,9},{5... | collective-permute-start | bytes 884744 | tf_op jit(solution)/shard_map/ppermute | solution.py:189
  381.5 5.1 %collective-permute-start.38 = (f32[12,768]{1,0:T(8,128)S(1)}, f32[12,768]{1,0:T(8,128)S(1)}, u32[]{:S(2)}, u32[]{:S(2)}) collective-permute-start(f32[12,768]{1,0:T(8,128)S(1)} %add.419), channel_id=1, source_target_pairs={{0,16},{4,20},{8,24},{12,28},{16,0},{20,4},{24,8},{28,12},{1,17},{... | collective-permute-start | bytes 110600 | tf_op jit(solution)/shard_map/ppermute | solution.py:189
  388.8 9.4 %collective-permute-start.41 = (bf16[117,768]{1,0:T(8,128)(2,1)S(1)}, bf16[117,768]{1,0:T(8,128)(2,1)S(1)}, u32[]{:S(2)}, u32[]{:S(2)}) collective-permute-start(bf16[117,768]{1,0:T(8,128)(2,1)S(1)} %get-tuple-element.377), channel_id=1, source_target_pairs={{0,1},{1,2},{2,3},{3,0},{4,5},{5,6},{6,7},{7,4},{8,9},{9,10},{10,1... | collective-permute-start | bytes 539144 | tf_op jit(solution)/shard_map/ppermute | solution.py:174
  388.9 13.9 %collective-permute-start.40 = (bf16[117,768]{1,0:T(8,128)(2,1)S(1)}, bf16[117,768]{1,0:T(8,128)(2,1)S(1)}, u32[]{:S(2)}, u32[]{:S(2)}) collective-permute-start(bf16[117,768]{1,0:T(8,128)(2,1)S(1)} %get-tuple-element.376), channel_id=1, source_target_pairs={{0,2},{1,3},{2,0},{3,1},{4,6},{5,7},{6,4},{7,5},{8,10},{9,11},{10,... | collective-permute-start | bytes 539144 | tf_op jit(solution)/shard_map/ppermute | solution.py:174
  389.0 13.8 %collective-permute-start.39 = (bf16[117,768]{1,0:T(8,128)(2,1)S(1)}, bf16[117,768]{1,0:T(8,128)(2,1)S(1)}, u32[]{:S(2)}, u32[]{:S(2)}) collective-permute-start(bf16[117,768]{1,0:T(8,128)(2,1)S(1)} %get-tuple-element.375), channel_id=1, source_target_pairs={{0,3},{1,0},{2,1},{3,2},{4,7},{5,4},{6,5},{7,6},{8,11},{9,8},{10,9... | collective-permute-start | bytes 539144 | tf_op jit(solution)/shard_map/ppermute | solution.py:174
  (36 other events, 114.0 us)
Sparse Core Ops, SparseCore 0:
  60.5 72.7 all-gather.1
  196.5 54.0 reduce-scatter.1

commit v10 on v9

--- a/solution.py
+++ b/solution.py
@@ -485,9 +485,11 @@
         jnp.concatenate(head_grads + [output_grad], axis=1), (tokens_grad, late)
     )
     late = total_over_fsdp(late)
-    tokens_grad = sent_back(by_arrival(tokens_grad))
-    heads_share, tokens_grad[:3] = scatter_near(heads_share, tokens_grad[:3])
-    heads_share, tokens_grad[3:] = scatter_far(heads_share, tokens_grad[3:])
+    tokens_grad = sent_back(by_arrival(tokens_grad), range(2, 3))
+    heads_share, tokens_grad[2:3] = scatter_near(heads_share, tokens_grad[2:3])
+    heads_share, tokens_grad = lax.optimization_barrier((heads_share, tokens_grad))
+    tokens_grad = sent_back(tokens_grad, [step for step in range(1, tp) if step != 2])
+    heads_share, tokens_grad = scatter_far(heads_share, tokens_grad)
     heads_share, late = lax.optimization_barrier((heads_share, late))
     high = late.astype(LOW)
     lower = (late - high.astype(WIDE)).astype(LOW)

time: 420 us -> 417 us (level)
  waiting for transfers between devices: 100 us -> 95.1 us
    unnamed x134 -> x138, local copies, waits for them, and re-layouts: 12.7 us -> 12.7 us
where the time goes in v10:
time: 417 us; the launch traced here: 410 us
  waiting for transfers between devices  95.1 us (23%)
  matrix products  86.7 us (21%)
  starting transfers between devices  64.2 us (15%)
  Pallas kernels  60.3 us (14%)
  other arithmetic  46.2 us (11%)
  local copies, waits for them, and re-layouts  41.5 us (10%)
  between operations  15.9 us (4%)
    dot_general x18, matrix products, dot(): return lax.dot_general(left, right, dims, preferred_element_type=WIDE)  86.7 us
    ppermute x12, waiting for transfers between devices, sent_back(): moved[step] = lax.ppermute(parts[step], 'tp', pairs)  40.8 us
    pallas_call x2, Pallas kernels, attend_back(): pl.pallas_call(body, grid=(count, pairs - first if part else pairs // 2),...  37.4 us
    ppermute x6, waiting for transfers between devices, dealt(): parts.append(lax.ppermute(block, 'tp', pairs) if step else block)  33.3 us
    pallas_call x1, Pallas kernels, attend(): pl.pallas_call(functools.partial(attend_kernel, scaling=scaling), grid=(c...  22.9 us
    ppermute x12, starting transfers between devices, sent_back(): moved[step] = lax.ppermute(parts[step], 'tp', pairs)  19.2 us
    ppermute x18, starting transfers between devices, flip(): return lax.ppermute(block, axis, [(i, i ^ bit) for i in range(members)])  16.5 us
    ppermute x6, starting transfers between devices, dealt(): parts.append(lax.ppermute(block, 'tp', pairs) if step else block)  14.2 us
  transfers between devices with their start and end apart: 44, of which 17 were waited for; matrix products, arithmetic and copies ran while one was open for 29% of the time, Pallas kernels for 15%

profile of v10, /device:TPU:0, one launch (start us, length us, event | category | flops | bytes accessed | tf_op | source)
XLA Modules:
  0.0 409.9 jit_solution(6797744337481380806)
XLA Ops:
  7.2 2.1 concatenate.97
  13.2 3.1 collective-permute-start
  16.3 2.6 collective-permute-start.1
  29.2 2.6 collective-permute-done.1
  32.7 4.7 %collective-permute-start.5 = (bf16[96,1536]{1,0:T(8,128)(2,1)S(1)}, bf16[96,1536]{1,0:T(8,128)(2,1)S(1)}, u32[]{:S(2)}, u32[]{:S(2)}) collective-permute-start(bf16[96,1536]{1,0:T(8,128)(2,1)S(1)} %pad_maximum_fusion.11), channel_id=1, source_target_pairs={{0,1},{1,2},{2,3},{3,0},{4,5},{5,6},{6,7},{7,4},{8,9},{9,10},{10,1... | collective-permute-start | bytes 884744 | tf_op jit(solution)/shard_map/ppermute | solution.py:156
  37.4 1.6 collective-permute-start.6
  40.1 1.5 collective-permute-start.3
  41.6 1.5 collective-permute-start.4
  46.5 4.1 %collective-permute-done.3 = bf16[96,1536]{0,1:T(8,128)(2,1)S(1)} collective-permute-done((bf16[96,1536]{0,1:T(8,128)(2,1)S(1)}, bf16[96,1536]{0,1:T(8,128)(2,1)S(1)}, u32[]{:S(2)}, u32[]{:S(2)}) %collective-permute-start.3) | collective-permute-done | bytes 294944 | tf_op jit(solution)/shard_map/ppermute | solution.py:189
  51.8 5.6 %collective-permute-done.6 = bf16[96,1536]{1,0:T(8,128)(2,1)S(1)} collective-permute-done((bf16[96,1536]{1,0:T(8,128)(2,1)S(1)}, bf16[96,1536]{1,0:T(8,128)(2,1)S(1)}, u32[]{:S(2)}, u32[]{:S(2)}) %collective-permute-start.6) | collective-permute-done | bytes 294944 | tf_op jit(solution)/shard_map/ppermute | solution.py:156
  63.2 1.6 collective-permute-start.9
  66.1 1.6 collective-permute-start.8
  68.5 6.9 %collective-permute-start.10 = (bf16[1,256,768]{2,1,0:T(8,128)(2,1)S(1)}, bf16[1,256,768]{2,1,0:T(8,128)(2,1)S(1)}, u32[]{:S(2)}, u32[]{:S(2)}) collective-permute-start(bf16[1,256,768]{2,1,0:T(8,128)(2,1)S(1)} %get-tuple-element.343), channel_id=1, source_target_pairs={{0,1},{1,2},{2,3},{3,0},{4,5},{5,6},{6,7},{7,4},{8,9},{9,10},{10,1... | collective-permute-start | bytes 1179656 | tf_op jit(solution)/shard_map/ppermute | solution.py:165
  75.4 2.2 collective-permute-start.11
  77.6 9.5 %collective-permute-done.10 = bf16[1,256,768]{2,1,0:T(8,128)(2,1)S(1)} collective-permute-done((bf16[1,256,768]{2,1,0:T(8,128)(2,1)S(1)}, bf16[1,256,768]{2,1,0:T(8,128)(2,1)S(1)}, u32[]{:S(2)}, u32[]{:S(2)}) %collective-permute-start.10) | collective-permute-done | bytes 393248 | tf_op jit(solution)/shard_map/ppermute | solution.py:165
  87.1 14.9 %collective-permute-done.11 = bf16[1,256,768]{2,1,0:T(8,128)(2,1)S(1)} collective-permute-done((bf16[1,256,768]{2,1,0:T(8,128)(2,1)S(1)}, bf16[1,256,768]{2,1,0:T(8,128)(2,1)S(1)}, u32[]{:S(2)}, u32[]{:S(2)}) %collective-permute-start.11) | collective-permute-done | bytes 393248 | tf_op jit(solution)/shard_map/ppermute | solution.py:165
  108.2 8.9 %collective-permute-done.13 = bf16[1,256,768]{2,1,0:T(8,128)(2,1)} collective-permute-done((bf16[1,256,768]{2,1,0:T(8,128)(2,1)}, bf16[1,256,768]{2,1,0:T(8,128)(2,1)}, u32[]{:S(2)}, u32[]{:S(2)}) %collective-permute-start.13) | collective-permute-done | bytes 393248 | tf_op jit(solution)/shard_map/ppermute | solution.py:165
  119.3 3.5 collective-permute-start.15
  123.3 2.2 bitcast_select_fusion
  125.5 2.6 fusion.63.k_ref.refs_1_
  128.1 2.5 fusion.35.v_ref.refs_2_
  130.7 2.5 fusion.34.q_ref.refs_0_
  133.2 22.9 %attend.1 = (bf16[1,1024,768]{2,1,0:T(8,128)(2,1)}, f32[1,6,2,1024]{3,2,1,0:T(2,128)}) custom-call(bf16[1,1024,768]{2,1,0:T(8,128)(2,1)} %fusion.34.q_ref.refs_0_, bf16[1,1024,768]{2,1,0:T(8,128)(2,1)} %fusion.63.k_ref.refs_1_, bf16[1,1024,768]{2,1,0:T(8,128)(2,1)} %fusion.35.v_ref.refs_2_, s32[1,1,1024]{2,1,0:T(1,128)} %broadcast_in_dim_reshape.6.row_ref.refs_6_, ...), custom_call_target="tpu_custom_call" | custom-call | flops 22548578304 | bytes 6291456 | tf_op jit(solution)/shard_map/attend/pallas_call | solution.py:93
  156.9 3.8 fusion.121
  161.2 11.1 %multiply_convert_fusion = (bf16[1024,3072]{1,0:T(8,128)(2,1)S(1)}, f32[1024,3072]{1,0:T(8,128)}) fusion(f32[3072]{0:T(1024)} %pad_maximum_fusion.17, bf16[768,6144]{1,0:T(8,128)(2,1)} %all-gather.2.cloned.1.call-done, f32[1024,768]{1,0:T(8,128)S(1)} %get-tuple-element.411, f32[768]{0:T(1024)} %convert_element_type.271, f32[768]{0:T(1024)S(1)} %convert_element_type.270, ...), kind=kOutput, calls=%fused_computation.8 | convolution fusion | flops 4854644736 | bytes 26766336 | tf_op jit(solution)/shard_map/dot_general | solution.py:22
  172.4 5.4 %fusion.109 = (f32[1024]{0:T(1024)S(1)}, f32[1024,768]{1,0:T(8,128)S(1)}) fusion(f32[768]{0:T(1024)S(1)} %copy-done.45, f32[768]{0:T(1024)S(1)} %copy-done.43, f32[768]{0:T(1024)S(1)} %convert_element_type.270, f32[1024]{0:T(1024)S(1)} %add_rsqrt_fusion.1, f32[1024,768]{1,0:T(8,128)S(1)} %get-tuple-element.411, f32[1024]{0:T(1024)S(1)} %broadcast_multiply_fusion.5, ...), kind=kOutput, calls=%fused_computation.262 | convolution fusion | flops 4837342208 | bytes 17326080 | tf_op jit(solution)/shard_map/dot_general | solution.py:22
  178.8 5.3 %fusion.29 = (f32[768]{0:T(1024)}, f32[1024]{0:T(1024)S(1)}, f32[1024]{0:T(1024)S(1)}, bf16[1024,768]{1,0:T(8,128)(2,1)}) fusion(f32[1024,768]{1,0:T(8,128)S(1)} %get-tuple-element.321, f32[1024]{0:T(1024)S(1)} %add_rsqrt_fusion, f32[1024]{0:T(1024)S(1)} %broadcast_multiply_fusion.4, bf16[1,256,768]{2,1,0:T(8,128)(2,1)} %collective-permute-done.16, ...), kind=kLoop, calls=%fused_computation.44 | loop fusion | flops 14939392 | bytes 6317056 | tf_op jit(solution)/shard_map/reduce_sum | solution.py:277
  184.2 3.5 fusion.106
  187.7 1.7 copy-done.8
  189.3 7.0 %convolution_convert_fusion = bf16[768,3072]{1,0:T(8,128)(2,1)} fusion(bf16[1024,3072]{1,0:T(8,128)(2,1)S(1)} %get-tuple-element.154, f32[1024,768]{1,0:T(8,128)S(1)} %get-tuple-element.317), kind=kOutput, calls=%fused_computation.13 | convolution fusion | flops 4834983936 | bytes 14155776 | tf_op jit(solution)/shard_map/dot_general | solution.py:22
  196.3 13.6 %convert_reduce_fusion = (f32[3072]{0:T(1024)}, bf16[1024,3072]{1,0:T(8,128)(2,1)S(1)}) fusion(f32[1024,3072]{1,0:T(8,128)} %get-tuple-element.413, f32[3072]{0:T(1024)} %pad_maximum_fusion.17, bf16[768,6144]{1,0:T(8,128)(2,1)} %all-gather.2.cloned.1.call-done, f32[1024,768]{1,0:T(8,128)} %copy-done.8), kind=kOutput, calls=%fused_computation.7 | convolution fusion | flops 4873516032 | bytes 26763264 | tf_op jit(solution)/shard_map/dot_general | solution.py:22
  210.0 6.8 %convolution_convert_fusion.1 = bf16[768,3072]{1,0:T(8,128)(2,1)S(1)} fusion(bf16[1024,3072]{1,0:T(8,128)(2,1)S(1)} %get-tuple-element.416, f32[1024,768]{1,0:T(8,128)S(1)} %get-tuple-element.411, f32[768]{0:T(1024)S(1)} %copy-done.44, f32[768]{0:T(1024)S(1)} %convert_element_type.270, f32[1024]{0:T(1024)S(1)} %copy-done.36, ...), kind=kOutput, calls=%fused_computation.14 | convolution fusion | flops 4838129664 | bytes 14170112 | tf_op jit(solution)/shard_map/dot_general | solution.py:22
  221.1 10.3 %multiply_reduce_fusion = (f32[768]{0:T(1024)}, f32[1024]{0:T(1024)S(1)}, f32[1024]{0:T(1024)S(1)}, f32[768]{0:T(1024)}, f32[1024,768]{1,0:T(8,128)S(1)}) fusion(f32[1024,768]{1,0:T(8,128)S(1)} %get-tuple-element.411, f32[1024]{0:T(1024)S(1)} %copy-done.36, f32[1024]{0:T(1024)S(1)} %broadcast_multiply_fusion.5, f32[768]{0:T(1024)S(1)} %convert_element_type.270, ...), kind=kOutput, calls=%fused_computation.48 | convolution fusion | flops 4839698432 | bytes 20472832 | tf_op jit(solution)/shard_map/dot_general | solution.py:22
  232.5 6.9 %collective-permute-done.18 = bf16[1,256,768]{2,1,0:T(8,128)(2,1)S(1)} collective-permute-done((bf16[1,256,768]{2,1,0:T(8,128)(2,1)S(1)}, bf16[1,256,768]{2,1,0:T(8,128)(2,1)S(1)}, u32[]{:S(2)}, u32[]{:S(2)}) %collective-permute-start.18) | collective-permute-done | bytes 393248 | tf_op jit(solution)/shard_map/ppermute | solution.py:174
  243.1 4.0 fusion.64.g_ref.refs_3_
  248.6 4.9 %fusion.51 = bf16[768,768]{1,0:T(8,128)(2,1)} fusion(bf16[1,1024,768]{2,1,0:T(8,128)(2,1)} %get-tuple-element.145.c_ref.refs_4_, f32[1024,768]{1,0:T(8,128)} %copy-done.1), kind=kOutput, calls=%fused_computation.89 | convolution fusion | flops 1209335808 | bytes 5898240 | tf_op jit(solution)/shard_map/dot_general | solution.py:22
  255.5 3.7 collective-permute-done.20
  261.6 1.5 collective-permute-start.22
  263.8 18.8 %attend_back.2 = (bf16[1,1024,768]{2,1,0:T(8,128)(2,1)}, bf16[1,1024,768]{2,1,0:T(8,128)(2,1)}, bf16[1,1024,768]{2,1,0:T(8,128)(2,1)}) custom-call(bf16[1,1024,768]{2,1,0:T(8,128)(2,1)} %fusion.34.q_ref.refs_0_, bf16[1,1024,768]{2,1,0:T(8,128)(2,1)} %fusion.63.k_ref.refs_1_, bf16[1,1024,768]{2,1,0:T(8,128)(2,1)} %fusion.35.v_ref.refs_2_, ...), custom_call_target="tpu_custom_call" | custom-call | flops 19327352832 | bytes 5505024 | tf_op jit(solution)/shard_map/attend_back/pallas_call | solution.py:128
  284.2 1.5 collective-permute-start.27
  286.5 2.4 collective-permute-start.26
  291.0 18.5 %attend_back.3 = (bf16[1,1024,768]{2,1,0:T(8,128)(2,1)}, bf16[1,1024,768]{2,1,0:T(8,128)(2,1)}, bf16[1,1024,768]{2,1,0:T(8,128)(2,1)}) custom-call(bf16[1,1024,768]{2,1,0:T(8,128)(2,1)} %fusion.34.q_ref.refs_0_, bf16[1,1024,768]{2,1,0:T(8,128)(2,1)} %fusion.63.k_ref.refs_1_, ...), custom_call_target="tpu_custom_call", output_to_operand_aliasing={{0}: (8, {}), {1}: (9, {}), {2}: (10, {})} | custom-call | flops 19327352832 | bytes 5505024 | tf_op jit(solution)/shard_map/attend_back/pallas_call | solution.py:128
  309.7 3.1 fusion.54
  312.8 1.5 fusion.57
  314.3 1.5 fusion.60
  316.7 1.5 dynamic-slice_bitcast_fusion
  322.8 1.5 stack.54
  324.3 3.3 fusion.44
  327.8 1.4 fusion.40
  330.2 1.5 add_convert_fusion
  335.1 1.5 collective-permute-start.29
  337.6 2.8 collective-permute-start.31
  341.6 1.4 collective-permute-start.37
  343.1 14.8 %collective-permute-done.31 = bf16[1,256,768]{2,1,0:T(8,128)(2,1)} collective-permute-done((bf16[1,256,768]{2,1,0:T(8,128)(2,1)}, bf16[1,256,768]{2,1,0:T(8,128)(2,1)}, u32[]{:S(2)}, u32[]{:S(2)}) %collective-permute-start.31) | collective-permute-done | bytes 393248 | tf_op jit(solution)/shard_map/ppermute | solution.py:174
  360.3 1.5 collective-permute-start.33
  362.4 3.4 collective-permute-start.34
  366.0 1.6 collective-permute-start.38
  368.4 1.7 collective-permute-done.38
  370.2 5.1 %collective-permute-done.34 = bf16[1,256,768]{2,1,0:T(8,128)(2,1)S(1)} collective-permute-done((bf16[1,256,768]{2,1,0:T(8,128)(2,1)S(1)}, bf16[1,256,768]{2,1,0:T(8,128)(2,1)S(1)}, u32[]{:S(2)}, u32[]{:S(2)}) %collective-permute-start.34) | collective-permute-done | bytes 393248 | tf_op jit(solution)/shard_map/ppermute | solution.py:174
  375.3 7.5 %collective-permute-done.35 = bf16[1,256,768]{2,1,0:T(8,128)(2,1)S(1)} collective-permute-done((bf16[1,256,768]{2,1,0:T(8,128)(2,1)S(1)}, bf16[1,256,768]{2,1,0:T(8,128)(2,1)S(1)}, u32[]{:S(2)}, u32[]{:S(2)}) %collective-permute-start.35) | collective-permute-done | bytes 393248 | tf_op jit(solution)/shard_map/ppermute | solution.py:174
  383.7 1.8 collective-permute-start.41
  386.1 1.9 collective-permute-start.39
  388.0 4.3 %fusion.36 = (f32[4,256,768]{2,1,0:T(8,128)}, bf16[4,256,768]{2,1,0:T(8,128)(2,1)}) fusion(s32[4]{0:T(128)S(1)} %get-tuple-element.421, s32[4]{0:T(128)S(1)} %get-tuple-element.422, pred[4]{0:T(512)(128)(4,1)S(1)} %compare_and_fusion, bf16[256,768]{1,0:T(8,128)(2,1)S(1)} %bitcast.183, bf16[256,768]{1,0:T(8,128)(2,1)S(1)} %bitcast.185, ...), kind=kLoop, calls=%fused_computation.72 | loop fusion | flops 8650752 | bytes 7864356 | tf_op jit(solution)/shard_map/convert_element_type | solution.py:512
  393.1 5.7 %collective-permute-done.40 = bf16[117,768]{1,0:T(8,128)(2,1)S(1)} collective-permute-done((bf16[117,768]{1,0:T(8,128)(2,1)S(1)}, bf16[117,768]{1,0:T(8,128)(2,1)S(1)}, u32[]{:S(2)}, u32[]{:S(2)}) %collective-permute-start.40) | collective-permute-done | bytes 179744 | tf_op jit(solution)/shard_map/ppermute | solution.py:174
  (342 shorter events, 81.8 us)
Async XLA Ops:
  7.2 32.8 %copy-start.34 = (bf16[192,96]{1,0:T(8,128)(2,1)S(1)}, bf16[192,96]{1,0:T(8,128)(2,1)}, u32[]{:S(2)}) copy-start(bf16[192,96]{1,0:T(8,128)(2,1)} %param.27) | copy-start | bytes 110596
  7.2 154.0 %all-gather.2.cloned.1.call-start = ((), (), s32[]{:S(2)}) async-start(), calls=%async_computation.1 | async-start | bytes 10616832 | tf_op jit(solution)/shard_map/all_gather | solution.py:392
  13.2 16.0 %collective-permute-start = (bf16[99,768]{0,1:T(8,128)(2,1)S(1)}, bf16[99,768]{0,1:T(8,128)(2,1)S(1)}, u32[]{:S(2)}, u32[]{:S(2)}) collective-permute-start(bf16[99,768]{0,1:T(8,128)(2,1)S(1)} %fusion.95), channel_id=1, source_target_pairs={{0,1},{1,2},{2,3},{3,0},{4,5},{5,6},{6,7},{7,4},{8,9},{9,10},{10,1... | collective-permute-start | bytes 456200 | tf_op jit(solution)/shard_map/ppermute | solution.py:156
  16.3 15.5 %collective-permute-start.1 = (bf16[99,768]{0,1:T(8,128)(2,1)S(1)}, bf16[99,768]{0,1:T(8,128)(2,1)S(1)}, u32[]{:S(2)}, u32[]{:S(2)}) collective-permute-start(bf16[99,768]{0,1:T(8,128)(2,1)S(1)} %fusion.95), channel_id=1, source_target_pairs={{0,2},{1,3},{2,0},{3,1},{4,6},{5,7},{6,4},{7,5},{8,10},{9,11},{10,... | collective-permute-start | bytes 456200 | tf_op jit(solution)/shard_map/ppermute | solution.py:156
  18.9 12.9 %collective-permute-start.2 = (bf16[99,768]{0,1:T(8,128)(2,1)S(1)}, bf16[99,768]{0,1:T(8,128)(2,1)S(1)}, u32[]{:S(2)}, u32[]{:S(2)}) collective-permute-start(bf16[99,768]{0,1:T(8,128)(2,1)S(1)} %fusion.95), channel_id=1, source_target_pairs={{0,3},{1,0},{2,1},{3,2},{4,7},{5,4},{6,5},{7,6},{8,11},{9,8},{10,9... | collective-permute-start | bytes 456200 | tf_op jit(solution)/shard_map/ppermute | solution.py:156
  32.7 13.8 %collective-permute-start.5 = (bf16[96,1536]{1,0:T(8,128)(2,1)S(1)}, bf16[96,1536]{1,0:T(8,128)(2,1)S(1)}, u32[]{:S(2)}, u32[]{:S(2)}) collective-permute-start(bf16[96,1536]{1,0:T(8,128)(2,1)S(1)} %pad_maximum_fusion.11), channel_id=1, source_target_pairs={{0,1},{1,2},{2,3},{3,0},{4,5},{5,6},{6,7},{7,4},{8,9},{9,10},{10,1... | collective-permute-start | bytes 884744 | tf_op jit(solution)/shard_map/ppermute | solution.py:156
  37.4 20.0 %collective-permute-start.6 = (bf16[96,1536]{1,0:T(8,128)(2,1)S(1)}, bf16[96,1536]{1,0:T(8,128)(2,1)S(1)}, u32[]{:S(2)}, u32[]{:S(2)}) collective-permute-start(bf16[96,1536]{1,0:T(8,128)(2,1)S(1)} %pad_maximum_fusion.11), channel_id=1, source_target_pairs={{0,2},{1,3},{2,0},{3,1},{4,6},{5,7},{6,4},{7,5},{8,10},{9,11},{10,... | collective-permute-start | bytes 884744 | tf_op jit(solution)/shard_map/ppermute | solution.py:156
  39.1 18.4 %collective-permute-start.7 = (bf16[96,1536]{1,0:T(8,128)(2,1)S(1)}, bf16[96,1536]{1,0:T(8,128)(2,1)}, u32[]{:S(2)}, u32[]{:S(2)}) collective-permute-start(bf16[96,1536]{1,0:T(8,128)(2,1)S(1)} %pad_maximum_fusion.11), channel_id=1, source_target_pairs={{0,3},{1,0},{2,1},{3,2},{4,7},{5,4},{6,5},{7,6},{8,11},{9,8},{10,9... | collective-permute-start | bytes 884744 | tf_op jit(solution)/shard_map/ppermute | solution.py:156
  40.1 17.4 %copy-start.21 = (bf16[96,1536]{0,1:T(8,128)(2,1)}, bf16[96,1536]{0,1:T(8,128)(2,1)S(1)}, u32[]{:S(2)}) copy-start(bf16[96,1536]{0,1:T(8,128)(2,1)S(1)} %get-tuple-element.377) | copy-start | bytes 884740
  40.1 10.5 %collective-permute-start.3 = (bf16[96,1536]{0,1:T(8,128)(2,1)S(1)}, bf16[96,1536]{0,1:T(8,128)(2,1)S(1)}, u32[]{:S(2)}, u32[]{:S(2)}) collective-permute-start(bf16[96,1536]{0,1:T(8,128)(2,1)S(1)} %get-tuple-element.378), channel_id=1, source_target_pairs={{0,8},{4,12},{8,0},{12,4},{16,24},{20,28},{24,16},{28,20},{1,9},{5... | collective-permute-start | bytes 884744 | tf_op jit(solution)/shard_map/ppermute | solution.py:189
  41.6 10.2 %collective-permute-start.4 = (bf16[96,1536]{0,1:T(8,128)(2,1)S(1)}, bf16[96,1536]{0,1:T(8,128)(2,1)S(1)}, u32[]{:S(2)}, u32[]{:S(2)}) collective-permute-start(bf16[96,1536]{0,1:T(8,128)(2,1)S(1)} %get-tuple-element.377), channel_id=1, source_target_pairs={{0,16},{4,20},{8,24},{12,28},{16,0},{20,4},{24,8},{28,12},{1,17},{... | collective-permute-start | bytes 884744 | tf_op jit(solution)/shard_map/ppermute | solution.py:189
  60.4 222.5 %reduce-scatter.2.cloned.1.call-start = ((), (), s32[]{:S(2)}) async-start(), calls=%async_computation.2 | async-start | bytes 5308416 | tf_op jit(solution)/shard_map/reduce_scatter | solution.py:424
  63.2 38.8 %collective-permute-start.9 = (bf16[2,96,1536]{2,1,0:T(8,128)(2,1)S(1)}, bf16[2,96,1536]{2,1,0:T(8,128)(2,1)}, u32[]{:S(2)}, u32[]{:S(2)}) collective-permute-start(bf16[2,96,1536]{2,1,0:T(8,128)(2,1)S(1)} %broadcast_select_fusion.2), channel_id=1, source_target_pairs={{0,8},{4,12},{8,0},{12,4},{16,24},{20,28},{24,16},{28,20},{1,9},{5... | collective-permute-start | bytes 1769480 | tf_op jit(solution)/shard_map/ppermute | solution.py:189
  66.1 36.0 %collective-permute-start.8 = (bf16[2,96,1536]{2,1,0:T(8,128)(2,1)S(1)}, bf16[2,96,1536]{2,1,0:T(8,128)(2,1)}, u32[]{:S(2)}, u32[]{:S(2)}) collective-permute-start(bf16[2,96,1536]{2,1,0:T(8,128)(2,1)S(1)} %broadcast_select_fusion.3), channel_id=1, source_target_pairs={{0,16},{4,20},{8,24},{12,28},{16,0},{20,4},{24,8},{28,12},{1,17},{... | collective-permute-start | bytes 1769480 | tf_op jit(solution)/shard_map/ppermute | solution.py:189
  68.5 18.6 %collective-permute-start.10 = (bf16[1,256,768]{2,1,0:T(8,128)(2,1)S(1)}, bf16[1,256,768]{2,1,0:T(8,128)(2,1)S(1)}, u32[]{:S(2)}, u32[]{:S(2)}) collective-permute-start(bf16[1,256,768]{2,1,0:T(8,128)(2,1)S(1)} %get-tuple-element.343), channel_id=1, source_target_pairs={{0,1},{1,2},{2,3},{3,0},{4,5},{5,6},{6,7},{7,4},{8,9},{9,10},{10,1... | collective-permute-start | bytes 1179656 | tf_op jit(solution)/shard_map/ppermute | solution.py:165
  75.4 26.6 %collective-permute-start.11 = (bf16[1,256,768]{2,1,0:T(8,128)(2,1)S(1)}, bf16[1,256,768]{2,1,0:T(8,128)(2,1)S(1)}, u32[]{:S(2)}, u32[]{:S(2)}) collective-permute-start(bf16[1,256,768]{2,1,0:T(8,128)(2,1)S(1)} %get-tuple-element.342), channel_id=1, source_target_pairs={{0,2},{1,3},{2,0},{3,1},{4,6},{5,7},{6,4},{7,5},{8,10},{9,11},{10,... | collective-permute-start | bytes 1179656 | tf_op jit(solution)/shard_map/ppermute | solution.py:165
  104.9 12.2 %copy-start.27 = (bf16[1,256,768]{2,1,0:T(8,128)(2,1)S(1)}, bf16[1,256,768]{2,1,0:T(8,128)(2,1)}, u32[]{:S(2)}) copy-start(bf16[1,256,768]{2,1,0:T(8,128)(2,1)} %copy-done.26) | copy-start | bytes 1179652
  105.2 11.9 %collective-permute-start.12 = (bf16[2,2,96,3072]{3,2,1,0:T(8,128)(2,1)S(1)}, bf16[2,2,96,3072]{3,2,1,0:T(8,128)(2,1)}, u32[]{:S(2)}, u32[]{:S(2)}) collective-permute-start(bf16[2,2,96,3072]{3,2,1,0:T(8,128)(2,1)S(1)} %pad_maximum_fusion.1), channel_id=1, source_target_pairs={{0,4},{4,0},{8,12},{12,8},{16,20},{20,16},{24,28},{28,24},{1,5},{5... | collective-permute-start | bytes 7077896 | tf_op jit(solution)/shard_map/ppermute | solution.py:189
  105.3 11.8 %collective-permute-start.13 = (bf16[1,256,768]{2,1,0:T(8,128)(2,1)}, bf16[1,256,768]{2,1,0:T(8,128)(2,1)}, u32[]{:S(2)}, u32[]{:S(2)}) collective-permute-start(bf16[1,256,768]{2,1,0:T(8,128)(2,1)} %get-tuple-element.341), channel_id=1, source_target_pairs={{0,3},{1,0},{2,1},{3,2},{4,7},{5,4},{6,5},{7,6},{8,11},{9,8},{10,9... | collective-permute-start | bytes 1179656 | tf_op jit(solution)/shard_map/ppermute | solution.py:165
  108.2 10.0 %copy-start.16 = (bf16[4,256,768]{2,1,0:T(8,128)(2,1)S(1)}, bf16[4,256,768]{2,1,0:T(8,128)(2,1)}, u32[]{:S(2)}) copy-start(bf16[4,256,768]{2,1,0:T(8,128)(2,1)} %param.37) | copy-start | bytes 4718596
  108.2 15.1 %copy-start.40 = (pred[768]{0:T(1024)(128)(4,1)S(1)}, pred[768]{0:T(1024)(128)(4,1)}, u32[]{:S(2)}) copy-start(pred[768]{0:T(1024)(128)(4,1)} %iota.68) | copy-start | bytes 2308
  118.2 12.4 %copy-start.11 = (bf16[1024,768]{1,0:T(8,128)(2,1)}, bf16[1024,768]{1,0:T(8,128)(2,1)S(1)}, u32[]{:S(2)}) copy-start(bf16[1024,768]{1,0:T(8,128)(2,1)S(1)} %maximum_bitcast_fusion) | copy-start | bytes 4718596
  119.3 36.8 %collective-permute-start.14 = (bf16[1,256,768]{2,1,0:T(8,128)(2,1)S(1)}, bf16[1,256,768]{2,1,0:T(8,128)(2,1)S(1)}, u32[]{:S(2)}, u32[]{:S(2)}) collective-permute-start(bf16[1,256,768]{2,1,0:T(8,128)(2,1)S(1)} %get-tuple-element.340), channel_id=1, source_target_pairs={{0,2},{1,3},{2,0},{3,1},{4,6},{5,7},{6,4},{7,5},{8,10},{9,11},{10,... | collective-permute-start | bytes 1179656 | tf_op jit(solution)/shard_map/ppermute | solution.py:165
  119.3 53.0 %collective-permute-start.15 = (bf16[1,256,768]{2,1,0:T(8,128)(2,1)}, bf16[1,256,768]{2,1,0:T(8,128)(2,1)}, u32[]{:S(2)}, u32[]{:S(2)}) collective-permute-start(bf16[1,256,768]{2,1,0:T(8,128)(2,1)} %get-tuple-element.339), channel_id=1, source_target_pairs={{0,1},{1,2},{2,3},{3,0},{4,5},{5,6},{6,7},{7,4},{8,9},{9,10},{10,1... | collective-permute-start | bytes 1179656 | tf_op jit(solution)/shard_map/ppermute | solution.py:165
  122.8 49.5 %collective-permute-start.16 = (bf16[1,256,768]{2,1,0:T(8,128)(2,1)}, bf16[1,256,768]{2,1,0:T(8,128)(2,1)}, u32[]{:S(2)}, u32[]{:S(2)}) collective-permute-start(bf16[1,256,768]{2,1,0:T(8,128)(2,1)} %get-tuple-element.338), channel_id=1, source_target_pairs={{0,3},{1,0},{2,1},{3,2},{4,7},{5,4},{6,5},{7,6},{8,11},{9,8},{10,9... | collective-permute-start | bytes 1179656 | tf_op jit(solution)/shard_map/ppermute | solution.py:165
  133.2 23.7 %copy-start.46 = (f32[768]{0:T(1024)S(1)}, f32[768]{0:T(1024)}, u32[]{:S(2)}) copy-start(f32[768]{0:T(1024)} %convert_element_type.269) | copy-start | bytes 9220
  161.2 11.2 %copy-start.35 = (f32[1024]{0:T(1024)}, f32[1024]{0:T(1024)S(1)}, u32[]{:S(2)}) copy-start(f32[1024]{0:T(1024)S(1)} %add_rsqrt_fusion.1) | copy-start | bytes 12292
  161.2 11.2 %copy-start.43 = (f32[768]{0:T(1024)S(1)}, f32[768]{0:T(1024)}, u32[]{:S(2)}) copy-start(f32[768]{0:T(1024)} %convert_element_type.271) | copy-start | bytes 9220
  161.2 11.1 %copy-start.45 = (f32[768]{0:T(1024)S(1)}, f32[768]{0:T(1024)}, u32[]{:S(2)}) copy-start(f32[768]{0:T(1024)} %convert_element_type.272) | copy-start | bytes 9220
  161.2 11.1 %copy-start.50 = (bf16[768,6144]{1,0:T(8,128)(2,1)S(1)}, bf16[768,6144]{1,0:T(8,128)(2,1)}, u32[]{:S(2)}) copy-start(bf16[768,6144]{1,0:T(8,128)(2,1)} %all-gather.2.cloned.1.call-done) | copy-start | bytes 28311556
  196.3 13.7 %copy-start.36 = (f32[1024]{0:T(1024)S(1)}, f32[1024]{0:T(1024)}, u32[]{:S(2)}) copy-start(f32[1024]{0:T(1024)} %copy-done.35) | copy-start | bytes 12292
  196.3 13.7 %copy-start.44 = (f32[768]{0:T(1024)S(1)}, f32[768]{0:T(1024)}, u32[]{:S(2)}) copy-start(f32[768]{0:T(1024)} %convert_element_type.271) | copy-start | bytes 9220
  217.4 22.0 %collective-permute-start.17 = (bf16[2,2,96,3072]{3,2,0,1:T(8,128)(2,1)S(1)}, bf16[2,2,96,3072]{3,2,0,1:T(8,128)(2,1)S(1)}, u32[]{:S(2)}, u32[]{:S(2)}) collective-permute-start(bf16[2,2,96,3072]{3,2,0,1:T(8,128)(2,1)S(1)} %bitcast.181), channel_id=1, source_target_pairs={{0,4},{4,0},{8,12},{12,8},{16,20},{20,16},{24,28},{28,24},{1,5},{5... | collective-permute-start | bytes 7077896 | tf_op jit(solution)/shard_map/ppermute | solution.py:189
  219.7 19.7 %collective-permute-start.18 = (bf16[1,256,768]{2,1,0:T(8,128)(2,1)S(1)}, bf16[1,256,768]{2,1,0:T(8,128)(2,1)S(1)}, u32[]{:S(2)}, u32[]{:S(2)}) collective-permute-start(bf16[1,256,768]{2,1,0:T(8,128)(2,1)S(1)} %get-tuple-element.336), channel_id=1, source_target_pairs={{0,2},{1,3},{2,0},{3,1},{4,6},{5,7},{6,4},{7,5},{8,10},{9,11},{10,... | collective-permute-start | bytes 1179656 | tf_op jit(solution)/shard_map/ppermute | solution.py:174
  232.5 10.6 %copy-start.1 = (f32[1024,768]{1,0:T(8,128)}, f32[1024,768]{1,0:T(8,128)S(1)}, u32[]{:S(2)}) copy-start(f32[1024,768]{1,0:T(8,128)S(1)} %get-tuple-element.319) | copy-start | bytes 9437188
  241.4 17.8 %collective-permute-start.20 = (bf16[2,96,1536]{2,1,0:T(8,128)(2,1)}, bf16[2,96,1536]{2,1,0:T(8,128)(2,1)}, u32[]{:S(2)}, u32[]{:S(2)}) collective-permute-start(bf16[2,96,1536]{2,1,0:T(8,128)(2,1)} %dynamic-slice_bitcast_fusion.3), channel_id=1, source_target_pairs={{0,8},{4,12},{8,0},{12,4},{16,24},{20,28},{24,16},{28,20},{1,9},{5... | collective-permute-start | bytes 1769480 | tf_op jit(solution)/shard_map/ppermute | solution.py:189
  242.7 16.5 %collective-permute-start.19 = (bf16[2,96,1536]{2,1,0:T(8,128)(2,1)}, bf16[2,96,1536]{2,1,0:T(8,128)(2,1)}, u32[]{:S(2)}, u32[]{:S(2)}) collective-permute-start(bf16[2,96,1536]{2,1,0:T(8,128)(2,1)} %dynamic-slice_bitcast_fusion.4), channel_id=1, source_target_pairs={{0,16},{4,20},{8,24},{12,28},{16,0},{20,4},{24,8},{28,12},{1,17},{... | collective-permute-start | bytes 1769480 | tf_op jit(solution)/shard_map/ppermute | solution.py:189
  253.5 29.4 %collective-permute-start.23 = (bf16[1,256,768]{2,1,0:T(8,128)(2,1)}, bf16[1,256,768]{2,1,0:T(8,128)(2,1)}, u32[]{:S(2)}, u32[]{:S(2)}) collective-permute-start(bf16[1,256,768]{2,1,0:T(8,128)(2,1)} %get-tuple-element.176), channel_id=1, source_target_pairs={{0,3},{1,0},{2,1},{3,2},{4,7},{5,4},{6,5},{7,6},{8,11},{9,8},{10,9... | collective-permute-start | bytes 1179656 | tf_op jit(solution)/shard_map/ppermute | solution.py:174
  254.9 28.0 %collective-permute-start.24 = (bf16[1,256,768]{2,1,0:T(8,128)(2,1)}, bf16[1,256,768]{2,1,0:T(8,128)(2,1)}, u32[]{:S(2)}, u32[]{:S(2)}) collective-permute-start(bf16[1,256,768]{2,1,0:T(8,128)(2,1)} %get-tuple-element.178), channel_id=1, source_target_pairs={{0,1},{1,2},{2,3},{3,0},{4,5},{5,6},{6,7},{7,4},{8,9},{9,10},{10,1... | collective-permute-start | bytes 1179656 | tf_op jit(solution)/shard_map/ppermute | solution.py:174
  261.6 21.0 %collective-permute-start.22 = (bf16[96,1536]{1,0:T(8,128)(2,1)S(1)}, bf16[96,1536]{1,0:T(8,128)(2,1)S(1)}, u32[]{:S(2)}, u32[]{:S(2)}) collective-permute-start(bf16[96,1536]{1,0:T(8,128)(2,1)S(1)} %dynamic-slice_bitcast_fusion.7), channel_id=1, source_target_pairs={{0,16},{4,20},{8,24},{12,28},{16,0},{20,4},{24,8},{28,12},{1,17},{... | collective-permute-start | bytes 884744 | tf_op jit(solution)/shard_map/ppermute | solution.py:189
  263.2 19.5 %collective-permute-start.21 = (bf16[96,1536]{1,0:T(8,128)(2,1)S(1)}, bf16[96,1536]{1,0:T(8,128)(2,1)S(1)}, u32[]{:S(2)}, u32[]{:S(2)}) collective-permute-start(bf16[96,1536]{1,0:T(8,128)(2,1)S(1)} %dynamic-slice_bitcast_fusion.8), channel_id=1, source_target_pairs={{0,8},{4,12},{8,0},{12,4},{16,24},{20,28},{24,16},{28,20},{1,9},{5... | collective-permute-start | bytes 884744 | tf_op jit(solution)/shard_map/ppermute | solution.py:189
  284.2 25.4 %collective-permute-start.27 = (bf16[96,1536]{1,0:T(8,128)(2,1)S(1)}, bf16[96,1536]{1,0:T(8,128)(2,1)S(1)}, u32[]{:S(2)}, u32[]{:S(2)}) collective-permute-start(bf16[96,1536]{1,0:T(8,128)(2,1)S(1)} %pad_maximum_fusion.15), channel_id=1, source_target_pairs={{0,1},{1,2},{2,3},{3,0},{4,5},{5,6},{6,7},{7,4},{8,9},{9,10},{10,1... | collective-permute-start | bytes 884744 | tf_op jit(solution)/shard_map/ppermute | solution.py:174
  286.5 23.1 %collective-permute-start.26 = (bf16[96,1536]{1,0:T(8,128)(2,1)}, bf16[96,1536]{1,0:T(8,128)(2,1)S(1)}, u32[]{:S(2)}, u32[]{:S(2)}) collective-permute-start(bf16[96,1536]{1,0:T(8,128)(2,1)} %pad_maximum_fusion.14), channel_id=1, source_target_pairs={{0,2},{1,3},{2,0},{3,1},{4,6},{5,7},{6,4},{7,5},{8,10},{9,11},{10,... | collective-permute-start | bytes 884744 | tf_op jit(solution)/shard_map/ppermute | solution.py:174
  289.6 20.0 %copy-start.12 = (bf16[1024,768]{1,0:T(8,128)(2,1)S(1)}, bf16[1024,768]{1,0:T(8,128)(2,1)}, u32[]{:S(2)}) copy-start(bf16[1024,768]{1,0:T(8,128)(2,1)} %copy-done.11) | copy-start | bytes 4718596
  289.6 20.0 %collective-permute-start.25 = (bf16[96,1536]{1,0:T(8,128)(2,1)}, bf16[96,1536]{1,0:T(8,128)(2,1)S(1)}, u32[]{:S(2)}, u32[]{:S(2)}) collective-permute-start(bf16[96,1536]{1,0:T(8,128)(2,1)} %pad_maximum_fusion.13), channel_id=1, source_target_pairs={{0,3},{1,0},{2,1},{3,2},{4,7},{5,4},{6,5},{7,6},{8,11},{9,8},{10,9... | collective-permute-start | bytes 884744 | tf_op jit(solution)/shard_map/ppermute | solution.py:174
  316.7 11.0 %slice-start.2 = ((s8[4718592]{0:T(1024)(128)(4,1)}), s8[524288]{0:T(1024)(128)(4,1)S(1)}, s32[]{:S(2)}) async-start(s8[4718592]{0:T(1024)(128)(4,1)} %bitcast.176), calls=%async_computation.5 | async-start | bytes 1048576
  318.2 13.4 %collective-permute-start.28 = (bf16[2,2,96,3072]{3,2,1,0:T(8,128)(2,1)}, bf16[2,2,96,3072]{3,2,1,0:T(8,128)(2,1)S(1)}, u32[]{:S(2)}, u32[]{:S(2)}) collective-permute-start(bf16[2,2,96,3072]{3,2,1,0:T(8,128)(2,1)} %dynamic-slice_bitcast_fusion), channel_id=1, source_target_pairs={{0,4},{4,0},{8,12},{12,8},{16,20},{20,16},{24,28},{28,24},{1,5},{5... | collective-permute-start | bytes 7077896 | tf_op jit(solution)/shard_map/ppermute | solution.py:189
  333.7 24.2 %collective-permute-start.30 = (bf16[2,96,1536]{2,1,0:T(8,128)(2,1)}, bf16[2,96,1536]{2,1,0:T(8,128)(2,1)}, u32[]{:S(2)}, u32[]{:S(2)}) collective-permute-start(bf16[2,96,1536]{2,1,0:T(8,128)(2,1)} %dynamic-slice_bitcast_fusion.1), channel_id=1, source_target_pairs={{0,8},{4,12},{8,0},{12,4},{16,24},{20,28},{24,16},{28,20},{1,9},{5... | collective-permute-start | bytes 1769480 | tf_op jit(solution)/shard_map/ppermute | solution.py:189
  335.1 22.8 %collective-permute-start.29 = (bf16[2,96,1536]{2,1,0:T(8,128)(2,1)}, bf16[2,96,1536]{2,1,0:T(8,128)(2,1)}, u32[]{:S(2)}, u32[]{:S(2)}) collective-permute-start(bf16[2,96,1536]{2,1,0:T(8,128)(2,1)} %dynamic-slice_bitcast_fusion.2), channel_id=1, source_target_pairs={{0,16},{4,20},{8,24},{12,28},{16,0},{20,4},{24,8},{28,12},{1,17},{... | collective-permute-start | bytes 1769480 | tf_op jit(solution)/shard_map/ppermute | solution.py:189
  337.6 20.2 %collective-permute-start.31 = (bf16[1,256,768]{2,1,0:T(8,128)(2,1)}, bf16[1,256,768]{2,1,0:T(8,128)(2,1)}, u32[]{:S(2)}, u32[]{:S(2)}) collective-permute-start(bf16[1,256,768]{2,1,0:T(8,128)(2,1)} %get-tuple-element.332), channel_id=1, source_target_pairs={{0,2},{1,3},{2,0},{3,1},{4,6},{5,7},{6,4},{7,5},{8,10},{9,11},{10,... | collective-permute-start | bytes 1179656 | tf_op jit(solution)/shard_map/ppermute | solution.py:174
  340.4 1.2 collective-permute-start.36
  340.4 22.0 %copy-start.25 = (bf16[1,256,768]{2,1,0:T(8,128)(2,1)S(1)}, bf16[1,256,768]{2,1,0:T(8,128)(2,1)}, u32[]{:S(2)}) copy-start(bf16[1,256,768]{2,1,0:T(8,128)(2,1)} %get-tuple-element.213) | copy-start | bytes 1179652
  340.4 25.4 %copy-start.24 = (bf16[1,256,768]{2,1,0:T(8,128)(2,1)S(1)}, bf16[1,256,768]{2,1,0:T(8,128)(2,1)}, u32[]{:S(2)}) copy-start(bf16[1,256,768]{2,1,0:T(8,128)(2,1)} %get-tuple-element.215) | copy-start | bytes 1179652
  340.4 25.4 %copy-start.31 = (bf16[96,1536]{1,0:T(8,128)(2,1)S(1)}, bf16[96,1536]{1,0:T(8,128)(2,1)}, u32[]{:S(2)}) copy-start(bf16[96,1536]{1,0:T(8,128)(2,1)} %copy-done.30) | copy-start | bytes 884740
  340.4 25.4 %copy-start.33 = (bf16[96,1536]{1,0:T(8,128)(2,1)S(1)}, bf16[96,1536]{1,0:T(8,128)(2,1)}, u32[]{:S(2)}) copy-start(bf16[96,1536]{1,0:T(8,128)(2,1)} %copy-done.32) | copy-start | bytes 884740
  341.6 24.4 %collective-permute-start.37 = (f32[12,768]{1,0:T(8,128)S(1)}, f32[12,768]{1,0:T(8,128)S(1)}, u32[]{:S(2)}, u32[]{:S(2)}) collective-permute-start(f32[12,768]{1,0:T(8,128)S(1)} %add.418), channel_id=1, source_target_pairs={{0,8},{4,12},{8,0},{12,4},{16,24},{20,28},{24,16},{28,20},{1,9},{5... | collective-permute-start | bytes 110600 | tf_op jit(solution)/shard_map/ppermute | solution.py:189
  360.3 9.9 %collective-permute-start.33 = (bf16[96,1536]{1,0:T(8,128)(2,1)S(1)}, bf16[96,1536]{1,0:T(8,128)(2,1)S(1)}, u32[]{:S(2)}, u32[]{:S(2)}) collective-permute-start(bf16[96,1536]{1,0:T(8,128)(2,1)S(1)} %dynamic-slice_bitcast_fusion.5), channel_id=1, source_target_pairs={{0,16},{4,20},{8,24},{12,28},{16,0},{20,4},{24,8},{28,12},{1,17},{... | collective-permute-start | bytes 884744 | tf_op jit(solution)/shard_map/ppermute | solution.py:189
  361.8 8.4 %collective-permute-start.32 = (bf16[96,1536]{1,0:T(8,128)(2,1)S(1)}, bf16[96,1536]{1,0:T(8,128)(2,1)S(1)}, u32[]{:S(2)}, u32[]{:S(2)}) collective-permute-start(bf16[96,1536]{1,0:T(8,128)(2,1)S(1)} %dynamic-slice_bitcast_fusion.6), channel_id=1, source_target_pairs={{0,8},{4,12},{8,0},{12,4},{16,24},{20,28},{24,16},{28,20},{1,9},{5... | collective-permute-start | bytes 884744 | tf_op jit(solution)/shard_map/ppermute | solution.py:189
  362.4 12.9 %collective-permute-start.34 = (bf16[1,256,768]{2,1,0:T(8,128)(2,1)S(1)}, bf16[1,256,768]{2,1,0:T(8,128)(2,1)S(1)}, u32[]{:S(2)}, u32[]{:S(2)}) collective-permute-start(bf16[1,256,768]{2,1,0:T(8,128)(2,1)S(1)} %copy-done.25), channel_id=1, source_target_pairs={{0,3},{1,0},{2,1},{3,2},{4,7},{5,4},{6,5},{7,6},{8,11},{9,8},{10,9... | collective-permute-start | bytes 1179656 | tf_op jit(solution)/shard_map/ppermute | solution.py:174
  365.8 17.0 %collective-permute-start.35 = (bf16[1,256,768]{2,1,0:T(8,128)(2,1)S(1)}, bf16[1,256,768]{2,1,0:T(8,128)(2,1)S(1)}, u32[]{:S(2)}, u32[]{:S(2)}) collective-permute-start(bf16[1,256,768]{2,1,0:T(8,128)(2,1)S(1)} %copy-done.24), channel_id=1, source_target_pairs={{0,1},{1,2},{2,3},{3,0},{4,5},{5,6},{6,7},{7,4},{8,9},{9,10},{10,1... | collective-permute-start | bytes 1179656 | tf_op jit(solution)/shard_map/ppermute | solution.py:174
  366.0 4.2 %collective-permute-start.38 = (f32[12,768]{1,0:T(8,128)S(1)}, f32[12,768]{1,0:T(8,128)S(1)}, u32[]{:S(2)}, u32[]{:S(2)}) collective-permute-start(f32[12,768]{1,0:T(8,128)S(1)} %add.419), channel_id=1, source_target_pairs={{0,16},{4,20},{8,24},{12,28},{16,0},{20,4},{24,8},{28,12},{1,17},{... | collective-permute-start | bytes 110600 | tf_op jit(solution)/shard_map/ppermute | solution.py:189
  383.7 9.4 %collective-permute-start.41 = (bf16[117,768]{1,0:T(8,128)(2,1)S(1)}, bf16[117,768]{1,0:T(8,128)(2,1)S(1)}, u32[]{:S(2)}, u32[]{:S(2)}) collective-permute-start(bf16[117,768]{1,0:T(8,128)(2,1)S(1)} %get-tuple-element.391), channel_id=1, source_target_pairs={{0,1},{1,2},{2,3},{3,0},{4,5},{5,6},{6,7},{7,4},{8,9},{9,10},{10,1... | collective-permute-start | bytes 539144 | tf_op jit(solution)/shard_map/ppermute | solution.py:174
  385.5 13.3 %collective-permute-start.40 = (bf16[117,768]{1,0:T(8,128)(2,1)S(1)}, bf16[117,768]{1,0:T(8,128)(2,1)S(1)}, u32[]{:S(2)}, u32[]{:S(2)}) collective-permute-start(bf16[117,768]{1,0:T(8,128)(2,1)S(1)} %get-tuple-element.390), channel_id=1, source_target_pairs={{0,2},{1,3},{2,0},{3,1},{4,6},{5,7},{6,4},{7,5},{8,10},{9,11},{10,... | collective-permute-start | bytes 539144 | tf_op jit(solution)/shard_map/ppermute | solution.py:174
  386.1 12.7 %collective-permute-start.39 = (bf16[117,768]{1,0:T(8,128)(2,1)S(1)}, bf16[117,768]{1,0:T(8,128)(2,1)S(1)}, u32[]{:S(2)}, u32[]{:S(2)}) collective-permute-start(bf16[117,768]{1,0:T(8,128)(2,1)S(1)} %get-tuple-element.389), channel_id=1, source_target_pairs={{0,3},{1,0},{2,1},{3,2},{4,7},{5,4},{6,5},{7,6},{8,11},{9,8},{10,9... | collective-permute-start | bytes 539144 | tf_op jit(solution)/shard_map/ppermute | solution.py:174
  (38 other events, 131.7 us)
Sparse Core Ops, SparseCore 0:
  60.5 72.7 all-gather.1
  196.4 54.0 reduce-scatter.1
